TPU v7x, 32 devices: a whole 2x2x4 slice. The times are simulated.
32 devices in a mesh: dp: 4 (over y, core), fsdp: 8 (over z, x).
Axes of the slice: x: 2, y: 2, z: 4, core: 2. Of those that a mesh axis runs over, the one named last changes fastest.
Arguments:
- tokens: bfloat16 [64, 1024, 768], P(None, ('dp', 'fsdp')), may hold values from -6 to 6
- cotangent: bfloat16 [64, 1024, 768], P(None, ('dp', 'fsdp')), may hold values from -6 to 6
- lengths: int32 [64], replicated, may hold values from 64 to 1024, as said below
- permutation: int32 [64], replicated, may hold values from 0 to 63, as said below
- q_weight: bfloat16 [768, 192], P(('dp', 'fsdp')), may hold values from -0.625 to 0.625
- q_bias: bfloat16 [768], P(('dp', 'fsdp')), may hold values from -4 to 4
- k_weight: bfloat16 [768, 192], P(('dp', 'fsdp')), may hold values from -0.625 to 0.625
- v_weight: bfloat16 [768, 192], P(('dp', 'fsdp')), may hold values from -0.4375 to 0.4375
- v_bias: bfloat16 [768], P(('dp', 'fsdp')), may hold values from -4 to 4
- o_weight: bfloat16 [768, 768], P(('dp', 'fsdp')), may hold values from -0.625 to 0.625
- o_bias: bfloat16 [768], P(('dp', 'fsdp')), may hold values from -3 to 3
- norm1_gain: bfloat16 [768], P(('dp', 'fsdp')), may hold values from 0.25 to 1.75
- norm1_bias: bfloat16 [768], P(('dp', 'fsdp')), may hold values from -3 to 3
- up_weight: bfloat16 [3072, 192], P(('dp', 'fsdp')), may hold values from -0.4375 to 0.4375
- up_bias: bfloat16 [3072], P(('dp', 'fsdp')), may hold values from -3 to 3
- down_weight: bfloat16 [768, 768], P(('dp', 'fsdp')), may hold values from -0.21875 to 0.21875
- down_bias: bfloat16 [768], P(('dp', 'fsdp')), may hold values from -3 to 3
- norm2_gain: bfloat16 [768], P(('dp', 'fsdp')), may hold values from 0.25 to 1.75
- norm2_bias: bfloat16 [768], P(('dp', 'fsdp')), may hold values from -3 to 3
Outputs:
- output: bfloat16 [64, 1024, 768], P(None, ('dp', 'fsdp'))
- input_grad: bfloat16 [64, 1024, 768], P(None, ('dp', 'fsdp'))
- q_weight_grad: float32 [768, 192], P(('dp', 'fsdp'))
- q_bias_grad: float32 [768], P(('dp', 'fsdp'))
- k_weight_grad: float32 [768, 192], P(('dp', 'fsdp'))
- v_weight_grad: float32 [768, 192], P(('dp', 'fsdp'))
- v_bias_grad: float32 [768], P(('dp', 'fsdp'))
- o_weight_grad: float32 [768, 768], P(('dp', 'fsdp'))
- o_bias_grad: float32 [768], P(('dp', 'fsdp'))
- norm1_gain_grad: float32 [768], P(('dp', 'fsdp'))
- norm1_bias_grad: float32 [768], P(('dp', 'fsdp'))
- up_weight_grad: float32 [3072, 192], P(('dp', 'fsdp'))
- up_bias_grad: float32 [3072], P(('dp', 'fsdp'))
- down_weight_grad: float32 [768, 768], P(('dp', 'fsdp'))
- down_bias_grad: float32 [768], P(('dp', 'fsdp'))
- norm2_gain_grad: float32 [768], P(('dp', 'fsdp'))
- norm2_bias_grad: float32 [768], P(('dp', 'fsdp'))
- stream_rms: float32 [4, 64], P(None, ('dp', 'fsdp'))
Inputs may be any that keep to these rules, and one draw needn't show every extreme that they name: `lengths`: some sequence has exactly 1024 valid tokens and some exactly 64. A permutation of the 64 sequences; the sequences at dealt positions 2 j and 2 j + 1 have 1024 + 64 valid tokens together.
All inputs are finite; a program needn't handle non-finite values.
Results may differ from a plain program's by a relative error of at most 0.014.
The roundings to bfloat16 on the way count: a program that leaves them out, or rounds other values in their place, can miss the bound.
Values may be sent and summed in bfloat16 or wider, within the bound.
A program may use at most 320 MiB of HBM per device.

v0:
```python
import jax
import jax.numpy as jnp
from jax import lax
from jax.sharding import PartitionSpec as P

H = 12
GROUPS = 4
MICRO = 2


norm_eps = 1e-12
rms_eps = 1e-06
neg_fill = -1e30


def grouped(operand, kernel, groups):
    row_count = operand.shape[0]
    in_width = kernel.shape[1]
    out_width = kernel.shape[0] // groups
    shaped = operand.reshape(row_count, groups, in_width)
    blocks = kernel.reshape(groups, out_width, in_width)
    result = jnp.einsum("rgi,goi->rgo", shaped, blocks, preferred_element_type=jnp.float32)
    return result.reshape(row_count, groups * out_width)


def grouped_back(gradient, kernel, groups):
    row_count = gradient.shape[0]
    in_width = kernel.shape[1]
    out_width = kernel.shape[0] // groups
    shaped = gradient.reshape(row_count, groups, out_width)
    blocks = kernel.reshape(groups, out_width, in_width)
    result = jnp.einsum("rgo,goi->rgi", shaped, blocks, preferred_element_type=jnp.float32)
    return result.reshape(row_count, groups * in_width)


def grouped_grad(gradient, operand, groups):
    row_count = operand.shape[0]
    in_width = operand.shape[1] // groups
    out_width = gradient.shape[1] // groups
    result = jnp.einsum(
        "rgo,rgi->goi",
        gradient.reshape(row_count, groups, out_width),
        operand.reshape(row_count, groups, in_width),
        preferred_element_type=jnp.float32,
    )
    return result.reshape(groups * out_width, in_width)


def normalize(values, norm_gain, norm_shift):
    row_mean = jnp.mean(values, axis=-1, keepdims=True)
    centered = values - row_mean
    row_var = jnp.mean(centered * centered, axis=-1, keepdims=True)
    return centered * lax.rsqrt(row_var + norm_eps) * norm_gain + norm_shift


def gelu_exact(values):
    return jax.nn.gelu(values, approximate=False)


def seq_rms(values, live, lengths_now):
    seq_count = lengths_now.shape[0]
    sums = jnp.sum((values * values * live).reshape(seq_count, -1), axis=1)
    return jnp.sqrt(sums / (lengths_now.astype(jnp.float32) * values.shape[1]) + rms_eps)


def masked_scores(piece, key_seq, length_now, score_scale):
    scores = (
        jnp.einsum("qhd,khd->hqk", piece, key_seq, preferred_element_type=jnp.float32) * score_scale
    )
    key_live = jnp.arange(key_seq.shape[0]) < length_now
    return jnp.where(key_live[None, None, :], scores, neg_fill)


def attend(queries, key_rows, value_rows, lengths_now, block_rows):
    seq_count, seq_len = (queries.shape[0], queries.shape[1])
    per_seq = seq_len // block_rows
    score_scale = queries.shape[3] ** (-0.5)

    def one_block(index):
        which = index // per_seq
        start = index % per_seq * block_rows
        piece = lax.dynamic_slice_in_dim(
            lax.dynamic_index_in_dim(queries, which, 0, False), start, block_rows, 0
        )
        key_seq = lax.dynamic_index_in_dim(key_rows, which, 0, False)
        value_seq = lax.dynamic_index_in_dim(value_rows, which, 0, False)
        length_now = lax.dynamic_index_in_dim(lengths_now, which, 0, False)
        scores = masked_scores(piece, key_seq, length_now, score_scale)
        top_score = jnp.max(scores, axis=-1, keepdims=True)
        weights = jnp.exp(scores - top_score)
        row_total = jnp.sum(weights, axis=-1, keepdims=True)
        probs_low = (weights / row_total).astype(jnp.bfloat16)
        context = jnp.einsum(
            "hqk,khd->qhd", probs_low, value_seq, preferred_element_type=jnp.float32
        )
        return (context.astype(jnp.bfloat16), (top_score + jnp.log(row_total))[..., 0])

    contexts, log_totals = lax.map(one_block, jnp.arange(seq_count * per_seq, dtype=jnp.int32))
    return (contexts.reshape(queries.shape), log_totals)


def add_into(stack, which, part):
    current = lax.dynamic_index_in_dim(stack, which, 0, False)
    return lax.dynamic_update_index_in_dim(stack, current + part, which, 0)


def attend_back(queries, key_rows, value_rows, lengths_now, log_totals, grad_context, block_rows):
    seq_count, seq_len = (queries.shape[0], queries.shape[1])
    per_seq = seq_len // block_rows
    score_scale = queries.shape[3] ** (-0.5)

    def one_block(carry, item):
        key_grads, value_grads = carry
        index, log_total = item
        which = index // per_seq
        start = index % per_seq * block_rows
        piece = lax.dynamic_slice_in_dim(
            lax.dynamic_index_in_dim(queries, which, 0, False), start, block_rows, 0
        )
        grad_piece = lax.dynamic_slice_in_dim(
            lax.dynamic_index_in_dim(grad_context, which, 0, False), start, block_rows, 0
        )
        key_seq = lax.dynamic_index_in_dim(key_rows, which, 0, False)
        value_seq = lax.dynamic_index_in_dim(value_rows, which, 0, False)
        length_now = lax.dynamic_index_in_dim(lengths_now, which, 0, False)
        scores = masked_scores(piece, key_seq, length_now, score_scale)
        probs = jnp.exp(scores - log_total[:, :, None])
        grad_probs = jnp.einsum(
            "qhd,khd->hqk", grad_piece, value_seq, preferred_element_type=jnp.float32
        )
        value_part = jnp.einsum(
            "hqk,qhd->khd",
            probs.astype(jnp.bfloat16),
            grad_piece,
            preferred_element_type=jnp.float32,
        )
        row_inner = jnp.sum(grad_probs * probs, axis=-1, keepdims=True)
        grad_scores = (probs * (grad_probs - row_inner)).astype(jnp.bfloat16)
        query_part = (
            jnp.einsum("hqk,khd->qhd", grad_scores, key_seq, preferred_element_type=jnp.float32)
            * score_scale
        )
        key_part = (
            jnp.einsum("hqk,qhd->khd", grad_scores, piece, preferred_element_type=jnp.float32)
            * score_scale
        )
        return (
            (add_into(key_grads, which, key_part), add_into(value_grads, which, value_part)),
            query_part,
        )

    zeros = jnp.zeros(key_rows.shape, jnp.float32)
    indices = jnp.arange(seq_count * per_seq, dtype=jnp.int32)
    (key_grads, value_grads), query_parts = lax.scan(
        one_block, (zeros, zeros), (indices, log_totals)
    )
    return (query_parts.reshape(queries.shape), key_grads, value_grads)


def forward_micro(rows_in, lengths_now, full, block_rows):
    (
        q_weight,
        q_bias,
        k_weight,
        v_weight,
        v_bias,
        o_weight,
        o_bias,
        norm1_gain,
        norm1_bias,
        up_weight,
        up_bias,
        down_weight,
        down_bias,
        norm2_gain,
        norm2_bias,
    ) = full
    seq_count, seq_len, model_width = rows_in.shape
    row_count = seq_count * seq_len
    flat_rows = rows_in.reshape(row_count, model_width)
    queries = (grouped(flat_rows, q_weight, GROUPS) + q_bias.astype(jnp.float32)).astype(
        jnp.bfloat16
    )
    key_rows = grouped(flat_rows, k_weight, GROUPS).astype(jnp.bfloat16)
    value_rows = (grouped(flat_rows, v_weight, GROUPS) + v_bias.astype(jnp.float32)).astype(
        jnp.bfloat16
    )
    head_shape = (seq_count, seq_len, H, model_width // H)
    contexts, log_totals = attend(
        queries.reshape(head_shape),
        key_rows.reshape(head_shape),
        value_rows.reshape(head_shape),
        lengths_now,
        block_rows,
    )
    context = contexts.reshape(row_count, model_width)
    branch_attn = grouped(context, o_weight, 1) + o_bias.astype(jnp.float32)
    input_rows = flat_rows.astype(jnp.float32)
    first_sum = input_rows + branch_attn
    first_norm, first_back = jax.vjp(
        normalize, first_sum, norm1_gain.astype(jnp.float32), norm1_bias.astype(jnp.float32)
    )
    first_low = first_norm.astype(jnp.bfloat16)
    up_rows = grouped(first_low, up_weight, GROUPS) + up_bias.astype(jnp.float32)
    act_rows, act_back = jax.vjp(gelu_exact, up_rows)
    act_low = act_rows.astype(jnp.bfloat16)
    branch_ffn = grouped(act_low, down_weight, GROUPS) + down_bias.astype(jnp.float32)
    final_norm, final_back = jax.vjp(
        normalize,
        first_norm + branch_ffn,
        norm2_gain.astype(jnp.float32),
        norm2_bias.astype(jnp.float32),
    )
    live = (
        (jnp.arange(seq_len)[None, :] < lengths_now[:, None])
        .astype(jnp.float32)
        .reshape(row_count, 1)
    )
    output_rows = (final_norm * live).astype(jnp.bfloat16).reshape(seq_count, seq_len, model_width)
    stats = jnp.stack(
        [
            seq_rms(input_rows, live, lengths_now),
            seq_rms(branch_attn, live, lengths_now),
            seq_rms(first_norm, live, lengths_now),
            seq_rms(branch_ffn, live, lengths_now),
        ],
        axis=0,
    )
    kept = (
        flat_rows,
        queries,
        key_rows,
        value_rows,
        log_totals,
        context,
        first_back,
        first_low,
        act_back,
        act_low,
        final_back,
        live,
        lengths_now,
    )
    return (output_rows, stats, kept)


def backward_micro(cot_rows, kept, full, block_rows):
    (
        q_weight,
        q_bias,
        k_weight,
        v_weight,
        v_bias,
        o_weight,
        o_bias,
        norm1_gain,
        norm1_bias,
        up_weight,
        up_bias,
        down_weight,
        down_bias,
        norm2_gain,
        norm2_bias,
    ) = full
    (
        flat_rows,
        queries,
        key_rows,
        value_rows,
        log_totals,
        context,
        first_back,
        first_low,
        act_back,
        act_low,
        final_back,
        live,
        lengths_now,
    ) = kept
    row_count, model_width = flat_rows.shape
    seq_count = lengths_now.shape[0]
    grad_out = cot_rows.reshape(row_count, model_width).astype(jnp.float32) * live
    grad_sum2, gain2_grad, shift2_grad = final_back(grad_out)
    grad_ffn = grad_sum2.astype(jnp.bfloat16)
    down_grad = grouped_grad(grad_ffn, act_low, GROUPS)
    down_bias_grad = jnp.sum(grad_ffn, axis=0, dtype=jnp.float32)
    (grad_up_rows,) = act_back(grouped_back(grad_ffn, down_weight, GROUPS))
    grad_up = grad_up_rows.astype(jnp.bfloat16)
    up_grad = grouped_grad(grad_up, first_low, GROUPS)
    up_bias_grad = jnp.sum(grad_up, axis=0, dtype=jnp.float32)
    grad_first = grouped_back(grad_up, up_weight, GROUPS) + grad_sum2
    grad_sum1, gain1_grad, shift1_grad = first_back(grad_first)
    grad_branch = grad_sum1.astype(jnp.bfloat16)
    o_grad = grouped_grad(grad_branch, context, 1)
    o_bias_grad = jnp.sum(grad_branch, axis=0, dtype=jnp.float32)
    grad_context = grouped_back(grad_branch, o_weight, 1).astype(jnp.bfloat16)
    head_shape = (seq_count, row_count // seq_count, H, model_width // H)
    query_grads, key_grads, value_grads = attend_back(
        queries.reshape(head_shape),
        key_rows.reshape(head_shape),
        value_rows.reshape(head_shape),
        lengths_now,
        log_totals,
        grad_context.reshape(head_shape),
        block_rows,
    )
    grad_queries = query_grads.reshape(row_count, model_width).astype(jnp.bfloat16)
    grad_keys = key_grads.reshape(row_count, model_width).astype(jnp.bfloat16)
    grad_values = value_grads.reshape(row_count, model_width).astype(jnp.bfloat16)
    q_grad = grouped_grad(grad_queries, flat_rows, GROUPS)
    q_bias_grad = jnp.sum(grad_queries, axis=0, dtype=jnp.float32)
    k_grad = grouped_grad(grad_keys, flat_rows, GROUPS)
    v_grad = grouped_grad(grad_values, flat_rows, GROUPS)
    v_bias_grad = jnp.sum(grad_values, axis=0, dtype=jnp.float32)
    grad_input = (
        grouped_back(grad_queries, q_weight, GROUPS)
        + grouped_back(grad_keys, k_weight, GROUPS)
        + grouped_back(grad_values, v_weight, GROUPS)
        + grad_sum1
    )
    grads = (
        q_grad,
        q_bias_grad,
        k_grad,
        v_grad,
        v_bias_grad,
        o_grad,
        o_bias_grad,
        gain1_grad,
        shift1_grad,
        up_grad,
        up_bias_grad,
        down_grad,
        down_bias_grad,
        gain2_grad,
        shift2_grad,
    )
    return (
        grads,
        grad_input.astype(jnp.bfloat16).reshape(seq_count, row_count // seq_count, model_width),
    )


def on_device(
    tokens,
    cotangent,
    lengths,
    permutation,
    q_weight,
    q_bias,
    k_weight,
    v_weight,
    v_bias,
    o_weight,
    o_bias,
    norm1_gain,
    norm1_bias,
    up_weight,
    up_bias,
    down_weight,
    down_bias,
    norm2_gain,
    norm2_bias,
):
    devices = lax.axis_size(("dp", "fsdp"))
    my_index = lax.axis_index(("dp", "fsdp"))
    seq_total, piece_len, model_width = tokens.shape
    seq_dev = seq_total // devices
    seq_len = piece_len * devices
    block_rows = min(512, seq_len)
    per_micro = seq_dev // MICRO
    dealt_tokens = jnp.take(tokens, permutation, axis=0)
    dealt_cot = jnp.take(cotangent, permutation, axis=0)
    direct_shape = (devices, seq_dev, 1, piece_len, model_width)
    moved_tokens, moved_cot = (
        lax.all_to_all(
            dealt_tokens.reshape(direct_shape),
            ("dp", "fsdp"),
            split_axis=0,
            concat_axis=2,
            tiled=True,
        ),
        lax.all_to_all(
            dealt_cot.reshape(direct_shape), ("dp", "fsdp"), split_axis=0, concat_axis=2, tiled=True
        ),
    )
    local_tokens = moved_tokens.reshape(seq_dev, seq_len, model_width)
    local_cot = moved_cot.reshape(seq_dev, seq_len, model_width)
    dealt_lengths = jnp.take(lengths, permutation, axis=0)
    my_lengths = lax.dynamic_slice_in_dim(dealt_lengths, my_index * seq_dev, seq_dev)
    outputs = []
    stats_list = []
    kept_list = []
    for micro_step in range(MICRO):
        full = (
            lax.all_gather(q_weight, ("dp", "fsdp"), axis=0, tiled=True),
            lax.all_gather(q_bias, ("dp", "fsdp"), axis=0, tiled=True),
            lax.all_gather(k_weight, ("dp", "fsdp"), axis=0, tiled=True),
            lax.all_gather(v_weight, ("dp", "fsdp"), axis=0, tiled=True),
            lax.all_gather(v_bias, ("dp", "fsdp"), axis=0, tiled=True),
            lax.all_gather(o_weight, ("dp", "fsdp"), axis=0, tiled=True),
            lax.all_gather(o_bias, ("dp", "fsdp"), axis=0, tiled=True),
            lax.all_gather(norm1_gain, ("dp", "fsdp"), axis=0, tiled=True),
            lax.all_gather(norm1_bias, ("dp", "fsdp"), axis=0, tiled=True),
            lax.all_gather(up_weight, ("dp", "fsdp"), axis=0, tiled=True),
            lax.all_gather(up_bias, ("dp", "fsdp"), axis=0, tiled=True),
            lax.all_gather(down_weight, ("dp", "fsdp"), axis=0, tiled=True),
            lax.all_gather(down_bias, ("dp", "fsdp"), axis=0, tiled=True),
            lax.all_gather(norm2_gain, ("dp", "fsdp"), axis=0, tiled=True),
            lax.all_gather(norm2_bias, ("dp", "fsdp"), axis=0, tiled=True),
        )
        first_seq = micro_step * per_micro
        output_rows, stats, kept = forward_micro(
            local_tokens[first_seq : first_seq + per_micro],
            my_lengths[first_seq : first_seq + per_micro],
            full,
            block_rows,
        )
        outputs.append(output_rows)
        stats_list.append(stats)
        kept_list.append(kept)
    accum = None
    input_parts = [None] * MICRO
    for micro_step in reversed(range(MICRO)):
        full = (
            lax.all_gather(q_weight, ("dp", "fsdp"), axis=0, tiled=True),
            lax.all_gather(q_bias, ("dp", "fsdp"), axis=0, tiled=True),
            lax.all_gather(k_weight, ("dp", "fsdp"), axis=0, tiled=True),
            lax.all_gather(v_weight, ("dp", "fsdp"), axis=0, tiled=True),
            lax.all_gather(v_bias, ("dp", "fsdp"), axis=0, tiled=True),
            lax.all_gather(o_weight, ("dp", "fsdp"), axis=0, tiled=True),
            lax.all_gather(o_bias, ("dp", "fsdp"), axis=0, tiled=True),
            lax.all_gather(norm1_gain, ("dp", "fsdp"), axis=0, tiled=True),
            lax.all_gather(norm1_bias, ("dp", "fsdp"), axis=0, tiled=True),
            lax.all_gather(up_weight, ("dp", "fsdp"), axis=0, tiled=True),
            lax.all_gather(up_bias, ("dp", "fsdp"), axis=0, tiled=True),
            lax.all_gather(down_weight, ("dp", "fsdp"), axis=0, tiled=True),
            lax.all_gather(down_bias, ("dp", "fsdp"), axis=0, tiled=True),
            lax.all_gather(norm2_gain, ("dp", "fsdp"), axis=0, tiled=True),
            lax.all_gather(norm2_bias, ("dp", "fsdp"), axis=0, tiled=True),
        )
        first_seq = micro_step * per_micro
        grads, grad_rows = backward_micro(
            local_cot[first_seq : first_seq + per_micro], kept_list[micro_step], full, block_rows
        )
        accum = (
            grads if accum is None else tuple((total + part for total, part in zip(accum, grads)))
        )
        input_parts[micro_step] = grad_rows
    reduced = (
        lax.psum_scatter(accum[0], ("dp", "fsdp"), scatter_dimension=0, tiled=True),
        lax.psum_scatter(accum[1], ("dp", "fsdp"), scatter_dimension=0, tiled=True),
        lax.psum_scatter(accum[2], ("dp", "fsdp"), scatter_dimension=0, tiled=True),
        lax.psum_scatter(accum[3], ("dp", "fsdp"), scatter_dimension=0, tiled=True),
        lax.psum_scatter(accum[4], ("dp", "fsdp"), scatter_dimension=0, tiled=True),
        lax.psum_scatter(accum[5], ("dp", "fsdp"), scatter_dimension=0, tiled=True),
        lax.psum_scatter(accum[6], ("dp", "fsdp"), scatter_dimension=0, tiled=True),
        lax.psum_scatter(accum[7], ("dp", "fsdp"), scatter_dimension=0, tiled=True),
        lax.psum_scatter(accum[8], ("dp", "fsdp"), scatter_dimension=0, tiled=True),
        lax.psum_scatter(accum[9], ("dp", "fsdp"), scatter_dimension=0, tiled=True),
        lax.psum_scatter(accum[10], ("dp", "fsdp"), scatter_dimension=0, tiled=True),
        lax.psum_scatter(accum[11], ("dp", "fsdp"), scatter_dimension=0, tiled=True),
        lax.psum_scatter(accum[12], ("dp", "fsdp"), scatter_dimension=0, tiled=True),
        lax.psum_scatter(accum[13], ("dp", "fsdp"), scatter_dimension=0, tiled=True),
        lax.psum_scatter(accum[14], ("dp", "fsdp"), scatter_dimension=0, tiled=True),
    )
    out_rows = jnp.concatenate(outputs, axis=0)
    grad_input_rows = jnp.concatenate(input_parts, axis=0)
    direct_back = (1, seq_dev, devices, piece_len, model_width)
    back_out, back_grad = (
        lax.all_to_all(
            out_rows.reshape(direct_back), ("dp", "fsdp"), split_axis=2, concat_axis=0, tiled=True
        ),
        lax.all_to_all(
            grad_input_rows.reshape(direct_back),
            ("dp", "fsdp"),
            split_axis=2,
            concat_axis=0,
            tiled=True,
        ),
    )
    inverse = (
        jnp.zeros_like(permutation).at[permutation].set(jnp.arange(seq_total, dtype=jnp.int32))
    )
    output = jnp.take(back_out.reshape(seq_total, piece_len, model_width), inverse, axis=0)
    input_grad = jnp.take(back_grad.reshape(seq_total, piece_len, model_width), inverse, axis=0)
    stream_rms = jnp.concatenate(stats_list, axis=1)
    return (output, input_grad) + tuple(reduced) + (stream_rms,)


def solution(mesh):
    in_specs = (
        P(None, ("dp", "fsdp"), None),
        P(None, ("dp", "fsdp"), None),
        P(),
        P(),
        P(("dp", "fsdp"), None),
        P(("dp", "fsdp")),
        P(("dp", "fsdp"), None),
        P(("dp", "fsdp"), None),
        P(("dp", "fsdp")),
        P(("dp", "fsdp"), None),
        P(("dp", "fsdp")),
        P(("dp", "fsdp")),
        P(("dp", "fsdp")),
        P(("dp", "fsdp"), None),
        P(("dp", "fsdp")),
        P(("dp", "fsdp"), None),
        P(("dp", "fsdp")),
        P(("dp", "fsdp")),
        P(("dp", "fsdp")),
    )
    out_specs = (
        P(None, ("dp", "fsdp"), None),
        P(None, ("dp", "fsdp"), None),
        P(("dp", "fsdp"), None),
        P(("dp", "fsdp")),
        P(("dp", "fsdp"), None),
        P(("dp", "fsdp"), None),
        P(("dp", "fsdp")),
        P(("dp", "fsdp"), None),
        P(("dp", "fsdp")),
        P(("dp", "fsdp")),
        P(("dp", "fsdp")),
        P(("dp", "fsdp"), None),
        P(("dp", "fsdp")),
        P(("dp", "fsdp"), None),
        P(("dp", "fsdp")),
        P(("dp", "fsdp")),
        P(("dp", "fsdp")),
        P(None, ("dp", "fsdp")),
    )
    return jax.shard_map(
        on_device, mesh=mesh, in_specs=in_specs, out_specs=out_specs, check_vma=False
    )
```

profile of v0, /device:TPU:0, one launch (start us, length us, event | category | flops | bytes accessed | tf_op | source)
XLA Modules:
  0.0 1858.7 jit_solution(8401303978710734929)
XLA Ops:
  34.5 93.0 %all-reduce.19 = (bf16[768]{0:T(1024)(128)(2,1)S(1)}, bf16[768]{0:T(1024)(128)(2,1)S(1)}, bf16[3072]{0:T(1024)(128)(2,1)S(1)}, bf16[768]{0:T(1024)(128)(2,1)S(1)...) all-reduce(bf16[768]{0:T(1024)(128)(2,1)S(1)} %dynamic-update-slice, ...), channel_id=1, replica_groups=mesh['dp'=4,'fsdp'=8] {'dp','fsdp'}, use_global_device_ids=true, to_apply=%add | all-reduce | flops 9216 | bytes 36864
  140.3 73.3 %all_gather.30 = bf16[768,192]{1,0:T(8,128)(2,1)} all-gather(bf16[24,192]{1,0:T(8,128)(2,1)S(1)} %copy-done.217), channel_id=1, replica_groups=mesh['dp'=4,'fsdp'=8] {'dp','fsdp'}, dimensions={0}, use_global_device_ids=true | all-gather | bytes 304128 | tf_op jit(solution)/shard_map/all_gather | solution.py:396
  213.6 66.1 %all_gather.33 = bf16[768,192]{1,0:T(8,128)(2,1)S(1)} all-gather(bf16[24,192]{1,0:T(8,128)(2,1)} %param.36), channel_id=1, replica_groups=mesh['dp'=4,'fsdp'=8] {'dp','fsdp'}, dimensions={0}, use_global_device_ids=true | all-gather | bytes 304128 | tf_op jit(solution)/shard_map/all_gather | solution.py:399
  279.7 72.5 %all_gather.32 = bf16[768,192]{1,0:T(8,128)(2,1)} all-gather(bf16[24,192]{1,0:T(8,128)(2,1)} %param.35), channel_id=1, replica_groups=mesh['dp'=4,'fsdp'=8] {'dp','fsdp'}, dimensions={0}, use_global_device_ids=true | all-gather | bytes 304128 | tf_op jit(solution)/shard_map/all_gather | solution.py:398
  390.3 74.3 %while.60 = (s32[]{:T(128)}, bf16[2,512,12,64]{1,3,2,0:T(8,128)(2,1)}, f32[2,12,512]{2,1,0:T(8,128)S(1)}, s32[1]{0:T(128)}, s32[2]{0:T(128)S(1)}, /*index=5*/bf1...) while((s32[]{:T(128)}, ...), condition=%wide.region_3.5_spmd, body=%wide.region_0.4_spmd.sunk | while | flops 1686498304 | bytes 86733648 | solution.py:98
  415.2 12.1 fusion.345
  452.1 12.1 fusion.345
  472.2 74.1 %while.61 = (s32[]{:T(128)}, bf16[2,512,12,64]{1,3,2,0:T(8,128)(2,1)}, f32[2,12,512]{2,1,0:T(8,128)S(1)}, s32[1]{0:T(128)}, s32[2]{0:T(128)S(1)}, /*index=5*/bf1...) while((s32[]{:T(128)}, ...), condition=%wide.region_11.13_spmd, body=%wide.region_8.12_spmd.sunk | while | flops 1686498304 | bytes 86733648 | solution.py:98
  497.1 12.1 fusion.349
  534.0 12.1 fusion.349
  587.1 63.0 %fusion.119 = (bf16[1024,4,768]{2,0,1:T(8,128)(2,1)}, f32[1024,4,768]{2,0,1:T(8,128)}, bf16[1024,4,768]{2,0,1:T(8,128)(2,1)}, f32[1024,4,768]{2,0,1:T(8,128)}, f32[4,1024,768]{2,1,0:T(8,128)}) fusion(f32[4,768]{1,0:T(4,128)S(1)} %copy-done.218, f32[4,1024,768]{2,1,0:T(8,128)S(1)} %fusion.228, bf16[1024,4,192]{0,2,1:T(8,128)(2,1)S(1)} %copy-done.81, ...), kind=kOutput, calls=%fused_computation.145 | convolution fusion | flops 1623195648 | bytes 65679360 | tf_op jit(solution)/shard_map/rgi,goi->rgo/dot_general | solution.py:22
  728.0 13.5 convert_reduce_fusion
  787.6 13.9 convert_reduce_fusion.1
  864.8 159.1 %while.62 = (s32[]{:T(128)}, f32[1,1024,12,64]{1,3,2,0:T(8,128)}, f32[1,1024,12,64]{1,3,2,0:T(8,128)}, bf16[2,512,12,64]{1,3,2,0:T(8,128)(2,1)}, s32[2]{0:T(128)...) while((s32[]{:T(128)}, f32[1,1024,12,64]{1,3,2,0:T(8,128)}, ...), condition=%wide.region_23.25_spmd, body=%wide.region_21.24_spmd.sunk | while | flops 4123651072 | bytes 261272432 | solution.py:154
  878.4 17.5 multiply_reduce_fusion.26
  895.9 16.7 multiply_convert_fusion.6
  930.4 14.0 fusion.360
  957.9 17.5 multiply_reduce_fusion.26
  975.3 16.7 multiply_convert_fusion.6
  1009.8 14.0 fusion.360
  1042.3 159.9 %while.63 = (s32[]{:T(128)}, f32[1,1024,12,64]{1,3,2,0:T(8,128)}, f32[1,1024,12,64]{1,3,2,0:T(8,128)}, bf16[2,512,12,64]{1,3,2,0:T(8,128)(2,1)}, s32[2]{0:T(128)...) while((s32[]{:T(128)}, f32[1,1024,12,64]{1,3,2,0:T(8,128)}, ...), condition=%wide.region_30.32_spmd, body=%wide.region_28.31_spmd.sunk | while | flops 4123651072 | bytes 261272432 | solution.py:154
  1056.2 17.5 multiply_reduce_fusion.27
  1073.7 16.7 multiply_convert_fusion.7
  1108.2 14.1 fusion.371
  1135.8 17.6 multiply_reduce_fusion.27
  1153.4 16.7 multiply_convert_fusion.7
  1188.0 14.2 fusion.371
  1365.9 64.6 %all-reduce.18 = (f32[768]{0:T(1024)S(1)}, f32[768]{0:T(1024)S(1)}, f32[768]{0:T(1024)S(1)}, f32[768]{0:T(1024)S(1)}, f32[768]{0:T(1024)S(1)}, /*index=5*/f32[30...) all-reduce(f32[768]{0:T(1024)S(1)} %add.1208, ...), channel_id=3, replica_groups=mesh['dp'=4,'fsdp'=8] {'dp','fsdp'}, use_global_device_ids=true, to_apply=%region_34.36.clone | all-reduce | flops 9216 | bytes 73728
  1451.4 84.1 %reduce-scatter.9.cloned.1.call-done = f32[24,192]{1,0:T(8,128)} async-done(((f32[768,192]{1,0:T(8,128)}), f32[24,192]{1,0:T(8,128)}) %reduce-scatter.9.cloned.1.call-update) | async-done | bytes 18448 | tf_op jit(solution)/shard_map/reduce_scatter | solution.py:451
  1535.5 104.5 %reduce-scatter.17.cloned.1.call-done = f32[24,768]{1,0:T(8,128)} async-done(((f32[768,768]{1,0:T(8,128)}), f32[24,768]{1,0:T(8,128)}) %reduce-scatter.17.cloned.1.call-update) | async-done | bytes 73744 | tf_op jit(solution)/shard_map/reduce_scatter | solution.py:462
  1640.0 107.3 %reduce-scatter.19.cloned.1.call-done = f32[96,192]{1,0:T(8,128)} async-done(((f32[3072,192]{1,0:T(8,128)}), f32[96,192]{1,0:T(8,128)}) %reduce-scatter.19.cloned.1.call-update) | async-done | bytes 73744
  1747.3 104.4 %reduce-scatter.15.cloned.1.call-done = f32[24,768]{1,0:T(8,128)} async-done(((f32[768,768]{1,0:T(8,128)}), f32[24,768]{1,0:T(8,128)}) %reduce-scatter.15.cloned.1.call-update) | async-done | bytes 73744 | tf_op jit(solution)/shard_map/reduce_scatter | solution.py:456
  (795 shorter events, 715.5 us)
Async XLA Ops:
  22.8 11.5 copy-start.233
  22.8 117.5 %copy-start.217 = (bf16[24,192]{1,0:T(8,128)(2,1)S(1)}, bf16[24,192]{1,0:T(8,128)(2,1)}, u32[]{:S(2)}) copy-start(bf16[24,192]{1,0:T(8,128)(2,1)} %param.33) | copy-start | bytes 27652
  22.8 329.4 %all-to-all-start = ((bf16[32,2,1,32,768]{4,3,1,2,0:T(8,128)(2,1)}), bf16[32,2,1,32,768]{4,3,1,2,0:T(8,128)(2,1)S(1)}, u32[]{:S(2)}, u32[]{:S(2)}) async-start(bf16[32,2,1,32,768]{4,3,1,2,0:T(8,128)(2,1)} %bitcast.792), calls=%async_computation | async-start | bytes 6291456 | tf_op jit(solution)/shard_map/all_to_all | solution.py:376
  30.1 519.7 %all-gather.4.cloned.1.call-start = ((), (), s32[]{:S(2)}) async-start(), calls=%async_computation.10 | async-start | bytes 1216512 | tf_op jit(solution)/shard_map/all_gather | solution.py:401
  30.9 547.6 %all-gather.6.cloned.1.call-start = ((), (), s32[]{:S(2)}) async-start(), calls=%async_computation.11 | async-start | bytes 1622016 | tf_op jit(solution)/shard_map/all_gather | solution.py:405
  31.6 618.6 %all-gather.8.cloned.1.call-start = ((), (), s32[]{:S(2)}) async-start(), calls=%async_computation.12 | async-start | bytes 1216512 | tf_op jit(solution)/shard_map/all_gather | solution.py:407
  279.7 101.9 %copy-start.74 = (bf16[768,192]{1,0:T(8,128)(2,1)}, bf16[768,192]{1,0:T(8,128)(2,1)S(1)}, u32[]{:S(2)}) copy-start(bf16[768,192]{1,0:T(8,128)(2,1)S(1)} %all_gather.33) | copy-start | bytes 884740
  353.9 343.5 %all-to-all-start.2 = ((bf16[32,2,1,32,768]{4,3,1,2,0:T(8,128)(2,1)}), bf16[32,2,1,32,768]{4,3,1,2,0:T(8,128)(2,1)}, u32[]{:S(2)}, u32[]{:S(2)}) async-start(bf16[32,2,1,32,768]{4,3,1,2,0:T(8,128)(2,1)} %bitcast.790), calls=%async_computation.2 | async-start | bytes 6291456 | tf_op jit(solution)/shard_map/all_to_all | solution.py:383
  357.4 1093.9 %reduce-scatter.13.cloned.1.call-start = ((), (), s32[]{:S(2)}) async-start(), calls=%async_computation.15 | async-start | bytes 811008 | tf_op jit(solution)/shard_map/reduce_scatter | solution.py:454
  559.9 13.5 copy-start.167
  697.3 58.9 %copy-start.98 = (f32[32,32]{1,0:T(8,128)}, f32[32,32]{1,0:T(8,128)S(1)}, u32[]{:S(2)}) copy-start(f32[32,32]{1,0:T(8,128)S(1)} %broadcast_multiply_fusion.2) | copy-start | bytes 12292
  705.0 51.2 %copy-start.124 = (f32[32,32]{1,0:T(8,128)}, f32[32,32]{1,0:T(8,128)S(1)}, u32[]{:S(2)}) copy-start(f32[32,32]{1,0:T(8,128)S(1)} %get-tuple-element.729) | copy-start | bytes 12292
  705.0 51.2 %copy-start.138 = (f32[32,32]{1,0:T(8,128)}, f32[32,32]{1,0:T(8,128)S(1)}, u32[]{:S(2)}) copy-start(f32[32,32]{1,0:T(8,128)S(1)} %get-tuple-element.730) | copy-start | bytes 12292
  705.1 113.3 %copy-start.101 = (f32[32,32]{1,0:T(8,128)}, f32[32,32]{1,0:T(8,128)S(1)}, u32[]{:S(2)}) copy-start(f32[32,32]{1,0:T(8,128)S(1)} %broadcast_multiply_fusion) | copy-start | bytes 12292
  705.2 72.8 %copy-start.190 = (f32[1024]{0:T(1024)}, f32[1024]{0:T(1024)S(1)}, u32[]{:S(2)}) copy-start(f32[1024]{0:T(1024)S(1)} %div.188) | copy-start | bytes 12292
  711.9 44.3 %copy-start.142 = (f32[32,32]{1,0:T(8,128)}, f32[32,32]{1,0:T(8,128)S(1)}, u32[]{:S(2)}) copy-start(f32[32,32]{1,0:T(8,128)S(1)} %negate_multiply_fusion.3) | copy-start | bytes 12292
  728.0 13.6 copy-start.41
  728.0 13.6 copy-start.51
  763.7 62.2 %copy-start.159 = (f32[32,32]{1,0:T(8,128)}, f32[32,32]{1,0:T(8,128)S(1)}, u32[]{:S(2)}) copy-start(f32[32,32]{1,0:T(8,128)S(1)} %get-tuple-element.570) | copy-start | bytes 12292
  763.8 54.6 %copy-start.127 = (f32[32,32]{1,0:T(8,128)}, f32[32,32]{1,0:T(8,128)S(1)}, u32[]{:S(2)}) copy-start(f32[32,32]{1,0:T(8,128)S(1)} %get-tuple-element.732) | copy-start | bytes 12292
  763.8 54.6 %copy-start.140 = (f32[32,32]{1,0:T(8,128)}, f32[32,32]{1,0:T(8,128)S(1)}, u32[]{:S(2)}) copy-start(f32[32,32]{1,0:T(8,128)S(1)} %get-tuple-element.733) | copy-start | bytes 12292
  766.9 51.5 %copy-start.144 = (f32[32,32]{1,0:T(8,128)}, f32[32,32]{1,0:T(8,128)S(1)}, u32[]{:S(2)}) copy-start(f32[32,32]{1,0:T(8,128)S(1)} %negate_multiply_fusion.2) | copy-start | bytes 12292
  787.6 13.9 copy-start.42
  1242.3 88.1 %all-to-all-start.1 = ((bf16[1,2,32,32,768]{4,3,1,0,2:T(8,128)(2,1)}), bf16[1,2,32,32,768]{4,3,1,0,2:T(8,128)(2,1)}, u32[]{:S(2)}, u32[]{:S(2)}) async-start(bf16[1,2,32,32,768]{4,3,1,0,2:T(8,128)(2,1)} %copy.193), calls=%async_computation.1 | async-start | bytes 6291456 | tf_op jit(solution)/shard_map/all_to_all | solution.py:471
  1248.2 203.2 %reduce-scatter.11.cloned.1.call-start = ((), (), s32[]{:S(2)}) async-start(), calls=%async_computation.14 | async-start | bytes 811008 | tf_op jit(solution)/shard_map/reduce_scatter | solution.py:453
  1252.8 282.7 %reduce-scatter.9.cloned.1.call-start = ((), (), s32[]{:S(2)}) async-start(), calls=%async_computation.13 | async-start | bytes 811008 | tf_op jit(solution)/shard_map/reduce_scatter | solution.py:451
  1261.2 378.8 %reduce-scatter.17.cloned.1.call-start = ((), (), s32[]{:S(2)}) async-start(), calls=%async_computation.17 | async-start | bytes 2433024 | tf_op jit(solution)/shard_map/reduce_scatter | solution.py:462
  1311.4 16.1 slice-start.2
  1330.3 110.4 %all-to-all-start.3 = ((bf16[1,2,32,32,768]{4,3,1,0,2:T(8,128)(2,1)}), bf16[1,2,32,32,768]{4,3,1,0,2:T(8,128)(2,1)}, u32[]{:S(2)}, u32[]{:S(2)}) async-start(bf16[1,2,32,32,768]{4,3,1,0,2:T(8,128)(2,1)} %copy.218), calls=%async_computation.3 | async-start | bytes 6291456 | tf_op jit(solution)/shard_map/all_to_all | solution.py:474
  1336.3 411.1 %reduce-scatter.19.cloned.1.call-start = ((), (), s32[]{:S(2)}) async-start(), calls=%async_computation.18 | async-start | bytes 3244032
  1346.3 505.5 %reduce-scatter.15.cloned.1.call-start = ((), (), s32[]{:S(2)}) async-start(), calls=%async_computation.16 | async-start | bytes 2433024 | tf_op jit(solution)/shard_map/reduce_scatter | solution.py:456
  1445.0 406.7 %copy-start.1 = (bf16[64,32,768]{2,1,0:T(8,128)(2,1)S(1)}, bf16[64,32,768]{2,1,0:T(8,128)(2,1)}, u32[]{:S(2)}) copy-start(bf16[64,32,768]{2,1,0:T(8,128)(2,1)} %param.29) | copy-start | bytes 9437188
  (223 other events, 1234.1 us)
Sparse Core Ops, SparseCore 0:
  33.9 75.8 all-gather.3
  112.8 53.5 all-gather.5
  169.3 53.7 all-gather.7
  1209.2 115.8 reduce-scatter.12
  1330.7 103.8 reduce-scatter.10
  1440.1 95.3 reduce-scatter.8
  1541.3 98.6 reduce-scatter.16
  1646.0 101.2 reduce-scatter.18
  1753.2 98.5 reduce-scatter.14
where the time goes:
time: 1870 us; the launch traced here: 1860 us
  matrix products  511 us (27%)
  waiting for transfers between devices  403 us (22%)
  blocking collectives  370 us (20%)
  other arithmetic  269 us (14%)
  local copies, waits for them, and re-layouts  242 us (13%)
  between operations  23.8 us (1%)
  starting transfers between devices  23.1 us (1%)
    unnamed x2, blocking collectives  158 us
    unnamed x10, waiting for transfers between devices  109 us
    reduce_scatter x1, waiting for transfers between devices, on_device(): lax.psum_scatter(accum[11], ('dp', 'fsdp'), scatter_dimension=0, tiled=True)  105 us
    reduce_scatter x1, waiting for transfers between devices, on_device(): lax.psum_scatter(accum[5], ('dp', 'fsdp'), scatter_dimension=0, tiled=True)  104 us
    dot_general x12, matrix products, grouped(): jnp.einsum('rgi,goi->rgo', shaped, blocks, preferred_element_type=jnp.flo...  91.5 us
    reduce_scatter x1, waiting for transfers between devices, on_device(): lax.psum_scatter(accum[0], ('dp', 'fsdp'), scatter_dimension=0, tiled=True)  84.1 us
    dot_general x8, matrix products, masked_scores(): jnp.einsum('qhd,khd->hqk', piece, key_seq, preferred_element_type=jnp.flo...  82.1 us
    all_gather x1, blocking collectives, on_device(): lax.all_gather(q_weight, ('dp', 'fsdp'), axis=0, tiled=True)  73.3 us
  transfers between devices with their start and end apart: 13, of which 4 were waited for; matrix products, arithmetic and copies ran while one was open for 26% of the time, Pallas kernels for 0%

commit v1 on v0

v1 whole, which is shorter than its diff:
```python
import functools

import jax
import jax.numpy as jnp
from jax import lax
from jax.experimental import pallas as pl
from jax.experimental.pallas import tpu as pltpu
from jax.sharding import PartitionSpec as P

AXES = ("dp", "fsdp")
D = 768
FF = 3072
HALF = D // 2
HEAD = 64
WIN = 256
SEQ = 1024
SHORT = 64
ROWS = SEQ + SHORT
TILE = 272
TILES = ROWS // TILE
BIG = 1e30

norm_eps = 1e-12
rms_eps = 1e-06
bf16 = jnp.bfloat16
f32 = jnp.float32

NN = (((1,), (0,)), ((), ()))
NT = (((1,), (1,)), ((), ()))
TN = (((0,), (0,)), ((), ()))


def mm(left, right, dims):
    return lax.dot_general(left, right, dims, preferred_element_type=f32)


def exchange():
    row = lax.broadcasted_iota(jnp.int32, (WIN, WIN), 0)
    col = lax.broadcasted_iota(jnp.int32, (WIN, WIN), 1)
    return jnp.where(row + col == WIN - 1, 1.0, 0.0).astype(bf16)


def row_ids(start, count, width):
    return start + lax.broadcasted_iota(jnp.int32, (count, width), 0)


def merge_rows(pair_ref, packed_ref, first_len):
    width = packed_ref.shape[1]
    flip = exchange()
    packed_ref[0:SHORT, :] = pair_ref[0, 0:SHORT, :]
    for step in range(SEQ // WIN):
        start = SHORT + WIN * step
        source = SEQ - WIN * (step + 1)
        flipped = mm(flip, pair_ref[1, source : source + WIN, :], NN)
        inside = min(WIN, SEQ - start)
        own = pair_ref[0, start : start + inside, :].astype(f32)
        keep = row_ids(start, inside, width) < first_len
        packed_ref[start : start + inside, :] = jnp.where(keep, own, flipped[0:inside]).astype(bf16)
        if inside < WIN:
            packed_ref[start + inside : start + WIN, :] = flipped[inside:].astype(bf16)


def unmerge_rows(packed_ref, pair_ref, first_len):
    width = packed_ref.shape[1]
    flip = exchange()
    for step in range(SEQ // WIN):
        start = WIN * step
        ids = row_ids(start, WIN, width)
        own = packed_ref[start : start + WIN, :].astype(f32)
        pair_ref[0, start : start + WIN, :] = jnp.where(ids < first_len, own, 0.0).astype(bf16)
        source = ROWS - WIN * (step + 1)
        flipped = mm(flip, packed_ref[source : source + WIN, :], NN)
        pair_ref[1, start : start + WIN, :] = jnp.where(
            ids < ROWS - first_len, flipped, 0.0
        ).astype(bf16)


def windows(values, count):
    parts = []
    for group in range(count):
        start = (group // 2) * HALF + (group % 2) * 128
        parts.append(values[:, start : start + WIN])
    return parts


def join(parts):
    pieces = []
    for first, second in zip(parts[0::2], parts[1::2]):
        pieces += [first[:, :128], first[:, 128:] + second[:, :128], second[:, 128:]]
    return jnp.concatenate(pieces, axis=1)


def split_three(value):
    high = value.astype(bf16)
    rest = value - high.astype(f32)
    mid = rest.astype(bf16)
    low = (rest - mid.astype(f32)).astype(bf16)
    return high, mid, low


def attn_fwd_kernel(
    len_ref, tok_ref, w_ref, b_ref, x_ref, qa_ref, ka_ref, va_ref, ctx_ref, q_s, k_s, v_s
):
    pair = pl.program_id(0)
    first_len = len_ref[0]

    @pl.when(pair == 0)
    def _():
        merge_rows(tok_ref, x_ref, first_len)
        cols = windows(x_ref[...], 2)
        for which, target in enumerate((q_s, k_s, v_s)):
            value = join([mm(cols[g], w_ref[which, g], NT) for g in range(2)])
            value = value + b_ref[which : which + 1, :]
            if which == 0:
                value = value.astype(bf16).astype(f32) * (HEAD**-0.5)
            target[...] = value.astype(bf16)

    lane0 = pl.multiple_of(pair * 128, 128)
    q_pair = q_s[:, pl.ds(lane0, 128)]
    k_pair = k_s[:, pl.ds(lane0, 128)]
    v_pair = v_s[:, pl.ds(lane0, 128)]
    lane = lax.broadcasted_iota(jnp.int32, (ROWS, 128), 1)
    in_first = row_ids(0, ROWS, 128) < first_len
    one = jnp.ones((ROWS, 128), f32)
    zero = jnp.zeros((ROWS, 128), f32)
    for head in range(2):
        spare = 64 * (1 - head)
        own = (lane // 64) == head
        first_one = jnp.where(in_first, one, zero)
        q_extra = jnp.where(
            lane == spare, first_one, jnp.where(lane == spare + 1, one - first_one, zero)
        )
        k_extra = jnp.where(
            lane == spare,
            (first_one - one) * BIG,
            jnp.where(
                lane == spare + 1,
                first_one * (-BIG),
                jnp.where((lane >= spare + 2) & (lane < spare + 5), one, zero),
            ),
        )
        v_extra = jnp.where((lane >= spare) & (lane < spare + 3), one, zero)
        cols = slice(128 * head, 128 * (head + 1))
        qa_ref[:, cols] = jnp.where(own, q_pair.astype(f32), q_extra).astype(bf16)
        ka_ref[:, cols] = jnp.where(own, k_pair.astype(f32), k_extra).astype(bf16)
        va_ref[:, cols] = jnp.where(own, v_pair.astype(f32), v_extra).astype(bf16)

    tile_lane = lax.broadcasted_iota(jnp.int32, (TILE, 128), 1)

    def one_tile(index, carry):
        start = pl.multiple_of(index * TILE, 16)
        rows = pl.ds(start, TILE)
        result = None
        for head in range(2):
            cols = slice(128 * head, 128 * (head + 1))
            spare = 64 * (1 - head)
            q_tile = qa_ref[rows, cols]
            scores = mm(q_tile, ka_ref[:, cols], NT)
            top = jnp.max(scores, axis=1, keepdims=True)
            weights = jnp.exp(scores - top)
            mixed = mm(weights.astype(bf16), va_ref[:, cols], NN)
            total = mixed[:, spare : spare + 1]
            mixed = mixed / total
            log_total = top + jnp.log(total)
            high, mid, low = split_three(-log_total)
            q_new = jnp.where(
                tile_lane == spare + 2,
                high.astype(f32),
                jnp.where(
                    tile_lane == spare + 3,
                    mid.astype(f32),
                    jnp.where(tile_lane == spare + 4, low.astype(f32), q_tile.astype(f32)),
                ),
            )
            qa_ref[rows, cols] = q_new.astype(bf16)
            result = mixed if head == 0 else jnp.where(tile_lane < 64, result, mixed)
        ctx_ref[rows, :] = result.astype(bf16)
        return carry

    lax.fori_loop(0, TILES, one_tile, 0)


def attn_bwd_kernel(
    len_ref, qa_ref, ka_ref, va_ref, ctx_ref, gctx_ref, x_ref, base_ref, w_ref,
    ig_ref, dw_ref, db_ref, dq_s, dk_s, dv_s, do_s, dqt_s, ig_s,
):
    pair = pl.program_id(0)
    lane0 = pl.multiple_of(pair * 128, 128)
    lane = lax.broadcasted_iota(jnp.int32, (ROWS, 128), 1)
    grad = gctx_ref[...].astype(f32)
    product = grad * ctx_ref[...].astype(f32)
    for head in range(2):
        own = (lane // 64) == head
        spare = 64 * (1 - head)
        inner = -jnp.sum(jnp.where(own, product, 0.0), axis=1, keepdims=True)
        high, mid, low = split_three(inner)
        extra = jnp.where(
            lane == spare,
            high.astype(f32),
            jnp.where(
                lane == spare + 1,
                mid.astype(f32),
                jnp.where(lane == spare + 2, low.astype(f32), 0.0),
            ),
        )
        do_s[:, 128 * head : 128 * (head + 1)] = jnp.where(own, grad, extra).astype(bf16)
    dqt_s[...] = jnp.zeros_like(dqt_s)
    tile_lane = lax.broadcasted_iota(jnp.int32, (TILE, 128), 1)

    def one_tile(index, carry):
        start = pl.multiple_of(index * TILE, 16)
        rows = pl.ds(start, TILE)
        dk_tile = None
        dv_tile = None
        for head in range(2):
            cols = slice(128 * head, 128 * (head + 1))
            k_tile = ka_ref[rows, cols]
            probs = jnp.exp(mm(k_tile, qa_ref[:, cols], NT))
            scaled = mm(va_ref[rows, cols], do_s[:, cols], NT) * probs
            grad_scores = scaled.astype(bf16)
            dv_new = mm(probs.astype(bf16), do_s[:, cols], NN)
            dk_new = mm(grad_scores, qa_ref[:, cols], NN)
            dq_new = mm(k_tile, grad_scores, TN)
            dqt_s[64 * head : 64 * (head + 1), :] += dq_new[64 * head : 64 * (head + 1), :]
            dk_tile = dk_new if head == 0 else jnp.where(tile_lane < 64, dk_tile, dk_new)
            dv_tile = dv_new if head == 0 else jnp.where(tile_lane < 64, dv_tile, dv_new)
        dk_s[rows, pl.ds(lane0, 128)] = dk_tile.astype(bf16)
        dv_s[rows, pl.ds(lane0, 128)] = dv_tile.astype(bf16)
        return carry

    lax.fori_loop(0, TILES, one_tile, 0)
    dq_s[:, pl.ds(lane0, 128)] = (jnp.transpose(dqt_s[...]) * (HEAD**-0.5)).astype(bf16)

    @pl.when(pair == pl.num_programs(0) - 1)
    def _():
        x_cols = windows(x_ref[...], 2)
        total = [None, None]
        for which, source in enumerate((dq_s, dk_s, dv_s)):
            value = source[...]
            db_ref[which : which + 1, :] = jnp.sum(value.astype(f32), axis=0, keepdims=True)
            cols = windows(value, 2)
            for g in range(2):
                dw_ref[which, g] = mm(cols[g], x_cols[g], TN)
                part = mm(cols[g], w_ref[which, g], NN)
                total[g] = part if which == 0 else total[g] + part
        ig_s[...] = (join(total) + base_ref[...]).astype(bf16)
        unmerge_rows(ig_s, ig_ref, len_ref[0])


def mid_kernel(
    len_ref, x0_ref, x1_ref, ctx0_ref, ctx1_ref, cot_ref, wo_ref, wu_ref, wd_ref, vec_ref, ub_ref,
    out_ref, gctx_ref, base_ref, dwo_ref, dwu_ref, dwd_ref, dvec_ref, dub_ref, stat_ref,
    cot_s, out_s, act_s, slope_s, stat_s,
):
    step = pl.program_id(0)
    first_len = len_ref[0]

    @pl.when(step == 0)
    def _():
        merge_rows(cot_ref, cot_s, first_len)
        for target in (dwo_ref, dwu_ref, dwd_ref, dvec_ref, dub_ref, stat_s):
            target[...] = jnp.zeros_like(target)

    o_bias, gain1, shift1, down_bias, gain2, shift2 = (vec_ref[i : i + 1, :] for i in range(6))
    start = pl.multiple_of(step * TILE, 16)
    rows = pl.ds(start, TILE)
    keep = jnp.where(row_ids(start, TILE, D) < first_len, 1.0, 0.0)

    def note(slot, values):
        square = values * values
        stat_s[slot : slot + 1, :] += jnp.sum(square, axis=0, keepdims=True)
        stat_s[slot + 4 : slot + 5, :] += jnp.sum(square * keep, axis=0, keepdims=True)

    def add_vec(slot, values):
        dvec_ref[slot : slot + 1, :] += jnp.sum(values, axis=0, keepdims=True)

    def norm(values):
        mean = jnp.mean(values, axis=1, keepdims=True)
        centered = values - mean
        var = jnp.mean(centered * centered, axis=1, keepdims=True)
        inv = lax.rsqrt(var + norm_eps)
        return centered * inv, inv

    def norm_back(grad_n, n, inv):
        mean_g = jnp.mean(grad_n, axis=1, keepdims=True)
        mean_gn = jnp.mean(grad_n * n, axis=1, keepdims=True)
        return (grad_n - mean_g - n * mean_gn) * inv

    inputs = jnp.concatenate([x0_ref[...], x1_ref[...]], axis=1).astype(f32)
    context = jnp.concatenate([ctx0_ref[...], ctx1_ref[...]], axis=1)
    note(0, inputs)
    branch_attn = mm(context, wo_ref[...], NT) + o_bias
    note(1, branch_attn)
    n1, inv1 = norm(inputs + branch_attn)
    first_norm = n1 * gain1 + shift1
    note(2, first_norm)
    first_low = first_norm.astype(bf16)
    low_cols = windows(first_low, 4)
    parts = []
    for g in range(4):
        cols = slice(D * g, D * (g + 1))
        up = mm(low_cols[g], wu_ref[g], NT) + ub_ref[0:1, cols]
        gate = 0.5 * (1.0 + lax.erf(up * (2.0**-0.5)))
        slope_s[:, cols] = gate + up * jnp.exp(up * up * -0.5) * 0.3989422804014327
        act = (up * gate).astype(bf16)
        act_s[:, cols] = act
        parts.append(mm(act, wd_ref[g], NT))
    branch_ffn = join(parts) + down_bias
    note(3, branch_ffn)
    n2, inv2 = norm(first_norm + branch_ffn)
    out_s[rows, :] = (n2 * gain2 + shift2).astype(bf16)

    grad_out = cot_s[rows, :].astype(f32)
    add_vec(4, grad_out * n2)
    add_vec(5, grad_out)
    grad_sum2 = norm_back(grad_out * gain2, n2, inv2)
    grad_ffn = grad_sum2.astype(bf16)
    add_vec(3, grad_ffn.astype(f32))
    ffn_cols = windows(grad_ffn, 4)
    parts = []
    for g in range(4):
        cols = slice(D * g, D * (g + 1))
        dwd_ref[g] += mm(ffn_cols[g], act_s[:, cols], TN)
        grad_up = (mm(ffn_cols[g], wd_ref[g], NN) * slope_s[:, cols]).astype(bf16)
        dub_ref[0:1, cols] += jnp.sum(grad_up.astype(f32), axis=0, keepdims=True)
        dwu_ref[g] += mm(low_cols[g], grad_up, TN)
        parts.append(mm(grad_up, wu_ref[g], NN))
    grad_first = join(parts) + grad_sum2
    add_vec(1, grad_first * n1)
    add_vec(2, grad_first)
    grad_sum1 = norm_back(grad_first * gain1, n1, inv1)
    base_ref[...] = grad_sum1
    grad_branch = grad_sum1.astype(bf16)
    add_vec(0, grad_branch.astype(f32))
    dwo_ref[...] += mm(grad_branch, context, TN)
    gctx_ref[...] = mm(grad_branch, wo_ref[...], NN).astype(bf16)

    @pl.when(step == pl.num_programs(0) - 1)
    def _():
        unmerge_rows(out_s, out_ref, first_len)
        stat_ref[...] = jnp.broadcast_to(
            jnp.sum(stat_s[...], axis=1, keepdims=True), stat_ref.shape
        )


def whole(shape):
    zeros = (0,) * len(shape)
    return pl.BlockSpec(shape, lambda i, *_: zeros, pipeline_mode=pl.Buffered(1))


def kept(shape):
    zeros = (0,) * len(shape)
    return pl.BlockSpec(shape, lambda i, *_: zeros)


def struct(shape, dtype):
    return jax.ShapeDtypeStruct(shape, dtype)


PARAMS = pltpu.CompilerParams(
    dimension_semantics=("arbitrary",), vmem_limit_bytes=63_000_000
)


def attn_fwd(len_arr, tok, w, bias):
    pair_cols = lambda width: pl.BlockSpec((ROWS, width), lambda i, *_: (0, i))
    return pl.pallas_call(
        attn_fwd_kernel,
        name="attn_fwd",
        grid_spec=pltpu.PrefetchScalarGridSpec(
            num_scalar_prefetch=1,
            grid=(3,),
            in_specs=[whole(tok.shape), whole(w.shape), whole(bias.shape)],
            out_specs=[
                kept((ROWS, HALF)), pair_cols(256), pair_cols(256), pair_cols(256), pair_cols(128),
            ],
            scratch_shapes=[pltpu.VMEM((ROWS, HALF), bf16)] * 3,
        ),
        out_shape=[
            struct((ROWS, HALF), bf16), struct((ROWS, D), bf16), struct((ROWS, D), bf16),
            struct((ROWS, D), bf16), struct((ROWS, HALF), bf16),
        ],
        compiler_params=PARAMS,
        cost_estimate=pl.CostEstimate(
            flops=30_000_000_000, bytes_accessed=12_000_000, transcendentals=7_000_000
        ),
    )(len_arr, tok, w, bias)


def attn_bwd(len_arr, qa, ka, va, ctx, gctx, x, base, w, half):
    pair_cols = lambda width, first: pl.BlockSpec((ROWS, width), lambda i, *_: (0, i + first))
    return pl.pallas_call(
        attn_bwd_kernel,
        name="attn_bwd",
        grid_spec=pltpu.PrefetchScalarGridSpec(
            num_scalar_prefetch=1,
            grid=(3,),
            in_specs=[
                pair_cols(256, 0), pair_cols(256, 0), pair_cols(256, 0), pair_cols(128, 0),
                pair_cols(128, 3 * half), whole(x.shape),
                pl.BlockSpec((ROWS, HALF), lambda i, *_: (0, half), pipeline_mode=pl.Buffered(1)),
                whole(w.shape),
            ],
            out_specs=[kept((2, SEQ, HALF)), kept((3, 2, WIN, WIN)), kept((8, HALF))],
            scratch_shapes=[
                pltpu.VMEM((ROWS, HALF), bf16),
                pltpu.VMEM((ROWS, HALF), bf16),
                pltpu.VMEM((ROWS, HALF), bf16),
                pltpu.VMEM((ROWS, 256), bf16),
                pltpu.VMEM((128, ROWS), f32),
                pltpu.VMEM((ROWS, HALF), bf16),
            ],
        ),
        out_shape=[
            struct((2, SEQ, HALF), bf16), struct((3, 2, WIN, WIN), f32), struct((8, HALF), f32),
        ],
        compiler_params=PARAMS,
        cost_estimate=pl.CostEstimate(
            flops=70_000_000_000, bytes_accessed=16_000_000, transcendentals=7_000_000
        ),
    )(len_arr, qa, ka, va, ctx, gctx, x, base, w)


def middle(len_arr, x0, x1, ctx0, ctx1, cot, wo, wu, wd, vecs, ub):
    row_tile = lambda width: pl.BlockSpec((TILE, width), lambda i, *_: (i, 0))
    return pl.pallas_call(
        mid_kernel,
        name="middle",
        grid_spec=pltpu.PrefetchScalarGridSpec(
            num_scalar_prefetch=1,
            grid=(TILES,),
            in_specs=[row_tile(HALF)] * 4
            + [whole(a.shape) for a in (cot, wo, wu, wd, vecs, ub)],
            out_specs=[
                kept((2, SEQ, D)), row_tile(D), row_tile(D), kept((D, D)), kept((4, WIN, D)),
                kept((4, WIN, D)), kept((8, D)), kept((8, FF)), kept((8, 128)),
            ],
            scratch_shapes=[
                pltpu.VMEM((ROWS, D), bf16),
                pltpu.VMEM((ROWS, D), bf16),
                pltpu.VMEM((TILE, FF), bf16),
                pltpu.VMEM((TILE, FF), f32),
                pltpu.VMEM((8, D), f32),
            ],
        ),
        out_shape=[
            struct((2, SEQ, D), bf16), struct((ROWS, D), bf16), struct((ROWS, D), f32),
            struct((D, D), f32), struct((4, WIN, D), f32), struct((4, WIN, D), f32),
            struct((8, D), f32), struct((8, FF), f32), struct((8, 128), f32),
        ],
        compiler_params=PARAMS,
        cost_estimate=pl.CostEstimate(
            flops=30_000_000_000, bytes_accessed=30_000_000, transcendentals=10_000_000
        ),
    )(len_arr, x0, x1, ctx0, ctx1, cot, wo, wu, wd, vecs, ub)


def spread(weight, axis):
    even = [(0, 0)] * weight.ndim
    odd = [(0, 0)] * weight.ndim
    even[axis], odd[axis] = (0, 64), (64, 0)
    return even, odd


def window_weight(weight, axes):
    even = [(0, 0)] * 3
    odd = [(0, 0)] * 3
    for axis in axes:
        even[axis], odd[axis] = (0, 64), (64, 0)
    pairs = weight.reshape((2, 2) + weight.shape[1:])
    both = jnp.stack([jnp.pad(pairs[:, 0], even), jnp.pad(pairs[:, 1], odd)], axis=1)
    return both.reshape((4,) + both.shape[2:])


def unwindow(grad, axes):
    parts = []
    for group in range(4):
        index = [slice(None)] * 2
        for axis in axes:
            index[axis] = slice(0, 192) if group % 2 == 0 else slice(64, 256)
        parts.append(grad[group][tuple(index)])
    return jnp.stack(parts, axis=0)


def on_device(
    tokens, cotangent, lengths, permutation, q_weight, q_bias, k_weight, v_weight, v_bias, o_weight,
    o_bias, norm1_gain, norm1_bias, up_weight, up_bias, down_weight, down_bias, norm2_gain,
    norm2_bias,
):
    devices = lax.axis_size(AXES)
    my_index = lax.axis_index(AXES)
    seq_total, piece_len, _ = tokens.shape
    seq_dev = seq_total // devices
    dealt_lengths = jnp.take(lengths, permutation, axis=0).reshape(devices, seq_dev)
    swap = dealt_lengths[:, 0] < dealt_lengths[:, 1]
    dealt = permutation.reshape(devices, seq_dev)
    order = jnp.where(swap[:, None], dealt[:, ::-1], dealt).reshape(seq_total)
    inverse = (
        jnp.zeros_like(permutation).at[order].set(jnp.arange(seq_total, dtype=jnp.int32))
    )
    my_swap = lax.dynamic_index_in_dim(swap, my_index, 0, False)
    len_arr = jnp.max(lax.dynamic_slice_in_dim(dealt_lengths, my_index, 1, 0)).reshape(1)

    def arrive(rows):
        width = rows.shape[-1]
        moved = lax.all_to_all(
            rows.reshape(devices, seq_dev, 1, piece_len, width), AXES, split_axis=0, concat_axis=2,
            tiled=True,
        )
        return moved.reshape(seq_dev, SEQ, width)

    def leave(rows):
        width = rows.shape[-1]
        moved = lax.all_to_all(
            rows.reshape(1, seq_dev, devices, piece_len, width), AXES, split_axis=2, concat_axis=0,
            tiled=True,
        )
        return moved.reshape(seq_total, piece_len, width)

    dealt_tokens = jnp.take(tokens, order, axis=0)
    tok0 = arrive(dealt_tokens[:, :, :HALF])
    tok1 = arrive(dealt_tokens[:, :, HALF:])
    cot = arrive(jnp.take(cotangent, order, axis=0))

    rows_dev = q_weight.shape[0]
    up_dev = up_weight.shape[0]
    small = jnp.concatenate(
        [q_bias, v_bias, o_bias, norm1_gain, norm1_bias, down_bias, norm2_gain, norm2_bias, up_bias]
    )
    packed = jnp.concatenate(
        [
            o_weight,
            down_weight,
            q_weight,
            k_weight,
            v_weight,
            up_weight.reshape(4, rows_dev, 192).transpose(1, 0, 2).reshape(rows_dev, D),
            jnp.pad(small.reshape(12, rows_dev).transpose(1, 0), ((0, 0), (0, 52))),
        ],
        axis=1,
    )
    full = lax.all_gather(packed, AXES, axis=0, tiled=True)
    wo = full[:, :D]
    wd = window_weight(full[:, D : 2 * D].reshape(4, 192, D), (1,))
    wqkv = [
        window_weight(full[:, 2 * D + 192 * i : 2 * D + 192 * (i + 1)].reshape(4, 192, 192), (1, 2))
        for i in range(3)
    ]
    wu = window_weight(
        full[:, 2112:2880].reshape(devices, rows_dev, 4, 192).transpose(0, 2, 1, 3).reshape(4, D, 192),
        (2,),
    )
    wqkv = jnp.stack(wqkv, axis=0)
    smalls = full[:, 2880:2892].astype(f32)
    qb, vb, ob, g1, b1, db, g2, b2 = (smalls[:, i] for i in range(8))
    ub = smalls[:, 8:12].reshape(devices, rows_dev, 4).transpose(0, 2, 1).reshape(1, FF)
    vecs = jnp.stack([ob, g1, b1, db, g2, b2, ob, ob], axis=0)
    qkv_bias = jnp.stack([qb, jnp.zeros_like(qb), vb, qb, qb, qb, qb, qb], axis=0)

    x0, qa0, ka0, va0, ctx0 = attn_fwd(len_arr, tok0, wqkv[:, :2], qkv_bias[:, :HALF])
    x1, qa1, ka1, va1, ctx1 = attn_fwd(len_arr, tok1, wqkv[:, 2:], qkv_bias[:, HALF:])
    out, gctx, base, dwo, dwu, dwd, dvec, dub, stat = middle(
        len_arr, x0, x1, ctx0, ctx1, cot, wo, wu, wd, vecs, ub
    )
    back_out = leave(out)
    ig0, dw0, db0 = attn_bwd(len_arr, qa0, ka0, va0, ctx0, gctx, x0, base, wqkv[:, :2], 0)
    ig1, dw1, db1 = attn_bwd(len_arr, qa1, ka1, va1, ctx1, gctx, x1, base, wqkv[:, 2:], 1)
    back_grad = jnp.concatenate([leave(ig0), leave(ig1)], axis=-1)

    dw = jnp.concatenate([dw0, dw1], axis=1)
    dqkv = [unwindow(dw[i], (0, 1)).reshape(D, 192) for i in range(3)]
    dbias = jnp.concatenate([db0, db1], axis=1)
    d_down = unwindow(dwd, (0,)).reshape(D, D)
    d_up = unwindow(dwu, (0,)).transpose(0, 2, 1).reshape(FF, 192)
    up_back = d_up.reshape(devices, 4, rows_dev, 192).transpose(0, 2, 1, 3).reshape(D, D)
    vec_back = jnp.stack(
        [dbias[0], dbias[2], dvec[0], dvec[1], dvec[2], dvec[3], dvec[4], dvec[5]], axis=1
    )
    ub_back = dub[0].reshape(devices, 4, rows_dev).transpose(0, 2, 1).reshape(D, 4)
    grads = jnp.concatenate(
        [dwo, d_down] + dqkv + [up_back, jnp.pad(jnp.concatenate([vec_back, ub_back], 1), ((0, 0), (0, 52)))],
        axis=1,
    )
    mine = lax.psum_scatter(grads, "dp", scatter_dimension=0, tiled=True)
    mine = lax.psum_scatter(mine, "fsdp", scatter_dimension=0, tiled=True)

    output = jnp.take(back_out, inverse, axis=0)
    input_grad = jnp.take(back_grad, inverse, axis=0)
    lens = jnp.stack([len_arr[0], ROWS - len_arr[0]]).astype(f32)
    sums = jnp.stack([stat[4:8, 0], stat[0:4, 0] - stat[4:8, 0]], axis=1)
    rms = jnp.sqrt(sums / (lens[None, :] * D) + rms_eps)
    stream_rms = jnp.where(my_swap, rms[:, ::-1], rms)
    vec = lambda i: mine[:, 2880 + i]
    return (
        output,
        input_grad,
        mine[:, 1536:1728],
        vec(0),
        mine[:, 1728:1920],
        mine[:, 1920:2112],
        vec(1),
        mine[:, :D],
        vec(2),
        vec(3),
        vec(4),
        mine[:, 2112:2880].reshape(rows_dev, 4, 192).transpose(1, 0, 2).reshape(up_dev, 192),
        mine[:, 2888:2892].transpose(1, 0).reshape(up_dev),
        mine[:, D : 2 * D],
        vec(5),
        vec(6),
        vec(7),
        stream_rms,
    )


def solution(mesh):
    rows = P(None, AXES, None)
    mat = P(AXES, None)
    vec = P(AXES)
    in_specs = (
        rows, rows, P(), P(), mat, vec, mat, mat, vec, mat, vec, vec, vec, mat, vec, mat, vec, vec,
        vec,
    )
    out_specs = (
        rows, rows, mat, vec, mat, mat, vec, mat, vec, vec, vec, mat, vec, mat, vec, vec, vec,
        P(None, AXES),
    )
    return jax.shard_map(
        on_device, mesh=mesh, in_specs=in_specs, out_specs=out_specs, check_vma=False
    )
```

time: 1870 us -> 708 us (0.38)
  matrix products: 511 us -> 0 us
  blocking collectives: 370 us -> 45.9 us
  other arithmetic: 269 us -> 26.4 us
  Pallas kernels: 0 us -> 162 us
  local copies, waits for them, and re-layouts: 242 us -> 101 us
  waiting for transfers between devices: 403 us -> 333 us
    dot_general x64 -> x0, matrix products: 511 us -> none  [the longest x12 91.5 us: grouped(): jnp.einsum('rgi,goi->rgo', shaped, blocks, preferred_element_type=jnp.flo...]
    reduce_scatter x5 -> x1, waiting for transfers between devices: 293 us -> 5.23 us  [on_device(): mine = lax.psum_scatter(grads, 'dp', scatter_dimension=0, tiled=True)]
    all_to_all x4 -> x5, waiting for transfers between devices: 0.01 us -> 274 us  [the longest x3 150 us: leave(): lax.all_to_all(rows.reshape(1, seq_dev, devices, piece_len, width), AXES,...]
    all_gather x3 -> x0, blocking collectives: 212 us -> none  [the longest x1 73.3 us: on_device(): lax.all_gather(q_weight, ('dp', 'fsdp'), axis=0, tiled=True)]
    pallas_call x0 -> x5, Pallas kernels: none -> 162 us  [the longest x2 68.9 us: attn_bwd(): pl.pallas_call(attn_bwd_kernel, name='attn_bwd', grid_spec=pltpu.Prefetch...]
    unnamed x2 -> x0, blocking collectives: 158 us -> none
    convert_element_type x24 -> x1, other arithmetic: 124 us -> 1.04 us  [on_device(): smalls = full[:, 2880:2892].astype(f32)]
    reduce_sum x21 -> x0, other arithmetic: 119 us -> none  [the longest x4 45.3 us: one_block(): row_total = jnp.sum(weights, axis=-1, keepdims=True)]
  transfers between devices with their start and end apart: 13 -> 8, of which waited for: 4 -> 7; matrix products, arithmetic and copies ran while one was open for 26% -> 5% of each run, Pallas kernels for 0% -> 0%
where the time goes in v1:
time: 708 us; the launch traced here: 700 us
  waiting for transfers between devices  333 us (47%)
  Pallas kernels  162 us (23%)
  local copies, waits for them, and re-layouts  101 us (14%)
  blocking collectives  45.9 us (6%)
  other arithmetic  26.4 us (4%)
  between operations  16.2 us (2%)
  starting transfers between devices  14.7 us (2%)
    all_to_all x3, waiting for transfers between devices, leave(): lax.all_to_all(rows.reshape(1, seq_dev, devices, piece_len, width), AXES,...  150 us
    all_to_all x2, waiting for transfers between devices, arrive(): lax.all_to_all(rows.reshape(devices, seq_dev, 1, piece_len, width), AXES,...  124 us
    pallas_call x2, Pallas kernels, attn_bwd(): pl.pallas_call(attn_bwd_kernel, name='attn_bwd', grid_spec=pltpu.Prefetch...  68.9 us
    unnamed x4, waiting for transfers between devices  53.7 us
    pallas_call x2, Pallas kernels, attn_fwd(): pl.pallas_call(attn_fwd_kernel, name='attn_fwd', grid_spec=pltpu.Prefetch...  51.1 us
    all_to_all x1, blocking collectives, arrive(): lax.all_to_all(rows.reshape(devices, seq_dev, 1, piece_len, width), AXES,...  45.9 us
    pallas_call x1, Pallas kernels, middle(): pl.pallas_call(mid_kernel, name='middle', grid_spec=pltpu.PrefetchScalarG...  42.4 us
  transfers between devices with their start and end apart: 8, of which 7 were waited for; matrix products, arithmetic and copies ran while one was open for 5% of the time, Pallas kernels for 0%

profile of v1, /device:TPU:0, one launch (start us, length us, event | category | flops | bytes accessed | tf_op | source)
XLA Modules:
  0.0 700.4 jit_solution(10711387047186165267)
XLA Ops:
  12.2 2.4 gather_fusion.2
  14.6 4.3 gather_fusion.1
  18.9 5.1 broadcast_select_fusion.2
  25.5 45.9 %all_to_all.90 = bf16[32,2,1,32,384]{4,3,1,2,0:T(8,128)(2,1)} all-to-all(bf16[32,2,1,32,384]{4,3,1,2,0:T(8,128)(2,1)S(1)} %bitcast.207), channel_id=1, replica_groups=mesh['dp'=4,'fsdp'=8] {'dp','fsdp'}, dimensions={0} | all-to-all | bytes 3145728 | tf_op jit(solution)/shard_map/all_to_all | solution.py:506
  71.6 2.8 all-to-all-start.1
  75.9 44.3 %all-to-all-done.1 = bf16[32,2,1,32,384]{4,3,1,2,0:T(8,128)(2,1)S(1)} async-done(((bf16[32,2,1,32,384]{4,3,1,2,0:T(8,128)(2,1)}), bf16[32,2,1,32,384]{4,3,1,2,0:T(8,128)(2,1)S(1)}, u32[]{:S(2)}, u32[]{:S(2)}) %all-to-all-start.1) | async-done | bytes 1572896 | tf_op jit(solution)/shard_map/all_to_all | solution.py:506
  121.3 2.8 all-to-all-start.2
  124.9 2.8 copy.115
  129.0 79.8 %all-to-all-done.2 = bf16[32,2,1,32,768]{4,3,1,2,0:T(8,128)(2,1)S(1)} async-done(((bf16[32,2,1,32,768]{4,3,1,2,0:T(8,128)(2,1)}), bf16[32,2,1,32,768]{4,3,1,2,0:T(8,128)(2,1)S(1)}, u32[]{:S(2)}, u32[]{:S(2)}) %all-to-all-start.2) | async-done | bytes 3145760 | tf_op jit(solution)/shard_map/all_to_all | solution.py:506
  216.8 4.1 fusion.5
  224.0 3.7 reshape.257
  232.0 25.6 %attn_fwd.3 = (bf16[1088,384]{1,0:T(8,128)(2,1)}, bf16[1088,768]{1,0:T(8,128)(2,1)}, bf16[1088,768]{1,0:T(8,128)(2,1)}, bf16[1088,768]{1,0:T(8,128)(2,1)}, bf16[1088,384]{1,0:T(8,128)(2,1)}) custom-call(s32[1]{0:T(128)} %bitcast.1.len_ref, bf16[2,1024,384]{2,1,0:T(8,128)(2,1)} %bitcast.219, bf16[3,2,256,256]{3,2,1,0:T(8,128)(2,1)} %get-tuple-element.195.w_ref, ...), custom_call_target="tpu_custom_call" | custom-call | flops 30000001024 | bytes 12000000 | tf_op jit(solution)/shard_map/attn_fwd/pallas_call | solution.py:367
  257.6 25.5 %attn_fwd.2 = (bf16[1088,384]{1,0:T(8,128)(2,1)}, bf16[1088,768]{1,0:T(8,128)(2,1)}, bf16[1088,768]{1,0:T(8,128)(2,1)}, bf16[1088,768]{1,0:T(8,128)(2,1)}, bf16[1088,384]{1,0:T(8,128)(2,1)}) custom-call(s32[1]{0:T(128)} %bitcast.1.len_ref, bf16[2,1024,384]{2,1,0:T(8,128)(2,1)} %bitcast.217, bf16[3,2,256,256]{3,2,1,0:T(8,128)(2,1)} %get-tuple-element.196.w_ref, ...), custom_call_target="tpu_custom_call" | custom-call | flops 30000001024 | bytes 12000000 | tf_op jit(solution)/shard_map/attn_fwd/pallas_call | solution.py:367
  283.8 42.4 %middle.1 = (bf16[2,1024,768]{2,1,0:T(8,128)(2,1)}, bf16[1088,768]{1,0:T(8,128)(2,1)}, f32[1088,768]{1,0:T(8,128)}, f32[768,768]{1,0:T(8,128)}, f32[4,256,768]{2...) custom-call(s32[1]{0:T(128)} %bitcast.1.len_ref, ...), custom_call_target="tpu_custom_call" | custom-call | flops 30000001024 | bytes 30000000 | tf_op jit(solution)/shard_map/middle/pallas_call | solution.py:426
  328.1 34.5 %attn_bwd.2 = (bf16[2,1024,384]{2,1,0:T(8,128)(2,1)}, f32[3,2,256,256]{3,2,1,0:T(8,128)}, f32[8,384]{1,0:T(8,128)}) custom-call(s32[1]{0:T(128)} %bitcast.1.len_ref, bf16[1088,768]{1,0:T(8,128)(2,1)} %get-tuple-element.49.qa_ref, bf16[1088,768]{1,0:T(8,128)(2,1)} %get-tuple-element.50.ka_ref, bf16[1088,768]{1,0:T(8,128)(2,1)} %get-tuple-element.51.va_ref, ...), custom_call_target="tpu_custom_call" | custom-call | flops 70000001024 | bytes 16000000 | tf_op jit(solution)/shard_map/attn_bwd/pallas_call | solution.py:392
  363.3 34.5 %attn_bwd.3 = (bf16[2,1024,384]{2,1,0:T(8,128)(2,1)}, f32[3,2,256,256]{3,2,1,0:T(8,128)}, f32[8,384]{1,0:T(8,128)}) custom-call(s32[1]{0:T(128)} %bitcast.1.len_ref, bf16[1088,768]{1,0:T(8,128)(2,1)} %get-tuple-element.55.qa_ref, bf16[1088,768]{1,0:T(8,128)(2,1)} %get-tuple-element.56.ka_ref, bf16[1088,768]{1,0:T(8,128)(2,1)} %get-tuple-element.57.va_ref, ...), custom_call_target="tpu_custom_call" | custom-call | flops 70000001024 | bytes 16000000 | tf_op jit(solution)/shard_map/attn_bwd/pallas_call | solution.py:392
  415.2 2.9 copy.136
  418.1 4.8 reshape.273
  425.5 9.8 %concatenate.28 = f32[768,2944]{1,0:T(8,128)} concatenate(f32[768,768]{1,0:T(8,128)} %get-tuple-element.59, f32[768,768]{1,0:T(8,128)S(1)} %bitcast.201, f32[768,192]{1,0:T(8,128)} %bitcast.211, f32[768,192]{1,0:T(8,128)} %bitcast.210, f32[768,192]{1,0:T(8,128)S(1)} %bitcast.209, f32[768,768]{1,0:T(8,128)} %reshape.273, f32[768,64]{1,0:T(8,128)S(1)} %pad.55), dimensions={1} | concatenate | bytes 18087936 | tf_op jit(solution)/shard_map/concatenate | solution.py:580
  438.2 3.5 all-to-all-start.5
  443.1 37.2 %all-to-all-done.5 = bf16[1,2,32,32,384]{4,3,1,0,2:T(8,128)(2,1)S(1)} async-done(((bf16[1,2,32,32,384]{4,3,1,0,2:T(8,128)(2,1)}), bf16[1,2,32,32,384]{4,3,1,0,2:T(8,128)(2,1)S(1)}, u32[]{:S(2)}, u32[]{:S(2)}) %all-to-all-start.5) | async-done | bytes 1572896 | tf_op jit(solution)/shard_map/all_to_all | solution.py:514
  480.4 2.7 all-to-all-start.4
  483.1 4.1 copy.132
  487.2 34.6 %all-to-all-done.4 = bf16[1,2,32,32,384]{4,3,1,0,2:T(8,128)(2,1)S(1)} async-done(((bf16[1,2,32,32,384]{4,3,1,0,2:T(8,128)(2,1)}), bf16[1,2,32,32,384]{4,3,1,0,2:T(8,128)(2,1)S(1)}, u32[]{:S(2)}, u32[]{:S(2)}) %all-to-all-start.4) | async-done | bytes 1572896 | tf_op jit(solution)/shard_map/all_to_all | solution.py:514
  522.9 2.8 all-to-all-start.3
  529.0 5.2 reduce-scatter.2.cloned.1.call-done
  537.4 3.9 pad_maximum_fusion
  541.3 4.3 gather_fusion.4
  545.6 78.2 %all-to-all-done.3 = bf16[1,2,32,32,768]{4,3,1,0,2:T(8,128)(2,1)S(1)} async-done(((bf16[1,2,32,32,768]{4,3,1,0,2:T(8,128)(2,1)}), bf16[1,2,32,32,768]{4,3,1,0,2:T(8,128)(2,1)S(1)}, u32[]{:S(2)}, u32[]{:S(2)}) %all-to-all-start.3) | async-done | bytes 3145760 | tf_op jit(solution)/shard_map/all_to_all | solution.py:514
  623.8 2.4 gather_fusion.3
  626.2 6.4 broadcast_select_fusion
  632.6 53.7 %all-reduce.15.cloned.1.call-done = f32[192,2944]{1,0:T(8,128)} async-done(((f32[192,2944]{1,0:T(8,128)}), f32[192,2944]{1,0:T(8,128)}) %all-reduce.15.cloned.1.call-update) | async-done | bytes 2261008
  (224 shorter events, 67.0 us)
Async XLA Ops:
  7.2 5.0 copy-start
  71.5 3.4 copy-start.32
  71.5 3.5 copy-start.33
  71.6 3.5 copy-start.34
  71.6 3.5 copy-start.35
  71.6 3.5 copy-start.36
  71.6 3.5 copy-start.37
  71.6 48.6 %all-to-all-start.1 = ((bf16[32,2,1,32,384]{4,3,1,2,0:T(8,128)(2,1)}), bf16[32,2,1,32,384]{4,3,1,2,0:T(8,128)(2,1)S(1)}, u32[]{:S(2)}, u32[]{:S(2)}) async-start(bf16[32,2,1,32,384]{4,3,1,2,0:T(8,128)(2,1)} %bitcast.27), calls=%async_computation.1 | async-start | bytes 3145728 | tf_op jit(solution)/shard_map/all_to_all | solution.py:506
  74.5 136.2 %all-gather.2.cloned.1.call-start = ((), (), s32[]{:S(2)}) async-start(), calls=%async_computation.7 | async-start | bytes 4663296 | tf_op jit(solution)/shard_map/all_gather | solution.py:542
  121.3 87.4 %all-to-all-start.2 = ((bf16[32,2,1,32,768]{4,3,1,2,0:T(8,128)(2,1)}), bf16[32,2,1,32,768]{4,3,1,2,0:T(8,128)(2,1)S(1)}, u32[]{:S(2)}, u32[]{:S(2)}) async-start(bf16[32,2,1,32,768]{4,3,1,2,0:T(8,128)(2,1)} %bitcast.199), calls=%async_computation.2 | async-start | bytes 6291456 | tf_op jit(solution)/shard_map/all_to_all | solution.py:506
  124.2 410.0 %reduce-scatter.2.cloned.1.call-start = ((), (), s32[]{:S(2)}) async-start(), calls=%async_computation.8 | async-start | bytes 11304960 | tf_op jit(solution)/shard_map/reduce_scatter | solution.py:584
  124.2 3.4 copy-start.3
  399.2 4.6 copy-start.16
  403.8 4.6 copy-start.13
  418.1 4.9 copy-start.20
  418.1 4.9 copy-start.23
  418.1 4.9 copy-start.26
  418.1 4.9 copy-start.29
  418.1 5.1 copy-start.19
  418.1 5.1 copy-start.21
  418.1 5.1 copy-start.25
  418.1 5.1 copy-start.27
  438.2 3.5 copy-start.14
  438.2 42.2 %all-to-all-start.5 = ((bf16[1,2,32,32,384]{4,3,1,0,2:T(8,128)(2,1)}), bf16[1,2,32,32,384]{4,3,1,0,2:T(8,128)(2,1)S(1)}, u32[]{:S(2)}, u32[]{:S(2)}) async-start(bf16[1,2,32,32,384]{4,3,1,0,2:T(8,128)(2,1)} %copy.134), calls=%async_computation.5 | async-start | bytes 3145728 | tf_op jit(solution)/shard_map/all_to_all | solution.py:514
  480.4 6.8 copy-start.4
  480.4 41.4 %all-to-all-start.4 = ((bf16[1,2,32,32,384]{4,3,1,0,2:T(8,128)(2,1)}), bf16[1,2,32,32,384]{4,3,1,0,2:T(8,128)(2,1)S(1)}, u32[]{:S(2)}, u32[]{:S(2)}) async-start(bf16[1,2,32,32,384]{4,3,1,0,2:T(8,128)(2,1)} %copy.133), calls=%async_computation.4 | async-start | bytes 3145728 | tf_op jit(solution)/shard_map/all_to_all | solution.py:514
  487.2 38.6 %copy-start.31 = (s32[32,2]{1,0:T(8,128)S(1)}, s32[32,2]{1,0:T(8,128)}, u32[]{:S(2)}) copy-start(s32[32,2]{1,0:T(8,128)} %copy-done.30) | copy-start | bytes 772
  487.2 40.6 %copy-start.48 = (u32[32]{0:T(128)S(1)}, u32[32]{0:T(128)}, u32[]{:S(2)}) copy-start(u32[32]{0:T(128)} %constant.97) | copy-start | bytes 388
  522.9 100.9 %all-to-all-start.3 = ((bf16[1,2,32,32,768]{4,3,1,0,2:T(8,128)(2,1)}), bf16[1,2,32,32,768]{4,3,1,0,2:T(8,128)(2,1)S(1)}, u32[]{:S(2)}, u32[]{:S(2)}) async-start(bf16[1,2,32,32,768]{4,3,1,0,2:T(8,128)(2,1)} %copy.132), calls=%async_computation.3 | async-start | bytes 6291456 | tf_op jit(solution)/shard_map/all_to_all | solution.py:514
  525.7 10.1 %copy-start.38 = (f32[8,128]{1,0:T(8,128)S(1)}, f32[8,128]{1,0:T(8,128)}, u32[]{:S(2)}) copy-start(f32[8,128]{1,0:T(8,128)} %get-tuple-element.68) | copy-start | bytes 12292
  525.7 160.6 %all-reduce.15.cloned.1.call-start = ((), (), s32[]{:S(2)}) async-start(), calls=%async_computation.9 | async-start | bytes 4521984
  626.2 67.4 %copy-start.1 = (bf16[64,32,768]{2,1,0:T(8,128)(2,1)S(1)}, bf16[64,32,768]{2,1,0:T(8,128)(2,1)}, u32[]{:S(2)}) copy-start(bf16[64,32,768]{2,1,0:T(8,128)(2,1)} %param.22) | copy-start | bytes 9437188
  (25 other events, 55.2 us)
Sparse Core Ops, SparseCore 0:
  78.1 90.9 all-gather.1
  435.5 98.6 reduce-scatter.1
  537.8 148.4 all-reduce.14

commit v2 on v1

v2 whole, which is shorter than its diff:
```python
import functools

import jax
import jax.numpy as jnp
from jax import lax
from jax.experimental import pallas as pl
from jax.experimental.pallas import tpu as pltpu
from jax.sharding import PartitionSpec as P

AXES = ("dp", "fsdp")
D = 768
FF = 3072
HALF = D // 2
HEAD = 64
WIN = 256
SEQ = 1024
SHORT = 64
BLOCK = 32
ROWS = SEQ + SHORT
TILE = 272
TILES = ROWS // TILE
BIG = 1e30

norm_eps = 1e-12
rms_eps = 1e-06
bf16 = jnp.bfloat16
f32 = jnp.float32

NN = (((1,), (0,)), ((), ()))
NT = (((1,), (1,)), ((), ()))
TN = (((0,), (0,)), ((), ()))


def mm(left, right, dims):
    return lax.dot_general(left, right, dims, preferred_element_type=f32)


def exchange():
    row = lax.broadcasted_iota(jnp.int32, (WIN, WIN), 0)
    col = lax.broadcasted_iota(jnp.int32, (WIN, WIN), 1)
    return jnp.where(row + col == WIN - 1, 1.0, 0.0).astype(bf16)


def row_ids(start, count, width):
    return start + lax.broadcasted_iota(jnp.int32, (count, width), 0)


def block_rows(ref, seq, start, count):
    values = ref[start // BLOCK : (start + count) // BLOCK, seq]
    return values.reshape(count, values.shape[-1])


def merge_rows(pair_ref, packed_ref, first_len):
    width = packed_ref.shape[1]
    flip = exchange()
    packed_ref[0:SHORT, :] = block_rows(pair_ref, 0, 0, SHORT)
    for step in range(SEQ // WIN):
        start = SHORT + WIN * step
        flipped = mm(flip, block_rows(pair_ref, 1, SEQ - WIN * (step + 1), WIN), NN)
        inside = min(WIN, SEQ - start)
        own = block_rows(pair_ref, 0, start, inside).astype(f32)
        keep = row_ids(start, inside, width) < first_len
        packed_ref[start : start + inside, :] = jnp.where(keep, own, flipped[0:inside]).astype(bf16)
        if inside < WIN:
            packed_ref[start + inside : start + WIN, :] = flipped[inside:].astype(bf16)


def unmerge_rows(packed_ref, pair_ref, first_len):
    width = packed_ref.shape[1]
    flip = exchange()
    blocks = WIN // BLOCK
    for step in range(SEQ // WIN):
        start = WIN * step
        ids = row_ids(start, WIN, width)
        own = packed_ref[start : start + WIN, :].astype(f32)
        own = jnp.where(ids < first_len, own, 0.0).astype(bf16)
        pair_ref[blocks * step : blocks * (step + 1), 0] = own.reshape(blocks, BLOCK, width)
        source = ROWS - WIN * (step + 1)
        flipped = mm(flip, packed_ref[source : source + WIN, :], NN)
        flipped = jnp.where(ids < ROWS - first_len, flipped, 0.0).astype(bf16)
        pair_ref[blocks * step : blocks * (step + 1), 1] = flipped.reshape(blocks, BLOCK, width)


def spare_of(group):
    return 192 if group % 2 == 0 else 0


def with_ones(window, group):
    lane = lax.broadcasted_iota(jnp.int32, window.shape, 1)
    return jnp.where(lane == spare_of(group), 1.0, window.astype(f32)).astype(bf16)


def without_bias(window, group):
    lane = lax.broadcasted_iota(jnp.int32, window.shape, 1)
    return jnp.where(lane == spare_of(group), 0.0, window.astype(f32)).astype(bf16)


def first_row(group):
    return 0 if group % 2 == 0 else 64


def windows(values, count):
    parts = []
    for group in range(count):
        start = (group // 2) * HALF + (group % 2) * 128
        parts.append(values[:, start : start + WIN])
    return parts


def join(parts):
    pieces = []
    for first, second in zip(parts[0::2], parts[1::2]):
        pieces += [first[:, :128], first[:, 128:] + second[:, :128], second[:, 128:]]
    return jnp.concatenate(pieces, axis=1)


def split_three(value):
    high = value.astype(bf16)
    rest = value - high.astype(f32)
    mid = rest.astype(bf16)
    low = (rest - mid.astype(f32)).astype(bf16)
    return high, mid, low


def attn_fwd_kernel(
    len_ref, tok_ref, full_ref, x_ref, qa_ref, ka_ref, va_ref, ctx_ref, q_s, k_s, v_s, w_s
):
    pair = pl.program_id(0)
    first_len = len_ref[0]

    @pl.when(pair == 0)
    def _():
        merge_rows(tok_ref, x_ref, first_len)
        w_s[...] = jnp.zeros_like(w_s)
        for which in range(3):
            for g in range(2):
                w_s[which, g, first_row(g) : first_row(g) + 192, :] = full_ref[
                    192 * g : 192 * (g + 1), WIN * which : WIN * (which + 1)
                ]
        cols = [with_ones(part, g) for g, part in enumerate(windows(x_ref[...], 2))]
        for which, target in enumerate((q_s, k_s, v_s)):
            value = join([mm(cols[g], w_s[which, g], NT) for g in range(2)])
            if which == 0:
                value = value.astype(bf16).astype(f32) * (HEAD**-0.5)
            target[...] = value.astype(bf16)

    lane0 = pl.multiple_of(pair * 128, 128)
    q_pair = q_s[:, pl.ds(lane0, 128)]
    k_pair = k_s[:, pl.ds(lane0, 128)]
    v_pair = v_s[:, pl.ds(lane0, 128)]
    lane = lax.broadcasted_iota(jnp.int32, (ROWS, 128), 1)
    in_first = row_ids(0, ROWS, 128) < first_len
    one = jnp.ones((ROWS, 128), f32)
    zero = jnp.zeros((ROWS, 128), f32)
    for head in range(2):
        spare = 64 * (1 - head)
        own = (lane // 64) == head
        first_one = jnp.where(in_first, one, zero)
        q_extra = jnp.where(
            lane == spare, first_one, jnp.where(lane == spare + 1, one - first_one, zero)
        )
        k_extra = jnp.where(
            lane == spare,
            (first_one - one) * BIG,
            jnp.where(
                lane == spare + 1,
                first_one * (-BIG),
                jnp.where((lane >= spare + 2) & (lane < spare + 5), one, zero),
            ),
        )
        v_extra = jnp.where((lane >= spare) & (lane < spare + 3), one, zero)
        cols = slice(128 * head, 128 * (head + 1))
        qa_ref[:, cols] = jnp.where(own, q_pair.astype(f32), q_extra).astype(bf16)
        ka_ref[:, cols] = jnp.where(own, k_pair.astype(f32), k_extra).astype(bf16)
        va_ref[:, cols] = jnp.where(own, v_pair.astype(f32), v_extra).astype(bf16)

    tile_lane = lax.broadcasted_iota(jnp.int32, (TILE, 128), 1)

    def one_tile(index, carry):
        start = pl.multiple_of(index * TILE, 16)
        rows = pl.ds(start, TILE)
        result = None
        for head in range(2):
            cols = slice(128 * head, 128 * (head + 1))
            spare = 64 * (1 - head)
            q_tile = qa_ref[rows, cols]
            scores = mm(q_tile, ka_ref[:, cols], NT)
            top = jnp.max(scores, axis=1, keepdims=True)
            weights = jnp.exp(scores - top)
            mixed = mm(weights.astype(bf16), va_ref[:, cols], NN)
            total = mixed[:, spare : spare + 1]
            mixed = mixed / total
            log_total = top + jnp.log(total)
            high, mid, low = split_three(-log_total)
            q_new = jnp.where(
                tile_lane == spare + 2,
                high.astype(f32),
                jnp.where(
                    tile_lane == spare + 3,
                    mid.astype(f32),
                    jnp.where(tile_lane == spare + 4, low.astype(f32), q_tile.astype(f32)),
                ),
            )
            qa_ref[rows, cols] = q_new.astype(bf16)
            result = mixed if head == 0 else jnp.where(tile_lane < 64, result, mixed)
        ctx_ref[rows, :] = result.astype(bf16)
        return carry

    lax.fori_loop(0, TILES, one_tile, 0)


def attn_bwd_kernel(
    len_ref, qa_ref, ka_ref, va_ref, ctx_ref, gctx_ref, x_ref, base_ref, full_ref,
    ig_ref, dw_ref, dq_s, dk_s, dv_s, do_s, dqt_s, ig_s, w_s,
):
    pair = pl.program_id(0)
    lane0 = pl.multiple_of(pair * 128, 128)
    lane = lax.broadcasted_iota(jnp.int32, (ROWS, 128), 1)
    grad = gctx_ref[...].astype(f32)
    product = grad * ctx_ref[...].astype(f32)
    for head in range(2):
        own = (lane // 64) == head
        spare = 64 * (1 - head)
        inner = -jnp.sum(jnp.where(own, product, 0.0), axis=1, keepdims=True)
        high, mid, low = split_three(inner)
        extra = jnp.where(
            lane == spare,
            high.astype(f32),
            jnp.where(
                lane == spare + 1,
                mid.astype(f32),
                jnp.where(lane == spare + 2, low.astype(f32), 0.0),
            ),
        )
        do_s[:, 128 * head : 128 * (head + 1)] = jnp.where(own, grad, extra).astype(bf16)
    dqt_s[...] = jnp.zeros_like(dqt_s)
    tile_lane = lax.broadcasted_iota(jnp.int32, (TILE, 128), 1)

    def one_tile(index, carry):
        start = pl.multiple_of(index * TILE, 16)
        rows = pl.ds(start, TILE)
        dk_tile = None
        dv_tile = None
        for head in range(2):
            cols = slice(128 * head, 128 * (head + 1))
            k_tile = ka_ref[rows, cols]
            probs = jnp.exp(mm(k_tile, qa_ref[:, cols], NT))
            scaled = mm(va_ref[rows, cols], do_s[:, cols], NT) * probs
            grad_scores = scaled.astype(bf16)
            dv_new = mm(probs.astype(bf16), do_s[:, cols], NN)
            dk_new = mm(grad_scores, qa_ref[:, cols], NN)
            dq_new = mm(k_tile, grad_scores, TN)
            dqt_s[64 * head : 64 * (head + 1), :] += dq_new[64 * head : 64 * (head + 1), :]
            dk_tile = dk_new if head == 0 else jnp.where(tile_lane < 64, dk_tile, dk_new)
            dv_tile = dv_new if head == 0 else jnp.where(tile_lane < 64, dv_tile, dv_new)
        dk_s[rows, pl.ds(lane0, 128)] = dk_tile.astype(bf16)
        dv_s[rows, pl.ds(lane0, 128)] = dv_tile.astype(bf16)
        return carry

    lax.fori_loop(0, TILES, one_tile, 0)
    dq_s[:, pl.ds(lane0, 128)] = (jnp.transpose(dqt_s[...]) * (HEAD**-0.5)).astype(bf16)

    @pl.when(pair == pl.num_programs(0) - 1)
    def _():
        x_cols = [with_ones(part, g) for g, part in enumerate(windows(x_ref[...], 2))]
        total = [None, None]
        for which, source in enumerate((dq_s, dk_s, dv_s)):
            cols = windows(source[...], 2)
            for g in range(2):
                own = slice(first_row(g), first_row(g) + 192)
                w_s[own, :] = without_bias(
                    full_ref[192 * g : 192 * (g + 1), WIN * which : WIN * (which + 1)], g
                )
                if first_row(g) == 0:
                    w_s[192:, :] = jnp.zeros((64, WIN), bf16)
                else:
                    w_s[:64, :] = jnp.zeros((64, WIN), bf16)
                grad = mm(cols[g], x_cols[g], TN)
                dw_ref[192 * g : 192 * (g + 1), WIN * which : WIN * (which + 1)] = grad[own].astype(
                    bf16
                )
                part = mm(cols[g], w_s[...], NN)
                total[g] = part if which == 0 else total[g] + part
        ig_s[...] = (join(total) + base_ref[...]).astype(bf16)
        unmerge_rows(ig_s, ig_ref, len_ref[0])


def norm(values):
    mean = jnp.mean(values, axis=1, keepdims=True)
    centered = values - mean
    var = jnp.mean(centered * centered, axis=1, keepdims=True)
    inv = lax.rsqrt(var + norm_eps)
    return centered * inv, inv


def norm_back(grad_n, n, inv):
    mean_g = jnp.mean(grad_n, axis=1, keepdims=True)
    mean_gn = jnp.mean(grad_n * n, axis=1, keepdims=True)
    return (grad_n - mean_g - n * mean_gn) * inv


def mid_fwd_kernel(
    len_ref, x0_ref, x1_ref, ctx0_ref, ctx1_ref, full_ref, wu_ref, vec_ref,
    out_ref, n1_ref, n2_ref, inv_ref, slope_ref, act_ref, stat_ref, out_s, wd_s, stat_s,
):
    step = pl.program_id(0)
    first_len = len_ref[0]

    @pl.when(step == 0)
    def _():
        stat_s[...] = jnp.zeros_like(stat_s)
        wd_s[...] = jnp.zeros_like(wd_s)
        for g in range(4):
            wd_s[g, first_row(g) : first_row(g) + 192, :] = full_ref[192 * g : 192 * (g + 1), D:]

    o_bias, gain1, shift1, down_bias, gain2, shift2 = (vec_ref[i : i + 1, :] for i in range(6))
    start = pl.multiple_of(step * TILE, 16)
    rows = pl.ds(start, TILE)
    keep = jnp.where(row_ids(start, TILE, D) < first_len, 1.0, 0.0)

    def note(slot, values):
        square = values * values
        stat_s[slot : slot + 1, :] += jnp.sum(square, axis=0, keepdims=True)
        stat_s[slot + 4 : slot + 5, :] += jnp.sum(square * keep, axis=0, keepdims=True)

    inputs = jnp.concatenate([x0_ref[...], x1_ref[...]], axis=1).astype(f32)
    context = jnp.concatenate([ctx0_ref[...], ctx1_ref[...]], axis=1)
    note(0, inputs)
    branch_attn = mm(context, full_ref[:, :D], NT) + o_bias
    note(1, branch_attn)
    n1, inv1 = norm(inputs + branch_attn)
    n1_ref[...] = n1
    first_norm = n1 * gain1 + shift1
    note(2, first_norm)
    low_cols = windows(first_norm.astype(bf16), 4)
    parts = []
    for g in range(4):
        cols = slice(D * g, D * (g + 1))
        up = mm(with_ones(low_cols[g], g), wu_ref[D * g : D * (g + 1), :], NT)
        gate = 0.5 * (1.0 + lax.erf(up * (2.0**-0.5)))
        slope_ref[:, cols] = gate + up * jnp.exp(up * up * -0.5) * 0.3989422804014327
        act = (up * gate).astype(bf16)
        act_ref[:, cols] = act
        parts.append(mm(act, wd_s[g], NT))
    branch_ffn = join(parts) + down_bias
    note(3, branch_ffn)
    n2, inv2 = norm(first_norm + branch_ffn)
    n2_ref[...] = n2
    lane = lax.broadcasted_iota(jnp.int32, (TILE, 128), 1)
    inv_ref[...] = jnp.where(lane < 64, inv1, inv2)
    out_s[rows, :] = (n2 * gain2 + shift2).astype(bf16)

    @pl.when(step == pl.num_programs(0) - 1)
    def _():
        unmerge_rows(out_s, out_ref, first_len)
        stat_ref[...] = jnp.broadcast_to(
            jnp.sum(stat_s[...], axis=1, keepdims=True), stat_ref.shape
        )


def mid_bwd_kernel(
    len_ref, cot_ref, ctx0_ref, ctx1_ref, n1_ref, n2_ref, inv_ref, slope_ref, act_ref,
    full_ref, wu_ref, vec_ref, gctx_ref, base_ref, grad_ref,
    cot_s, wd_s, dwd_s, dwu_s, vec_s, turn_s,
):
    step = pl.program_id(0)

    @pl.when(step == 0)
    def _():
        merge_rows(cot_ref, cot_s, len_ref[0])
        for target in (dwd_s, dwu_s, vec_s, wd_s):
            target[...] = jnp.zeros_like(target)
        grad_ref[:, :D] = jnp.zeros((D, D), f32)
        for g in range(4):
            wd_s[g, first_row(g) : first_row(g) + 192, :] = full_ref[192 * g : 192 * (g + 1), D:]

    gain1, shift1, gain2 = (vec_ref[i : i + 1, :] for i in (1, 2, 4))
    start = pl.multiple_of(step * TILE, 16)
    rows = pl.ds(start, TILE)

    def add_vec(slot, values):
        vec_s[slot : slot + 1, :] += jnp.sum(values, axis=0, keepdims=True)

    context = jnp.concatenate([ctx0_ref[...], ctx1_ref[...]], axis=1)
    n1 = n1_ref[...]
    n2 = n2_ref[...]
    inv1 = inv_ref[:, 0:1]
    inv2 = inv_ref[:, 64:65]
    low_cols = windows((n1 * gain1 + shift1).astype(bf16), 4)
    grad_out = cot_s[rows, :].astype(f32)
    add_vec(4, grad_out * n2)
    add_vec(5, grad_out)
    grad_sum2 = norm_back(grad_out * gain2, n2, inv2)
    grad_ffn = grad_sum2.astype(bf16)
    add_vec(3, grad_ffn.astype(f32))
    ffn_cols = windows(grad_ffn, 4)
    parts = []
    for g in range(4):
        cols = slice(D * g, D * (g + 1))
        dwd_s[g] += mm(ffn_cols[g], act_ref[:, cols], TN)
        grad_up = (mm(ffn_cols[g], wd_s[g], NN) * slope_ref[:, cols]).astype(bf16)
        dwu_s[g] += mm(with_ones(low_cols[g], g), grad_up, TN)
        parts.append(mm(grad_up, without_bias(wu_ref[D * g : D * (g + 1), :], g), NN))
    grad_first = join(parts) + grad_sum2
    add_vec(1, grad_first * n1)
    add_vec(2, grad_first)
    grad_sum1 = norm_back(grad_first * gain1, n1, inv1)
    base_ref[...] = grad_sum1
    grad_branch = grad_sum1.astype(bf16)
    add_vec(0, grad_branch.astype(f32))
    grad_ref[:, :D] += mm(grad_branch, context, TN)
    gctx_ref[...] = mm(grad_branch, full_ref[:, :D], NN).astype(bf16)

    @pl.when(step == pl.num_programs(0) - 1)
    def _():
        for g in range(4):
            own = slice(192 * g, 192 * (g + 1))
            grad_ref[own, D : 2 * D] = dwd_s[g, first_row(g) : first_row(g) + 192, :]
            turned = jnp.transpose(dwu_s[g])
            for half in range(2):
                turn_s[...] = turned[:, 128 * half : 128 * (half + 1)]
                for j in range(4):
                    lane0 = 2 * D + WIN * j + 128 * half
                    grad_ref[own, lane0 : lane0 + 128] = turn_s[pl.ds(j, 192, stride=4), :]
        grad_ref[:, 2 * D + 4 * WIN :] = jnp.transpose(vec_s[...])


def whole(shape):
    zeros = (0,) * len(shape)
    return pl.BlockSpec(shape, lambda i, *_: zeros, pipeline_mode=pl.Buffered(1))


def kept(shape):
    zeros = (0,) * len(shape)
    return pl.BlockSpec(shape, lambda i, *_: zeros)


def struct(shape, dtype):
    return jax.ShapeDtypeStruct(shape, dtype)


PARAMS = pltpu.CompilerParams(
    dimension_semantics=("arbitrary",), vmem_limit_bytes=63_000_000
)


GRAD_COLS = 2 * D + 4 * WIN + 128


def attn_fwd(len_arr, tok, full, half):
    pair_cols = lambda width: pl.BlockSpec((ROWS, width), lambda i, *_: (0, i))
    return pl.pallas_call(
        attn_fwd_kernel,
        name="attn_fwd",
        grid_spec=pltpu.PrefetchScalarGridSpec(
            num_scalar_prefetch=1,
            grid=(3,),
            in_specs=[
                whole(tok.shape),
                pl.BlockSpec((HALF, D), lambda i, *_: (half, 0), pipeline_mode=pl.Buffered(1)),
            ],
            out_specs=[
                kept((ROWS, HALF)), pair_cols(256), pair_cols(256), pair_cols(256), pair_cols(128),
            ],
            scratch_shapes=[pltpu.VMEM((ROWS, HALF), bf16)] * 3
            + [pltpu.VMEM((3, 2, WIN, WIN), bf16)],
        ),
        out_shape=[
            struct((ROWS, HALF), bf16), struct((ROWS, D), bf16), struct((ROWS, D), bf16),
            struct((ROWS, D), bf16), struct((ROWS, HALF), bf16),
        ],
        compiler_params=PARAMS,
        cost_estimate=pl.CostEstimate(
            flops=20_000_000_000, bytes_accessed=12_000_000, transcendentals=7_000_000
        ),
    )(len_arr, tok, full)


def attn_bwd(len_arr, qa, ka, va, ctx, gctx, x, base, full, half):
    pair_cols = lambda width, first: pl.BlockSpec((ROWS, width), lambda i, *_: (0, i + first))
    return pl.pallas_call(
        attn_bwd_kernel,
        name="attn_bwd",
        grid_spec=pltpu.PrefetchScalarGridSpec(
            num_scalar_prefetch=1,
            grid=(3,),
            in_specs=[
                pair_cols(256, 0), pair_cols(256, 0), pair_cols(256, 0), pair_cols(128, 0),
                pair_cols(128, 3 * half), whole(x.shape),
                pl.BlockSpec((ROWS, HALF), lambda i, *_: (0, half), pipeline_mode=pl.Buffered(1)),
                pl.BlockSpec((HALF, D), lambda i, *_: (half, 0), pipeline_mode=pl.Buffered(1)),
            ],
            out_specs=[kept((SEQ // BLOCK, 2, BLOCK, HALF)), kept((HALF, D))],
            scratch_shapes=[
                pltpu.VMEM((ROWS, HALF), bf16),
                pltpu.VMEM((ROWS, HALF), bf16),
                pltpu.VMEM((ROWS, HALF), bf16),
                pltpu.VMEM((ROWS, 256), bf16),
                pltpu.VMEM((128, ROWS), f32),
                pltpu.VMEM((ROWS, HALF), bf16),
                pltpu.VMEM((WIN, WIN), bf16),
            ],
        ),
        out_shape=[struct((SEQ // BLOCK, 2, BLOCK, HALF), bf16), struct((HALF, D), bf16)],
        compiler_params=PARAMS,
        cost_estimate=pl.CostEstimate(
            flops=30_000_000_000, bytes_accessed=16_000_000, transcendentals=7_000_000
        ),
    )(len_arr, qa, ka, va, ctx, gctx, x, base, full)


def row_tile(width):
    return pl.BlockSpec((TILE, width), lambda i, *_: (i, 0))


def mid_fwd(len_arr, x0, x1, ctx0, ctx1, full, wu, vecs):
    outs = [
        ((SEQ // BLOCK, 2, BLOCK, D), bf16), ((ROWS, D), f32), ((ROWS, D), f32), ((ROWS, 128), f32),
        ((ROWS, FF), f32), ((ROWS, FF), bf16), ((8, 128), f32),
    ]
    return pl.pallas_call(
        mid_fwd_kernel,
        name="mid_fwd",
        grid_spec=pltpu.PrefetchScalarGridSpec(
            num_scalar_prefetch=1,
            grid=(TILES,),
            in_specs=[row_tile(HALF)] * 4
            + [whole((D, 2 * D)), whole(wu.shape), whole(vecs.shape)],
            out_specs=[
                kept(outs[0][0]), row_tile(D), row_tile(D), row_tile(128), row_tile(FF),
                row_tile(FF), kept((8, 128)),
            ],
            scratch_shapes=[
                pltpu.VMEM((ROWS, D), bf16),
                pltpu.VMEM((4, WIN, D), bf16),
                pltpu.VMEM((8, D), f32),
            ],
        ),
        out_shape=[struct(*o) for o in outs],
        compiler_params=PARAMS,
        cost_estimate=pl.CostEstimate(
            flops=15_000_000_000, bytes_accessed=36_000_000, transcendentals=7_000_000
        ),
    )(len_arr, x0, x1, ctx0, ctx1, full, wu, vecs)


def mid_bwd(len_arr, cot, ctx0, ctx1, n1, n2, inv, slope, act, full, wu, vecs):
    outs = [((ROWS, D), bf16), ((ROWS, D), f32), ((D, GRAD_COLS), f32)]
    return pl.pallas_call(
        mid_bwd_kernel,
        name="mid_bwd",
        grid_spec=pltpu.PrefetchScalarGridSpec(
            num_scalar_prefetch=1,
            grid=(TILES,),
            in_specs=[
                whole(cot.shape), row_tile(HALF), row_tile(HALF), row_tile(D), row_tile(D),
                row_tile(128), row_tile(FF), row_tile(FF), whole((D, 2 * D)), whole(wu.shape),
                whole(vecs.shape),
            ],
            out_specs=[
                row_tile(D),
                row_tile(D),
                pl.BlockSpec((D, GRAD_COLS), lambda i, *_: (0, 0), pipeline_mode=pl.Buffered(1)),
            ],
            scratch_shapes=[
                pltpu.VMEM((ROWS, D), bf16),
                pltpu.VMEM((4, WIN, D), bf16),
                pltpu.VMEM((4, WIN, D), f32),
                pltpu.VMEM((4, WIN, D), f32),
                pltpu.VMEM((128, D), f32),
                pltpu.VMEM((D, 128), f32),
            ],
        ),
        out_shape=[struct(*o) for o in outs],
        compiler_params=PARAMS,
        cost_estimate=pl.CostEstimate(
            flops=30_000_000_000, bytes_accessed=50_000_000, transcendentals=10_000
        ),
    )(len_arr, cot, ctx0, ctx1, n1, n2, inv, slope, act, full, wu, vecs)


def pick(values, index):
    return values.at[index].get(mode="promise_in_bounds")


def tie(*values):
    return lax.optimization_barrier(values)


def on_device(
    tokens, cotangent, lengths, permutation, q_weight, q_bias, k_weight, v_weight, v_bias, o_weight,
    o_bias, norm1_gain, norm1_bias, up_weight, up_bias, down_weight, down_bias, norm2_gain,
    norm2_bias,
):
    devices = lax.axis_size(AXES)
    my_index = lax.axis_index(AXES)
    seq_total, piece_len, _ = tokens.shape
    seq_dev = seq_total // devices
    rows_dev = q_weight.shape[0]
    up_dev = up_weight.shape[0]
    odd = (my_index // (devices // 4)) % 2 == 1

    def padded(weight, bias):
        column = bias[:, None]
        gap = jnp.zeros((weight.shape[0], 63), bf16)
        return jnp.where(
            odd,
            jnp.concatenate([column, gap, weight], axis=1),
            jnp.concatenate([weight, column, gap], axis=1),
        )

    small = [o_bias, norm1_gain, norm1_bias, down_bias, norm2_gain, norm2_bias]
    full_in = lax.all_gather(
        jnp.concatenate(
            [
                padded(q_weight, q_bias),
                padded(k_weight, jnp.zeros_like(q_bias)),
                padded(v_weight, v_bias),
            ],
            axis=1,
        ),
        AXES,
        axis=0,
        tiled=True,
    )
    rest, full_in = tie(
        jnp.concatenate(
            [
                o_weight,
                down_weight,
                padded(up_weight, up_bias).reshape(rows_dev, 4 * WIN),
                jnp.pad(jnp.stack(small, axis=1), ((0, 0), (0, 122))),
            ],
            axis=1,
        ),
        full_in,
    )
    full = lax.all_gather(rest, AXES, axis=0, tiled=True)

    dealt_lengths = pick(lengths, permutation).reshape(devices, seq_dev)
    swap = dealt_lengths[:, 0] < dealt_lengths[:, 1]
    dealt = permutation.reshape(devices, seq_dev)
    order = jnp.where(swap[:, None], dealt[:, ::-1], dealt).reshape(seq_total)
    places = jnp.arange(seq_total, dtype=jnp.int32)
    inverse = jnp.sum(jnp.where(order[None, :] == places[:, None], places[None, :], 0), axis=1)
    my_swap = lax.dynamic_index_in_dim(swap, my_index, 0, False)
    len_arr = jnp.max(lax.dynamic_slice_in_dim(dealt_lengths, my_index, 1, 0)).reshape(1)

    def swap_blocks(rows):
        return lax.all_to_all(rows, AXES, split_axis=0, concat_axis=0, tiled=True)

    def arrive(rows):
        width = rows.shape[-1]
        moved = swap_blocks(rows.reshape(devices, seq_dev, piece_len, width))
        if piece_len == BLOCK:
            return moved
        moved = moved.transpose(1, 0, 2, 3).reshape(seq_dev, SEQ // BLOCK, BLOCK, width)
        return moved.transpose(1, 0, 2, 3)

    def leave(rows):
        width = rows.shape[-1]
        if piece_len != BLOCK:
            rows = rows.transpose(1, 0, 2, 3).reshape(seq_dev, devices, piece_len, width)
            rows = rows.transpose(1, 0, 2, 3)
        return swap_blocks(rows).reshape(seq_total, piece_len, width)

    dealt_tokens = pick(tokens, order)
    dealt_cot = pick(cotangent, order)
    tok0 = arrive(dealt_tokens[:, :, :HALF])
    second, tok0 = tie(dealt_tokens[:, :, HALF:], tok0)
    tok1 = arrive(second)
    dealt_cot, tok1 = tie(dealt_cot, tok1)
    cot = arrive(dealt_cot)

    x0, qa0, ka0, va0, ctx0 = attn_fwd(len_arr, tok0, full_in, 0)
    x1, qa1, ka1, va1, ctx1 = attn_fwd(len_arr, tok1, full_in, 1)
    wu = full[:, 2 * D : 2 * D + 4 * WIN].reshape(FF, WIN)
    vecs = jnp.pad(full[:, 2 * D + 4 * WIN : 2 * D + 4 * WIN + 6].astype(f32).T, ((0, 2), (0, 0)))
    out, n1, n2, inv, slope, act, stat = mid_fwd(len_arr, x0, x1, ctx0, ctx1, full, wu, vecs)
    cot, out = tie(cot, out)
    back_out = leave(out)
    gctx, base, grads = mid_bwd(
        len_arr, cot, ctx0, ctx1, n1, n2, inv, slope, act, full, wu, vecs
    )
    mine = lax.psum_scatter(grads, "dp", scatter_dimension=0, tiled=True)
    mine = lax.psum_scatter(mine, "fsdp", scatter_dimension=0, tiled=True)
    ig0, dw0 = attn_bwd(len_arr, qa0, ka0, va0, ctx0, gctx, x0, base, full_in, 0)
    ig0, back_out = tie(ig0, back_out)
    back0 = leave(ig0)
    ig1, dw1 = attn_bwd(len_arr, qa1, ka1, va1, ctx1, gctx, x1, base, full_in, 1)
    ig1, back0 = tie(ig1, back0)
    back1 = leave(ig1)
    moved = swap_blocks(jnp.concatenate([dw0, dw1], axis=0).reshape(devices, rows_dev, D))
    mine_in = jnp.sum(moved.astype(f32), axis=0)

    output = pick(back_out, inverse)
    input_grad = jnp.concatenate([pick(back0, inverse), pick(back1, inverse)], axis=-1)
    lens = jnp.stack([len_arr[0], ROWS - len_arr[0]]).astype(f32)
    sums = jnp.stack([stat[4:8, 0], stat[0:4, 0] - stat[4:8, 0]], axis=1)
    rms = jnp.sqrt(sums / (lens[None, :] * D) + rms_eps)
    stream_rms = jnp.where(my_swap, rms[:, ::-1], rms)
    vec = lambda i: mine[:, 2 * D + 4 * WIN + i]

    def unpadded(block):
        return (
            jnp.where(odd, block[:, 64:], block[:, :192]),
            jnp.where(odd, block[:, 0], block[:, 192]),
        )

    dq, dqb = unpadded(mine_in[:, :WIN])
    dk, _ = unpadded(mine_in[:, WIN : 2 * WIN])
    dv, dvb = unpadded(mine_in[:, 2 * WIN :])
    dup, dub = unpadded(mine[:, 2 * D : 2 * D + 4 * WIN].reshape(up_dev, WIN))
    return (
        output, input_grad, dq, dqb, dk, dv, dvb, mine[:, :D], vec(0), vec(1), vec(2), dup, dub,
        mine[:, D : 2 * D], vec(3), vec(4), vec(5), stream_rms,
    )


def solution(mesh):
    rows = P(None, AXES, None)
    mat = P(AXES, None)
    vec = P(AXES)
    in_specs = (
        rows, rows, P(), P(), mat, vec, mat, mat, vec, mat, vec, vec, vec, mat, vec, mat, vec, vec,
        vec,
    )
    out_specs = (
        rows, rows, mat, vec, mat, mat, vec, mat, vec, vec, vec, mat, vec, mat, vec, vec, vec,
        P(None, AXES),
    )
    return jax.shard_map(
        on_device, mesh=mesh, in_specs=in_specs, out_specs=out_specs, check_vma=False
    )
```

time: 708 us -> 556 us (0.79)
  local copies, waits for them, and re-layouts: 101 us -> 31.8 us
  blocking collectives: 45.9 us -> 0 us
  waiting for transfers between devices: 333 us -> 289 us
  starting transfers between devices: 14.7 us -> 28.3 us
  Pallas kernels: 162 us -> 173 us
  other arithmetic: 26.4 us -> 16.6 us
    all_to_all x5 -> x7, waiting for transfers between devices: 274 us -> 167 us  [swap_blocks(): return lax.all_to_all(rows, AXES, split_axis=0, concat_axis=0, tiled=True)]
    all_gather x1 -> x2, waiting for transfers between devices: 0.01 us -> 62.1 us  [the longest x1 62.1 us: on_device(): lax.all_gather(jnp.concatenate([padded(q_weight, q_bias), padded(k_weight...]
    all_to_all x1 -> x0, blocking collectives: 45.9 us -> none  [arrive(): lax.all_to_all(rows.reshape(devices, seq_dev, 1, piece_len, width), AXES,...]
    reshape x15 -> x3, local copies, waits for them, and re-layouts: 18 us -> 2.36 us  [the longest x1 2.23 us: on_device(): wu = full[:, 2 * D:2 * D + 4 * WIN].reshape(FF, WIN)]
    all_to_all x5 -> x7, starting transfers between devices: 14.6 us -> 27.9 us  [swap_blocks(): return lax.all_to_all(rows, AXES, split_axis=0, concat_axis=0, tiled=True)]
    another operation x32 -> x3, local copies, waits for them, and re-layouts: 13 us -> 0.04 us  [the longest x1 0.03 us: on_device(): jnp.stack(small, axis=1)]
    concatenate x6 -> x0, local copies, waits for them, and re-layouts: 11.7 us -> none  [the longest x1 9.81 us: on_device(): jnp.concatenate([dwo, d_down] + dqkv + [up_back, jnp.pad(jnp.concatenate(...]
    pallas_call x1 -> x2, Pallas kernels: 42.4 us -> 53.6 us  [the longest x1 33.6 us: mid_bwd(): pl.pallas_call(mid_bwd_kernel, name='mid_bwd', grid_spec=pltpu.PrefetchSc...]
  transfers between devices with their start and end apart: 8 -> 11, of which waited for: 7 -> 8; matrix products, arithmetic and copies ran while one was open for 5% -> 6% of each run, Pallas kernels for 0% -> 25%
where the time goes in v2:
time: 556 us; the launch traced here: 555 us
  waiting for transfers between devices  289 us (52%)
  Pallas kernels  173 us (31%)
  local copies, waits for them, and re-layouts  31.8 us (6%)
  starting transfers between devices  28.3 us (5%)
  other arithmetic  16.6 us (3%)
  between operations  15.6 us (3%)
    all_to_all x7, waiting for transfers between devices, swap_blocks(): return lax.all_to_all(rows, AXES, split_axis=0, concat_axis=0, tiled=True)  167 us
    pallas_call x2, Pallas kernels, attn_bwd(): pl.pallas_call(attn_bwd_kernel, name='attn_bwd', grid_spec=pltpu.Prefetch...  68.8 us
    all_gather x1, waiting for transfers between devices, on_device(): lax.all_gather(jnp.concatenate([padded(q_weight, q_bias), padded(k_weight...  62.1 us
    unnamed x5, waiting for transfers between devices  60.4 us
    pallas_call x2, Pallas kernels, attn_fwd(): pl.pallas_call(attn_fwd_kernel, name='attn_fwd', grid_spec=pltpu.Prefetch...  50.9 us
    pallas_call x1, Pallas kernels, mid_bwd(): pl.pallas_call(mid_bwd_kernel, name='mid_bwd', grid_spec=pltpu.PrefetchSc...  33.6 us
    all_to_all x7, starting transfers between devices, swap_blocks(): return lax.all_to_all(rows, AXES, split_axis=0, concat_axis=0, tiled=True)  27.9 us
    pallas_call x1, Pallas kernels, mid_fwd(): pl.pallas_call(mid_fwd_kernel, name='mid_fwd', grid_spec=pltpu.PrefetchSc...  20 us
  transfers between devices with their start and end apart: 11, of which 8 were waited for; matrix products, arithmetic and copies ran while one was open for 6% of the time, Pallas kernels for 25%

profile of v2, /device:TPU:0, one launch (start us, length us, event | category | flops | bytes accessed | tf_op | source)
XLA Modules:
  0.0 555.0 jit_solution(14836595535315137842)
XLA Ops:
  11.6 2.4 gather_fusion.1
  14.0 3.9 fusion.15
  18.0 7.4 %all-to-all-start = ((bf16[32,2,32,384]{3,2,1,0:T(8,128)(2,1)}), bf16[32,2,32,384]{3,2,1,0:T(8,128)(2,1)}, u32[]{:S(2)}, u32[]{:S(2)}) async-start(bf16[32,2,32,384]{3,2,1,0:T(8,128)(2,1)} %bitcast.2), calls=%async_computation | async-start | bytes 3145728 | tf_op jit(solution)/shard_map/all_to_all | solution.py:650
  27.8 62.1 %all-gather.3.cloned.1.call-done.full_ref = bf16[768,768]{1,0:T(8,128)(2,1)} async-done(((bf16[24,768]{1,0:T(8,128)(2,1)}), bf16[768,768]{1,0:T(8,128)(2,1)}) %all-gather.3.cloned.1.call-update) | async-done | bytes 1179664 | tf_op jit(solution)/shard_map/all_gather | solution.py:613
  89.9 3.6 all-to-all-start.1
  93.6 2.4 gather_fusion.2
  96.0 44.6 %all-to-all-done.1.tok_ref = bf16[32,2,32,384]{3,2,1,0:T(8,128)(2,1)} async-done(((bf16[32,2,32,384]{3,2,1,0:T(8,128)(2,1)}), bf16[32,2,32,384]{3,2,1,0:T(8,128)(2,1)}, u32[]{:S(2)}, u32[]{:S(2)}) %all-to-all-start.1) | async-done | bytes 1572896 | tf_op jit(solution)/shard_map/all_to_all | solution.py:650
  140.6 3.5 all-to-all-start.2
  145.0 25.4 %attn_fwd.2 = (bf16[1088,384]{1,0:T(8,128)(2,1)}, bf16[1088,768]{1,0:T(8,128)(2,1)}, bf16[1088,768]{1,0:T(8,128)(2,1)}, bf16[1088,768]{1,0:T(8,128)(2,1)}, bf16[1088,384]{1,0:T(8,128)(2,1)}) custom-call(s32[1]{0:T(128)} %bitcast.len_ref, bf16[32,2,32,384]{3,2,1,0:T(8,128)(2,1)} %all-to-all-done.tok_ref, bf16[768,768]{1,0:T(8,128)(2,1)} %all-gather.3.cloned.1.call-done.full_ref), custom_call_target="tpu_custom_call" | custom-call | flops 20000000000 | bytes 12000000 | tf_op jit(solution)/shard_map/attn_fwd/pallas_call | solution.py:452
  170.4 25.5 %attn_fwd.3 = (bf16[1088,384]{1,0:T(8,128)(2,1)}, bf16[1088,768]{1,0:T(8,128)(2,1)}, bf16[1088,768]{1,0:T(8,128)(2,1)}, bf16[1088,768]{1,0:T(8,128)(2,1)}, bf16[1088,384]{1,0:T(8,128)(2,1)}) custom-call(s32[1]{0:T(128)} %bitcast.len_ref, bf16[32,2,32,384]{3,2,1,0:T(8,128)(2,1)} %all-to-all-done.1.tok_ref, bf16[768,768]{1,0:T(8,128)(2,1)} %all-gather.3.cloned.1.call-done.full_ref), custom_call_target="tpu_custom_call" | custom-call | flops 20000000000 | bytes 12000000 | tf_op jit(solution)/shard_map/attn_fwd/pallas_call | solution.py:452
  197.4 2.2 reshape.157.wu_ref
  200.2 20.0 %mid_fwd.1 = (bf16[32,2,32,768]{3,2,1,0:T(8,128)(2,1)}, f32[1088,768]{1,0:T(8,128)}, f32[1088,768]{1,0:T(8,128)}, f32[1088,128]{1,0:T(8,128)}, f32[1088,3072]{1,...) custom-call(s32[1]{0:T(128)} %bitcast.len_ref, bf16[1088,384]{1,0:T(8,128)(2,1)} %get-tuple-element.62.x0_ref.x_ref, ...), custom_call_target="tpu_custom_call" | custom-call | flops 15000000512 | bytes 36000000 | tf_op jit(solution)/shard_map/mid_fwd/pallas_call | solution.py:521
  220.2 6.1 %all-to-all-done.2.cot_ref = bf16[32,2,32,768]{3,2,1,0:T(8,128)(2,1)} async-done(((bf16[32,2,32,768]{3,2,1,0:T(8,128)(2,1)}), bf16[32,2,32,768]{3,2,1,0:T(8,128)(2,1)}, u32[]{:S(2)}, u32[]{:S(2)}) %all-to-all-start.2) | async-done | bytes 3145760 | tf_op jit(solution)/shard_map/all_to_all | solution.py:650
  226.3 33.6 %mid_bwd.1 = (bf16[1088,768]{1,0:T(8,128)(2,1)}, f32[1088,768]{1,0:T(8,128)}, f32[768,2688]{1,0:T(8,128)}) custom-call(s32[1]{0:T(128)} %bitcast.len_ref, bf16[32,2,32,768]{3,2,1,0:T(8,128)(2,1)} %all-to-all-done.2.cot_ref, bf16[1088,384]{1,0:T(8,128)(2,1)} %get-tuple-element.59.ctx0_ref.ctx_ref, bf16[1088,384]{1,0:T(8,128)(2,1)} %get-tuple-element.65.ctx1_ref.ctx_ref, ...), custom_call_target="tpu_custom_call" | custom-call | flops 30000001024 | bytes 50000000 | tf_op jit(solution)/shard_map/mid_bwd/pallas_call | solution.py:549
  259.9 3.1 all-to-all-start.3
  263.0 34.8 %attn_bwd.2 = (bf16[32,2,32,384]{3,2,1,0:T(8,128)(2,1)}, bf16[384,768]{1,0:T(8,128)(2,1)}) custom-call(s32[1]{0:T(128)} %bitcast.len_ref, bf16[1088,768]{1,0:T(8,128)(2,1)} %get-tuple-element.56.qa_ref, bf16[1088,768]{1,0:T(8,128)(2,1)} %get-tuple-element.57.ka_ref, bf16[1088,768]{1,0:T(8,128)(2,1)} %get-tuple-element.58.va_ref, ...), custom_call_target="tpu_custom_call" | custom-call | flops 30000001024 | bytes 16000000 | tf_op jit(solution)/shard_map/attn_bwd/pallas_call | solution.py:481
  297.8 37.6 %all-to-all-done.3 = bf16[32,2,32,768]{3,2,1,0:T(8,128)(2,1)S(1)} async-done(((bf16[32,2,32,768]{3,2,1,0:T(8,128)(2,1)}), bf16[32,2,32,768]{3,2,1,0:T(8,128)(2,1)S(1)}, u32[]{:S(2)}, u32[]{:S(2)}) %all-to-all-start.3) | async-done | bytes 3145760 | tf_op jit(solution)/shard_map/all_to_all | solution.py:650
  335.3 3.4 all-to-all-start.4
  338.8 34.0 %attn_bwd.3 = (bf16[32,2,32,384]{3,2,1,0:T(8,128)(2,1)}, bf16[384,768]{1,0:T(8,128)(2,1)}) custom-call(s32[1]{0:T(128)} %bitcast.len_ref, bf16[1088,768]{1,0:T(8,128)(2,1)} %get-tuple-element.79.qa_ref, bf16[1088,768]{1,0:T(8,128)(2,1)} %get-tuple-element.80.ka_ref, bf16[1088,768]{1,0:T(8,128)(2,1)} %get-tuple-element.81.va_ref, ...), custom_call_target="tpu_custom_call" | custom-call | flops 30000001024 | bytes 16000000 | tf_op jit(solution)/shard_map/attn_bwd/pallas_call | solution.py:481
  372.8 2.2 pad_maximum_fusion.1
  375.0 2.5 all-to-all-done.4
  377.5 3.4 all-to-all-start.6
  380.9 30.2 %all-to-all-done.6 = bf16[32,24,768]{2,1,0:T(8,128)(2,1)} async-done(((bf16[32,24,768]{2,1,0:T(8,128)(2,1)}), bf16[32,24,768]{2,1,0:T(8,128)(2,1)}, u32[]{:S(2)}, u32[]{:S(2)}) %all-to-all-start.6) | async-done | bytes 1179680 | tf_op jit(solution)/shard_map/all_to_all | solution.py:650
  411.1 3.4 all-to-all-start.5
  423.7 2.4 gather_fusion.3
  426.1 3.3 gather_fusion.4
  429.4 46.0 %all-to-all-done.5 = bf16[32,2,32,384]{3,2,1,0:T(8,128)(2,1)} async-done(((bf16[32,2,32,384]{3,2,1,0:T(8,128)(2,1)}), bf16[32,2,32,384]{3,2,1,0:T(8,128)(2,1)}, u32[]{:S(2)}, u32[]{:S(2)}) %all-to-all-start.5) | async-done | bytes 1572896 | tf_op jit(solution)/shard_map/all_to_all | solution.py:650
  475.4 3.3 gather_fusion.5
  478.7 4.1 pad_maximum_fusion
  482.8 59.9 %all-reduce.5.cloned.1.call-done = f32[192,2688]{1,0:T(8,128)} async-done(((f32[192,2688]{1,0:T(8,128)}), f32[192,2688]{1,0:T(8,128)}) %all-reduce.5.cloned.1.call-update) | async-done | bytes 2064400
  545.1 1.6 fusion.16
  546.8 1.7 dynamic-slice_reduce_fusion
  (106 shorter events, 19.7 us)
Async XLA Ops:
  17.8 7.7 %copy-start.20 = (bf16[24]{0:T(256)(128)(2,1)S(1)}, bf16[24]{0:T(256)(128)(2,1)}, u32[]{:S(2)}) copy-start(bf16[24]{0:T(256)(128)(2,1)} %param.24) | copy-start | bytes 148
  17.8 7.8 %copy-start.21 = (bf16[24]{0:T(256)(128)(2,1)S(1)}, bf16[24]{0:T(256)(128)(2,1)}, u32[]{:S(2)}) copy-start(bf16[24]{0:T(256)(128)(2,1)} %param.27) | copy-start | bytes 148
  17.8 7.9 %copy-start.9 = (bf16[24,192]{1,0:T(8,128)(2,1)S(1)}, bf16[24,192]{1,0:T(8,128)(2,1)}, u32[]{:S(2)}) copy-start(bf16[24,192]{1,0:T(8,128)(2,1)} %param.23) | copy-start | bytes 27652
  17.9 7.9 %copy-start.10 = (bf16[24,192]{1,0:T(8,128)(2,1)S(1)}, bf16[24,192]{1,0:T(8,128)(2,1)}, u32[]{:S(2)}) copy-start(bf16[24,192]{1,0:T(8,128)(2,1)} %param.26) | copy-start | bytes 27652
  17.9 7.9 %copy-start.11 = (bf16[24,192]{1,0:T(8,128)(2,1)S(1)}, bf16[24,192]{1,0:T(8,128)(2,1)}, u32[]{:S(2)}) copy-start(bf16[24,192]{1,0:T(8,128)(2,1)} %param.25) | copy-start | bytes 27652
  17.9 8.7 %copy-start.13 = (bf16[24]{0:T(256)(128)(2,1)S(1)}, bf16[24]{0:T(256)(128)(2,1)}, u32[]{:S(2)}) copy-start(bf16[24]{0:T(256)(128)(2,1)} %param.29) | copy-start | bytes 148
  17.9 8.7 %copy-start.14 = (bf16[24]{0:T(256)(128)(2,1)S(1)}, bf16[24]{0:T(256)(128)(2,1)}, u32[]{:S(2)}) copy-start(bf16[24]{0:T(256)(128)(2,1)} %param.30) | copy-start | bytes 148
  17.9 8.7 %copy-start.15 = (bf16[24]{0:T(256)(128)(2,1)S(1)}, bf16[24]{0:T(256)(128)(2,1)}, u32[]{:S(2)}) copy-start(bf16[24]{0:T(256)(128)(2,1)} %param.31) | copy-start | bytes 148
  17.9 8.7 %copy-start.16 = (bf16[24]{0:T(256)(128)(2,1)S(1)}, bf16[24]{0:T(256)(128)(2,1)}, u32[]{:S(2)}) copy-start(bf16[24]{0:T(256)(128)(2,1)} %param.35) | copy-start | bytes 148
  17.9 8.7 %copy-start.17 = (bf16[24]{0:T(256)(128)(2,1)S(1)}, bf16[24]{0:T(256)(128)(2,1)}, u32[]{:S(2)}) copy-start(bf16[24]{0:T(256)(128)(2,1)} %param.36) | copy-start | bytes 148
  17.9 8.7 %copy-start.18 = (bf16[24]{0:T(256)(128)(2,1)S(1)}, bf16[24]{0:T(256)(128)(2,1)}, u32[]{:S(2)}) copy-start(bf16[24]{0:T(256)(128)(2,1)} %param.37) | copy-start | bytes 148
  17.9 8.8 %copy-start.19 = (bf16[96]{0:T(256)(128)(2,1)S(1)}, bf16[96]{0:T(256)(128)(2,1)}, u32[]{:S(2)}) copy-start(bf16[96]{0:T(256)(128)(2,1)} %param.33) | copy-start | bytes 580
  18.0 9.0 %copy-start.6 = (bf16[96,192]{1,0:T(8,128)(2,1)S(1)}, bf16[96,192]{1,0:T(8,128)(2,1)}, u32[]{:S(2)}) copy-start(bf16[96,192]{1,0:T(8,128)(2,1)} %param.32) | copy-start | bytes 110596
  18.0 9.1 %copy-start.7 = (bf16[24,768]{1,0:T(8,128)(2,1)S(1)}, bf16[24,768]{1,0:T(8,128)(2,1)}, u32[]{:S(2)}) copy-start(bf16[24,768]{1,0:T(8,128)(2,1)} %param.34) | copy-start | bytes 110596
  18.0 9.1 %copy-start.8 = (bf16[24,768]{1,0:T(8,128)(2,1)S(1)}, bf16[24,768]{1,0:T(8,128)(2,1)}, u32[]{:S(2)}) copy-start(bf16[24,768]{1,0:T(8,128)(2,1)} %param.28) | copy-start | bytes 110596
  18.0 71.9 %all-to-all-start = ((bf16[32,2,32,384]{3,2,1,0:T(8,128)(2,1)}), bf16[32,2,32,384]{3,2,1,0:T(8,128)(2,1)}, u32[]{:S(2)}, u32[]{:S(2)}) async-start(bf16[32,2,32,384]{3,2,1,0:T(8,128)(2,1)} %bitcast.2), calls=%async_computation | async-start | bytes 3145728 | tf_op jit(solution)/shard_map/all_to_all | solution.py:650
  25.4 64.5 %all-gather.3.cloned.1.call-start = ((), (), s32[]{:S(2)}) async-start(), calls=%async_computation.8 | async-start | bytes 1216512 | tf_op jit(solution)/shard_map/all_gather | solution.py:613
  25.5 68.1 %copy-start.2 = (bf16[64,32,768]{2,1,0:T(8,128)(2,1)S(1)}, bf16[64,32,768]{2,1,0:T(8,128)(2,1)}, u32[]{:S(2)}) copy-start(bf16[64,32,768]{2,1,0:T(8,128)(2,1)} %param.20) | copy-start | bytes 9437188
  26.5 169.3 %all-gather.5.cloned.1.call-start = ((), (), s32[]{:S(2)}) async-start(), calls=%async_computation.9 | async-start | bytes 4257792 | tf_op jit(solution)/shard_map/all_gather | solution.py:638
  89.9 50.6 %all-to-all-start.1 = ((bf16[32,2,32,384]{3,2,1,0:T(8,128)(2,1)}), bf16[32,2,32,384]{3,2,1,0:T(8,128)(2,1)}, u32[]{:S(2)}, u32[]{:S(2)}) async-start(bf16[32,2,32,384]{3,2,1,0:T(8,128)(2,1)} %bitcast.12), calls=%async_computation.1 | async-start | bytes 3145728 | tf_op jit(solution)/shard_map/all_to_all | solution.py:650
  140.6 85.8 %all-to-all-start.2 = ((bf16[32,2,32,768]{3,2,1,0:T(8,128)(2,1)}), bf16[32,2,32,768]{3,2,1,0:T(8,128)(2,1)}, u32[]{:S(2)}, u32[]{:S(2)}) async-start(bf16[32,2,32,768]{3,2,1,0:T(8,128)(2,1)} %bitcast.13), calls=%async_computation.2 | async-start | bytes 6291456 | tf_op jit(solution)/shard_map/all_to_all | solution.py:650
  144.1 270.5 %reduce-scatter.2.cloned.1.call-start = ((), (), s32[]{:S(2)}) async-start(), calls=%async_computation.10 | async-start | bytes 10321920 | tf_op jit(solution)/shard_map/reduce_scatter | solution.py:685
  259.9 75.4 %all-to-all-start.3 = ((bf16[32,2,32,768]{3,2,1,0:T(8,128)(2,1)}), bf16[32,2,32,768]{3,2,1,0:T(8,128)(2,1)S(1)}, u32[]{:S(2)}, u32[]{:S(2)}) async-start(bf16[32,2,32,768]{3,2,1,0:T(8,128)(2,1)} %get-tuple-element.77), calls=%async_computation.3 | async-start | bytes 6291456 | tf_op jit(solution)/shard_map/all_to_all | solution.py:650
  335.3 42.1 %all-to-all-start.4 = ((bf16[32,2,32,384]{3,2,1,0:T(8,128)(2,1)}), bf16[32,2,32,384]{3,2,1,0:T(8,128)(2,1)}, u32[]{:S(2)}, u32[]{:S(2)}) async-start(bf16[32,2,32,384]{3,2,1,0:T(8,128)(2,1)} %get-tuple-element.83), calls=%async_computation.4 | async-start | bytes 3145728 | tf_op jit(solution)/shard_map/all_to_all | solution.py:650
  338.8 34.1 %copy-start.3 = (bf16[384,768]{1,0:T(8,128)(2,1)S(1)}, bf16[384,768]{1,0:T(8,128)(2,1)}, u32[]{:S(2)}) copy-start(bf16[384,768]{1,0:T(8,128)(2,1)} %get-tuple-element.86) | copy-start | bytes 1769476
  377.5 33.7 %all-to-all-start.6 = ((bf16[32,24,768]{2,1,0:T(8,128)(2,1)}), bf16[32,24,768]{2,1,0:T(8,128)(2,1)}, u32[]{:S(2)}, u32[]{:S(2)}) async-start(bf16[32,24,768]{2,1,0:T(8,128)(2,1)} %bitcast.28), calls=%async_computation.6 | async-start | bytes 2359296 | tf_op jit(solution)/shard_map/all_to_all | solution.py:650
  380.9 34.3 %copy-start.5 = (s32[32,2]{1,0:T(8,128)S(1)}, s32[32,2]{1,0:T(8,128)}, u32[]{:S(2)}) copy-start(s32[32,2]{1,0:T(8,128)} %copy-done.4) | copy-start | bytes 772
  380.9 36.3 %copy-start.22 = (u32[32]{0:T(128)S(1)}, u32[32]{0:T(128)}, u32[]{:S(2)}) copy-start(u32[32]{0:T(128)} %constant.84) | copy-start | bytes 388
  380.9 38.3 %copy-start.12 = (f32[8,128]{1,0:T(8,128)S(1)}, f32[8,128]{1,0:T(8,128)}, u32[]{:S(2)}) copy-start(f32[8,128]{1,0:T(8,128)} %get-tuple-element.89) | copy-start | bytes 12292
  411.1 64.3 %all-to-all-start.5 = ((bf16[32,2,32,384]{3,2,1,0:T(8,128)(2,1)}), bf16[32,2,32,384]{3,2,1,0:T(8,128)(2,1)}, u32[]{:S(2)}, u32[]{:S(2)}) async-start(bf16[32,2,32,384]{3,2,1,0:T(8,128)(2,1)} %get-tuple-element.85), calls=%async_computation.5 | async-start | bytes 3145728 | tf_op jit(solution)/shard_map/all_to_all | solution.py:650
  414.6 128.1 %all-reduce.5.cloned.1.call-start = ((), (), s32[]{:S(2)}) async-start(), calls=%async_computation.11 | async-start | bytes 4128768
  478.7 69.8 %copy-start.1 = (bf16[64,32,768]{2,1,0:T(8,128)(2,1)S(1)}, bf16[64,32,768]{2,1,0:T(8,128)(2,1)}, u32[]{:S(2)}) copy-start(bf16[64,32,768]{2,1,0:T(8,128)(2,1)} %param.19) | copy-start | bytes 9437188
  (3 other events, 8.4 us)
Sparse Core Ops, SparseCore 0:
  29.8 60.0 all-gather.2
  93.3 88.8 all-gather.4
  260.1 97.5 reduce-scatter.1
  418.7 123.9 all-reduce.4

commit v3 on v2

--- a/solution.py
+++ b/solution.py
@@ -301,7 +301,8 @@
 
 def mid_fwd_kernel(
     len_ref, x0_ref, x1_ref, ctx0_ref, ctx1_ref, full_ref, wu_ref, vec_ref,
-    out_ref, n1_ref, n2_ref, inv_ref, slope_ref, act_ref, stat_ref, out_s, wd_s, stat_s,
+    out0_ref, out1_ref, n1_ref, n2_ref, inv_ref, slope_ref, act_ref, stat_ref,
+    out0_s, out1_s, wd_s, stat_s,
 ):
     step = pl.program_id(0)
     first_len = len_ref[0]
@@ -348,11 +349,14 @@
     n2_ref[...] = n2
     lane = lax.broadcasted_iota(jnp.int32, (TILE, 128), 1)
     inv_ref[...] = jnp.where(lane < 64, inv1, inv2)
-    out_s[rows, :] = (n2 * gain2 + shift2).astype(bf16)
+    result = (n2 * gain2 + shift2).astype(bf16)
+    out0_s[rows, :] = result[:, :HALF]
+    out1_s[rows, :] = result[:, HALF:]
 
     @pl.when(step == pl.num_programs(0) - 1)
     def _():
-        unmerge_rows(out_s, out_ref, first_len)
+        unmerge_rows(out0_s, out0_ref, first_len)
+        unmerge_rows(out1_s, out1_ref, first_len)
         stat_ref[...] = jnp.broadcast_to(
             jnp.sum(stat_s[...], axis=1, keepdims=True), stat_ref.shape
         )
@@ -361,16 +365,15 @@
 def mid_bwd_kernel(
     len_ref, cot_ref, ctx0_ref, ctx1_ref, n1_ref, n2_ref, inv_ref, slope_ref, act_ref,
     full_ref, wu_ref, vec_ref, gctx_ref, base_ref, grad_ref,
-    cot_s, wd_s, dwd_s, dwu_s, vec_s, turn_s,
+    cot_s, wd_s, dwo_s, dwd_s, dwu_s, vec_s, turn_s,
 ):
     step = pl.program_id(0)
 
     @pl.when(step == 0)
     def _():
         merge_rows(cot_ref, cot_s, len_ref[0])
-        for target in (dwd_s, dwu_s, vec_s, wd_s):
+        for target in (dwo_s, dwd_s, dwu_s, vec_s, wd_s):
             target[...] = jnp.zeros_like(target)
-        grad_ref[:, :D] = jnp.zeros((D, D), f32)
         for g in range(4):
             wd_s[g, first_row(g) : first_row(g) + 192, :] = full_ref[192 * g : 192 * (g + 1), D:]
 
@@ -408,21 +411,24 @@
     base_ref[...] = grad_sum1
     grad_branch = grad_sum1.astype(bf16)
     add_vec(0, grad_branch.astype(f32))
-    grad_ref[:, :D] += mm(grad_branch, context, TN)
+    dwo_s[...] += mm(grad_branch, context, TN)
     gctx_ref[...] = mm(grad_branch, full_ref[:, :D], NN).astype(bf16)
 
     @pl.when(step == pl.num_programs(0) - 1)
     def _():
+        grad_ref[:, :D] = dwo_s[...].astype(bf16)
         for g in range(4):
             own = slice(192 * g, 192 * (g + 1))
-            grad_ref[own, D : 2 * D] = dwd_s[g, first_row(g) : first_row(g) + 192, :]
+            grad_ref[own, D : 2 * D] = dwd_s[g, first_row(g) : first_row(g) + 192, :].astype(bf16)
             turned = jnp.transpose(dwu_s[g])
             for half in range(2):
                 turn_s[...] = turned[:, 128 * half : 128 * (half + 1)]
                 for j in range(4):
                     lane0 = 2 * D + WIN * j + 128 * half
-                    grad_ref[own, lane0 : lane0 + 128] = turn_s[pl.ds(j, 192, stride=4), :]
-        grad_ref[:, 2 * D + 4 * WIN :] = jnp.transpose(vec_s[...])
+                    grad_ref[own, lane0 : lane0 + 128] = turn_s[pl.ds(j, 192, stride=4), :].astype(
+                        bf16
+                    )
+        grad_ref[:, 2 * D + 4 * WIN :] = jnp.transpose(vec_s[...]).astype(bf16)
 
 
 def whole(shape):
@@ -457,7 +463,7 @@
             grid=(3,),
             in_specs=[
                 whole(tok.shape),
-                pl.BlockSpec((HALF, D), lambda i, *_: (half, 0), pipeline_mode=pl.Buffered(1)),
+                pl.BlockSpec((HALF, D), lambda i, *_: (half, 2), pipeline_mode=pl.Buffered(1)),
             ],
             out_specs=[
                 kept((ROWS, HALF)), pair_cols(256), pair_cols(256), pair_cols(256), pair_cols(128),
@@ -488,7 +494,7 @@
                 pair_cols(256, 0), pair_cols(256, 0), pair_cols(256, 0), pair_cols(128, 0),
                 pair_cols(128, 3 * half), whole(x.shape),
                 pl.BlockSpec((ROWS, HALF), lambda i, *_: (0, half), pipeline_mode=pl.Buffered(1)),
-                pl.BlockSpec((HALF, D), lambda i, *_: (half, 0), pipeline_mode=pl.Buffered(1)),
+                pl.BlockSpec((HALF, D), lambda i, *_: (half, 2), pipeline_mode=pl.Buffered(1)),
             ],
             out_specs=[kept((SEQ // BLOCK, 2, BLOCK, HALF)), kept((HALF, D))],
             scratch_shapes=[
@@ -515,8 +521,9 @@
 
 def mid_fwd(len_arr, x0, x1, ctx0, ctx1, full, wu, vecs):
     outs = [
-        ((SEQ // BLOCK, 2, BLOCK, D), bf16), ((ROWS, D), f32), ((ROWS, D), f32), ((ROWS, 128), f32),
-        ((ROWS, FF), f32), ((ROWS, FF), bf16), ((8, 128), f32),
+        ((SEQ // BLOCK, 2, BLOCK, HALF), bf16), ((SEQ // BLOCK, 2, BLOCK, HALF), bf16),
+        ((ROWS, D), f32), ((ROWS, D), f32), ((ROWS, 128), f32), ((ROWS, FF), f32),
+        ((ROWS, FF), bf16), ((8, 128), f32),
     ]
     return pl.pallas_call(
         mid_fwd_kernel,
@@ -527,11 +534,12 @@
             in_specs=[row_tile(HALF)] * 4
             + [whole((D, 2 * D)), whole(wu.shape), whole(vecs.shape)],
             out_specs=[
-                kept(outs[0][0]), row_tile(D), row_tile(D), row_tile(128), row_tile(FF),
-                row_tile(FF), kept((8, 128)),
+                kept(outs[0][0]), kept(outs[0][0]), row_tile(D), row_tile(D), row_tile(128),
+                row_tile(FF), row_tile(FF), kept((8, 128)),
             ],
             scratch_shapes=[
-                pltpu.VMEM((ROWS, D), bf16),
+                pltpu.VMEM((ROWS, HALF), bf16),
+                pltpu.VMEM((ROWS, HALF), bf16),
                 pltpu.VMEM((4, WIN, D), bf16),
                 pltpu.VMEM((8, D), f32),
             ],
@@ -545,7 +553,7 @@
 
 
 def mid_bwd(len_arr, cot, ctx0, ctx1, n1, n2, inv, slope, act, full, wu, vecs):
-    outs = [((ROWS, D), bf16), ((ROWS, D), f32), ((D, GRAD_COLS), f32)]
+    outs = [((ROWS, D), bf16), ((ROWS, D), f32), ((D, GRAD_COLS), bf16)]
     return pl.pallas_call(
         mid_bwd_kernel,
         name="mid_bwd",
@@ -565,6 +573,7 @@
             scratch_shapes=[
                 pltpu.VMEM((ROWS, D), bf16),
                 pltpu.VMEM((4, WIN, D), bf16),
+                pltpu.VMEM((D, D), f32),
                 pltpu.VMEM((4, WIN, D), f32),
                 pltpu.VMEM((4, WIN, D), f32),
                 pltpu.VMEM((128, D), f32),
@@ -610,12 +619,16 @@
         )
 
     small = [o_bias, norm1_gain, norm1_bias, down_bias, norm2_gain, norm2_bias]
-    full_in = lax.all_gather(
+    full = lax.all_gather(
         jnp.concatenate(
             [
+                o_weight,
+                down_weight,
                 padded(q_weight, q_bias),
                 padded(k_weight, jnp.zeros_like(q_bias)),
                 padded(v_weight, v_bias),
+                padded(up_weight, up_bias).reshape(rows_dev, 4 * WIN),
+                jnp.pad(jnp.stack(small, axis=1), ((0, 0), (0, 122))),
             ],
             axis=1,
         ),
@@ -623,19 +636,6 @@
         axis=0,
         tiled=True,
     )
-    rest, full_in = tie(
-        jnp.concatenate(
-            [
-                o_weight,
-                down_weight,
-                padded(up_weight, up_bias).reshape(rows_dev, 4 * WIN),
-                jnp.pad(jnp.stack(small, axis=1), ((0, 0), (0, 122))),
-            ],
-            axis=1,
-        ),
-        full_in,
-    )
-    full = lax.all_gather(rest, AXES, axis=0, tiled=True)
 
     dealt_lengths = pick(lengths, permutation).reshape(devices, seq_dev)
     swap = dealt_lengths[:, 0] < dealt_lengths[:, 1]
@@ -664,37 +664,57 @@
             rows = rows.transpose(1, 0, 2, 3)
         return swap_blocks(rows).reshape(seq_total, piece_len, width)
 
+    def send_over(partial, axis):
+        count = lax.axis_size(axis)
+        me = lax.axis_index(axis)
+        size = partial.shape[0] // count
+        block_of = lambda index: lax.dynamic_slice_in_dim(partial, index * size, size, 0)
+        parts = [block_of(me)]
+        for shift in range(1, count):
+            target = [(i, (i + shift) % count) for i in range(count)]
+            parts.append(lax.ppermute(block_of((me + shift) % count), axis, target))
+        return parts
+
+    def total(parts):
+        return sum(part.astype(f32) for part in parts)
+
     dealt_tokens = pick(tokens, order)
-    dealt_cot = pick(cotangent, order)
     tok0 = arrive(dealt_tokens[:, :, :HALF])
-    second, tok0 = tie(dealt_tokens[:, :, HALF:], tok0)
-    tok1 = arrive(second)
-    dealt_cot, tok1 = tie(dealt_cot, tok1)
+    tok1 = arrive(dealt_tokens[:, :, HALF:])
+    dealt_cot, tok0, tok1 = tie(pick(cotangent, order), tok0, tok1)
     cot = arrive(dealt_cot)
 
-    x0, qa0, ka0, va0, ctx0 = attn_fwd(len_arr, tok0, full_in, 0)
-    x1, qa1, ka1, va1, ctx1 = attn_fwd(len_arr, tok1, full_in, 1)
-    wu = full[:, 2 * D : 2 * D + 4 * WIN].reshape(FF, WIN)
-    vecs = jnp.pad(full[:, 2 * D + 4 * WIN : 2 * D + 4 * WIN + 6].astype(f32).T, ((0, 2), (0, 0)))
-    out, n1, n2, inv, slope, act, stat = mid_fwd(len_arr, x0, x1, ctx0, ctx1, full, wu, vecs)
-    cot, out = tie(cot, out)
-    back_out = leave(out)
+    x0, qa0, ka0, va0, ctx0 = attn_fwd(len_arr, tok0, full, 0)
+    x1, qa1, ka1, va1, ctx1 = attn_fwd(len_arr, tok1, full, 1)
+    wu = full[:, 3 * D : 3 * D + 4 * WIN].reshape(FF, WIN)
+    vecs = jnp.pad(full[:, 3 * D + 4 * WIN : 3 * D + 4 * WIN + 6].astype(f32).T, ((0, 2), (0, 0)))
+    out0, out1, n1, n2, inv, slope, act, stat = mid_fwd(
+        len_arr, x0, x1, ctx0, ctx1, full, wu, vecs
+    )
+    cot, out0, out1 = tie(cot, out0, out1)
+    back_out0 = leave(out0)
     gctx, base, grads = mid_bwd(
         len_arr, cot, ctx0, ctx1, n1, n2, inv, slope, act, full, wu, vecs
     )
-    mine = lax.psum_scatter(grads, "dp", scatter_dimension=0, tiled=True)
-    mine = lax.psum_scatter(mine, "fsdp", scatter_dimension=0, tiled=True)
-    ig0, dw0 = attn_bwd(len_arr, qa0, ka0, va0, ctx0, gctx, x0, base, full_in, 0)
-    ig0, back_out = tie(ig0, back_out)
+    gctx, out1, back_out0 = tie(gctx, out1, back_out0)
+    back_out1 = leave(out1)
+    parts = send_over(grads, "dp")
+    ig0, dw0 = attn_bwd(len_arr, qa0, ka0, va0, ctx0, gctx, x0, base, full, 0)
+    ig0, dw0, gctx, back_out1, *parts = tie(ig0, dw0, gctx, back_out1, *parts)
     back0 = leave(ig0)
-    ig1, dw1 = attn_bwd(len_arr, qa1, ka1, va1, ctx1, gctx, x1, base, full_in, 1)
-    ig1, back0 = tie(ig1, back0)
+    parts = send_over(total(parts).astype(bf16), "fsdp")
+    ig1, dw1 = attn_bwd(len_arr, qa1, ka1, va1, ctx1, gctx, x1, base, full, 1)
+    ig1, dw1, back0, *parts = tie(ig1, dw1, back0, *parts)
+    mine = total(parts)
     back1 = leave(ig1)
-    moved = swap_blocks(jnp.concatenate([dw0, dw1], axis=0).reshape(devices, rows_dev, D))
-    mine_in = jnp.sum(moved.astype(f32), axis=0)
-
-    output = pick(back_out, inverse)
-    input_grad = jnp.concatenate([pick(back0, inverse), pick(back1, inverse)], axis=-1)
+    parts = send_over(jnp.concatenate([dw0, dw1], axis=0), "dp")
+    mine_in = total(send_over(total(parts).astype(bf16), "fsdp"))
+
+    join_halves = lambda first, second: jnp.concatenate(
+        [pick(first, inverse), pick(second, inverse)], axis=-1
+    )
+    output = join_halves(back_out0, back_out1)
+    input_grad = join_halves(back0, back1)
     lens = jnp.stack([len_arr[0], ROWS - len_arr[0]]).astype(f32)
     sums = jnp.stack([stat[4:8, 0], stat[0:4, 0] - stat[4:8, 0]], axis=1)
     rms = jnp.sqrt(sums / (lens[None, :] * D) + rms_eps)

time: 556 us -> 495 us (0.89)
  waiting for transfers between devices: 289 us -> 100 us
  blocking collectives: 0 us -> 55.6 us
  starting transfers between devices: 28.3 us -> 79.6 us
  local copies, waits for them, and re-layouts: 31.8 us -> 46.6 us
  other arithmetic: 16.6 us -> 22.9 us
    all_to_all x7 -> x6, waiting for transfers between devices: 167 us -> 42.6 us  [swap_blocks(): return lax.all_to_all(rows, AXES, split_axis=0, concat_axis=0, tiled=True)]
    all_gather x2 -> x1, waiting for transfers between devices: 62.1 us -> 0.02 us  [on_device(): lax.all_gather(jnp.concatenate([o_weight, down_weight, padded(q_weight, q...]
    unnamed x5 -> x1, waiting for transfers between devices: 60.4 us -> 0.02 us
    ppermute x0 -> x20, waiting for transfers between devices: none -> 57.3 us  [send_over(): parts.append(lax.ppermute(block_of((me + shift) % count), axis, target))]
    all_to_all x0 -> x1, blocking collectives: none -> 55.6 us  [swap_blocks(): return lax.all_to_all(rows, AXES, split_axis=0, concat_axis=0, tiled=True)]
    ppermute x0 -> x20, starting transfers between devices: none -> 50.5 us  [send_over(): parts.append(lax.ppermute(block_of((me + shift) % count), axis, target))]
    unnamed x50 -> x37, local copies, waits for them, and re-layouts: 1.58 us -> 7.47 us
    gather x6 -> x7, local copies, waits for them, and re-layouts: 15.3 us -> 17 us  [pick(): return values.at[index].get(mode='promise_in_bounds')]
  transfers between devices with their start and end apart: 11 -> 27, of which waited for: 8 -> 9; matrix products, arithmetic and copies ran while one was open for 6% -> 10% of each run, Pallas kernels for 25% -> 35%
where the time goes in v3:
time: 495 us; the launch traced here: 491 us
  Pallas kernels  171 us (35%)
  waiting for transfers between devices  100 us (20%)
  starting transfers between devices  79.6 us (16%)
  blocking collectives  55.6 us (11%)
  local copies, waits for them, and re-layouts  46.6 us (9%)
  other arithmetic  22.9 us (5%)
  between operations  15.5 us (3%)
    pallas_call x2, Pallas kernels, attn_bwd(): pl.pallas_call(attn_bwd_kernel, name='attn_bwd', grid_spec=pltpu.Prefetch...  67.7 us
    ppermute x20, waiting for transfers between devices, send_over(): parts.append(lax.ppermute(block_of((me + shift) % count), axis, target))  57.3 us
    all_to_all x1, blocking collectives, swap_blocks(): return lax.all_to_all(rows, AXES, split_axis=0, concat_axis=0, tiled=True)  55.6 us
    pallas_call x2, Pallas kernels, attn_fwd(): pl.pallas_call(attn_fwd_kernel, name='attn_fwd', grid_spec=pltpu.Prefetch...  50.9 us
    ppermute x20, starting transfers between devices, send_over(): parts.append(lax.ppermute(block_of((me + shift) % count), axis, target))  50.5 us
    all_to_all x6, waiting for transfers between devices, swap_blocks(): return lax.all_to_all(rows, AXES, split_axis=0, concat_axis=0, tiled=True)  42.6 us
    pallas_call x1, Pallas kernels, mid_bwd(): pl.pallas_call(mid_bwd_kernel, name='mid_bwd', grid_spec=pltpu.PrefetchSc...  32.4 us
    all_to_all x6, starting transfers between devices, swap_blocks(): return lax.all_to_all(rows, AXES, split_axis=0, concat_axis=0, tiled=True)  29 us
  transfers between devices with their start and end apart: 27, of which 9 were waited for; matrix products, arithmetic and copies ran while one was open for 10% of the time, Pallas kernels for 35%

profile of v3, /device:TPU:0, one launch (start us, length us, event | category | flops | bytes accessed | tf_op | source)
XLA Modules:
  0.0 491.4 jit_solution(1366010146485658477)
XLA Ops:
  22.4 3.3 fusion.14
  25.7 55.6 %all_to_all.35.tok_ref = bf16[32,2,32,384]{3,2,1,0:T(8,128)(2,1)} all-to-all(bf16[32,2,32,384]{3,2,1,0:T(8,128)(2,1)S(1)} %bitcast.30), channel_id=1, replica_groups=mesh['dp'=4,'fsdp'=8] {'dp','fsdp'}, dimensions={0} | all-to-all | bytes 3145728 | tf_op jit(solution)/shard_map/all_to_all | solution.py:650
  81.3 6.9 %all-to-all-start.1 = ((bf16[32,2,32,384]{3,2,1,0:T(8,128)(2,1)}), bf16[32,2,32,384]{3,2,1,0:T(8,128)(2,1)}, u32[]{:S(2)}, u32[]{:S(2)}) async-start(bf16[32,2,32,384]{3,2,1,0:T(8,128)(2,1)} %bitcast.3), calls=%async_computation.1 | async-start | bytes 3145728 | tf_op jit(solution)/shard_map/all_to_all | solution.py:650
  90.7 38.9 %all-to-all-done.1.tok_ref = bf16[32,2,32,384]{3,2,1,0:T(8,128)(2,1)} async-done(((bf16[32,2,32,384]{3,2,1,0:T(8,128)(2,1)}), bf16[32,2,32,384]{3,2,1,0:T(8,128)(2,1)}, u32[]{:S(2)}, u32[]{:S(2)}) %all-to-all-start.1) | async-done | bytes 1572896 | tf_op jit(solution)/shard_map/all_to_all | solution.py:650
  129.6 4.1 all-to-all-start.2
  139.9 25.4 %attn_fwd.2 = (bf16[1088,384]{1,0:T(8,128)(2,1)}, bf16[1088,768]{1,0:T(8,128)(2,1)}, bf16[1088,768]{1,0:T(8,128)(2,1)}, bf16[1088,768]{1,0:T(8,128)(2,1)}, bf16[1088,384]{1,0:T(8,128)(2,1)}) custom-call(s32[1]{0:T(128)} %bitcast.len_ref, bf16[32,2,32,384]{3,2,1,0:T(8,128)(2,1)} %all_to_all.35.tok_ref, bf16[768,3456]{1,0:T(8,128)(2,1)} %all-gather.2.cloned.1.call-done.full_ref), custom_call_target="tpu_custom_call" | custom-call | flops 20000000000 | bytes 12000000 | tf_op jit(solution)/shard_map/attn_fwd/pallas_call | solution.py:458
  165.3 25.4 %attn_fwd.3 = (bf16[1088,384]{1,0:T(8,128)(2,1)}, bf16[1088,768]{1,0:T(8,128)(2,1)}, bf16[1088,768]{1,0:T(8,128)(2,1)}, bf16[1088,768]{1,0:T(8,128)(2,1)}, bf16[1088,384]{1,0:T(8,128)(2,1)}) custom-call(s32[1]{0:T(128)} %bitcast.len_ref, bf16[32,2,32,384]{3,2,1,0:T(8,128)(2,1)} %all-to-all-done.1.tok_ref, bf16[768,3456]{1,0:T(8,128)(2,1)} %all-gather.2.cloned.1.call-done.full_ref), custom_call_target="tpu_custom_call" | custom-call | flops 20000000000 | bytes 12000000 | tf_op jit(solution)/shard_map/attn_fwd/pallas_call | solution.py:458
  190.7 20.2 %mid_fwd.1 = (bf16[32,2,32,384]{3,2,1,0:T(8,128)(2,1)}, bf16[32,2,32,384]{3,2,1,0:T(8,128)(2,1)}, f32[1088,768]{1,0:T(8,128)}, f32[1088,768]{1,0:T(8,128)}, f32[...) custom-call(s32[1]{0:T(128)} %bitcast.len_ref, ...), custom_call_target="tpu_custom_call" | custom-call | flops 15000000512 | bytes 36000000 | tf_op jit(solution)/shard_map/mid_fwd/pallas_call | solution.py:528
  211.0 6.1 %all-to-all-start.3 = ((bf16[32,2,32,384]{3,2,1,0:T(8,128)(2,1)}), bf16[32,2,32,384]{3,2,1,0:T(8,128)(2,1)S(1)}, u32[]{:S(2)}, u32[]{:S(2)}) async-start(bf16[32,2,32,384]{3,2,1,0:T(8,128)(2,1)} %get-tuple-element.88), calls=%async_computation.3 | async-start | bytes 3145728 | tf_op jit(solution)/shard_map/all_to_all | solution.py:650
  219.7 32.4 %mid_bwd.1 = (bf16[1088,768]{1,0:T(8,128)(2,1)}, f32[1088,768]{1,0:T(8,128)}, bf16[768,2688]{1,0:T(8,128)(2,1)}) custom-call(s32[1]{0:T(128)} %bitcast.len_ref, bf16[32,2,32,768]{3,2,1,0:T(8,128)(2,1)} %all-to-all-done.2.cot_ref, bf16[1088,384]{1,0:T(8,128)(2,1)} %get-tuple-element.76.ctx0_ref.ctx_ref, bf16[1088,384]{1,0:T(8,128)(2,1)} %get-tuple-element.77.ctx1_ref.ctx_ref, ...), custom_call_target="tpu_custom_call" | custom-call | flops 30000001024 | bytes 50000000 | tf_op jit(solution)/shard_map/mid_bwd/pallas_call | solution.py:557
  252.1 3.7 all-to-all-done.3
  255.8 2.7 all-to-all-start.4
  258.5 4.2 constant_dynamic-slice_fusion.19
  264.8 33.8 %attn_bwd.2 = (bf16[32,2,32,384]{3,2,1,0:T(8,128)(2,1)}, bf16[384,768]{1,0:T(8,128)(2,1)}) custom-call(s32[1]{0:T(128)} %bitcast.len_ref, bf16[1088,768]{1,0:T(8,128)(2,1)} %get-tuple-element.90.qa_ref, bf16[1088,768]{1,0:T(8,128)(2,1)} %get-tuple-element.91.ka_ref, bf16[1088,768]{1,0:T(8,128)(2,1)} %get-tuple-element.92.va_ref, ...), custom_call_target="tpu_custom_call" | custom-call | flops 30000001024 | bytes 16000000 | tf_op jit(solution)/shard_map/attn_bwd/pallas_call | solution.py:487
  298.6 23.9 %collective-permute-done.1 = bf16[192,2688]{1,0:T(8,128)(2,1)} collective-permute-done((bf16[192,2688]{1,0:T(8,128)(2,1)}, bf16[192,2688]{1,0:T(8,128)(2,1)}, u32[]{:S(2)}, u32[]{:S(2)}) %collective-permute-start.1) | collective-permute-done | bytes 1032224 | tf_op jit(solution)/shard_map/ppermute | solution.py:675
  323.6 5.0 %all-to-all-start.5 = ((bf16[32,2,32,384]{3,2,1,0:T(8,128)(2,1)}), bf16[32,2,32,384]{3,2,1,0:T(8,128)(2,1)S(1)}, u32[]{:S(2)}, u32[]{:S(2)}) async-start(bf16[32,2,32,384]{3,2,1,0:T(8,128)(2,1)} %get-tuple-element.106), calls=%async_computation.5 | async-start | bytes 3145728 | tf_op jit(solution)/shard_map/all_to_all | solution.py:650
  332.3 4.5 collective-permute-start.9
  338.1 3.0 collective-permute-start.6
  341.1 16.8 %collective-permute-done.9 = bf16[24,2688]{1,0:T(8,128)(2,1)S(1)} collective-permute-done((bf16[24,2688]{1,0:T(8,128)(2,1)}, bf16[24,2688]{1,0:T(8,128)(2,1)S(1)}, u32[]{:S(2)}, u32[]{:S(2)}) %collective-permute-start.9) | collective-permute-done | bytes 129056 | tf_op jit(solution)/shard_map/ppermute | solution.py:675
  357.9 2.8 collective-permute-done.8
  360.7 22.1 %collective-permute-start.3 = (bf16[24,2688]{1,0:T(8,128)(2,1)}, bf16[24,2688]{1,0:T(8,128)(2,1)}, u32[]{:S(2)}, u32[]{:S(2)}) collective-permute-start(bf16[24,2688]{1,0:T(8,128)(2,1)} %get-tuple-element.239), channel_id=1, source_target_pairs={{0,1},{1,2},{2,3},{3,4},{4,5},{5,6},{6,7},{7,0},{8,9},{9,10},{10,1... | collective-permute-start | bytes 387080 | tf_op jit(solution)/shard_map/ppermute | solution.py:675
  382.8 33.9 %attn_bwd.3 = (bf16[32,2,32,384]{3,2,1,0:T(8,128)(2,1)}, bf16[384,768]{1,0:T(8,128)(2,1)}) custom-call(s32[1]{0:T(128)} %bitcast.len_ref, bf16[1088,768]{1,0:T(8,128)(2,1)} %get-tuple-element.100.qa_ref, bf16[1088,768]{1,0:T(8,128)(2,1)} %get-tuple-element.101.ka_ref, bf16[1088,768]{1,0:T(8,128)(2,1)} %get-tuple-element.102.va_ref, ...), custom_call_target="tpu_custom_call" | custom-call | flops 30000001024 | bytes 16000000 | tf_op jit(solution)/shard_map/attn_bwd/pallas_call | solution.py:487
  417.4 4.2 all-to-all-start.6
  426.8 3.4 gather_fusion.4
  432.2 3.5 pad_maximum_fusion
  443.1 5.4 %collective-permute-done.10 = bf16[192,768]{1,0:T(8,128)(2,1)S(1)} collective-permute-done((bf16[192,768]{1,0:T(8,128)(2,1)S(1)}, bf16[192,768]{1,0:T(8,128)(2,1)S(1)}, u32[]{:S(2)}, u32[]{:S(2)}) %collective-permute-start.10) | collective-permute-done | bytes 294944 | tf_op jit(solution)/shard_map/ppermute | solution.py:675
  449.2 7.4 %collective-permute-done.11 = bf16[192,768]{1,0:T(8,128)(2,1)S(1)} collective-permute-done((bf16[192,768]{1,0:T(8,128)(2,1)S(1)}, bf16[192,768]{1,0:T(8,128)(2,1)S(1)}, u32[]{:S(2)}, u32[]{:S(2)}) %collective-permute-start.11) | collective-permute-done | bytes 294944 | tf_op jit(solution)/shard_map/ppermute | solution.py:675
  456.8 6.0 %collective-permute-start.13 = (bf16[24,768]{1,0:T(8,128)(2,1)S(1)}, bf16[24,768]{1,0:T(8,128)(2,1)S(1)}, u32[]{:S(2)}, u32[]{:S(2)}) collective-permute-start(bf16[24,768]{1,0:T(8,128)(2,1)S(1)} %get-tuple-element.241), channel_id=1, source_target_pairs={{0,1},{1,2},{2,3},{3,4},{4,5},{5,6},{6,7},{7,0},{8,9},{9,10},{10,1... | collective-permute-start | bytes 110600 | tf_op jit(solution)/shard_map/ppermute | solution.py:675
  465.0 3.0 collective-permute-start.17
  469.6 2.7 collective-permute-start.14
  476.9 3.5 gather_fusion.6
  480.4 3.9 pad_maximum_fusion.1
  (135 shorter events, 57.9 us)
Async XLA Ops:
  7.2 12.8 %copy-start = (bf16[64,32,768]{2,1,0:T(8,128)(2,1)S(1)}, bf16[64,32,768]{2,1,0:T(8,128)(2,1)}, u32[]{:S(2)}) copy-start(bf16[64,32,768]{2,1,0:T(8,128)(2,1)} %param.19) | copy-start | bytes 9437188
  7.2 127.3 %all-gather.2.cloned.1.call-start = ((), (), s32[]{:S(2)}) async-start(), calls=%async_computation.7 | async-start | bytes 5474304 | tf_op jit(solution)/shard_map/all_gather | solution.py:622
  81.3 6.9 %copy-start.4 = (bf16[64,32,768]{2,1,0:T(8,128)(2,1)S(1)}, bf16[64,32,768]{2,1,0:T(8,128)(2,1)}, u32[]{:S(2)}) copy-start(bf16[64,32,768]{2,1,0:T(8,128)(2,1)} %param.20) | copy-start | bytes 9437188
  81.3 48.2 %all-to-all-start.1 = ((bf16[32,2,32,384]{3,2,1,0:T(8,128)(2,1)}), bf16[32,2,32,384]{3,2,1,0:T(8,128)(2,1)}, u32[]{:S(2)}, u32[]{:S(2)}) async-start(bf16[32,2,32,384]{3,2,1,0:T(8,128)(2,1)} %bitcast.3), calls=%async_computation.1 | async-start | bytes 3145728 | tf_op jit(solution)/shard_map/all_to_all | solution.py:650
  129.6 81.4 %all-to-all-start.2 = ((bf16[32,2,32,768]{3,2,1,0:T(8,128)(2,1)}), bf16[32,2,32,768]{3,2,1,0:T(8,128)(2,1)}, u32[]{:S(2)}, u32[]{:S(2)}) async-start(bf16[32,2,32,768]{3,2,1,0:T(8,128)(2,1)} %bitcast.4), calls=%async_computation.2 | async-start | bytes 6291456 | tf_op jit(solution)/shard_map/all_to_all | solution.py:650
  211.0 44.8 %all-to-all-start.3 = ((bf16[32,2,32,384]{3,2,1,0:T(8,128)(2,1)}), bf16[32,2,32,384]{3,2,1,0:T(8,128)(2,1)S(1)}, u32[]{:S(2)}, u32[]{:S(2)}) async-start(bf16[32,2,32,384]{3,2,1,0:T(8,128)(2,1)} %get-tuple-element.88), calls=%async_computation.3 | async-start | bytes 3145728 | tf_op jit(solution)/shard_map/all_to_all | solution.py:650
  255.8 66.7 %all-to-all-start.4 = ((bf16[32,2,32,384]{3,2,1,0:T(8,128)(2,1)}), bf16[32,2,32,384]{3,2,1,0:T(8,128)(2,1)S(1)}, u32[]{:S(2)}, u32[]{:S(2)}) async-start(bf16[32,2,32,384]{3,2,1,0:T(8,128)(2,1)} %get-tuple-element.97), calls=%async_computation.4 | async-start | bytes 3145728 | tf_op jit(solution)/shard_map/all_to_all | solution.py:650
  258.5 6.3 %copy-start.14 = (f32[8,128]{1,0:T(8,128)S(1)}, f32[8,128]{1,0:T(8,128)}, u32[]{:S(2)}) copy-start(f32[8,128]{1,0:T(8,128)} %get-tuple-element.123) | copy-start | bytes 12292
  262.7 35.9 %collective-permute-start.2 = (bf16[192,2688]{1,0:T(8,128)(2,1)}, bf16[192,2688]{1,0:T(8,128)(2,1)}, u32[]{:S(2)}, u32[]{:S(2)}) collective-permute-start(bf16[192,2688]{1,0:T(8,128)(2,1)} %get-tuple-element.224), channel_id=1, source_target_pairs={{0,24},{8,0},{16,8},{24,16},{1,25},{9,1},{17,9},{25,17},{2,26},{10... | collective-permute-start | bytes 3096584 | tf_op jit(solution)/shard_map/ppermute | solution.py:675
  264.1 58.4 %collective-permute-start.1 = (bf16[192,2688]{1,0:T(8,128)(2,1)}, bf16[192,2688]{1,0:T(8,128)(2,1)}, u32[]{:S(2)}, u32[]{:S(2)}) collective-permute-start(bf16[192,2688]{1,0:T(8,128)(2,1)} %get-tuple-element.225), channel_id=1, source_target_pairs={{0,16},{8,24},{16,0},{24,8},{1,17},{9,25},{17,1},{25,9},{2,18},{10... | collective-permute-start | bytes 3096584 | tf_op jit(solution)/shard_map/ppermute | solution.py:675
  264.5 58.0 %collective-permute-start = (bf16[192,2688]{1,0:T(8,128)(2,1)}, bf16[192,2688]{1,0:T(8,128)(2,1)}, u32[]{:S(2)}, u32[]{:S(2)}) collective-permute-start(bf16[192,2688]{1,0:T(8,128)(2,1)} %get-tuple-element.226), channel_id=1, source_target_pairs={{0,8},{8,16},{16,24},{24,0},{1,9},{9,17},{17,25},{25,1},{2,10},{10... | collective-permute-start | bytes 3096584 | tf_op jit(solution)/shard_map/ppermute | solution.py:675
  323.6 93.8 %all-to-all-start.5 = ((bf16[32,2,32,384]{3,2,1,0:T(8,128)(2,1)}), bf16[32,2,32,384]{3,2,1,0:T(8,128)(2,1)S(1)}, u32[]{:S(2)}, u32[]{:S(2)}) async-start(bf16[32,2,32,384]{3,2,1,0:T(8,128)(2,1)} %get-tuple-element.106), calls=%async_computation.5 | async-start | bytes 3145728 | tf_op jit(solution)/shard_map/all_to_all | solution.py:650
  331.4 6.0 %copy-start.15 = (f32[2]{0:T(128)S(1)}, f32[2]{0:T(128)}, u32[]{:S(2)}) copy-start(f32[2]{0:T(128)} %fusion.12) | copy-start | bytes 28
  332.3 25.6 %collective-permute-start.9 = (bf16[24,2688]{1,0:T(8,128)(2,1)}, bf16[24,2688]{1,0:T(8,128)(2,1)S(1)}, u32[]{:S(2)}, u32[]{:S(2)}) collective-permute-start(bf16[24,2688]{1,0:T(8,128)(2,1)} %get-tuple-element.233), channel_id=1, source_target_pairs={{0,7},{1,0},{2,1},{3,2},{4,3},{5,4},{6,5},{7,6},{8,15},{9,8},{10,9... | collective-permute-start | bytes 387080 | tf_op jit(solution)/shard_map/ppermute | solution.py:675
  336.9 23.8 %collective-permute-start.8 = (bf16[24,2688]{1,0:T(8,128)(2,1)}, bf16[24,2688]{1,0:T(8,128)(2,1)S(1)}, u32[]{:S(2)}, u32[]{:S(2)}) collective-permute-start(bf16[24,2688]{1,0:T(8,128)(2,1)} %get-tuple-element.234), channel_id=1, source_target_pairs={{0,6},{1,7},{2,0},{3,1},{4,2},{5,3},{6,4},{7,5},{8,14},{9,15},{10,... | collective-permute-start | bytes 387080 | tf_op jit(solution)/shard_map/ppermute | solution.py:675
  338.1 78.5 %collective-permute-start.7 = (bf16[24,2688]{1,0:T(8,128)(2,1)}, bf16[24,2688]{1,0:T(8,128)(2,1)S(1)}, u32[]{:S(2)}, u32[]{:S(2)}) collective-permute-start(bf16[24,2688]{1,0:T(8,128)(2,1)} %get-tuple-element.235), channel_id=1, source_target_pairs={{0,5},{1,6},{2,7},{3,0},{4,1},{5,2},{6,3},{7,4},{8,13},{9,14},{10,... | collective-permute-start | bytes 387080 | tf_op jit(solution)/shard_map/ppermute | solution.py:675
  338.1 78.6 %collective-permute-start.6 = (bf16[24,2688]{1,0:T(8,128)(2,1)}, bf16[24,2688]{1,0:T(8,128)(2,1)S(1)}, u32[]{:S(2)}, u32[]{:S(2)}) collective-permute-start(bf16[24,2688]{1,0:T(8,128)(2,1)} %get-tuple-element.236), channel_id=1, source_target_pairs={{0,4},{1,5},{2,6},{3,7},{4,0},{5,1},{6,2},{7,3},{8,12},{9,13},{10,... | collective-permute-start | bytes 387080 | tf_op jit(solution)/shard_map/ppermute | solution.py:675
  341.1 75.6 %collective-permute-start.5 = (bf16[24,2688]{1,0:T(8,128)(2,1)}, bf16[24,2688]{1,0:T(8,128)(2,1)S(1)}, u32[]{:S(2)}, u32[]{:S(2)}) collective-permute-start(bf16[24,2688]{1,0:T(8,128)(2,1)} %get-tuple-element.237), channel_id=1, source_target_pairs={{0,3},{1,4},{2,5},{3,6},{4,7},{5,0},{6,1},{7,2},{8,11},{9,12},{10,... | collective-permute-start | bytes 387080 | tf_op jit(solution)/shard_map/ppermute | solution.py:675
  357.9 58.8 %collective-permute-start.4 = (bf16[24,2688]{1,0:T(8,128)(2,1)}, bf16[24,2688]{1,0:T(8,128)(2,1)}, u32[]{:S(2)}, u32[]{:S(2)}) collective-permute-start(bf16[24,2688]{1,0:T(8,128)(2,1)} %get-tuple-element.238), channel_id=1, source_target_pairs={{0,2},{1,3},{2,4},{3,5},{4,6},{5,7},{6,0},{7,1},{8,10},{9,11},{10,... | collective-permute-start | bytes 387080 | tf_op jit(solution)/shard_map/ppermute | solution.py:675
  360.7 56.8 %collective-permute-start.3 = (bf16[24,2688]{1,0:T(8,128)(2,1)}, bf16[24,2688]{1,0:T(8,128)(2,1)}, u32[]{:S(2)}, u32[]{:S(2)}) collective-permute-start(bf16[24,2688]{1,0:T(8,128)(2,1)} %get-tuple-element.239), channel_id=1, source_target_pairs={{0,1},{1,2},{2,3},{3,4},{4,5},{5,6},{6,7},{7,0},{8,9},{9,10},{10,1... | collective-permute-start | bytes 387080 | tf_op jit(solution)/shard_map/ppermute | solution.py:675
  417.4 59.4 %all-to-all-start.6 = ((bf16[32,2,32,384]{3,2,1,0:T(8,128)(2,1)}), bf16[32,2,32,384]{3,2,1,0:T(8,128)(2,1)}, u32[]{:S(2)}, u32[]{:S(2)}) async-start(bf16[32,2,32,384]{3,2,1,0:T(8,128)(2,1)} %get-tuple-element.112), calls=%async_computation.6 | async-start | bytes 3145728 | tf_op jit(solution)/shard_map/all_to_all | solution.py:650
  438.2 10.3 %collective-permute-start.10 = (bf16[192,768]{1,0:T(8,128)(2,1)S(1)}, bf16[192,768]{1,0:T(8,128)(2,1)S(1)}, u32[]{:S(2)}, u32[]{:S(2)}) collective-permute-start(bf16[192,768]{1,0:T(8,128)(2,1)S(1)} %get-tuple-element.230), channel_id=1, source_target_pairs={{0,8},{8,16},{16,24},{24,0},{1,9},{9,17},{17,25},{25,1},{2,10},{10... | collective-permute-start | bytes 884744 | tf_op jit(solution)/shard_map/ppermute | solution.py:675
  438.5 10.7 %collective-permute-start.12 = (bf16[192,768]{1,0:T(8,128)(2,1)S(1)}, bf16[192,768]{1,0:T(8,128)(2,1)S(1)}, u32[]{:S(2)}, u32[]{:S(2)}) collective-permute-start(bf16[192,768]{1,0:T(8,128)(2,1)S(1)} %get-tuple-element.231), channel_id=1, source_target_pairs={{0,24},{8,0},{16,8},{24,16},{1,25},{9,1},{17,9},{25,17},{2,26},{10... | collective-permute-start | bytes 884744 | tf_op jit(solution)/shard_map/ppermute | solution.py:675
  440.0 16.5 %collective-permute-start.11 = (bf16[192,768]{1,0:T(8,128)(2,1)S(1)}, bf16[192,768]{1,0:T(8,128)(2,1)S(1)}, u32[]{:S(2)}, u32[]{:S(2)}) collective-permute-start(bf16[192,768]{1,0:T(8,128)(2,1)S(1)} %get-tuple-element.232), channel_id=1, source_target_pairs={{0,16},{8,24},{16,0},{24,8},{1,17},{9,25},{17,1},{25,9},{2,18},{10... | collective-permute-start | bytes 884744 | tf_op jit(solution)/shard_map/ppermute | solution.py:675
  456.8 12.3 %collective-permute-start.13 = (bf16[24,768]{1,0:T(8,128)(2,1)S(1)}, bf16[24,768]{1,0:T(8,128)(2,1)S(1)}, u32[]{:S(2)}, u32[]{:S(2)}) collective-permute-start(bf16[24,768]{1,0:T(8,128)(2,1)S(1)} %get-tuple-element.241), channel_id=1, source_target_pairs={{0,1},{1,2},{2,3},{3,4},{4,5},{5,6},{6,7},{7,0},{8,9},{9,10},{10,1... | collective-permute-start | bytes 110600 | tf_op jit(solution)/shard_map/ppermute | solution.py:675
  462.8 6.8 %collective-permute-start.19 = (bf16[24,768]{1,0:T(8,128)(2,1)S(1)}, bf16[24,768]{1,0:T(8,128)(2,1)S(1)}, u32[]{:S(2)}, u32[]{:S(2)}) collective-permute-start(bf16[24,768]{1,0:T(8,128)(2,1)S(1)} %get-tuple-element.242), channel_id=1, source_target_pairs={{0,7},{1,0},{2,1},{3,2},{4,3},{5,4},{6,5},{7,6},{8,15},{9,8},{10,9... | collective-permute-start | bytes 110600 | tf_op jit(solution)/shard_map/ppermute | solution.py:675
  464.2 10.8 %collective-permute-start.18 = (bf16[24,768]{1,0:T(8,128)(2,1)S(1)}, bf16[24,768]{1,0:T(8,128)(2,1)S(1)}, u32[]{:S(2)}, u32[]{:S(2)}) collective-permute-start(bf16[24,768]{1,0:T(8,128)(2,1)S(1)} %get-tuple-element.243), channel_id=1, source_target_pairs={{0,6},{1,7},{2,0},{3,1},{4,2},{5,3},{6,4},{7,5},{8,14},{9,15},{10,... | collective-permute-start | bytes 110600 | tf_op jit(solution)/shard_map/ppermute | solution.py:675
  465.0 9.9 %collective-permute-start.17 = (bf16[24,768]{1,0:T(8,128)(2,1)S(1)}, bf16[24,768]{1,0:T(8,128)(2,1)S(1)}, u32[]{:S(2)}, u32[]{:S(2)}) collective-permute-start(bf16[24,768]{1,0:T(8,128)(2,1)S(1)} %get-tuple-element.244), channel_id=1, source_target_pairs={{0,5},{1,6},{2,7},{3,0},{4,1},{5,2},{6,3},{7,4},{8,13},{9,14},{10,... | collective-permute-start | bytes 110600 | tf_op jit(solution)/shard_map/ppermute | solution.py:675
  468.1 6.9 %collective-permute-start.16 = (bf16[24,768]{1,0:T(8,128)(2,1)S(1)}, bf16[24,768]{1,0:T(8,128)(2,1)S(1)}, u32[]{:S(2)}, u32[]{:S(2)}) collective-permute-start(bf16[24,768]{1,0:T(8,128)(2,1)S(1)} %get-tuple-element.245), channel_id=1, source_target_pairs={{0,4},{1,5},{2,6},{3,7},{4,0},{5,1},{6,2},{7,3},{8,12},{9,13},{10,... | collective-permute-start | bytes 110600 | tf_op jit(solution)/shard_map/ppermute | solution.py:675
  469.1 6.4 %collective-permute-start.15 = (bf16[24,768]{1,0:T(8,128)(2,1)S(1)}, bf16[24,768]{1,0:T(8,128)(2,1)S(1)}, u32[]{:S(2)}, u32[]{:S(2)}) collective-permute-start(bf16[24,768]{1,0:T(8,128)(2,1)S(1)} %get-tuple-element.246), channel_id=1, source_target_pairs={{0,3},{1,4},{2,5},{3,6},{4,7},{5,0},{6,1},{7,2},{8,11},{9,12},{10,... | collective-permute-start | bytes 110600 | tf_op jit(solution)/shard_map/ppermute | solution.py:675
  469.6 5.9 %collective-permute-start.14 = (bf16[24,768]{1,0:T(8,128)(2,1)S(1)}, bf16[24,768]{1,0:T(8,128)(2,1)S(1)}, u32[]{:S(2)}, u32[]{:S(2)}) collective-permute-start(bf16[24,768]{1,0:T(8,128)(2,1)S(1)} %get-tuple-element.247), channel_id=1, source_target_pairs={{0,2},{1,3},{2,4},{3,5},{4,6},{5,7},{6,0},{7,1},{8,10},{9,11},{10,... | collective-permute-start | bytes 110600 | tf_op jit(solution)/shard_map/ppermute | solution.py:675
  476.9 7.4 %copy-start.1 = (bf16[64,32,768]{2,1,0:T(8,128)(2,1)S(1)}, bf16[64,32,768]{2,1,0:T(8,128)(2,1)}, u32[]{:S(2)}) copy-start(bf16[64,32,768]{2,1,0:T(8,128)(2,1)} %param.19) | copy-start | bytes 9437188
  (12 other events, 27.5 us)
Sparse Core Ops, SparseCore 0:
  16.6 84.7 all-gather.1

commit v4 on v3

--- a/solution.py
+++ b/solution.py
@@ -20,6 +20,7 @@
 TILE = 272
 TILES = ROWS // TILE
 BIG = 1e30
+STEPS = 4
 
 norm_eps = 1e-12
 rms_eps = 1e-06
@@ -448,6 +449,9 @@
 PARAMS = pltpu.CompilerParams(
     dimension_semantics=("arbitrary",), vmem_limit_bytes=63_000_000
 )
+SMALL = pltpu.CompilerParams(
+    dimension_semantics=("arbitrary",), vmem_limit_bytes=24_000_000
+)
 
 
 GRAD_COLS = 2 * D + 4 * WIN + 128
@@ -588,6 +592,147 @@
     )(len_arr, cot, ctx0, ctx1, n1, n2, inv, slope, act, full, wu, vecs)
 
 
+def pack_kernel(
+    odd_ref, bias_ref, o_ref, down_ref, q_ref, k_ref, v_ref, up_ref, out_ref, low_s, high_s
+):
+    rows = o_ref.shape[0]
+    odd = odd_ref[0]
+    eye = lax.broadcasted_iota(jnp.int32, (rows, rows), 0) == lax.broadcasted_iota(
+        jnp.int32, (rows, rows), 1
+    )
+    columns = mm(jnp.where(eye, 1.0, 0.0).astype(bf16), bias_ref[...], NT)
+    shift = lax.broadcasted_iota(jnp.int32, (192, WIN), 1) - lax.broadcasted_iota(
+        jnp.int32, (192, WIN), 0
+    )
+    move = jnp.where(shift == 64 * odd, 1.0, 0.0).astype(bf16)
+
+    def padded(weight, column):
+        lane = lax.broadcasted_iota(jnp.int32, (weight.shape[0], WIN), 1)
+        moved = mm(weight, move, NN)
+        return jnp.where(lane == 192 * (1 - odd), column, moved)
+
+    out_ref[:, :D] = o_ref[...]
+    out_ref[:, D : 2 * D] = down_ref[...]
+    zero = jnp.zeros((rows, 1), f32)
+    sources = ((q_ref, columns[:, 6:7]), (k_ref, zero), (v_ref, columns[:, 7:8]))
+    for which, (ref, column) in enumerate(sources):
+        start = 2 * D + WIN * which
+        out_ref[:, start : start + WIN] = padded(ref[...], column).astype(bf16)
+    column = jnp.concatenate([columns[:, 8 + i : 9 + i] for i in range(4)], axis=0)
+    up = padded(up_ref[...], column)
+    low_s[...] = up[:, :128]
+    high_s[...] = up[:, 128:]
+    for j in range(4):
+        for half, source in enumerate((low_s, high_s)):
+            start = 3 * D + WIN * j + 128 * half
+            out_ref[:, start : start + 128] = source[pl.ds(j, rows, stride=4), :].astype(bf16)
+    out_ref[:, 3 * D + 4 * WIN :] = columns.astype(bf16)
+
+
+def pack(odd, biases, up_bias, o_weight, down_weight, in_weights, up_weight):
+    rows = o_weight.shape[0]
+    flat = jnp.concatenate(biases + [up_bias]).reshape(-1, rows)
+    flat = jnp.pad(flat, ((0, 128 - flat.shape[0]), (0, 0)))
+    cols = 3 * D + 4 * WIN + 128
+    arrays = [flat, o_weight, down_weight, *in_weights, up_weight]
+    return pl.pallas_call(
+        pack_kernel,
+        name="pack",
+        grid_spec=pltpu.PrefetchScalarGridSpec(
+            num_scalar_prefetch=1,
+            grid=(1,),
+            in_specs=[whole(array.shape) for array in arrays],
+            out_specs=[kept((rows, cols))],
+            scratch_shapes=[pltpu.VMEM((4 * rows, 128), f32)] * 2,
+        ),
+        out_shape=[struct((rows, cols), bf16)],
+        compiler_params=SMALL,
+        cost_estimate=pl.CostEstimate(flops=0, bytes_accessed=400_000, transcendentals=0),
+    )(odd.astype(jnp.int32).reshape(1), *arrays)[0]
+
+
+def source_of(len_ref, perm_ref, place):
+    first = perm_ref[place - place % 2]
+    second = perm_ref[place - place % 2 + 1]
+    swapped = (len_ref[first] < len_ref[second]).astype(jnp.int32)
+    return jnp.where(swapped == place % 2, first, second)
+
+
+def deal_kernel(len_ref, perm_ref, rows_ref, *out_refs):
+    count = out_refs[0].shape[0]
+    start = pl.program_id(0) * count
+
+    def one(index, carry):
+        source = source_of(len_ref, perm_ref, start + index)
+        lane = 0
+        for out_ref in out_refs:
+            width = out_ref.shape[2]
+            out_ref[index] = rows_ref[source, :, lane : lane + width]
+            lane += width
+        return carry
+
+    lax.fori_loop(0, count, one, 0)
+
+
+def deal(rows, lengths, permutation, parts):
+    total, size, width = rows.shape
+    count = total // STEPS
+    return pl.pallas_call(
+        deal_kernel,
+        name="deal",
+        grid_spec=pltpu.PrefetchScalarGridSpec(
+            num_scalar_prefetch=2,
+            grid=(STEPS,),
+            in_specs=[whole(rows.shape)],
+            out_specs=[pl.BlockSpec((count, size, width // parts), lambda i, *_: (i, 0, 0))] * parts,
+        ),
+        out_shape=[struct((total, size, width // parts), rows.dtype)] * parts,
+        compiler_params=SMALL,
+        cost_estimate=pl.CostEstimate(flops=0, bytes_accessed=8_000_000, transcendentals=0),
+    )(lengths, permutation, rows)
+
+
+def restore_kernel(len_ref, perm_ref, first_ref, second_ref, out_ref, place_s):
+    count = out_ref.shape[0]
+    start = pl.program_id(0) * count
+    width = first_ref.shape[2]
+
+    @pl.when(pl.program_id(0) == 0)
+    def _():
+        def note(index, carry):
+            place_s[source_of(len_ref, perm_ref, index)] = index
+            return carry
+
+        lax.fori_loop(0, first_ref.shape[0], note, 0)
+
+    def one(index, carry):
+        place = place_s[start + index]
+        out_ref[index, :, :width] = first_ref[place]
+        out_ref[index, :, width:] = second_ref[place]
+        return carry
+
+    lax.fori_loop(0, count, one, 0)
+
+
+def restore(first, second, lengths, permutation):
+    total, size, width = first.shape
+    count = total // STEPS
+    return pl.pallas_call(
+        restore_kernel,
+        name="restore",
+        grid_spec=pltpu.PrefetchScalarGridSpec(
+            num_scalar_prefetch=2,
+            grid=(STEPS,),
+            in_specs=[whole(first.shape), whole(second.shape)],
+            out_specs=[pl.BlockSpec((count, size, 2 * width), lambda i, *_: (i, 0, 0))],
+            scratch_shapes=[pltpu.SMEM((total,), jnp.int32)],
+        ),
+        out_shape=[struct((total, size, 2 * width), first.dtype)],
+        compiler_params=SMALL,
+        cost_estimate=pl.CostEstimate(flops=0, bytes_accessed=8_000_000, transcendentals=0),
+    )(lengths, permutation, first, second)[0]
+
+
 def pick(values, index):
     return values.at[index].get(mode="promise_in_bounds")
 
@@ -618,9 +763,15 @@
             jnp.concatenate([weight, column, gap], axis=1),
         )
 
-    small = [o_bias, norm1_gain, norm1_bias, down_bias, norm2_gain, norm2_bias]
-    full = lax.all_gather(
-        jnp.concatenate(
+    if rows_dev % 8 == 0:
+        packed = pack(
+            odd,
+            [o_bias, norm1_gain, norm1_bias, down_bias, norm2_gain, norm2_bias, q_bias, v_bias],
+            up_bias, o_weight, down_weight, [q_weight, k_weight, v_weight], up_weight,
+        )
+    else:
+        small = [o_bias, norm1_gain, norm1_bias, down_bias, norm2_gain, norm2_bias]
+        packed = jnp.concatenate(
             [
                 o_weight,
                 down_weight,
@@ -631,18 +782,11 @@
                 jnp.pad(jnp.stack(small, axis=1), ((0, 0), (0, 122))),
             ],
             axis=1,
-        ),
-        AXES,
-        axis=0,
-        tiled=True,
-    )
+        )
+    full = lax.all_gather(packed, AXES, axis=0, tiled=True)
 
     dealt_lengths = pick(lengths, permutation).reshape(devices, seq_dev)
     swap = dealt_lengths[:, 0] < dealt_lengths[:, 1]
-    dealt = permutation.reshape(devices, seq_dev)
-    order = jnp.where(swap[:, None], dealt[:, ::-1], dealt).reshape(seq_total)
-    places = jnp.arange(seq_total, dtype=jnp.int32)
-    inverse = jnp.sum(jnp.where(order[None, :] == places[:, None], places[None, :], 0), axis=1)
     my_swap = lax.dynamic_index_in_dim(swap, my_index, 0, False)
     len_arr = jnp.max(lax.dynamic_slice_in_dim(dealt_lengths, my_index, 1, 0)).reshape(1)
 
@@ -664,24 +808,38 @@
             rows = rows.transpose(1, 0, 2, 3)
         return swap_blocks(rows).reshape(seq_total, piece_len, width)
 
-    def send_over(partial, axis):
+    def send_pair(partial, axis):
         count = lax.axis_size(axis)
-        me = lax.axis_index(axis)
-        size = partial.shape[0] // count
+        parity = lax.axis_index(axis) % 2
+        blocks = partial.reshape(count // 2, 2, partial.shape[0] // count, partial.shape[1])
+        kept_part, given = (
+            lax.dynamic_slice_in_dim(blocks, which, 1, 1) for which in (parity, 1 - parity)
+        )
+        return [kept_part, lax.ppermute(given, axis, [(i, i ^ 1) for i in range(count)])]
+
+    def send_rest(partial, axis):
+        count = lax.axis_size(axis)
+        half = count // 2
+        place = lax.axis_index(axis) // 2
+        size = partial.shape[0] // half
         block_of = lambda index: lax.dynamic_slice_in_dim(partial, index * size, size, 0)
-        parts = [block_of(me)]
-        for shift in range(1, count):
-            target = [(i, (i + shift) % count) for i in range(count)]
-            parts.append(lax.ppermute(block_of((me + shift) % count), axis, target))
+        parts = [block_of(place)]
+        for shift in range(1, half):
+            target = [(i, (i + 2 * shift) % count) for i in range(count)]
+            parts.append(lax.ppermute(block_of((place + shift) % half), axis, target))
         return parts
 
     def total(parts):
-        return sum(part.astype(f32) for part in parts)
-
-    dealt_tokens = pick(tokens, order)
-    tok0 = arrive(dealt_tokens[:, :, :HALF])
-    tok1 = arrive(dealt_tokens[:, :, HALF:])
-    dealt_cot, tok0, tok1 = tie(pick(cotangent, order), tok0, tok1)
+        result = sum(part.astype(f32) for part in parts)
+        return result.reshape(-1, result.shape[-1])
+
+    def total_low(parts):
+        return total(parts).astype(bf16)
+
+    tok0, tok1 = deal(tokens, lengths, permutation, 2)
+    tok0 = arrive(tok0)
+    tok1 = arrive(tok1)
+    dealt_cot, tok0, tok1 = tie(deal(cotangent, lengths, permutation, 1)[0], tok0, tok1)
     cot = arrive(dealt_cot)
 
     x0, qa0, ka0, va0, ctx0 = attn_fwd(len_arr, tok0, full, 0)
@@ -698,23 +856,21 @@
     )
     gctx, out1, back_out0 = tie(gctx, out1, back_out0)
     back_out1 = leave(out1)
-    parts = send_over(grads, "dp")
+    parts = send_pair(grads, "dp")
     ig0, dw0 = attn_bwd(len_arr, qa0, ka0, va0, ctx0, gctx, x0, base, full, 0)
     ig0, dw0, gctx, back_out1, *parts = tie(ig0, dw0, gctx, back_out1, *parts)
     back0 = leave(ig0)
-    parts = send_over(total(parts).astype(bf16), "fsdp")
+    parts = send_rest(total_low(parts), "dp")
     ig1, dw1 = attn_bwd(len_arr, qa1, ka1, va1, ctx1, gctx, x1, base, full, 1)
     ig1, dw1, back0, *parts = tie(ig1, dw1, back0, *parts)
-    mine = total(parts)
     back1 = leave(ig1)
-    parts = send_over(jnp.concatenate([dw0, dw1], axis=0), "dp")
-    mine_in = total(send_over(total(parts).astype(bf16), "fsdp"))
-
-    join_halves = lambda first, second: jnp.concatenate(
-        [pick(first, inverse), pick(second, inverse)], axis=-1
-    )
-    output = join_halves(back_out0, back_out1)
-    input_grad = join_halves(back0, back1)
+    mine = total(send_rest(total_low(send_pair(total_low(parts), "fsdp")), "fsdp"))
+    parts = send_rest(total_low(send_pair(jnp.concatenate([dw0, dw1], axis=0), "dp")), "dp")
+    mine_in = total(send_rest(total_low(send_pair(total_low(parts), "fsdp")), "fsdp"))
+
+    back_out0, back_out1, mine = tie(back_out0, back_out1, mine)
+    output = restore(back_out0, back_out1, lengths, permutation)
+    input_grad = restore(back0, back1, lengths, permutation)
     lens = jnp.stack([len_arr[0], ROWS - len_arr[0]]).astype(f32)
     sums = jnp.stack([stat[4:8, 0], stat[0:4, 0] - stat[4:8, 0]], axis=1)
     rms = jnp.sqrt(sums / (lens[None, :] * D) + rms_eps)

time: 495 us -> 440 us (0.89)
  starting transfers between devices: 79.6 us -> 44.7 us
  Pallas kernels: 171 us -> 187 us
  waiting for transfers between devices: 100 us -> 84.1 us
  local copies, waits for them, and re-layouts: 46.6 us -> 35.7 us
  other arithmetic: 22.9 us -> 15.8 us
    ppermute x20 -> x12, starting transfers between devices: 50.5 us -> 17.9 us  [the longest x8 14.8 us: send_rest(): parts.append(lax.ppermute(block_of((place + shift) % half), axis, target))]
    ppermute x20 -> x12, waiting for transfers between devices: 57.3 us -> 39.1 us  [the longest x8 34.3 us: send_rest(): parts.append(lax.ppermute(block_of((place + shift) % half), axis, target))]
    gather x7 -> x1, local copies, waits for them, and re-layouts: 17 us -> 0.77 us  [pick(): return values.at[index].get(mode='promise_in_bounds')]
    pallas_call x0 -> x5, Pallas kernels: none -> 15.5 us  [the longest x2 9.1 us: restore(): pl.pallas_call(restore_kernel, name='restore', grid_spec=pltpu.PrefetchSc...]
    concatenate x2 -> x1, other arithmetic: 7.4 us -> 1.32 us  [on_device(): jnp.concatenate([dw0, dw1], axis=0)]
    convert_element_type x2 -> x6, other arithmetic: 2.81 us -> 8.16 us  [total_low(): return total(parts).astype(bf16)]
    concatenate x2 -> x1, local copies, waits for them, and re-layouts: 1.11 us -> 6.1 us  [pack(): flat = jnp.concatenate(biases + [up_bias]).reshape(-1, rows)]
  transfers between devices with their start and end apart: 27 -> 19, of which waited for: 9 -> 9; matrix products, arithmetic and copies ran while one was open for 10% -> 7% of each run, Pallas kernels for 35% -> 41%
where the time goes in v4:
time: 440 us; the launch traced here: 439 us
  Pallas kernels  187 us (42%)
  waiting for transfers between devices  84.1 us (19%)
  blocking collectives  56.4 us (13%)
  starting transfers between devices  44.7 us (10%)
  local copies, waits for them, and re-layouts  35.7 us (8%)
  other arithmetic  15.8 us (4%)
  between operations  15.2 us (3%)
    pallas_call x2, Pallas kernels, attn_bwd(): pl.pallas_call(attn_bwd_kernel, name='attn_bwd', grid_spec=pltpu.Prefetch...  67.8 us
    all_to_all x1, blocking collectives, swap_blocks(): return lax.all_to_all(rows, AXES, split_axis=0, concat_axis=0, tiled=True)  56.4 us
    pallas_call x2, Pallas kernels, attn_fwd(): pl.pallas_call(attn_fwd_kernel, name='attn_fwd', grid_spec=pltpu.Prefetch...  50.9 us
    all_to_all x6, waiting for transfers between devices, swap_blocks(): return lax.all_to_all(rows, AXES, split_axis=0, concat_axis=0, tiled=True)  44.9 us
    ppermute x8, waiting for transfers between devices, send_rest(): parts.append(lax.ppermute(block_of((place + shift) % half), axis, target))  34.3 us
    pallas_call x1, Pallas kernels, mid_bwd(): pl.pallas_call(mid_bwd_kernel, name='mid_bwd', grid_spec=pltpu.PrefetchSc...  32.4 us
    all_to_all x6, starting transfers between devices, swap_blocks(): return lax.all_to_all(rows, AXES, split_axis=0, concat_axis=0, tiled=True)  26.8 us
    pallas_call x1, Pallas kernels, mid_fwd(): pl.pallas_call(mid_fwd_kernel, name='mid_fwd', grid_spec=pltpu.PrefetchSc...  20.2 us
  transfers between devices with their start and end apart: 19, of which 9 were waited for; matrix products, arithmetic and copies ran while one was open for 7% of the time, Pallas kernels for 41%

profile of v4, /device:TPU:0, one launch (start us, length us, event | category | flops | bytes accessed | tf_op | source)
XLA Modules:
  0.0 438.6 jit_solution(6379093503771526444)
XLA Ops:
  7.3 6.1 %concatenate.10 = bf16[288]{0:T(512)(128)(2,1)S(1)} concatenate(bf16[24]{0:T(256)(128)(2,1)} %param.29, bf16[24]{0:T(256)(128)(2,1)} %param.30, bf16[24]{0:T(256)(128)(2,1)} %param.31, bf16[24]{0:T(256)(128)(2,1)} %param.35, bf16[24]{0:T(256)(128)(2,1)} %param.36, bf16[24]{0:T(256)(128)(2,1)} %param.37, bf16[24]{0:T(256)(128)(2,1)} %param.24, bf16[24]{0:T(256)(128)(2,1)} %param.27, ...), dimensions={0} | concatenate | bytes 1152 | tf_op jit(solution)/shard_map/concatenate | solution.py:634
  22.2 2.1 deal.3
  24.3 56.4 %all_to_all.35.tok_ref = bf16[32,2,32,384]{3,2,1,0:T(8,128)(2,1)} all-to-all(bf16[32,2,32,384]{3,2,1,0:T(8,128)(2,1)S(1)} %bitcast.24), channel_id=1, replica_groups=mesh['dp'=4,'fsdp'=8] {'dp','fsdp'}, dimensions={0} | all-to-all | bytes 3145728 | tf_op jit(solution)/shard_map/all_to_all | solution.py:794
  80.7 3.8 all-to-all-start.1
  84.5 3.3 deal.2
  87.8 41.0 %all-to-all-done.1.tok_ref = bf16[32,2,32,384]{3,2,1,0:T(8,128)(2,1)} async-done(((bf16[32,2,32,384]{3,2,1,0:T(8,128)(2,1)}), bf16[32,2,32,384]{3,2,1,0:T(8,128)(2,1)}, u32[]{:S(2)}, u32[]{:S(2)}) %all-to-all-start.1) | async-done | bytes 1572896 | tf_op jit(solution)/shard_map/all_to_all | solution.py:794
  128.8 3.5 all-to-all-start.2
  136.1 2.2 reshape.133.wu_ref
  140.1 25.5 %attn_fwd.3 = (bf16[1088,384]{1,0:T(8,128)(2,1)}, bf16[1088,768]{1,0:T(8,128)(2,1)}, bf16[1088,768]{1,0:T(8,128)(2,1)}, bf16[1088,768]{1,0:T(8,128)(2,1)}, bf16[1088,384]{1,0:T(8,128)(2,1)}) custom-call(s32[1]{0:T(128)} %bitcast.len_ref, bf16[32,2,32,384]{3,2,1,0:T(8,128)(2,1)} %all-to-all-done.1.tok_ref, bf16[768,3456]{1,0:T(8,128)(2,1)} %all-gather.2.cloned.1.call-done.full_ref), custom_call_target="tpu_custom_call" | custom-call | flops 20000000000 | bytes 12000000 | tf_op jit(solution)/shard_map/attn_fwd/pallas_call | solution.py:462
  165.5 25.5 %attn_fwd.2 = (bf16[1088,384]{1,0:T(8,128)(2,1)}, bf16[1088,768]{1,0:T(8,128)(2,1)}, bf16[1088,768]{1,0:T(8,128)(2,1)}, bf16[1088,768]{1,0:T(8,128)(2,1)}, bf16[1088,384]{1,0:T(8,128)(2,1)}) custom-call(s32[1]{0:T(128)} %bitcast.len_ref, bf16[32,2,32,384]{3,2,1,0:T(8,128)(2,1)} %all_to_all.35.tok_ref, bf16[768,3456]{1,0:T(8,128)(2,1)} %all-gather.2.cloned.1.call-done.full_ref), custom_call_target="tpu_custom_call" | custom-call | flops 20000000000 | bytes 12000000 | tf_op jit(solution)/shard_map/attn_fwd/pallas_call | solution.py:462
  191.0 20.2 %mid_fwd.1 = (bf16[32,2,32,384]{3,2,1,0:T(8,128)(2,1)}, bf16[32,2,32,384]{3,2,1,0:T(8,128)(2,1)}, f32[1088,768]{1,0:T(8,128)}, f32[1088,768]{1,0:T(8,128)}, f32[...) custom-call(s32[1]{0:T(128)} %bitcast.len_ref, ...), custom_call_target="tpu_custom_call" | custom-call | flops 15000000512 | bytes 36000000 | tf_op jit(solution)/shard_map/mid_fwd/pallas_call | solution.py:532
  211.3 6.0 %all-to-all-start.3 = ((bf16[32,2,32,384]{3,2,1,0:T(8,128)(2,1)}), bf16[32,2,32,384]{3,2,1,0:T(8,128)(2,1)S(1)}, u32[]{:S(2)}, u32[]{:S(2)}) async-start(bf16[32,2,32,384]{3,2,1,0:T(8,128)(2,1)} %get-tuple-element.87), calls=%async_computation.3 | async-start | bytes 3145728 | tf_op jit(solution)/shard_map/all_to_all | solution.py:794
  219.7 32.4 %mid_bwd.1 = (bf16[1088,768]{1,0:T(8,128)(2,1)}, f32[1088,768]{1,0:T(8,128)}, bf16[768,2688]{1,0:T(8,128)(2,1)}) custom-call(s32[1]{0:T(128)} %bitcast.len_ref, bf16[32,2,32,768]{3,2,1,0:T(8,128)(2,1)} %all-to-all-done.2.cot_ref, bf16[1088,384]{1,0:T(8,128)(2,1)} %get-tuple-element.75.ctx0_ref.ctx_ref, bf16[1088,384]{1,0:T(8,128)(2,1)} %get-tuple-element.76.ctx1_ref.ctx_ref, ...), custom_call_target="tpu_custom_call" | custom-call | flops 30000001024 | bytes 50000000 | tf_op jit(solution)/shard_map/mid_bwd/pallas_call | solution.py:561
  252.1 3.7 all-to-all-done.3
  255.7 2.7 all-to-all-start.4
  258.4 4.5 %constant_dynamic-slice_fusion.14 = (bf16[2,1,192,2688]{3,2,1,0:T(8,128)(2,1)}, bf16[2,1,192,2688]{3,2,1,0:T(8,128)(2,1)}) fusion(bf16[2,2,192,2688]{3,2,1,0:T(8,128)(2,1)} %bitcast.30, s32[]{:T(128)S(6)} %select_n.170, s32[]{:T(128)S(6)} %select_n.169), kind=kLoop, calls=%fused_computation.42 | loop fusion | bytes 8257544 | tf_op jit(solution)/shard_map/dynamic_slice | solution.py:816
  263.1 33.9 %attn_bwd.2 = (bf16[32,2,32,384]{3,2,1,0:T(8,128)(2,1)}, bf16[384,768]{1,0:T(8,128)(2,1)}) custom-call(s32[1]{0:T(128)} %bitcast.len_ref, bf16[1088,768]{1,0:T(8,128)(2,1)} %get-tuple-element.89.qa_ref, bf16[1088,768]{1,0:T(8,128)(2,1)} %get-tuple-element.90.ka_ref, bf16[1088,768]{1,0:T(8,128)(2,1)} %get-tuple-element.91.va_ref, ...), custom_call_target="tpu_custom_call" | custom-call | flops 30000001024 | bytes 16000000 | tf_op jit(solution)/shard_map/attn_bwd/pallas_call | solution.py:491
  297.1 6.0 %all-to-all-start.5 = ((bf16[32,2,32,384]{3,2,1,0:T(8,128)(2,1)}), bf16[32,2,32,384]{3,2,1,0:T(8,128)(2,1)}, u32[]{:S(2)}, u32[]{:S(2)}) async-start(bf16[32,2,32,384]{3,2,1,0:T(8,128)(2,1)} %get-tuple-element.105), calls=%async_computation.5 | async-start | bytes 3145728 | tf_op jit(solution)/shard_map/all_to_all | solution.py:794
  303.2 2.7 add_convert_fusion
  308.8 33.9 %attn_bwd.3 = (bf16[32,2,32,384]{3,2,1,0:T(8,128)(2,1)}, bf16[384,768]{1,0:T(8,128)(2,1)}) custom-call(s32[1]{0:T(128)} %bitcast.len_ref, bf16[1088,768]{1,0:T(8,128)(2,1)} %get-tuple-element.99.qa_ref, bf16[1088,768]{1,0:T(8,128)(2,1)} %get-tuple-element.100.ka_ref, bf16[1088,768]{1,0:T(8,128)(2,1)} %get-tuple-element.101.va_ref, ...), custom_call_target="tpu_custom_call" | custom-call | flops 30000001024 | bytes 16000000 | tf_op jit(solution)/shard_map/attn_bwd/pallas_call | solution.py:491
  342.7 2.2 collective-permute-done.1
  354.7 4.8 %all-to-all-start.6 = ((bf16[32,2,32,384]{3,2,1,0:T(8,128)(2,1)}), bf16[32,2,32,384]{3,2,1,0:T(8,128)(2,1)}, u32[]{:S(2)}, u32[]{:S(2)}) async-start(bf16[32,2,32,384]{3,2,1,0:T(8,128)(2,1)} %get-tuple-element.113), calls=%async_computation.6 | async-start | bytes 3145728 | tf_op jit(solution)/shard_map/all_to_all | solution.py:794
  359.5 2.6 collective-permute-done.2
  363.5 4.3 collective-permute-start.3
  367.7 3.2 collective-permute-start.4
  374.2 18.4 %collective-permute-done.3 = bf16[24,2688]{1,0:T(8,128)(2,1)S(1)} collective-permute-done((bf16[24,2688]{1,0:T(8,128)(2,1)S(1)}, bf16[24,2688]{1,0:T(8,128)(2,1)S(1)}, u32[]{:S(2)}, u32[]{:S(2)}) %collective-permute-start.3) | collective-permute-done | bytes 129056 | tf_op jit(solution)/shard_map/ppermute | solution.py:829
  392.7 13.0 %collective-permute-done.4 = bf16[24,2688]{1,0:T(8,128)(2,1)S(1)} collective-permute-done((bf16[24,2688]{1,0:T(8,128)(2,1)S(1)}, bf16[24,2688]{1,0:T(8,128)(2,1)S(1)}, u32[]{:S(2)}, u32[]{:S(2)}) %collective-permute-start.4) | collective-permute-done | bytes 129056 | tf_op jit(solution)/shard_map/ppermute | solution.py:829
  412.1 2.2 collective-permute-done.8
  414.4 1.9 collective-permute-start.10
  416.3 3.4 collective-permute-start.11
  420.5 4.3 restore.2
  426.9 4.8 %restore.3 = bf16[64,32,768]{2,1,0:T(8,128)(2,1)} custom-call(s32[64]{0:T(128)S(1)} %copy-done.1, s32[64]{0:T(128)S(1)} %copy-done.12, bf16[64,32,384]{2,1,0:T(8,128)(2,1)} %bitcast.9.first_ref, bf16[64,32,384]{2,1,0:T(8,128)(2,1)} %bitcast.13.second_ref), custom_call_target="tpu_custom_call" | custom-call | bytes 8000000 | tf_op jit(solution)/shard_map/restore/pallas_call | solution.py:720
  (103 shorter events, 43.0 us)
Async XLA Ops:
  7.2 127.5 %all-gather.2.cloned.1.call-start = ((), (), s32[]{:S(2)}) async-start(), calls=%async_computation.7 | async-start | bytes 5474304 | tf_op jit(solution)/shard_map/all_gather | solution.py:786
  13.5 0.8 copy-start.5
  14.3 0.8 copy-start.6
  19.6 1.9 copy-start.2
  24.2 56.4 %copy-start.4 = (bf16[64,32,384]{2,1,0:T(8,128)(2,1)}, bf16[64,32,384]{2,1,0:T(8,128)(2,1)S(1)}, u32[]{:S(2)}) copy-start(bf16[64,32,384]{2,1,0:T(8,128)(2,1)S(1)} %get-tuple-element.69) | copy-start | bytes 4718596
  80.6 3.8 copy-start.1
  80.6 3.8 copy-start.3
  80.6 3.8 copy-start.12
  80.7 48.2 %all-to-all-start.1 = ((bf16[32,2,32,384]{3,2,1,0:T(8,128)(2,1)}), bf16[32,2,32,384]{3,2,1,0:T(8,128)(2,1)}, u32[]{:S(2)}, u32[]{:S(2)}) async-start(bf16[32,2,32,384]{3,2,1,0:T(8,128)(2,1)} %bitcast.23), calls=%async_computation.1 | async-start | bytes 3145728 | tf_op jit(solution)/shard_map/all_to_all | solution.py:794
  128.8 82.4 %all-to-all-start.2 = ((bf16[32,2,32,768]{3,2,1,0:T(8,128)(2,1)}), bf16[32,2,32,768]{3,2,1,0:T(8,128)(2,1)}, u32[]{:S(2)}, u32[]{:S(2)}) async-start(bf16[32,2,32,768]{3,2,1,0:T(8,128)(2,1)} %bitcast.3), calls=%async_computation.2 | async-start | bytes 6291456 | tf_op jit(solution)/shard_map/all_to_all | solution.py:794
  134.7 1.4 slice-start
  211.3 44.5 %all-to-all-start.3 = ((bf16[32,2,32,384]{3,2,1,0:T(8,128)(2,1)}), bf16[32,2,32,384]{3,2,1,0:T(8,128)(2,1)S(1)}, u32[]{:S(2)}, u32[]{:S(2)}) async-start(bf16[32,2,32,384]{3,2,1,0:T(8,128)(2,1)} %get-tuple-element.87), calls=%async_computation.3 | async-start | bytes 3145728 | tf_op jit(solution)/shard_map/all_to_all | solution.py:794
  255.7 41.4 %all-to-all-start.4 = ((bf16[32,2,32,384]{3,2,1,0:T(8,128)(2,1)}), bf16[32,2,32,384]{3,2,1,0:T(8,128)(2,1)S(1)}, u32[]{:S(2)}, u32[]{:S(2)}) async-start(bf16[32,2,32,384]{3,2,1,0:T(8,128)(2,1)} %get-tuple-element.96), calls=%async_computation.4 | async-start | bytes 3145728 | tf_op jit(solution)/shard_map/all_to_all | solution.py:794
  258.4 4.6 %copy-start.17 = (f32[8,128]{1,0:T(8,128)S(1)}, f32[8,128]{1,0:T(8,128)}, u32[]{:S(2)}) copy-start(f32[8,128]{1,0:T(8,128)} %get-tuple-element.117) | copy-start | bytes 12292
  262.9 34.0 %collective-permute-start = (bf16[2,1,192,2688]{3,2,1,0:T(8,128)(2,1)}, bf16[2,1,192,2688]{3,2,1,0:T(8,128)(2,1)}, u32[]{:S(2)}, u32[]{:S(2)}) collective-permute-start(bf16[2,1,192,2688]{3,2,1,0:T(8,128)(2,1)} %get-tuple-element.180), channel_id=1, source_target_pairs={{0,8},{8,0},{16,24},{24,16},{1,9},{9,1},{17,25},{25,17},{2,10},{10... | collective-permute-start | bytes 6193160 | tf_op jit(solution)/shard_map/ppermute | solution.py:818
  297.1 47.7 %all-to-all-start.5 = ((bf16[32,2,32,384]{3,2,1,0:T(8,128)(2,1)}), bf16[32,2,32,384]{3,2,1,0:T(8,128)(2,1)}, u32[]{:S(2)}, u32[]{:S(2)}) async-start(bf16[32,2,32,384]{3,2,1,0:T(8,128)(2,1)} %get-tuple-element.105), calls=%async_computation.5 | async-start | bytes 3145728 | tf_op jit(solution)/shard_map/all_to_all | solution.py:794
  307.3 37.6 %collective-permute-start.1 = (bf16[192,2688]{1,0:T(8,128)(2,1)}, bf16[192,2688]{1,0:T(8,128)(2,1)}, u32[]{:S(2)}, u32[]{:S(2)}) collective-permute-start(bf16[192,2688]{1,0:T(8,128)(2,1)} %get-tuple-element.182), channel_id=1, source_target_pairs={{0,16},{8,24},{16,0},{24,8},{1,17},{9,25},{17,1},{25,9},{2,18},{10... | collective-permute-start | bytes 3096584 | tf_op jit(solution)/shard_map/ppermute | solution.py:829
  346.6 1.0 copy-start.15
  348.4 13.6 %collective-permute-start.2 = (bf16[4,1,24,2688]{3,2,1,0:T(8,128)(2,1)}, bf16[4,1,24,2688]{3,2,1,0:T(8,128)(2,1)}, u32[]{:S(2)}, u32[]{:S(2)}) collective-permute-start(bf16[4,1,24,2688]{3,2,1,0:T(8,128)(2,1)} %constant_dynamic-slice_fusion.11), channel_id=1, source_target_pairs={{0,1},{1,0},{2,3},{3,2},{4,5},{5,4},{6,7},{7,6},{8,9},{9,8},{10,11... | collective-permute-start | bytes 1548296 | tf_op jit(solution)/shard_map/ppermute | solution.py:818
  352.8 1.0 copy-start.13
  354.7 16.2 %collective-permute-start.6 = (bf16[2,1,192,768]{3,2,1,0:T(8,128)(2,1)}, bf16[2,1,192,768]{3,2,1,0:T(8,128)(2,1)}, u32[]{:S(2)}, u32[]{:S(2)}) collective-permute-start(bf16[2,1,192,768]{3,2,1,0:T(8,128)(2,1)} %constant_dynamic-slice_fusion.7), channel_id=1, source_target_pairs={{0,8},{8,0},{16,24},{24,16},{1,9},{9,1},{17,25},{25,17},{2,10},{10... | collective-permute-start | bytes 1769480 | tf_op jit(solution)/shard_map/ppermute | solution.py:818
  354.7 72.2 %all-to-all-start.6 = ((bf16[32,2,32,384]{3,2,1,0:T(8,128)(2,1)}), bf16[32,2,32,384]{3,2,1,0:T(8,128)(2,1)}, u32[]{:S(2)}, u32[]{:S(2)}) async-start(bf16[32,2,32,384]{3,2,1,0:T(8,128)(2,1)} %get-tuple-element.113), calls=%async_computation.6 | async-start | bytes 3145728 | tf_op jit(solution)/shard_map/all_to_all | solution.py:794
  359.5 11.4 %copy-start.14 = (bf16[768,768]{1,0:T(8,128)(2,1)S(1)}, bf16[768,768]{1,0:T(8,128)(2,1)}, u32[]{:S(2)}) copy-start(bf16[768,768]{1,0:T(8,128)(2,1)} %copy-done.13) | copy-start | bytes 3538948
  363.5 29.2 %collective-permute-start.3 = (bf16[24,2688]{1,0:T(8,128)(2,1)S(1)}, bf16[24,2688]{1,0:T(8,128)(2,1)S(1)}, u32[]{:S(2)}, u32[]{:S(2)}) collective-permute-start(bf16[24,2688]{1,0:T(8,128)(2,1)S(1)} %get-tuple-element.184), channel_id=1, source_target_pairs={{0,2},{1,3},{2,4},{3,5},{4,6},{5,7},{6,0},{7,1},{8,10},{9,11},{10,... | collective-permute-start | bytes 387080 | tf_op jit(solution)/shard_map/ppermute | solution.py:829
  367.7 37.9 %collective-permute-start.4 = (bf16[24,2688]{1,0:T(8,128)(2,1)S(1)}, bf16[24,2688]{1,0:T(8,128)(2,1)S(1)}, u32[]{:S(2)}, u32[]{:S(2)}) collective-permute-start(bf16[24,2688]{1,0:T(8,128)(2,1)S(1)} %get-tuple-element.186), channel_id=1, source_target_pairs={{0,4},{1,5},{2,6},{3,7},{4,0},{5,1},{6,2},{7,3},{8,12},{9,13},{10,... | collective-permute-start | bytes 387080 | tf_op jit(solution)/shard_map/ppermute | solution.py:829
  370.9 34.8 %collective-permute-start.5 = (bf16[24,2688]{1,0:T(8,128)(2,1)S(1)}, bf16[24,2688]{1,0:T(8,128)(2,1)S(1)}, u32[]{:S(2)}, u32[]{:S(2)}) collective-permute-start(bf16[24,2688]{1,0:T(8,128)(2,1)S(1)} %get-tuple-element.185), channel_id=1, source_target_pairs={{0,6},{1,7},{2,0},{3,1},{4,2},{5,3},{6,4},{7,5},{8,14},{9,15},{10,... | collective-permute-start | bytes 387080 | tf_op jit(solution)/shard_map/ppermute | solution.py:829
  372.1 0.8 copy-start.16
  373.7 34.2 %collective-permute-start.7 = (bf16[192,768]{1,0:T(8,128)(2,1)}, bf16[192,768]{1,0:T(8,128)(2,1)}, u32[]{:S(2)}, u32[]{:S(2)}) collective-permute-start(bf16[192,768]{1,0:T(8,128)(2,1)} %constant_dynamic-slice_fusion.6), channel_id=1, source_target_pairs={{0,16},{8,24},{16,0},{24,8},{1,17},{9,25},{17,1},{25,9},{2,18},{10... | collective-permute-start | bytes 884744 | tf_op jit(solution)/shard_map/ppermute | solution.py:829
  409.1 5.2 %collective-permute-start.8 = (bf16[4,1,24,768]{3,2,1,0:T(8,128)(2,1)S(1)}, bf16[4,1,24,768]{3,2,1,0:T(8,128)(2,1)S(1)}, u32[]{:S(2)}, u32[]{:S(2)}) collective-permute-start(bf16[4,1,24,768]{3,2,1,0:T(8,128)(2,1)S(1)} %constant_dynamic-slice_fusion.5), channel_id=1, source_target_pairs={{0,1},{1,0},{2,3},{3,2},{4,5},{5,4},{6,7},{7,6},{8,9},{9,8},{10,11... | collective-permute-start | bytes 442376 | tf_op jit(solution)/shard_map/ppermute | solution.py:818
  414.4 10.4 %collective-permute-start.10 = (bf16[24,768]{1,0:T(8,128)(2,1)S(1)}, bf16[24,768]{1,0:T(8,128)(2,1)S(1)}, u32[]{:S(2)}, u32[]{:S(2)}) collective-permute-start(bf16[24,768]{1,0:T(8,128)(2,1)S(1)} %get-tuple-element.191), channel_id=1, source_target_pairs={{0,4},{1,5},{2,6},{3,7},{4,0},{5,1},{6,2},{7,3},{8,12},{9,13},{10,... | collective-permute-start | bytes 110600 | tf_op jit(solution)/shard_map/ppermute | solution.py:829
  416.3 8.4 %collective-permute-start.11 = (bf16[24,768]{1,0:T(8,128)(2,1)S(1)}, bf16[24,768]{1,0:T(8,128)(2,1)S(1)}, u32[]{:S(2)}, u32[]{:S(2)}) collective-permute-start(bf16[24,768]{1,0:T(8,128)(2,1)S(1)} %get-tuple-element.190), channel_id=1, source_target_pairs={{0,6},{1,7},{2,0},{3,1},{4,2},{5,3},{6,4},{7,5},{8,14},{9,15},{10,... | collective-permute-start | bytes 110600 | tf_op jit(solution)/shard_map/ppermute | solution.py:829
  419.7 5.8 %collective-permute-start.9 = (bf16[24,768]{1,0:T(8,128)(2,1)S(1)}, bf16[24,768]{1,0:T(8,128)(2,1)S(1)}, u32[]{:S(2)}, u32[]{:S(2)}) collective-permute-start(bf16[24,768]{1,0:T(8,128)(2,1)S(1)} %get-tuple-element.189), channel_id=1, source_target_pairs={{0,2},{1,3},{2,4},{3,5},{4,6},{5,7},{6,0},{7,1},{8,10},{9,11},{10,... | collective-permute-start | bytes 110600 | tf_op jit(solution)/shard_map/ppermute | solution.py:829
  (6 other events, 4.2 us)
Sparse Core Ops, SparseCore 0:
  19.1 84.9 all-gather.1

commit v5 on v4

--- a/solution.py
+++ b/solution.py
@@ -212,7 +212,7 @@
 
 def attn_bwd_kernel(
     len_ref, qa_ref, ka_ref, va_ref, ctx_ref, gctx_ref, x_ref, base_ref, full_ref,
-    ig_ref, dw_ref, dq_s, dk_s, dv_s, do_s, dqt_s, ig_s, w_s,
+    ig_ref, kept_ref, given_ref, dq_s, dk_s, dv_s, do_s, dqt_s, ig_s, w_s, dw_ref,
 ):
     pair = pl.program_id(0)
     lane0 = pl.multiple_of(pair * 128, 128)
@@ -284,6 +284,20 @@
                 total[g] = part if which == 0 else total[g] + part
         ig_s[...] = (join(total) + base_ref[...]).astype(bf16)
         unmerge_rows(ig_s, ig_ref, len_ref[0])
+        split_chunks(dw_ref, kept_ref, given_ref, len_ref[1])
+
+
+def split_chunks(rows_ref, kept_ref, given_ref, parity):
+    pairs, size, _ = kept_ref.shape
+    for own in range(2):
+
+        @pl.when(parity == own)
+        def _():
+            for pair in range(pairs):
+                for which in range(2):
+                    start = (2 * pair + which) * size
+                    target = kept_ref if which == own else given_ref
+                    target[pair] = rows_ref[start : start + size, :]
 
 
 def norm(values):
@@ -302,8 +316,8 @@
 
 def mid_fwd_kernel(
     len_ref, x0_ref, x1_ref, ctx0_ref, ctx1_ref, full_ref, wu_ref, vec_ref,
-    out0_ref, out1_ref, n1_ref, n2_ref, inv_ref, slope_ref, act_ref, stat_ref,
-    out0_s, out1_s, wd_s, stat_s,
+    out_ref, n1_ref, n2_ref, inv_ref, slope_ref, act_ref, stat_ref,
+    out_s, wd_s, stat_s,
 ):
     step = pl.program_id(0)
     first_len = len_ref[0]
@@ -350,14 +364,11 @@
     n2_ref[...] = n2
     lane = lax.broadcasted_iota(jnp.int32, (TILE, 128), 1)
     inv_ref[...] = jnp.where(lane < 64, inv1, inv2)
-    result = (n2 * gain2 + shift2).astype(bf16)
-    out0_s[rows, :] = result[:, :HALF]
-    out1_s[rows, :] = result[:, HALF:]
+    out_s[rows, :] = (n2 * gain2 + shift2).astype(bf16)
 
     @pl.when(step == pl.num_programs(0) - 1)
     def _():
-        unmerge_rows(out0_s, out0_ref, first_len)
-        unmerge_rows(out1_s, out1_ref, first_len)
+        unmerge_rows(out_s, out_ref, first_len)
         stat_ref[...] = jnp.broadcast_to(
             jnp.sum(stat_s[...], axis=1, keepdims=True), stat_ref.shape
         )
@@ -365,8 +376,8 @@
 
 def mid_bwd_kernel(
     len_ref, cot_ref, ctx0_ref, ctx1_ref, n1_ref, n2_ref, inv_ref, slope_ref, act_ref,
-    full_ref, wu_ref, vec_ref, gctx_ref, base_ref, grad_ref,
-    cot_s, wd_s, dwo_s, dwd_s, dwu_s, vec_s, turn_s,
+    full_ref, wu_ref, vec_ref, gctx_ref, base_ref, kept_ref, given_ref,
+    cot_s, wd_s, dwo_s, dwd_s, dwu_s, vec_s, turn_s, grad_ref,
 ):
     step = pl.program_id(0)
 
@@ -430,6 +441,7 @@
                         bf16
                     )
         grad_ref[:, 2 * D + 4 * WIN :] = jnp.transpose(vec_s[...]).astype(bf16)
+        split_chunks(grad_ref, kept_ref, given_ref, len_ref[1])
 
 
 def whole(shape):
@@ -449,11 +461,6 @@
 PARAMS = pltpu.CompilerParams(
     dimension_semantics=("arbitrary",), vmem_limit_bytes=63_000_000
 )
-SMALL = pltpu.CompilerParams(
-    dimension_semantics=("arbitrary",), vmem_limit_bytes=24_000_000
-)
-
-
 GRAD_COLS = 2 * D + 4 * WIN + 128
 
 
@@ -486,7 +493,8 @@
     )(len_arr, tok, full)
 
 
-def attn_bwd(len_arr, qa, ka, va, ctx, gctx, x, base, full, half):
+def attn_bwd(len_arr, qa, ka, va, ctx, gctx, x, base, full, half, chunks):
+    part = (chunks // 4, D // chunks, D)
     pair_cols = lambda width, first: pl.BlockSpec((ROWS, width), lambda i, *_: (0, i + first))
     return pl.pallas_call(
         attn_bwd_kernel,
@@ -500,7 +508,7 @@
                 pl.BlockSpec((ROWS, HALF), lambda i, *_: (0, half), pipeline_mode=pl.Buffered(1)),
                 pl.BlockSpec((HALF, D), lambda i, *_: (half, 2), pipeline_mode=pl.Buffered(1)),
             ],
-            out_specs=[kept((SEQ // BLOCK, 2, BLOCK, HALF)), kept((HALF, D))],
+            out_specs=[kept((SEQ // BLOCK, 2, BLOCK, HALF)), kept(part), kept(part)],
             scratch_shapes=[
                 pltpu.VMEM((ROWS, HALF), bf16),
                 pltpu.VMEM((ROWS, HALF), bf16),
@@ -509,12 +517,15 @@
                 pltpu.VMEM((128, ROWS), f32),
                 pltpu.VMEM((ROWS, HALF), bf16),
                 pltpu.VMEM((WIN, WIN), bf16),
+                pltpu.VMEM((HALF, D), bf16),
             ],
         ),
-        out_shape=[struct((SEQ // BLOCK, 2, BLOCK, HALF), bf16), struct((HALF, D), bf16)],
+        out_shape=[
+            struct((SEQ // BLOCK, 2, BLOCK, HALF), bf16), struct(part, bf16), struct(part, bf16),
+        ],
         compiler_params=PARAMS,
         cost_estimate=pl.CostEstimate(
-            flops=30_000_000_000, bytes_accessed=16_000_000, transcendentals=7_000_000
+            flops=100_000_000, bytes_accessed=1_000_000, transcendentals=0
         ),
     )(len_arr, qa, ka, va, ctx, gctx, x, base, full)
 
@@ -525,9 +536,8 @@
 
 def mid_fwd(len_arr, x0, x1, ctx0, ctx1, full, wu, vecs):
     outs = [
-        ((SEQ // BLOCK, 2, BLOCK, HALF), bf16), ((SEQ // BLOCK, 2, BLOCK, HALF), bf16),
-        ((ROWS, D), f32), ((ROWS, D), f32), ((ROWS, 128), f32), ((ROWS, FF), f32),
-        ((ROWS, FF), bf16), ((8, 128), f32),
+        ((SEQ // BLOCK, 2, BLOCK, D), bf16), ((ROWS, D), f32), ((ROWS, D), f32),
+        ((ROWS, 128), f32), ((ROWS, FF), f32), ((ROWS, FF), bf16), ((8, 128), f32),
     ]
     return pl.pallas_call(
         mid_fwd_kernel,
@@ -538,12 +548,11 @@
             in_specs=[row_tile(HALF)] * 4
             + [whole((D, 2 * D)), whole(wu.shape), whole(vecs.shape)],
             out_specs=[
-                kept(outs[0][0]), kept(outs[0][0]), row_tile(D), row_tile(D), row_tile(128),
-                row_tile(FF), row_tile(FF), kept((8, 128)),
+                kept(outs[0][0]), row_tile(D), row_tile(D), row_tile(128), row_tile(FF),
+                row_tile(FF), kept((8, 128)),
             ],
             scratch_shapes=[
-                pltpu.VMEM((ROWS, HALF), bf16),
-                pltpu.VMEM((ROWS, HALF), bf16),
+                pltpu.VMEM((ROWS, D), bf16),
                 pltpu.VMEM((4, WIN, D), bf16),
                 pltpu.VMEM((8, D), f32),
             ],
@@ -556,8 +565,9 @@
     )(len_arr, x0, x1, ctx0, ctx1, full, wu, vecs)
 
 
-def mid_bwd(len_arr, cot, ctx0, ctx1, n1, n2, inv, slope, act, full, wu, vecs):
-    outs = [((ROWS, D), bf16), ((ROWS, D), f32), ((D, GRAD_COLS), bf16)]
+def mid_bwd(len_arr, cot, ctx0, ctx1, n1, n2, inv, slope, act, full, wu, vecs, chunks):
+    part = (chunks // 2, D // chunks, GRAD_COLS)
+    outs = [((ROWS, D), bf16), ((ROWS, D), f32), (part, bf16), (part, bf16)]
     return pl.pallas_call(
         mid_bwd_kernel,
         name="mid_bwd",
@@ -572,7 +582,8 @@
             out_specs=[
                 row_tile(D),
                 row_tile(D),
-                pl.BlockSpec((D, GRAD_COLS), lambda i, *_: (0, 0), pipeline_mode=pl.Buffered(1)),
+                whole(part),
+                whole(part),
             ],
             scratch_shapes=[
                 pltpu.VMEM((ROWS, D), bf16),
@@ -582,25 +593,32 @@
                 pltpu.VMEM((4, WIN, D), f32),
                 pltpu.VMEM((128, D), f32),
                 pltpu.VMEM((D, 128), f32),
+                pltpu.VMEM((D, GRAD_COLS), bf16),
             ],
         ),
         out_shape=[struct(*o) for o in outs],
         compiler_params=PARAMS,
         cost_estimate=pl.CostEstimate(
-            flops=30_000_000_000, bytes_accessed=50_000_000, transcendentals=10_000
+            flops=100_000_000, bytes_accessed=1_000_000, transcendentals=0
         ),
     )(len_arr, cot, ctx0, ctx1, n1, n2, inv, slope, act, full, wu, vecs)
 
 
-def pack_kernel(
-    odd_ref, bias_ref, o_ref, down_ref, q_ref, k_ref, v_ref, up_ref, out_ref, low_s, high_s
-):
+def column_of(row_ref):
+    count = row_ref.shape[1]
+    row = lax.broadcasted_iota(jnp.int32, (count, count), 0)
+    col = lax.broadcasted_iota(jnp.int32, (count, count), 1)
+    values = jnp.broadcast_to(row_ref[...].astype(f32), (count, count))
+    return jnp.sum(jnp.where(row == col, values, 0.0), axis=1, keepdims=True)
+
+
+def pack_kernel(odd_ref, *refs):
+    bias_refs, (up_bias_ref, o_ref, down_ref, q_ref, k_ref, v_ref, up_ref, out_ref) = (
+        refs[:8], refs[8:16],
+    )
+    low_s, high_s = refs[16:]
     rows = o_ref.shape[0]
     odd = odd_ref[0]
-    eye = lax.broadcasted_iota(jnp.int32, (rows, rows), 0) == lax.broadcasted_iota(
-        jnp.int32, (rows, rows), 1
-    )
-    columns = mm(jnp.where(eye, 1.0, 0.0).astype(bf16), bias_ref[...], NT)
     shift = lax.broadcasted_iota(jnp.int32, (192, WIN), 1) - lax.broadcasted_iota(
         jnp.int32, (192, WIN), 0
     )
@@ -611,30 +629,32 @@
         moved = mm(weight, move, NN)
         return jnp.where(lane == 192 * (1 - odd), column, moved)
 
+    columns = [column_of(ref) for ref in bias_refs]
     out_ref[:, :D] = o_ref[...]
     out_ref[:, D : 2 * D] = down_ref[...]
-    zero = jnp.zeros((rows, 1), f32)
-    sources = ((q_ref, columns[:, 6:7]), (k_ref, zero), (v_ref, columns[:, 7:8]))
+    sources = ((q_ref, columns[6]), (k_ref, jnp.zeros((rows, 1), f32)), (v_ref, columns[7]))
     for which, (ref, column) in enumerate(sources):
         start = 2 * D + WIN * which
         out_ref[:, start : start + WIN] = padded(ref[...], column).astype(bf16)
-    column = jnp.concatenate([columns[:, 8 + i : 9 + i] for i in range(4)], axis=0)
-    up = padded(up_ref[...], column)
+    up = padded(up_ref[...], column_of(up_bias_ref))
     low_s[...] = up[:, :128]
     high_s[...] = up[:, 128:]
     for j in range(4):
         for half, source in enumerate((low_s, high_s)):
             start = 3 * D + WIN * j + 128 * half
             out_ref[:, start : start + 128] = source[pl.ds(j, rows, stride=4), :].astype(bf16)
-    out_ref[:, 3 * D + 4 * WIN :] = columns.astype(bf16)
+    lane = lax.broadcasted_iota(jnp.int32, (rows, 128), 1)
+    small = jnp.zeros((rows, 128), f32)
+    for index, column in enumerate(columns[:6]):
+        small = jnp.where(lane == index, column, small)
+    out_ref[:, 3 * D + 4 * WIN :] = small.astype(bf16)
 
 
 def pack(odd, biases, up_bias, o_weight, down_weight, in_weights, up_weight):
     rows = o_weight.shape[0]
-    flat = jnp.concatenate(biases + [up_bias]).reshape(-1, rows)
-    flat = jnp.pad(flat, ((0, 128 - flat.shape[0]), (0, 0)))
     cols = 3 * D + 4 * WIN + 128
-    arrays = [flat, o_weight, down_weight, *in_weights, up_weight]
+    arrays = [bias[None, :] for bias in (*biases, up_bias)]
+    arrays += [o_weight, down_weight, *in_weights, up_weight]
     return pl.pallas_call(
         pack_kernel,
         name="pack",
@@ -646,7 +666,7 @@
             scratch_shapes=[pltpu.VMEM((4 * rows, 128), f32)] * 2,
         ),
         out_shape=[struct((rows, cols), bf16)],
-        compiler_params=SMALL,
+        compiler_params=PARAMS,
         cost_estimate=pl.CostEstimate(flops=0, bytes_accessed=400_000, transcendentals=0),
     )(odd.astype(jnp.int32).reshape(1), *arrays)[0]
 
@@ -687,15 +707,15 @@
             out_specs=[pl.BlockSpec((count, size, width // parts), lambda i, *_: (i, 0, 0))] * parts,
         ),
         out_shape=[struct((total, size, width // parts), rows.dtype)] * parts,
-        compiler_params=SMALL,
+        compiler_params=PARAMS,
         cost_estimate=pl.CostEstimate(flops=0, bytes_accessed=8_000_000, transcendentals=0),
     )(lengths, permutation, rows)
 
 
-def restore_kernel(len_ref, perm_ref, first_ref, second_ref, out_ref, place_s):
+def restore_kernel(len_ref, perm_ref, *refs):
+    part_refs, out_ref, place_s = refs[:-2], refs[-2], refs[-1]
     count = out_ref.shape[0]
     start = pl.program_id(0) * count
-    width = first_ref.shape[2]
 
     @pl.when(pl.program_id(0) == 0)
     def _():
@@ -703,19 +723,23 @@
             place_s[source_of(len_ref, perm_ref, index)] = index
             return carry
 
-        lax.fori_loop(0, first_ref.shape[0], note, 0)
+        lax.fori_loop(0, part_refs[0].shape[0], note, 0)
 
     def one(index, carry):
         place = place_s[start + index]
-        out_ref[index, :, :width] = first_ref[place]
-        out_ref[index, :, width:] = second_ref[place]
+        lane = 0
+        for ref in part_refs:
+            width = ref.shape[2]
+            out_ref[index, :, lane : lane + width] = ref[place]
+            lane += width
         return carry
 
     lax.fori_loop(0, count, one, 0)
 
 
-def restore(first, second, lengths, permutation):
-    total, size, width = first.shape
+def restore(parts, lengths, permutation):
+    total, size, _ = parts[0].shape
+    width = sum(part.shape[2] for part in parts)
     count = total // STEPS
     return pl.pallas_call(
         restore_kernel,
@@ -723,14 +747,14 @@
         grid_spec=pltpu.PrefetchScalarGridSpec(
             num_scalar_prefetch=2,
             grid=(STEPS,),
-            in_specs=[whole(first.shape), whole(second.shape)],
-            out_specs=[pl.BlockSpec((count, size, 2 * width), lambda i, *_: (i, 0, 0))],
+            in_specs=[whole(part.shape) for part in parts],
+            out_specs=[pl.BlockSpec((count, size, width), lambda i, *_: (i, 0, 0))],
             scratch_shapes=[pltpu.SMEM((total,), jnp.int32)],
         ),
-        out_shape=[struct((total, size, 2 * width), first.dtype)],
-        compiler_params=SMALL,
+        out_shape=[struct((total, size, width), bf16)],
+        compiler_params=PARAMS,
         cost_estimate=pl.CostEstimate(flops=0, bytes_accessed=8_000_000, transcendentals=0),
-    )(lengths, permutation, first, second)[0]
+    )(lengths, permutation, *parts)[0]
 
 
 def pick(values, index):
@@ -783,12 +807,17 @@
             ],
             axis=1,
         )
-    full = lax.all_gather(packed, AXES, axis=0, tiled=True)
+    gathered = lax.all_gather(packed, "fsdp", axis=0, tiled=True)
 
     dealt_lengths = pick(lengths, permutation).reshape(devices, seq_dev)
     swap = dealt_lengths[:, 0] < dealt_lengths[:, 1]
     my_swap = lax.dynamic_index_in_dim(swap, my_index, 0, False)
-    len_arr = jnp.max(lax.dynamic_slice_in_dim(dealt_lengths, my_index, 1, 0)).reshape(1)
+    chunks = lax.axis_size("dp")
+    parity = lax.axis_index("dp") % 2
+    pairing = [(i, i ^ 1) for i in range(chunks)]
+    len_arr = jnp.stack(
+        [jnp.max(lax.dynamic_slice_in_dim(dealt_lengths, my_index, 1, 0)), parity]
+    ).astype(jnp.int32)
 
     def swap_blocks(rows):
         return lax.all_to_all(rows, AXES, split_axis=0, concat_axis=0, tiled=True)
@@ -838,6 +867,8 @@
 
     tok0, tok1 = deal(tokens, lengths, permutation, 2)
     tok0 = arrive(tok0)
+    gathered, tok0 = tie(gathered, tok0)
+    full = lax.all_gather(gathered, "dp", axis=0, tiled=True)
     tok1 = arrive(tok1)
     dealt_cot, tok0, tok1 = tie(deal(cotangent, lengths, permutation, 1)[0], tok0, tok1)
     cot = arrive(dealt_cot)
@@ -846,31 +877,38 @@
     x1, qa1, ka1, va1, ctx1 = attn_fwd(len_arr, tok1, full, 1)
     wu = full[:, 3 * D : 3 * D + 4 * WIN].reshape(FF, WIN)
     vecs = jnp.pad(full[:, 3 * D + 4 * WIN : 3 * D + 4 * WIN + 6].astype(f32).T, ((0, 2), (0, 0)))
-    out0, out1, n1, n2, inv, slope, act, stat = mid_fwd(
-        len_arr, x0, x1, ctx0, ctx1, full, wu, vecs
+    out, n1, n2, inv, slope, act, stat = mid_fwd(len_arr, x0, x1, ctx0, ctx1, full, wu, vecs)
+    cot, out = tie(cot, out)
+    back_out = leave(out)
+    gctx, base, mine, given = mid_bwd(
+        len_arr, cot, ctx0, ctx1, n1, n2, inv, slope, act, full, wu, vecs, chunks
     )
-    cot, out0, out1 = tie(cot, out0, out1)
-    back_out0 = leave(out0)
-    gctx, base, grads = mid_bwd(
-        len_arr, cot, ctx0, ctx1, n1, n2, inv, slope, act, full, wu, vecs
+    mine = total_low([mine, lax.ppermute(given, "dp", pairing)])
+    gctx, mine = tie(gctx, mine)
+    parts = send_rest(mine, "dp")
+    ig0, dw0, given0 = attn_bwd(
+        len_arr, qa0, ka0, va0, ctx0, gctx, x0, base, full, 0, chunks
     )
-    gctx, out1, back_out0 = tie(gctx, out1, back_out0)
-    back_out1 = leave(out1)
-    parts = send_pair(grads, "dp")
-    ig0, dw0 = attn_bwd(len_arr, qa0, ka0, va0, ctx0, gctx, x0, base, full, 0)
-    ig0, dw0, gctx, back_out1, *parts = tie(ig0, dw0, gctx, back_out1, *parts)
+    ig0, dw0, given0, gctx, back_out, *parts = tie(ig0, dw0, given0, gctx, back_out, *parts)
     back0 = leave(ig0)
-    parts = send_rest(total_low(parts), "dp")
-    ig1, dw1 = attn_bwd(len_arr, qa1, ka1, va1, ctx1, gctx, x1, base, full, 1)
-    ig1, dw1, back0, *parts = tie(ig1, dw1, back0, *parts)
+    given0 = lax.ppermute(given0, "dp", pairing)
+    parts = send_pair(total_low(parts), "fsdp")
+    ig1, dw1, given1 = attn_bwd(
+        len_arr, qa1, ka1, va1, ctx1, gctx, x1, base, full, 1, chunks
+    )
+    ig1, dw0, dw1, given0, given1, back0, *parts = tie(
+        ig1, dw0, dw1, given0, given1, back0, *parts
+    )
     back1 = leave(ig1)
-    mine = total(send_rest(total_low(send_pair(total_low(parts), "fsdp")), "fsdp"))
-    parts = send_rest(total_low(send_pair(jnp.concatenate([dw0, dw1], axis=0), "dp")), "dp")
-    mine_in = total(send_rest(total_low(send_pair(total_low(parts), "fsdp")), "fsdp"))
-
-    back_out0, back_out1, mine = tie(back_out0, back_out1, mine)
-    output = restore(back_out0, back_out1, lengths, permutation)
-    input_grad = restore(back0, back1, lengths, permutation)
+    mine = total(send_rest(total_low(parts), "fsdp"))
+    given1 = lax.ppermute(given1, "dp", pairing)
+    mine_in = jnp.concatenate([total_low([dw0, given0]), total_low([dw1, given1])], axis=0)
+    parts = send_pair(total_low(send_rest(mine_in, "dp")), "fsdp")
+    mine_in = total(send_rest(total_low(parts), "fsdp"))
+
+    back_out, stat, mine = tie(back_out, stat, mine)
+    output = restore([back_out], lengths, permutation)
+    input_grad = restore([back0, back1], lengths, permutation)
     lens = jnp.stack([len_arr[0], ROWS - len_arr[0]]).astype(f32)
     sums = jnp.stack([stat[4:8, 0], stat[0:4, 0] - stat[4:8, 0]], axis=1)
     rms = jnp.sqrt(sums / (lens[None, :] * D) + rms_eps)

time: 440 us -> 438 us (level)
  waiting for transfers between devices: 84.1 us -> 159 us
  blocking collectives: 56.4 us -> 0 us
  local copies, waits for them, and re-layouts: 35.7 us -> 13.4 us
  Pallas kernels: 187 us -> 194 us
    all_gather x1 -> x2, waiting for transfers between devices: 0.02 us -> 69.5 us  [the longest x1 52.7 us: on_device(): gathered = lax.all_gather(packed, 'fsdp', axis=0, tiled=True)]
    all_to_all x1 -> x0, blocking collectives: 56.4 us -> none  [swap_blocks(): return lax.all_to_all(rows, AXES, split_axis=0, concat_axis=0, tiled=True)]
    ppermute x8, waiting for transfers between devices: 34.3 us -> 49.4 us  [send_rest(): parts.append(lax.ppermute(block_of((place + shift) % half), axis, target))]
    all_to_all x6, waiting for transfers between devices: 44.9 us -> 33.1 us  [swap_blocks(): return lax.all_to_all(rows, AXES, split_axis=0, concat_axis=0, tiled=True)]
    unnamed x37 -> x20, local copies, waits for them, and re-layouts: 11.1 us -> 4.23 us
    dynamic_slice x4 -> x1, local copies, waits for them, and re-layouts: 6.19 us -> 0.02 us  [send_pair(): lax.dynamic_slice_in_dim(blocks, which, 1, 1)]
    concatenate x1 -> x0, local copies, waits for them, and re-layouts: 6.1 us -> none  [pack(): flat = jnp.concatenate(biases + [up_bias]).reshape(-1, rows)]
    pallas_call x2, Pallas kernels: 5.38 us -> 11 us  [deal(): pl.pallas_call(deal_kernel, name='deal', grid_spec=pltpu.PrefetchScalarGr...]
  transfers between devices with their start and end apart: 19 -> 21, of which waited for: 9 -> 8; matrix products, arithmetic and copies ran while one was open for 7% -> 5% of each run, Pallas kernels for 41% -> 42%
where the time goes in v5:
time: 438 us; the launch traced here: 437 us
  Pallas kernels  194 us (44%)
  waiting for transfers between devices  159 us (36%)
  starting transfers between devices  41.8 us (10%)
  between operations  15.2 us (3%)
  other arithmetic  13.8 us (3%)
  local copies, waits for them, and re-layouts  13.4 us (3%)
    pallas_call x2, Pallas kernels, attn_bwd(): pl.pallas_call(attn_bwd_kernel, name='attn_bwd', grid_spec=pltpu.Prefetch...  68 us
    all_gather x1, waiting for transfers between devices, on_device(): gathered = lax.all_gather(packed, 'fsdp', axis=0, tiled=True)  52.7 us
    pallas_call x2, Pallas kernels, attn_fwd(): pl.pallas_call(attn_fwd_kernel, name='attn_fwd', grid_spec=pltpu.Prefetch...  51 us
    ppermute x8, waiting for transfers between devices, send_rest(): parts.append(lax.ppermute(block_of((place + shift) % half), axis, target))  49.4 us
    all_to_all x6, waiting for transfers between devices, swap_blocks(): return lax.all_to_all(rows, AXES, split_axis=0, concat_axis=0, tiled=True)  33.1 us
    pallas_call x1, Pallas kernels, mid_bwd(): pl.pallas_call(mid_bwd_kernel, name='mid_bwd', grid_spec=pltpu.PrefetchSc...  32.7 us
    all_to_all x6, starting transfers between devices, swap_blocks(): return lax.all_to_all(rows, AXES, split_axis=0, concat_axis=0, tiled=True)  26.6 us
    pallas_call x1, Pallas kernels, mid_fwd(): pl.pallas_call(mid_fwd_kernel, name='mid_fwd', grid_spec=pltpu.PrefetchSc...  20 us
  transfers between devices with their start and end apart: 21, of which 8 were waited for; matrix products, arithmetic and copies ran while one was open for 5% of the time, Pallas kernels for 42%

profile of v5, /device:TPU:0, one launch (start us, length us, event | category | flops | bytes accessed | tf_op | source)
XLA Modules:
  0.0 437.3 jit_solution(11237929987941332364)
XLA Ops:
  7.2 5.4 %deal.3 = (bf16[64,32,384]{2,1,0:T(8,128)(2,1)}, bf16[64,32,384]{2,1,0:T(8,128)(2,1)}) custom-call(s32[64]{0:T(128)} %len_ref.7, s32[64]{0:T(128)} %perm_ref.7, bf16[64,32,768]{2,1,0:T(8,128)(2,1)} %rows_ref.3), custom_call_target="tpu_custom_call" | custom-call | bytes 8000000 | tf_op jit(solution)/shard_map/deal/pallas_call | solution.py:700
  12.6 7.3 %all-to-all-start = ((bf16[32,2,32,384]{3,2,1,0:T(8,128)(2,1)}), bf16[32,2,32,384]{3,2,1,0:T(8,128)(2,1)S(1)}, u32[]{:S(2)}, u32[]{:S(2)}) async-start(bf16[32,2,32,384]{3,2,1,0:T(8,128)(2,1)} %bitcast.42), calls=%async_computation | async-start | bytes 3145728 | tf_op jit(solution)/shard_map/all_to_all | solution.py:823
  20.0 1.9 pack.1
  22.0 52.7 %all-gather.3.cloned.1.call-done = bf16[192,3456]{1,0:T(8,128)(2,1)} async-done(((bf16[24,3456]{1,0:T(8,128)(2,1)}), bf16[192,3456]{1,0:T(8,128)(2,1)}) %all-gather.3.cloned.1.call-update) | async-done | bytes 1327120 | tf_op jit(solution)/shard_map/all_gather | solution.py:810
  75.8 2.8 all-to-all-start.1
  78.6 5.6 %deal.2 = bf16[64,32,768]{2,1,0:T(8,128)(2,1)} custom-call(s32[64]{0:T(128)} %len_ref.7, s32[64]{0:T(128)} %perm_ref.7, bf16[64,32,768]{2,1,0:T(8,128)(2,1)} %rows_ref.2), custom_call_target="tpu_custom_call" | custom-call | bytes 8000000 | tf_op jit(solution)/shard_map/deal/pallas_call | solution.py:700
  84.2 33.1 %all-to-all-done.1.tok_ref = bf16[32,2,32,384]{3,2,1,0:T(8,128)(2,1)S(1)} async-done(((bf16[32,2,32,384]{3,2,1,0:T(8,128)(2,1)}), bf16[32,2,32,384]{3,2,1,0:T(8,128)(2,1)S(1)}, u32[]{:S(2)}, u32[]{:S(2)}) %all-to-all-start.1) | async-done | bytes 1572896 | tf_op jit(solution)/shard_map/all_to_all | solution.py:823
  118.5 3.7 all-to-all-start.2
  125.0 16.8 %all-gather.5.cloned.1.call-done.full_ref = bf16[768,3456]{1,0:T(8,128)(2,1)} async-done(((bf16[192,3456]{1,0:T(8,128)(2,1)}), bf16[768,3456]{1,0:T(8,128)(2,1)}) %all-gather.5.cloned.1.call-update) | async-done | bytes 5308432 | tf_op jit(solution)/shard_map/all_gather | solution.py:871
  144.1 2.2 reshape.118.wu_ref
  146.4 25.5 %attn_fwd.3 = (bf16[1088,384]{1,0:T(8,128)(2,1)}, bf16[1088,768]{1,0:T(8,128)(2,1)}, bf16[1088,768]{1,0:T(8,128)(2,1)}, bf16[1088,768]{1,0:T(8,128)(2,1)}, bf16[1088,384]{1,0:T(8,128)(2,1)}) custom-call(s32[2]{0:T(128)} %pad_add_fusion.len_ref, bf16[32,2,32,384]{3,2,1,0:T(8,128)(2,1)} %copy-done.4, bf16[768,3456]{1,0:T(8,128)(2,1)} %all-gather.5.cloned.1.call-done.full_ref), custom_call_target="tpu_custom_call" | custom-call | flops 20000000000 | bytes 12000000 | tf_op jit(solution)/shard_map/attn_fwd/pallas_call | solution.py:469
  171.8 25.5 %attn_fwd.2 = (bf16[1088,384]{1,0:T(8,128)(2,1)}, bf16[1088,768]{1,0:T(8,128)(2,1)}, bf16[1088,768]{1,0:T(8,128)(2,1)}, bf16[1088,768]{1,0:T(8,128)(2,1)}, bf16[1088,384]{1,0:T(8,128)(2,1)}) custom-call(s32[2]{0:T(128)} %pad_add_fusion.len_ref, bf16[32,2,32,384]{3,2,1,0:T(8,128)(2,1)} %copy-done.3, bf16[768,3456]{1,0:T(8,128)(2,1)} %all-gather.5.cloned.1.call-done.full_ref), custom_call_target="tpu_custom_call" | custom-call | flops 20000000000 | bytes 12000000 | tf_op jit(solution)/shard_map/attn_fwd/pallas_call | solution.py:469
  197.3 20.0 %mid_fwd.1 = (bf16[32,2,32,768]{3,2,1,0:T(8,128)(2,1)}, f32[1088,768]{1,0:T(8,128)}, f32[1088,768]{1,0:T(8,128)}, f32[1088,128]{1,0:T(8,128)}, f32[1088,3072]{1,...) custom-call(s32[2]{0:T(128)} %pad_add_fusion.len_ref, bf16[1088,384]{1,0:T(8,128)(2,1)} %get-tuple-element.84.x0_ref.x_ref, ...), custom_call_target="tpu_custom_call" | custom-call | flops 15000000512 | bytes 36000000 | tf_op jit(solution)/shard_map/mid_fwd/pallas_call | solution.py:542
  217.4 3.0 all-to-all-start.3
  220.3 32.7 %mid_bwd.1 = (bf16[1088,768]{1,0:T(8,128)(2,1)}, f32[1088,768]{1,0:T(8,128)}, bf16[2,192,2688]{2,1,0:T(8,128)(2,1)}, bf16[2,192,2688]{2,1,0:T(8,128)(2,1)}) custom-call(s32[2]{0:T(128)} %pad_add_fusion.len_ref, bf16[32,2,32,768]{3,2,1,0:T(8,128)(2,1)} %all-to-all-done.2.cot_ref, bf16[1088,384]{1,0:T(8,128)(2,1)} %get-tuple-element.82.ctx0_ref.ctx_ref, ...), custom_call_target="tpu_custom_call" | custom-call | flops 100000000 | bytes 1000000 | tf_op jit(solution)/shard_map/mid_bwd/pallas_call | solution.py:571
  253.2 4.4 %collective-permute-done = bf16[2,192,2688]{2,1,0:T(8,128)(2,1)} collective-permute-done((bf16[2,192,2688]{2,1,0:T(8,128)(2,1)}, bf16[2,192,2688]{2,1,0:T(8,128)(2,1)}, u32[]{:S(2)}, u32[]{:S(2)}) %collective-permute-start) | collective-permute-done | bytes 2064416 | tf_op jit(solution)/shard_map/ppermute | solution.py:886
  257.6 2.7 add_convert_fusion
  263.2 34.1 %attn_bwd.2 = (bf16[32,2,32,384]{3,2,1,0:T(8,128)(2,1)}, bf16[1,192,768]{2,1,0:T(8,128)(2,1)}, bf16[1,192,768]{2,1,0:T(8,128)(2,1)}) custom-call(s32[2]{0:T(128)} %pad_add_fusion.len_ref, bf16[1088,768]{1,0:T(8,128)(2,1)} %get-tuple-element.79.qa_ref, bf16[1088,768]{1,0:T(8,128)(2,1)} %get-tuple-element.80.ka_ref, ...), custom_call_target="tpu_custom_call" | custom-call | flops 100000000 | bytes 1000000 | tf_op jit(solution)/shard_map/attn_bwd/pallas_call | solution.py:499
  297.3 4.9 %all-to-all-start.4 = ((bf16[32,2,32,384]{3,2,1,0:T(8,128)(2,1)}), bf16[32,2,32,384]{3,2,1,0:T(8,128)(2,1)}, u32[]{:S(2)}, u32[]{:S(2)}) async-start(bf16[32,2,32,384]{3,2,1,0:T(8,128)(2,1)} %get-tuple-element.116), calls=%async_computation.4 | async-start | bytes 3145728 | tf_op jit(solution)/shard_map/all_to_all | solution.py:823
  302.2 1.8 add_convert_fusion.1
  304.1 1.8 collective-permute-start.3
  309.1 33.9 %attn_bwd.3 = (bf16[32,2,32,384]{3,2,1,0:T(8,128)(2,1)}, bf16[1,192,768]{2,1,0:T(8,128)(2,1)}, bf16[1,192,768]{2,1,0:T(8,128)(2,1)}) custom-call(s32[2]{0:T(128)} %pad_add_fusion.len_ref, bf16[1088,768]{1,0:T(8,128)(2,1)} %get-tuple-element.107.qa_ref, bf16[1088,768]{1,0:T(8,128)(2,1)} %get-tuple-element.108.ka_ref, ...), custom_call_target="tpu_custom_call" | custom-call | flops 100000000 | bytes 1000000 | tf_op jit(solution)/shard_map/attn_bwd/pallas_call | solution.py:499
  343.1 5.0 %all-to-all-start.5 = ((bf16[32,2,32,384]{3,2,1,0:T(8,128)(2,1)}), bf16[32,2,32,384]{3,2,1,0:T(8,128)(2,1)S(1)}, u32[]{:S(2)}, u32[]{:S(2)}) async-start(bf16[32,2,32,384]{3,2,1,0:T(8,128)(2,1)} %get-tuple-element.123), calls=%async_computation.5 | async-start | bytes 3145728 | tf_op jit(solution)/shard_map/all_to_all | solution.py:823
  348.4 1.7 collective-permute-start.4
  350.0 2.2 collective-permute-start.6
  353.0 28.1 %collective-permute-done.4 = bf16[24,2688]{1,0:T(8,128)(2,1)S(1)} collective-permute-done((bf16[24,2688]{1,0:T(8,128)(2,1)S(1)}, bf16[24,2688]{1,0:T(8,128)(2,1)S(1)}, u32[]{:S(2)}, u32[]{:S(2)}) %collective-permute-start.4) | collective-permute-done | bytes 129056 | tf_op jit(solution)/shard_map/ppermute | solution.py:858
  381.2 15.2 %collective-permute-done.5 = bf16[24,2688]{1,0:T(8,128)(2,1)S(1)} collective-permute-done((bf16[24,2688]{1,0:T(8,128)(2,1)S(1)}, bf16[24,2688]{1,0:T(8,128)(2,1)S(1)}, u32[]{:S(2)}, u32[]{:S(2)}) %collective-permute-start.5) | collective-permute-done | bytes 129056 | tf_op jit(solution)/shard_map/ppermute | solution.py:858
  400.9 6.1 %collective-permute-done.8 = bf16[192,768]{1,0:T(8,128)(2,1)S(1)} collective-permute-done((bf16[192,768]{1,0:T(8,128)(2,1)S(1)}, bf16[192,768]{1,0:T(8,128)(2,1)S(1)}, u32[]{:S(2)}, u32[]{:S(2)}) %collective-permute-start.8) | collective-permute-done | bytes 294944 | tf_op jit(solution)/shard_map/ppermute | solution.py:858
  410.3 2.3 collective-permute-done.9
  412.7 3.8 collective-permute-start.12
  417.3 4.8 %restore.2 = bf16[64,32,768]{2,1,0:T(8,128)(2,1)} custom-call(s32[64]{0:T(128)} %len_ref.7, s32[64]{0:T(128)} %perm_ref.7, bf16[64,32,768]{2,1,0:T(8,128)(2,1)} %bitcast.35), custom_call_target="tpu_custom_call" | custom-call | bytes 8000000 | tf_op jit(solution)/shard_map/restore/pallas_call | solution.py:744
  425.5 5.0 %restore.3 = bf16[64,32,768]{2,1,0:T(8,128)(2,1)} custom-call(s32[64]{0:T(128)} %len_ref.7, s32[64]{0:T(128)} %perm_ref.7, bf16[64,32,384]{2,1,0:T(8,128)(2,1)} %bitcast.18.refs_0_, bf16[64,32,384]{2,1,0:T(8,128)(2,1)} %bitcast.38), custom_call_target="tpu_custom_call" | custom-call | bytes 8000000 | tf_op jit(solution)/shard_map/restore/pallas_call | solution.py:744
  (85 shorter events, 26.2 us)
Async XLA Ops:
  12.6 62.1 %all-to-all-start = ((bf16[32,2,32,384]{3,2,1,0:T(8,128)(2,1)}), bf16[32,2,32,384]{3,2,1,0:T(8,128)(2,1)S(1)}, u32[]{:S(2)}, u32[]{:S(2)}) async-start(bf16[32,2,32,384]{3,2,1,0:T(8,128)(2,1)} %bitcast.42), calls=%async_computation | async-start | bytes 3145728 | tf_op jit(solution)/shard_map/all_to_all | solution.py:823
  19.9 54.7 %all-gather.3.cloned.1.call-start = ((), (), s32[]{:S(2)}) async-start(), calls=%async_computation.6 | async-start | bytes 1492992 | tf_op jit(solution)/shard_map/all_gather | solution.py:810
  21.9 119.8 %all-gather.5.cloned.1.call-start = ((), (), s32[]{:S(2)}) async-start(), calls=%async_computation.7 | async-start | bytes 6635520 | tf_op jit(solution)/shard_map/all_gather | solution.py:871
  74.7 1.1 copy-start.3
  75.8 41.5 %all-to-all-start.1 = ((bf16[32,2,32,384]{3,2,1,0:T(8,128)(2,1)}), bf16[32,2,32,384]{3,2,1,0:T(8,128)(2,1)S(1)}, u32[]{:S(2)}, u32[]{:S(2)}) async-start(bf16[32,2,32,384]{3,2,1,0:T(8,128)(2,1)} %bitcast.13), calls=%async_computation.1 | async-start | bytes 3145728 | tf_op jit(solution)/shard_map/all_to_all | solution.py:823
  117.3 1.2 copy-start.4
  118.5 3.7 copy-start.7
  118.5 3.7 copy-start
  118.5 98.9 %all-to-all-start.2 = ((bf16[32,2,32,768]{3,2,1,0:T(8,128)(2,1)}), bf16[32,2,32,768]{3,2,1,0:T(8,128)(2,1)}, u32[]{:S(2)}, u32[]{:S(2)}) async-start(bf16[32,2,32,768]{3,2,1,0:T(8,128)(2,1)} %bitcast.36), calls=%async_computation.2 | async-start | bytes 6291456 | tf_op jit(solution)/shard_map/all_to_all | solution.py:823
  142.7 1.4 slice-start
  217.4 80.0 %all-to-all-start.3 = ((bf16[32,2,32,768]{3,2,1,0:T(8,128)(2,1)}), bf16[32,2,32,768]{3,2,1,0:T(8,128)(2,1)S(1)}, u32[]{:S(2)}, u32[]{:S(2)}) async-start(bf16[32,2,32,768]{3,2,1,0:T(8,128)(2,1)} %get-tuple-element.103), calls=%async_computation.3 | async-start | bytes 6291456 | tf_op jit(solution)/shard_map/all_to_all | solution.py:823
  253.1 4.5 %collective-permute-start = (bf16[2,192,2688]{2,1,0:T(8,128)(2,1)}, bf16[2,192,2688]{2,1,0:T(8,128)(2,1)}, u32[]{:S(2)}, u32[]{:S(2)}) collective-permute-start(bf16[2,192,2688]{2,1,0:T(8,128)(2,1)} %get-tuple-element.97), channel_id=1, source_target_pairs={{0,8},{8,0},{16,24},{24,16},{1,9},{9,1},{17,25},{25,17},{2,10},{10... | collective-permute-start | bytes 6193160 | tf_op jit(solution)/shard_map/ppermute | solution.py:886
  261.8 35.6 %collective-permute-start.1 = (bf16[192,2688]{1,0:T(8,128)(2,1)}, bf16[192,2688]{1,0:T(8,128)(2,1)}, u32[]{:S(2)}, u32[]{:S(2)}) collective-permute-start(bf16[192,2688]{1,0:T(8,128)(2,1)} %get-tuple-element.192), channel_id=1, source_target_pairs={{0,16},{8,24},{16,0},{24,8},{1,17},{9,25},{17,1},{25,9},{2,18},{10... | collective-permute-start | bytes 3096584 | tf_op jit(solution)/shard_map/ppermute | solution.py:858
  297.3 6.7 %copy-start.1 = (bf16[32,2,32,768]{3,2,1,0:T(8,128)(2,1)}, bf16[32,2,32,768]{3,2,1,0:T(8,128)(2,1)S(1)}, u32[]{:S(2)}) copy-start(bf16[32,2,32,768]{3,2,1,0:T(8,128)(2,1)S(1)} %all-to-all-done.3) | copy-start | bytes 9437188
  297.3 45.7 %all-to-all-start.4 = ((bf16[32,2,32,384]{3,2,1,0:T(8,128)(2,1)}), bf16[32,2,32,384]{3,2,1,0:T(8,128)(2,1)}, u32[]{:S(2)}, u32[]{:S(2)}) async-start(bf16[32,2,32,384]{3,2,1,0:T(8,128)(2,1)} %get-tuple-element.116), calls=%async_computation.4 | async-start | bytes 3145728 | tf_op jit(solution)/shard_map/all_to_all | solution.py:823
  304.1 38.9 %collective-permute-start.3 = (bf16[4,1,24,2688]{3,2,0,1:T(8,128)(2,1)S(1)}, bf16[4,1,24,2688]{3,2,0,1:T(8,128)(2,1)S(1)}, u32[]{:S(2)}, u32[]{:S(2)}) collective-permute-start(bf16[4,1,24,2688]{3,2,0,1:T(8,128)(2,1)S(1)} %get-tuple-element.194), channel_id=1, source_target_pairs={{0,1},{1,0},{2,3},{3,2},{4,5},{5,4},{6,7},{7,6},{8,9},{9,8},{10,11... | collective-permute-start | bytes 1548296 | tf_op jit(solution)/shard_map/ppermute | solution.py:847
  306.6 36.5 %collective-permute-start.2 = (bf16[1,192,768]{2,1,0:T(8,128)(2,1)}, bf16[1,192,768]{2,1,0:T(8,128)(2,1)S(1)}, u32[]{:S(2)}, u32[]{:S(2)}) collective-permute-start(bf16[1,192,768]{2,1,0:T(8,128)(2,1)} %get-tuple-element.114), channel_id=1, source_target_pairs={{0,8},{8,0},{16,24},{24,16},{1,9},{9,1},{17,25},{25,17},{2,10},{10... | collective-permute-start | bytes 884744 | tf_op jit(solution)/shard_map/ppermute | solution.py:894
  343.0 9.9 %copy-start.5 = (bf16[1,192,768]{2,1,0:T(8,128)(2,1)S(1)}, bf16[1,192,768]{2,1,0:T(8,128)(2,1)}, u32[]{:S(2)}) copy-start(bf16[1,192,768]{2,1,0:T(8,128)(2,1)} %get-tuple-element.124) | copy-start | bytes 884740
  343.1 81.2 %all-to-all-start.5 = ((bf16[32,2,32,384]{3,2,1,0:T(8,128)(2,1)}), bf16[32,2,32,384]{3,2,1,0:T(8,128)(2,1)S(1)}, u32[]{:S(2)}, u32[]{:S(2)}) async-start(bf16[32,2,32,384]{3,2,1,0:T(8,128)(2,1)} %get-tuple-element.123), calls=%async_computation.5 | async-start | bytes 3145728 | tf_op jit(solution)/shard_map/all_to_all | solution.py:823
  348.1 48.3 %copy-start.8 = (f32[8,128]{1,0:T(8,128)S(1)}, f32[8,128]{1,0:T(8,128)}, u32[]{:S(2)}) copy-start(f32[8,128]{1,0:T(8,128)} %get-tuple-element.129) | copy-start | bytes 12292
  348.1 49.1 %copy-start.6 = (bf16[1,192,768]{2,1,0:T(8,128)(2,1)S(1)}, bf16[1,192,768]{2,1,0:T(8,128)(2,1)}, u32[]{:S(2)}) copy-start(bf16[1,192,768]{2,1,0:T(8,128)(2,1)} %get-tuple-element.126) | copy-start | bytes 884740
  348.1 49.1 %collective-permute-start.7 = (bf16[1,192,768]{2,1,0:T(8,128)(2,1)}, bf16[1,192,768]{2,1,0:T(8,128)(2,1)}, u32[]{:S(2)}, u32[]{:S(2)}) collective-permute-start(bf16[1,192,768]{2,1,0:T(8,128)(2,1)} %get-tuple-element.127), channel_id=1, source_target_pairs={{0,8},{8,0},{16,24},{24,16},{1,9},{9,1},{17,25},{25,17},{2,10},{10... | collective-permute-start | bytes 884744 | tf_op jit(solution)/shard_map/ppermute | solution.py:904
  348.4 32.8 %collective-permute-start.4 = (bf16[24,2688]{1,0:T(8,128)(2,1)S(1)}, bf16[24,2688]{1,0:T(8,128)(2,1)S(1)}, u32[]{:S(2)}, u32[]{:S(2)}) collective-permute-start(bf16[24,2688]{1,0:T(8,128)(2,1)S(1)} %get-tuple-element.196), channel_id=1, source_target_pairs={{0,2},{1,3},{2,4},{3,5},{4,6},{5,7},{6,0},{7,1},{8,10},{9,11},{10,... | collective-permute-start | bytes 387080 | tf_op jit(solution)/shard_map/ppermute | solution.py:858
  350.0 31.1 %collective-permute-start.6 = (bf16[24,2688]{1,0:T(8,128)(2,1)S(1)}, bf16[24,2688]{1,0:T(8,128)(2,1)S(1)}, u32[]{:S(2)}, u32[]{:S(2)}) collective-permute-start(bf16[24,2688]{1,0:T(8,128)(2,1)S(1)} %get-tuple-element.197), channel_id=1, source_target_pairs={{0,6},{1,7},{2,0},{3,1},{4,2},{5,3},{6,4},{7,5},{8,14},{9,15},{10,... | collective-permute-start | bytes 387080 | tf_op jit(solution)/shard_map/ppermute | solution.py:858
  352.2 44.1 %collective-permute-start.5 = (bf16[24,2688]{1,0:T(8,128)(2,1)S(1)}, bf16[24,2688]{1,0:T(8,128)(2,1)S(1)}, u32[]{:S(2)}, u32[]{:S(2)}) collective-permute-start(bf16[24,2688]{1,0:T(8,128)(2,1)S(1)} %get-tuple-element.198), channel_id=1, source_target_pairs={{0,4},{1,5},{2,6},{3,7},{4,0},{5,1},{6,2},{7,3},{8,12},{9,13},{10,... | collective-permute-start | bytes 387080 | tf_op jit(solution)/shard_map/ppermute | solution.py:858
  398.5 8.5 %collective-permute-start.8 = (bf16[192,768]{1,0:T(8,128)(2,1)S(1)}, bf16[192,768]{1,0:T(8,128)(2,1)S(1)}, u32[]{:S(2)}, u32[]{:S(2)}) collective-permute-start(bf16[192,768]{1,0:T(8,128)(2,1)S(1)} %fusion.2), channel_id=1, source_target_pairs={{0,16},{8,24},{16,0},{24,8},{1,17},{9,25},{17,1},{25,9},{2,18},{10... | collective-permute-start | bytes 884744 | tf_op jit(solution)/shard_map/ppermute | solution.py:858
  407.4 5.2 %collective-permute-start.9 = (bf16[4,1,24,768]{3,2,1,0:T(8,128)(2,1)S(1)}, bf16[4,1,24,768]{3,2,1,0:T(8,128)(2,1)S(1)}, u32[]{:S(2)}, u32[]{:S(2)}) collective-permute-start(bf16[4,1,24,768]{3,2,1,0:T(8,128)(2,1)S(1)} %constant_dynamic-slice_fusion.4), channel_id=1, source_target_pairs={{0,1},{1,0},{2,3},{3,2},{4,5},{5,4},{6,7},{7,6},{8,9},{9,8},{10,11... | collective-permute-start | bytes 442376 | tf_op jit(solution)/shard_map/ppermute | solution.py:847
  412.7 10.2 %collective-permute-start.10 = (bf16[24,768]{1,0:T(8,128)(2,1)S(1)}, bf16[24,768]{1,0:T(8,128)(2,1)S(1)}, u32[]{:S(2)}, u32[]{:S(2)}) collective-permute-start(bf16[24,768]{1,0:T(8,128)(2,1)S(1)} %get-tuple-element.201), channel_id=1, source_target_pairs={{0,2},{1,3},{2,4},{3,5},{4,6},{5,7},{6,0},{7,1},{8,10},{9,11},{10,... | collective-permute-start | bytes 110600 | tf_op jit(solution)/shard_map/ppermute | solution.py:858
  412.7 10.1 %collective-permute-start.12 = (bf16[24,768]{1,0:T(8,128)(2,1)S(1)}, bf16[24,768]{1,0:T(8,128)(2,1)S(1)}, u32[]{:S(2)}, u32[]{:S(2)}) collective-permute-start(bf16[24,768]{1,0:T(8,128)(2,1)S(1)} %get-tuple-element.202), channel_id=1, source_target_pairs={{0,6},{1,7},{2,0},{3,1},{4,2},{5,3},{6,4},{7,5},{8,14},{9,15},{10,... | collective-permute-start | bytes 110600 | tf_op jit(solution)/shard_map/ppermute | solution.py:858
  416.5 6.3 %collective-permute-start.11 = (bf16[24,768]{1,0:T(8,128)(2,1)S(1)}, bf16[24,768]{1,0:T(8,128)(2,1)S(1)}, u32[]{:S(2)}, u32[]{:S(2)}) collective-permute-start(bf16[24,768]{1,0:T(8,128)(2,1)S(1)} %get-tuple-element.203), channel_id=1, source_target_pairs={{0,4},{1,5},{2,6},{3,7},{4,0},{5,1},{6,2},{7,3},{8,12},{9,13},{10,... | collective-permute-start | bytes 110600 | tf_op jit(solution)/shard_map/ppermute | solution.py:858
  424.3 1.2 copy-start.2
Sparse Core Ops, SparseCore 0:
  23.5 51.0 all-gather.2
  76.2 65.4 all-gather.4

commit v6 on v5

--- a/solution.py
+++ b/solution.py
@@ -473,8 +473,12 @@
             num_scalar_prefetch=1,
             grid=(3,),
             in_specs=[
-                whole(tok.shape),
-                pl.BlockSpec((HALF, D), lambda i, *_: (half, 2), pipeline_mode=pl.Buffered(1)),
+                pl.BlockSpec(
+                    (SEQ // BLOCK, 2, BLOCK, HALF),
+                    lambda i, *_: (0, 0, 0, half),
+                    pipeline_mode=pl.Buffered(1),
+                ),
+                pl.BlockSpec((HALF, D), lambda i, *_: (half, 0), pipeline_mode=pl.Buffered(1)),
             ],
             out_specs=[
                 kept((ROWS, HALF)), pair_cols(256), pair_cols(256), pair_cols(256), pair_cols(128),
@@ -506,7 +510,7 @@
                 pair_cols(256, 0), pair_cols(256, 0), pair_cols(256, 0), pair_cols(128, 0),
                 pair_cols(128, 3 * half), whole(x.shape),
                 pl.BlockSpec((ROWS, HALF), lambda i, *_: (0, half), pipeline_mode=pl.Buffered(1)),
-                pl.BlockSpec((HALF, D), lambda i, *_: (half, 2), pipeline_mode=pl.Buffered(1)),
+                pl.BlockSpec((HALF, D), lambda i, *_: (half, 0), pipeline_mode=pl.Buffered(1)),
             ],
             out_specs=[kept((SEQ // BLOCK, 2, BLOCK, HALF)), kept(part), kept(part)],
             scratch_shapes=[
@@ -613,10 +617,8 @@
 
 
 def pack_kernel(odd_ref, *refs):
-    bias_refs, (up_bias_ref, o_ref, down_ref, q_ref, k_ref, v_ref, up_ref, out_ref) = (
-        refs[:8], refs[8:16],
-    )
-    low_s, high_s = refs[16:]
+    bias_refs, (up_bias_ref, o_ref, down_ref, q_ref, k_ref, v_ref, up_ref) = refs[:8], refs[8:15]
+    in_ref, out_ref, low_s, high_s = refs[15:]
     rows = o_ref.shape[0]
     odd = odd_ref[0]
     shift = lax.broadcasted_iota(jnp.int32, (192, WIN), 1) - lax.broadcasted_iota(
@@ -634,25 +636,23 @@
     out_ref[:, D : 2 * D] = down_ref[...]
     sources = ((q_ref, columns[6]), (k_ref, jnp.zeros((rows, 1), f32)), (v_ref, columns[7]))
     for which, (ref, column) in enumerate(sources):
-        start = 2 * D + WIN * which
-        out_ref[:, start : start + WIN] = padded(ref[...], column).astype(bf16)
+        in_ref[:, WIN * which : WIN * (which + 1)] = padded(ref[...], column).astype(bf16)
     up = padded(up_ref[...], column_of(up_bias_ref))
     low_s[...] = up[:, :128]
     high_s[...] = up[:, 128:]
     for j in range(4):
         for half, source in enumerate((low_s, high_s)):
-            start = 3 * D + WIN * j + 128 * half
+            start = 2 * D + WIN * j + 128 * half
             out_ref[:, start : start + 128] = source[pl.ds(j, rows, stride=4), :].astype(bf16)
     lane = lax.broadcasted_iota(jnp.int32, (rows, 128), 1)
     small = jnp.zeros((rows, 128), f32)
     for index, column in enumerate(columns[:6]):
         small = jnp.where(lane == index, column, small)
-    out_ref[:, 3 * D + 4 * WIN :] = small.astype(bf16)
+    out_ref[:, 2 * D + 4 * WIN :] = small.astype(bf16)
 
 
 def pack(odd, biases, up_bias, o_weight, down_weight, in_weights, up_weight):
     rows = o_weight.shape[0]
-    cols = 3 * D + 4 * WIN + 128
     arrays = [bias[None, :] for bias in (*biases, up_bias)]
     arrays += [o_weight, down_weight, *in_weights, up_weight]
     return pl.pallas_call(
@@ -662,13 +662,13 @@
             num_scalar_prefetch=1,
             grid=(1,),
             in_specs=[whole(array.shape) for array in arrays],
-            out_specs=[kept((rows, cols))],
+            out_specs=[kept((rows, D)), kept((rows, GRAD_COLS))],
             scratch_shapes=[pltpu.VMEM((4 * rows, 128), f32)] * 2,
         ),
-        out_shape=[struct((rows, cols), bf16)],
+        out_shape=[struct((rows, D), bf16), struct((rows, GRAD_COLS), bf16)],
         compiler_params=PARAMS,
         cost_estimate=pl.CostEstimate(flops=0, bytes_accessed=400_000, transcendentals=0),
-    )(odd.astype(jnp.int32).reshape(1), *arrays)[0]
+    )(odd.astype(jnp.int32).reshape(1), *arrays)
 
 
 def source_of(len_ref, perm_ref, place):
@@ -678,83 +678,94 @@
     return jnp.where(swapped == place % 2, first, second)
 
 
-def deal_kernel(len_ref, perm_ref, rows_ref, *out_refs):
-    count = out_refs[0].shape[0]
-    start = pl.program_id(0) * count
-
-    def one(index, carry):
-        source = source_of(len_ref, perm_ref, start + index)
+def moved_rows(source_at, rows_refs, out_ref, buffer_ref, in_sems, out_sems):
+    count = out_ref.shape[0] // STEPS
+
+    def group(step):
+        return pl.ds(step * count, count)
+
+    for step in range(STEPS):
+
+        def one(index, carry):
+            place = step * count + index
+            source = source_at(place)
+            lane = 0
+            for which, rows_ref in enumerate(rows_refs):
+                width = rows_ref.shape[2]
+                pltpu.make_async_copy(
+                    rows_ref.at[source],
+                    buffer_ref.at[place, :, pl.ds(lane, width)],
+                    in_sems.at[step, which],
+                ).start()
+                lane += width
+            return carry
+
+        lax.fori_loop(0, count, one, 0)
+    for step in range(STEPS):
         lane = 0
-        for out_ref in out_refs:
-            width = out_ref.shape[2]
-            out_ref[index] = rows_ref[source, :, lane : lane + width]
+        for which, rows_ref in enumerate(rows_refs):
+            width = rows_ref.shape[2]
+            pltpu.make_async_copy(
+                rows_ref.at[group(step)],
+                buffer_ref.at[group(step), :, pl.ds(lane, width)],
+                in_sems.at[step, which],
+            ).wait()
             lane += width
-        return carry
-
-    lax.fori_loop(0, count, one, 0)
-
-
-def deal(rows, lengths, permutation, parts):
-    total, size, width = rows.shape
-    count = total // STEPS
+        pltpu.make_async_copy(
+            buffer_ref.at[group(step)], out_ref.at[group(step)], out_sems.at[step]
+        ).start()
+    for step in range(STEPS):
+        pltpu.make_async_copy(
+            buffer_ref.at[group(step)], out_ref.at[group(step)], out_sems.at[step]
+        ).wait()
+
+
+def moved_call(kernel, name, parts, lengths, permutation):
+    total, size, _ = parts[0].shape
+    shape = (total, size, sum(part.shape[2] for part in parts))
     return pl.pallas_call(
-        deal_kernel,
-        name="deal",
+        kernel,
+        name=name,
         grid_spec=pltpu.PrefetchScalarGridSpec(
             num_scalar_prefetch=2,
-            grid=(STEPS,),
-            in_specs=[whole(rows.shape)],
-            out_specs=[pl.BlockSpec((count, size, width // parts), lambda i, *_: (i, 0, 0))] * parts,
+            grid=(1,),
+            in_specs=[pl.BlockSpec(memory_space=pltpu.HBM)] * len(parts),
+            out_specs=[pl.BlockSpec(memory_space=pltpu.HBM)],
+            scratch_shapes=[
+                pltpu.VMEM(shape, bf16),
+                pltpu.SMEM((total,), jnp.int32),
+                pltpu.SemaphoreType.DMA((STEPS, len(parts))),
+                pltpu.SemaphoreType.DMA((STEPS,)),
+            ],
         ),
-        out_shape=[struct((total, size, width // parts), rows.dtype)] * parts,
+        out_shape=[struct(shape, bf16)],
         compiler_params=PARAMS,
-        cost_estimate=pl.CostEstimate(flops=0, bytes_accessed=8_000_000, transcendentals=0),
-    )(lengths, permutation, rows)
+        cost_estimate=pl.CostEstimate(flops=0, bytes_accessed=100_000, transcendentals=0),
+    )(lengths, permutation, *parts)[0]
+
+
+def deal_kernel(len_ref, perm_ref, rows_ref, out_ref, buffer_ref, place_s, in_sems, out_sems):
+    source_at = lambda place: source_of(len_ref, perm_ref, place)
+    moved_rows(source_at, [rows_ref], out_ref, buffer_ref, in_sems, out_sems)
+
+
+def deal(rows, lengths, permutation):
+    return moved_call(deal_kernel, "deal", [rows], lengths, permutation)
 
 
 def restore_kernel(len_ref, perm_ref, *refs):
-    part_refs, out_ref, place_s = refs[:-2], refs[-2], refs[-1]
-    count = out_ref.shape[0]
-    start = pl.program_id(0) * count
-
-    @pl.when(pl.program_id(0) == 0)
-    def _():
-        def note(index, carry):
-            place_s[source_of(len_ref, perm_ref, index)] = index
-            return carry
-
-        lax.fori_loop(0, part_refs[0].shape[0], note, 0)
-
-    def one(index, carry):
-        place = place_s[start + index]
-        lane = 0
-        for ref in part_refs:
-            width = ref.shape[2]
-            out_ref[index, :, lane : lane + width] = ref[place]
-            lane += width
+    part_refs, (out_ref, buffer_ref, place_s, in_sems, out_sems) = refs[:-5], refs[-5:]
+
+    def note(index, carry):
+        place_s[source_of(len_ref, perm_ref, index)] = index
         return carry
 
-    lax.fori_loop(0, count, one, 0)
+    lax.fori_loop(0, out_ref.shape[0], note, 0)
+    moved_rows(lambda place: place_s[place], part_refs, out_ref, buffer_ref, in_sems, out_sems)
 
 
 def restore(parts, lengths, permutation):
-    total, size, _ = parts[0].shape
-    width = sum(part.shape[2] for part in parts)
-    count = total // STEPS
-    return pl.pallas_call(
-        restore_kernel,
-        name="restore",
-        grid_spec=pltpu.PrefetchScalarGridSpec(
-            num_scalar_prefetch=2,
-            grid=(STEPS,),
-            in_specs=[whole(part.shape) for part in parts],
-            out_specs=[pl.BlockSpec((count, size, width), lambda i, *_: (i, 0, 0))],
-            scratch_shapes=[pltpu.SMEM((total,), jnp.int32)],
-        ),
-        out_shape=[struct((total, size, width), bf16)],
-        compiler_params=PARAMS,
-        cost_estimate=pl.CostEstimate(flops=0, bytes_accessed=8_000_000, transcendentals=0),
-    )(lengths, permutation, *parts)[0]
+    return moved_call(restore_kernel, "restore", parts, lengths, permutation)
 
 
 def pick(values, index):
@@ -788,30 +799,35 @@
         )
 
     if rows_dev % 8 == 0:
-        packed = pack(
+        packed_in, packed = pack(
             odd,
             [o_bias, norm1_gain, norm1_bias, down_bias, norm2_gain, norm2_bias, q_bias, v_bias],
             up_bias, o_weight, down_weight, [q_weight, k_weight, v_weight], up_weight,
         )
     else:
         small = [o_bias, norm1_gain, norm1_bias, down_bias, norm2_gain, norm2_bias]
+        packed_in = jnp.concatenate(
+            [
+                padded(q_weight, q_bias),
+                padded(k_weight, jnp.zeros_like(q_bias)),
+                padded(v_weight, v_bias),
+            ],
+            axis=1,
+        )
         packed = jnp.concatenate(
             [
                 o_weight,
                 down_weight,
-                padded(q_weight, q_bias),
-                padded(k_weight, jnp.zeros_like(q_bias)),
-                padded(v_weight, v_bias),
                 padded(up_weight, up_bias).reshape(rows_dev, 4 * WIN),
                 jnp.pad(jnp.stack(small, axis=1), ((0, 0), (0, 122))),
             ],
             axis=1,
         )
-    gathered = lax.all_gather(packed, "fsdp", axis=0, tiled=True)
+    full_in = lax.all_gather(packed_in, AXES, axis=0, tiled=True)
+    packed, full_in = tie(packed, full_in)
+    full = lax.all_gather(packed, AXES, axis=0, tiled=True)
 
     dealt_lengths = pick(lengths, permutation).reshape(devices, seq_dev)
-    swap = dealt_lengths[:, 0] < dealt_lengths[:, 1]
-    my_swap = lax.dynamic_index_in_dim(swap, my_index, 0, False)
     chunks = lax.axis_size("dp")
     parity = lax.axis_index("dp") % 2
     pairing = [(i, i ^ 1) for i in range(chunks)]
@@ -865,18 +881,14 @@
     def total_low(parts):
         return total(parts).astype(bf16)
 
-    tok0, tok1 = deal(tokens, lengths, permutation, 2)
-    tok0 = arrive(tok0)
-    gathered, tok0 = tie(gathered, tok0)
-    full = lax.all_gather(gathered, "dp", axis=0, tiled=True)
-    tok1 = arrive(tok1)
-    dealt_cot, tok0, tok1 = tie(deal(cotangent, lengths, permutation, 1)[0], tok0, tok1)
+    tok = arrive(deal(tokens, lengths, permutation))
+    dealt_cot, tok = tie(deal(cotangent, lengths, permutation), tok)
     cot = arrive(dealt_cot)
 
-    x0, qa0, ka0, va0, ctx0 = attn_fwd(len_arr, tok0, full, 0)
-    x1, qa1, ka1, va1, ctx1 = attn_fwd(len_arr, tok1, full, 1)
-    wu = full[:, 3 * D : 3 * D + 4 * WIN].reshape(FF, WIN)
-    vecs = jnp.pad(full[:, 3 * D + 4 * WIN : 3 * D + 4 * WIN + 6].astype(f32).T, ((0, 2), (0, 0)))
+    x0, qa0, ka0, va0, ctx0 = attn_fwd(len_arr, tok, full_in, 0)
+    x1, qa1, ka1, va1, ctx1 = attn_fwd(len_arr, tok, full_in, 1)
+    wu = full[:, 2 * D : 2 * D + 4 * WIN].reshape(FF, WIN)
+    vecs = jnp.pad(full[:, 2 * D + 4 * WIN : 2 * D + 4 * WIN + 6].astype(f32).T, ((0, 2), (0, 0)))
     out, n1, n2, inv, slope, act, stat = mid_fwd(len_arr, x0, x1, ctx0, ctx1, full, wu, vecs)
     cot, out = tie(cot, out)
     back_out = leave(out)
@@ -887,26 +899,28 @@
     gctx, mine = tie(gctx, mine)
     parts = send_rest(mine, "dp")
     ig0, dw0, given0 = attn_bwd(
-        len_arr, qa0, ka0, va0, ctx0, gctx, x0, base, full, 0, chunks
+        len_arr, qa0, ka0, va0, ctx0, gctx, x0, base, full_in, 0, chunks
     )
     ig0, dw0, given0, gctx, back_out, *parts = tie(ig0, dw0, given0, gctx, back_out, *parts)
     back0 = leave(ig0)
     given0 = lax.ppermute(given0, "dp", pairing)
     parts = send_pair(total_low(parts), "fsdp")
     ig1, dw1, given1 = attn_bwd(
-        len_arr, qa1, ka1, va1, ctx1, gctx, x1, base, full, 1, chunks
+        len_arr, qa1, ka1, va1, ctx1, gctx, x1, base, full_in, 1, chunks
     )
     ig1, dw0, dw1, given0, given1, back0, *parts = tie(
         ig1, dw0, dw1, given0, given1, back0, *parts
     )
     back1 = leave(ig1)
-    mine = total(send_rest(total_low(parts), "fsdp"))
     given1 = lax.ppermute(given1, "dp", pairing)
     mine_in = jnp.concatenate([total_low([dw0, given0]), total_low([dw1, given1])], axis=0)
-    parts = send_pair(total_low(send_rest(mine_in, "dp")), "fsdp")
-    mine_in = total(send_rest(total_low(parts), "fsdp"))
-
-    back_out, stat, mine = tie(back_out, stat, mine)
+    mine_in = total_low(send_pair(total_low(send_rest(mine_in, "dp")), "fsdp"))
+    mine = total(send_rest(jnp.concatenate([total_low(parts), mine_in], axis=1), "fsdp"))
+    mine_in = mine[:, GRAD_COLS:]
+
+    back_out, stat, dealt_lengths, mine = tie(back_out, stat, dealt_lengths, mine)
+    swap = dealt_lengths[:, 0] < dealt_lengths[:, 1]
+    my_swap = lax.dynamic_index_in_dim(swap, my_index, 0, False)
     output = restore([back_out], lengths, permutation)
     input_grad = restore([back0, back1], lengths, permutation)
     lens = jnp.stack([len_arr[0], ROWS - len_arr[0]]).astype(f32)

time: 438 us -> 426 us (0.973)
  starting transfers between devices: 41.8 us -> 28.2 us
    all_gather x2, waiting for transfers between devices: 69.5 us -> 105 us  [the longest x1 76.9 us: on_device(): full_in = lax.all_gather(packed_in, AXES, axis=0, tiled=True)]
    all_to_all x6 -> x5, waiting for transfers between devices: 33.1 us -> 0.86 us  [swap_blocks(): return lax.all_to_all(rows, AXES, split_axis=0, concat_axis=0, tiled=True)]
    ppermute x8 -> x5, waiting for transfers between devices: 49.4 us -> 37.7 us  [send_rest(): parts.append(lax.ppermute(block_of((place + shift) % half), axis, target))]
    ppermute x8 -> x5, starting transfers between devices: 11.5 us -> 4.53 us  [send_rest(): parts.append(lax.ppermute(block_of((place + shift) % half), axis, target))]
    ppermute x2, waiting for transfers between devices: 2.26 us -> 8.91 us  [send_pair(): lax.ppermute(given, axis, [(i, i ^ 1) for i in range(count)])]
    all_to_all x6 -> x5, starting transfers between devices: 26.6 us -> 21.8 us  [swap_blocks(): return lax.all_to_all(rows, AXES, split_axis=0, concat_axis=0, tiled=True)]
  transfers between devices with their start and end apart: 21 -> 17, of which waited for: 8 -> 9; matrix products, arithmetic and copies ran while one was open for 5% -> 6% of each run, Pallas kernels for 42% -> 43%
where the time goes in v6:
time: 426 us; the launch traced here: 424 us
  Pallas kernels  191 us (45%)
  waiting for transfers between devices  159 us (37%)
  starting transfers between devices  28.2 us (7%)
  local copies, waits for them, and re-layouts  15.6 us (4%)
  other arithmetic  15.6 us (4%)
  between operations  15.2 us (4%)
    all_gather x1, waiting for transfers between devices, on_device(): full_in = lax.all_gather(packed_in, AXES, axis=0, tiled=True)  76.9 us
    pallas_call x2, Pallas kernels, attn_bwd(): pl.pallas_call(attn_bwd_kernel, name='attn_bwd', grid_spec=pltpu.Prefetch...  68 us
    pallas_call x2, Pallas kernels, attn_fwd(): pl.pallas_call(attn_fwd_kernel, name='attn_fwd', grid_spec=pltpu.Prefetch...  50.9 us
    ppermute x5, waiting for transfers between devices, send_rest(): parts.append(lax.ppermute(block_of((place + shift) % half), axis, target))  37.7 us
    pallas_call x1, Pallas kernels, mid_bwd(): pl.pallas_call(mid_bwd_kernel, name='mid_bwd', grid_spec=pltpu.PrefetchSc...  32.7 us
    all_gather x1, waiting for transfers between devices, on_device(): full = lax.all_gather(packed, AXES, axis=0, tiled=True)  28.5 us
    all_to_all x5, starting transfers between devices, swap_blocks(): return lax.all_to_all(rows, AXES, split_axis=0, concat_axis=0, tiled=True)  21.8 us
    pallas_call x1, Pallas kernels, mid_fwd(): pl.pallas_call(mid_fwd_kernel, name='mid_fwd', grid_spec=pltpu.PrefetchSc...  20 us
  transfers between devices with their start and end apart: 17, of which 9 were waited for; matrix products, arithmetic and copies ran while one was open for 6% of the time, Pallas kernels for 43%

profile of v6, /device:TPU:0, one launch (start us, length us, event | category | flops | bytes accessed | tf_op | source)
XLA Modules:
  0.0 424.2 jit_solution(13251849684223872089)
XLA Ops:
  7.2 3.7 deal.3
  10.9 7.3 %all-to-all-start = ((bf16[32,2,32,768]{3,2,1,0:T(8,128)(2,1)}), bf16[32,2,32,768]{3,2,1,0:T(8,128)(2,1)S(1)}, u32[]{:S(2)}, u32[]{:S(2)}) async-start(bf16[32,2,32,768]{3,2,1,0:T(8,128)(2,1)} %bitcast.34), calls=%async_computation | async-start | bytes 6291456 | tf_op jit(solution)/shard_map/all_to_all | solution.py:839
  18.3 1.8 pack.1
  20.2 76.9 %all-gather.3.cloned.1.call-done.full_ref = bf16[768,768]{1,0:T(8,128)(2,1)} async-done(((bf16[24,768]{1,0:T(8,128)(2,1)}), bf16[768,768]{1,0:T(8,128)(2,1)}) %all-gather.3.cloned.1.call-update) | async-done | bytes 1179664 | tf_op jit(solution)/shard_map/all_gather | solution.py:826
  97.1 3.7 deal.2
  100.9 1.6 copy-done.4
  102.5 2.8 all-to-all-start.1
  108.1 25.4 %attn_fwd.2 = (bf16[1088,384]{1,0:T(8,128)(2,1)}, bf16[1088,768]{1,0:T(8,128)(2,1)}, bf16[1088,768]{1,0:T(8,128)(2,1)}, bf16[1088,768]{1,0:T(8,128)(2,1)}, bf16[1088,384]{1,0:T(8,128)(2,1)}) custom-call(s32[2]{0:T(128)} %pad_add_fusion.len_ref, bf16[32,2,32,768]{3,2,1,0:T(8,128)(2,1)} %copy-done.4, bf16[768,768]{1,0:T(8,128)(2,1)} %all-gather.3.cloned.1.call-done.full_ref), custom_call_target="tpu_custom_call" | custom-call | flops 20000000000 | bytes 12000000 | tf_op jit(solution)/shard_map/attn_fwd/pallas_call | solution.py:469
  133.5 25.5 %attn_fwd.3 = (bf16[1088,384]{1,0:T(8,128)(2,1)}, bf16[1088,768]{1,0:T(8,128)(2,1)}, bf16[1088,768]{1,0:T(8,128)(2,1)}, bf16[1088,768]{1,0:T(8,128)(2,1)}, bf16[1088,384]{1,0:T(8,128)(2,1)}) custom-call(s32[2]{0:T(128)} %pad_add_fusion.len_ref, bf16[32,2,32,768]{3,2,1,0:T(8,128)(2,1)} %copy-done.4, bf16[768,768]{1,0:T(8,128)(2,1)} %all-gather.3.cloned.1.call-done.full_ref), custom_call_target="tpu_custom_call" | custom-call | flops 20000000000 | bytes 12000000 | tf_op jit(solution)/shard_map/attn_fwd/pallas_call | solution.py:469
  159.0 28.5 %all-gather.5.cloned.1.call-done.full_ref = bf16[768,2688]{1,0:T(8,128)(2,1)} async-done(((bf16[24,2688]{1,0:T(8,128)(2,1)}), bf16[768,2688]{1,0:T(8,128)(2,1)}) %all-gather.5.cloned.1.call-update) | async-done | bytes 4128784 | tf_op jit(solution)/shard_map/all_gather | solution.py:828
  187.5 2.7 slice.136
  190.1 3.8 reshape.114.wu_ref
  194.6 20.0 %mid_fwd.1 = (bf16[32,2,32,768]{3,2,1,0:T(8,128)(2,1)}, f32[1088,768]{1,0:T(8,128)}, f32[1088,768]{1,0:T(8,128)}, f32[1088,128]{1,0:T(8,128)}, f32[1088,3072]{1,...) custom-call(s32[2]{0:T(128)} %pad_add_fusion.len_ref, bf16[1088,384]{1,0:T(8,128)(2,1)} %get-tuple-element.83.x0_ref.x_ref, ...), custom_call_target="tpu_custom_call" | custom-call | flops 15000000512 | bytes 36000000 | tf_op jit(solution)/shard_map/mid_fwd/pallas_call | solution.py:546
  214.7 1.7 copy-done.2
  216.3 3.0 all-to-all-start.2
  219.3 32.7 %mid_bwd.1 = (bf16[1088,768]{1,0:T(8,128)(2,1)}, f32[1088,768]{1,0:T(8,128)}, bf16[2,192,2688]{2,1,0:T(8,128)(2,1)}, bf16[2,192,2688]{2,1,0:T(8,128)(2,1)}) custom-call(s32[2]{0:T(128)} %pad_add_fusion.len_ref, bf16[32,2,32,768]{3,2,1,0:T(8,128)(2,1)} %copy-done.2, bf16[1088,384]{1,0:T(8,128)(2,1)} %get-tuple-element.81.ctx0_ref.ctx_ref, ...), custom_call_target="tpu_custom_call" | custom-call | flops 100000000 | bytes 1000000 | tf_op jit(solution)/shard_map/mid_bwd/pallas_call | solution.py:575
  252.2 4.4 %collective-permute-done = bf16[2,192,2688]{2,1,0:T(8,128)(2,1)} collective-permute-done((bf16[2,192,2688]{2,1,0:T(8,128)(2,1)}, bf16[2,192,2688]{2,1,0:T(8,128)(2,1)}, u32[]{:S(2)}, u32[]{:S(2)}) %collective-permute-start) | collective-permute-done | bytes 2064416 | tf_op jit(solution)/shard_map/ppermute | solution.py:898
  256.6 2.7 add_convert_fusion
  260.7 1.5 collective-permute-start.1
  262.3 33.9 %attn_bwd.2 = (bf16[32,2,32,384]{3,2,1,0:T(8,128)(2,1)}, bf16[1,192,768]{2,1,0:T(8,128)(2,1)}, bf16[1,192,768]{2,1,0:T(8,128)(2,1)}) custom-call(s32[2]{0:T(128)} %pad_add_fusion.len_ref, bf16[1088,768]{1,0:T(8,128)(2,1)} %get-tuple-element.78.qa_ref, bf16[1088,768]{1,0:T(8,128)(2,1)} %get-tuple-element.79.ka_ref, ...), custom_call_target="tpu_custom_call" | custom-call | flops 100000000 | bytes 1000000 | tf_op jit(solution)/shard_map/attn_bwd/pallas_call | solution.py:503
  296.2 5.0 %all-to-all-start.3 = ((bf16[32,2,32,384]{3,2,1,0:T(8,128)(2,1)}), bf16[32,2,32,384]{3,2,1,0:T(8,128)(2,1)}, u32[]{:S(2)}, u32[]{:S(2)}) async-start(bf16[32,2,32,384]{3,2,1,0:T(8,128)(2,1)} %get-tuple-element.115), calls=%async_computation.3 | async-start | bytes 3145728 | tf_op jit(solution)/shard_map/all_to_all | solution.py:839
  301.3 1.8 add_convert_fusion.1
  303.2 1.6 collective-permute-start.3
  304.8 34.1 %attn_bwd.3 = (bf16[32,2,32,384]{3,2,1,0:T(8,128)(2,1)}, bf16[1,192,768]{2,1,0:T(8,128)(2,1)}, bf16[1,192,768]{2,1,0:T(8,128)(2,1)}) custom-call(s32[2]{0:T(128)} %pad_add_fusion.len_ref, bf16[1088,768]{1,0:T(8,128)(2,1)} %get-tuple-element.106.qa_ref, bf16[1088,768]{1,0:T(8,128)(2,1)} %get-tuple-element.107.ka_ref, ...), custom_call_target="tpu_custom_call" | custom-call | flops 100000000 | bytes 1000000 | tf_op jit(solution)/shard_map/attn_bwd/pallas_call | solution.py:503
  339.8 1.7 collective-permute-done.4
  343.8 3.7 all-to-all-start.4
  347.5 11.1 %collective-permute-done.5 = bf16[192,768]{1,0:T(8,128)(2,1)} collective-permute-done((bf16[192,768]{1,0:T(8,128)(2,1)S(1)}, bf16[192,768]{1,0:T(8,128)(2,1)}, u32[]{:S(2)}, u32[]{:S(2)}) %collective-permute-start.5) | collective-permute-done | bytes 294944 | tf_op jit(solution)/shard_map/ppermute | solution.py:874
  360.1 8.9 %collective-permute-done.6 = bf16[4,1,24,768]{3,2,1,0:T(8,128)(2,1)S(1)} collective-permute-done((bf16[4,1,24,768]{3,2,1,0:T(8,128)(2,1)S(1)}, bf16[4,1,24,768]{3,2,1,0:T(8,128)(2,1)S(1)}, u32[]{:S(2)}, u32[]{:S(2)}) %collective-permute-start.6) | collective-permute-done | bytes 147488 | tf_op jit(solution)/shard_map/ppermute | solution.py:863
  372.5 5.6 %collective-permute-done.9 = bf16[24,3456]{1,0:T(8,128)(2,1)S(1)} collective-permute-done((bf16[24,3456]{1,0:T(8,128)(2,1)S(1)}, bf16[24,3456]{1,0:T(8,128)(2,1)S(1)}, u32[]{:S(2)}, u32[]{:S(2)}) %collective-permute-start.9) | collective-permute-done | bytes 165920 | tf_op jit(solution)/shard_map/ppermute | solution.py:874
  378.2 21.0 %collective-permute-done.8 = bf16[24,3456]{1,0:T(8,128)(2,1)S(1)} collective-permute-done((bf16[24,3456]{1,0:T(8,128)(2,1)S(1)}, bf16[24,3456]{1,0:T(8,128)(2,1)S(1)}, u32[]{:S(2)}, u32[]{:S(2)}) %collective-permute-start.8) | collective-permute-done | bytes 165920 | tf_op jit(solution)/shard_map/ppermute | solution.py:874
  399.3 5.0 %restore.2 = bf16[64,32,768]{2,1,0:T(8,128)(2,1)} custom-call(s32[64]{0:T(128)} %len_ref.7, s32[64]{0:T(128)} %perm_ref.7, bf16[64,32,768]{2,1,0:T(8,128)(2,1)} %bitcast.33), custom_call_target="tpu_custom_call" | custom-call | bytes 100000 | tf_op jit(solution)/shard_map/restore/pallas_call | solution.py:726
  412.5 4.9 %restore.3 = bf16[64,32,768]{2,1,0:T(8,128)(2,1)} custom-call(s32[64]{0:T(128)} %len_ref.7, s32[64]{0:T(128)} %perm_ref.7, bf16[64,32,384]{2,1,0:T(8,128)(2,1)} %bitcast.17.refs_0_, bf16[64,32,384]{2,1,0:T(8,128)(2,1)} %bitcast.37), custom_call_target="tpu_custom_call" | custom-call | bytes 100000 | tf_op jit(solution)/shard_map/restore/pallas_call | solution.py:726
  (74 shorter events, 21.1 us)
Async XLA Ops:
  10.9 89.9 %all-to-all-start = ((bf16[32,2,32,768]{3,2,1,0:T(8,128)(2,1)}), bf16[32,2,32,768]{3,2,1,0:T(8,128)(2,1)S(1)}, u32[]{:S(2)}, u32[]{:S(2)}) async-start(bf16[32,2,32,768]{3,2,1,0:T(8,128)(2,1)} %bitcast.34), calls=%async_computation | async-start | bytes 6291456 | tf_op jit(solution)/shard_map/all_to_all | solution.py:839
  18.2 78.9 %all-gather.3.cloned.1.call-start = ((), (), s32[]{:S(2)}) async-start(), calls=%async_computation.5 | async-start | bytes 1216512 | tf_op jit(solution)/shard_map/all_gather | solution.py:826
  20.2 167.3 %all-gather.5.cloned.1.call-start = ((), (), s32[]{:S(2)}) async-start(), calls=%async_computation.6 | async-start | bytes 4257792 | tf_op jit(solution)/shard_map/all_gather | solution.py:828
  100.8 1.7 copy-start.4
  100.8 4.5 %copy-start.6 = (s32[64]{0:T(128)S(1)}, s32[64]{0:T(128)}, u32[]{:S(2)}) copy-start(s32[64]{0:T(128)} %perm_ref.7) | copy-start | bytes 772
  100.8 4.5 %copy-start = (s32[64]{0:T(128)S(1)}, s32[64]{0:T(128)}, u32[]{:S(2)}) copy-start(s32[64]{0:T(128)} %len_ref.7) | copy-start | bytes 772
  102.5 112.2 %all-to-all-start.1 = ((bf16[32,2,32,768]{3,2,1,0:T(8,128)(2,1)}), bf16[32,2,32,768]{3,2,1,0:T(8,128)(2,1)S(1)}, u32[]{:S(2)}, u32[]{:S(2)}) async-start(bf16[32,2,32,768]{3,2,1,0:T(8,128)(2,1)} %bitcast.35), calls=%async_computation.1 | async-start | bytes 6291456 | tf_op jit(solution)/shard_map/all_to_all | solution.py:839
  190.1 3.8 slice-start
  214.7 1.7 copy-start.2
  216.3 79.9 %all-to-all-start.2 = ((bf16[32,2,32,768]{3,2,1,0:T(8,128)(2,1)}), bf16[32,2,32,768]{3,2,1,0:T(8,128)(2,1)S(1)}, u32[]{:S(2)}, u32[]{:S(2)}) async-start(bf16[32,2,32,768]{3,2,1,0:T(8,128)(2,1)} %get-tuple-element.102), calls=%async_computation.2 | async-start | bytes 6291456 | tf_op jit(solution)/shard_map/all_to_all | solution.py:839
  252.0 4.5 %collective-permute-start = (bf16[2,192,2688]{2,1,0:T(8,128)(2,1)}, bf16[2,192,2688]{2,1,0:T(8,128)(2,1)}, u32[]{:S(2)}, u32[]{:S(2)}) collective-permute-start(bf16[2,192,2688]{2,1,0:T(8,128)(2,1)} %get-tuple-element.96), channel_id=1, source_target_pairs={{0,8},{8,0},{16,24},{24,16},{1,9},{9,1},{17,25},{25,17},{2,10},{10... | collective-permute-start | bytes 6193160 | tf_op jit(solution)/shard_map/ppermute | solution.py:898
  260.7 35.4 %collective-permute-start.1 = (bf16[192,2688]{1,0:T(8,128)(2,1)}, bf16[192,2688]{1,0:T(8,128)(2,1)}, u32[]{:S(2)}, u32[]{:S(2)}) collective-permute-start(bf16[192,2688]{1,0:T(8,128)(2,1)} %get-tuple-element.192), channel_id=1, source_target_pairs={{0,16},{8,24},{16,0},{24,8},{1,17},{9,25},{17,1},{25,9},{2,18},{10... | collective-permute-start | bytes 3096584 | tf_op jit(solution)/shard_map/ppermute | solution.py:874
  296.2 6.9 %copy-start.1 = (bf16[32,2,32,768]{3,2,1,0:T(8,128)(2,1)}, bf16[32,2,32,768]{3,2,1,0:T(8,128)(2,1)S(1)}, u32[]{:S(2)}) copy-start(bf16[32,2,32,768]{3,2,1,0:T(8,128)(2,1)S(1)} %all-to-all-done.2) | copy-start | bytes 9437188
  296.2 43.5 %all-to-all-start.3 = ((bf16[32,2,32,384]{3,2,1,0:T(8,128)(2,1)}), bf16[32,2,32,384]{3,2,1,0:T(8,128)(2,1)}, u32[]{:S(2)}, u32[]{:S(2)}) async-start(bf16[32,2,32,384]{3,2,1,0:T(8,128)(2,1)} %get-tuple-element.115), calls=%async_computation.3 | async-start | bytes 3145728 | tf_op jit(solution)/shard_map/all_to_all | solution.py:839
  301.3 3.5 copy-start.8
  303.2 35.7 %collective-permute-start.3 = (bf16[4,1,24,2688]{3,2,0,1:T(8,128)(2,1)S(1)}, bf16[4,1,24,2688]{3,2,0,1:T(8,128)(2,1)S(1)}, u32[]{:S(2)}, u32[]{:S(2)}) collective-permute-start(bf16[4,1,24,2688]{3,2,0,1:T(8,128)(2,1)S(1)} %get-tuple-element.194), channel_id=1, source_target_pairs={{0,1},{1,0},{2,3},{3,2},{4,5},{5,4},{6,7},{7,6},{8,9},{9,8},{10,11... | collective-permute-start | bytes 1548296 | tf_op jit(solution)/shard_map/ppermute | solution.py:863
  304.8 34.1 %collective-permute-start.2 = (bf16[1,192,768]{2,1,0:T(8,128)(2,1)S(1)}, bf16[1,192,768]{2,1,0:T(8,128)(2,1)S(1)}, u32[]{:S(2)}, u32[]{:S(2)}) collective-permute-start(bf16[1,192,768]{2,1,0:T(8,128)(2,1)S(1)} %copy-done.8), channel_id=1, source_target_pairs={{0,8},{8,0},{16,24},{24,16},{1,9},{9,1},{17,25},{25,17},{2,10},{10... | collective-permute-start | bytes 884744 | tf_op jit(solution)/shard_map/ppermute | solution.py:906
  304.8 34.9 %copy-start.5 = (bf16[1,192,768]{2,1,0:T(8,128)(2,1)S(1)}, bf16[1,192,768]{2,1,0:T(8,128)(2,1)}, u32[]{:S(2)}) copy-start(bf16[1,192,768]{2,1,0:T(8,128)(2,1)} %get-tuple-element.120) | copy-start | bytes 884740
  339.7 1.8 collective-permute-start.4
  342.9 15.7 %collective-permute-start.5 = (bf16[192,768]{1,0:T(8,128)(2,1)S(1)}, bf16[192,768]{1,0:T(8,128)(2,1)}, u32[]{:S(2)}, u32[]{:S(2)}) collective-permute-start(bf16[192,768]{1,0:T(8,128)(2,1)S(1)} %fusion.2), channel_id=1, source_target_pairs={{0,16},{8,24},{16,0},{24,8},{1,17},{9,25},{17,1},{25,9},{2,18},{10... | collective-permute-start | bytes 884744 | tf_op jit(solution)/shard_map/ppermute | solution.py:874
  343.8 67.5 %all-to-all-start.4 = ((bf16[32,2,32,384]{3,2,1,0:T(8,128)(2,1)}), bf16[32,2,32,384]{3,2,1,0:T(8,128)(2,1)S(1)}, u32[]{:S(2)}, u32[]{:S(2)}) async-start(bf16[32,2,32,384]{3,2,1,0:T(8,128)(2,1)} %get-tuple-element.126), calls=%async_computation.4 | async-start | bytes 3145728 | tf_op jit(solution)/shard_map/all_to_all | solution.py:839
  359.8 9.1 %collective-permute-start.6 = (bf16[4,1,24,768]{3,2,1,0:T(8,128)(2,1)S(1)}, bf16[4,1,24,768]{3,2,1,0:T(8,128)(2,1)S(1)}, u32[]{:S(2)}, u32[]{:S(2)}) collective-permute-start(bf16[4,1,24,768]{3,2,1,0:T(8,128)(2,1)S(1)} %constant_dynamic-slice_fusion.1), channel_id=1, source_target_pairs={{0,1},{1,0},{2,3},{3,2},{4,5},{5,4},{6,7},{7,6},{8,9},{9,8},{10,11... | collective-permute-start | bytes 442376 | tf_op jit(solution)/shard_map/ppermute | solution.py:863
  369.1 9.1 %collective-permute-start.9 = (bf16[24,3456]{1,0:T(8,128)(2,1)S(1)}, bf16[24,3456]{1,0:T(8,128)(2,1)S(1)}, u32[]{:S(2)}, u32[]{:S(2)}) collective-permute-start(bf16[24,3456]{1,0:T(8,128)(2,1)S(1)} %get-tuple-element.198), channel_id=1, source_target_pairs={{0,6},{1,7},{2,0},{3,1},{4,2},{5,3},{6,4},{7,5},{8,14},{9,15},{10,... | collective-permute-start | bytes 497672 | tf_op jit(solution)/shard_map/ppermute | solution.py:874
  370.5 28.7 %collective-permute-start.8 = (bf16[24,3456]{1,0:T(8,128)(2,1)S(1)}, bf16[24,3456]{1,0:T(8,128)(2,1)S(1)}, u32[]{:S(2)}, u32[]{:S(2)}) collective-permute-start(bf16[24,3456]{1,0:T(8,128)(2,1)S(1)} %get-tuple-element.197), channel_id=1, source_target_pairs={{0,4},{1,5},{2,6},{3,7},{4,0},{5,1},{6,2},{7,3},{8,12},{9,13},{10,... | collective-permute-start | bytes 497672 | tf_op jit(solution)/shard_map/ppermute | solution.py:874
  370.5 28.7 %collective-permute-start.7 = (bf16[24,3456]{1,0:T(8,128)(2,1)S(1)}, bf16[24,3456]{1,0:T(8,128)(2,1)S(1)}, u32[]{:S(2)}, u32[]{:S(2)}) collective-permute-start(bf16[24,3456]{1,0:T(8,128)(2,1)S(1)} %get-tuple-element.196), channel_id=1, source_target_pairs={{0,2},{1,3},{2,4},{3,5},{4,6},{5,7},{6,0},{7,1},{8,10},{9,11},{10,... | collective-permute-start | bytes 497672 | tf_op jit(solution)/shard_map/ppermute | solution.py:874
  399.3 5.1 %copy-start.7 = (f32[8,128]{1,0:T(8,128)S(1)}, f32[8,128]{1,0:T(8,128)}, u32[]{:S(2)}) copy-start(f32[8,128]{1,0:T(8,128)} %get-tuple-element.129) | copy-start | bytes 12292
  411.3 1.2 copy-start.3
Sparse Core Ops, SparseCore 0:
  22.6 74.4 all-gather.2
  99.9 87.4 all-gather.4

commit v7 on v6

--- a/solution.py
+++ b/solution.py
@@ -21,6 +21,7 @@
 TILES = ROWS // TILE
 BIG = 1e30
 STEPS = 4
+SPLIT = 1664
 
 norm_eps = 1e-12
 rms_eps = 1e-06
@@ -462,6 +463,7 @@
     dimension_semantics=("arbitrary",), vmem_limit_bytes=63_000_000
 )
 GRAD_COLS = 2 * D + 4 * WIN + 128
+ALL_COLS = GRAD_COLS + D
 
 
 def attn_fwd(len_arr, tok, full, half):
@@ -478,7 +480,7 @@
                     lambda i, *_: (0, 0, 0, half),
                     pipeline_mode=pl.Buffered(1),
                 ),
-                pl.BlockSpec((HALF, D), lambda i, *_: (half, 0), pipeline_mode=pl.Buffered(1)),
+                pl.BlockSpec((HALF, D), lambda i, *_: (half, 2), pipeline_mode=pl.Buffered(1)),
             ],
             out_specs=[
                 kept((ROWS, HALF)), pair_cols(256), pair_cols(256), pair_cols(256), pair_cols(128),
@@ -510,7 +512,7 @@
                 pair_cols(256, 0), pair_cols(256, 0), pair_cols(256, 0), pair_cols(128, 0),
                 pair_cols(128, 3 * half), whole(x.shape),
                 pl.BlockSpec((ROWS, HALF), lambda i, *_: (0, half), pipeline_mode=pl.Buffered(1)),
-                pl.BlockSpec((HALF, D), lambda i, *_: (half, 0), pipeline_mode=pl.Buffered(1)),
+                pl.BlockSpec((HALF, D), lambda i, *_: (half, 2), pipeline_mode=pl.Buffered(1)),
             ],
             out_specs=[kept((SEQ // BLOCK, 2, BLOCK, HALF)), kept(part), kept(part)],
             scratch_shapes=[
@@ -618,7 +620,7 @@
 
 def pack_kernel(odd_ref, *refs):
     bias_refs, (up_bias_ref, o_ref, down_ref, q_ref, k_ref, v_ref, up_ref) = refs[:8], refs[8:15]
-    in_ref, out_ref, low_s, high_s = refs[15:]
+    out_ref, low_s, high_s = refs[15:]
     rows = o_ref.shape[0]
     odd = odd_ref[0]
     shift = lax.broadcasted_iota(jnp.int32, (192, WIN), 1) - lax.broadcasted_iota(
@@ -636,19 +638,20 @@
     out_ref[:, D : 2 * D] = down_ref[...]
     sources = ((q_ref, columns[6]), (k_ref, jnp.zeros((rows, 1), f32)), (v_ref, columns[7]))
     for which, (ref, column) in enumerate(sources):
-        in_ref[:, WIN * which : WIN * (which + 1)] = padded(ref[...], column).astype(bf16)
+        start = 2 * D + WIN * which
+        out_ref[:, start : start + WIN] = padded(ref[...], column).astype(bf16)
     up = padded(up_ref[...], column_of(up_bias_ref))
     low_s[...] = up[:, :128]
     high_s[...] = up[:, 128:]
     for j in range(4):
         for half, source in enumerate((low_s, high_s)):
-            start = 2 * D + WIN * j + 128 * half
+            start = 3 * D + WIN * j + 128 * half
             out_ref[:, start : start + 128] = source[pl.ds(j, rows, stride=4), :].astype(bf16)
     lane = lax.broadcasted_iota(jnp.int32, (rows, 128), 1)
     small = jnp.zeros((rows, 128), f32)
     for index, column in enumerate(columns[:6]):
         small = jnp.where(lane == index, column, small)
-    out_ref[:, 2 * D + 4 * WIN :] = small.astype(bf16)
+    out_ref[:, 3 * D + 4 * WIN :] = small.astype(bf16)
 
 
 def pack(odd, biases, up_bias, o_weight, down_weight, in_weights, up_weight):
@@ -662,13 +665,113 @@
             num_scalar_prefetch=1,
             grid=(1,),
             in_specs=[whole(array.shape) for array in arrays],
-            out_specs=[kept((rows, D)), kept((rows, GRAD_COLS))],
+            out_specs=[kept((rows, ALL_COLS))],
             scratch_shapes=[pltpu.VMEM((4 * rows, 128), f32)] * 2,
         ),
-        out_shape=[struct((rows, D), bf16), struct((rows, GRAD_COLS), bf16)],
+        out_shape=[struct((rows, ALL_COLS), bf16)],
         compiler_params=PARAMS,
         cost_estimate=pl.CostEstimate(flops=0, bytes_accessed=400_000, transcendentals=0),
-    )(odd.astype(jnp.int32).reshape(1), *arrays)
+    )(odd.astype(jnp.int32).reshape(1), *arrays)[0]
+
+
+def minor_of(count):
+    return max(2, count // 4)
+
+
+def spread_kernel(sizes, packed_ref, full_ref, own_sem, send_sems, recv_sems):
+    far, pair, major, minor = sizes
+    dp, fsdp = lax.axis_index("dp"), lax.axis_index("fsdp")
+    spot = (dp // 2, dp % 2, fsdp // minor, fsdp % minor)
+
+    def device(place):
+        return (place[0] * 2 + place[1], place[2] * minor + place[3])
+
+    def moved(dim, shift):
+        place = list(spot)
+        place[dim] = lax.rem(place[dim] + shift, sizes[dim])
+        return tuple(place)
+
+    barrier = pltpu.get_barrier_semaphore()
+    peers = [(dim, shift) for dim in range(4) for shift in range(1, sizes[dim])]
+    for dim, shift in peers:
+        pl.semaphore_signal(
+            barrier,
+            inc=1,
+            device_id=device(moved(dim, shift)),
+            device_id_type=pl.DeviceIdType.MESH,
+        )
+    pl.semaphore_wait(barrier, len(peers))
+
+    own = pltpu.make_async_copy(packed_ref, full_ref.at[spot], own_sem)
+    own.start()
+    orders = ((2, 3, 0, 1), (2, 0, 3, 1))
+    lanes = (pl.ds(0, SPLIT), pl.ds(SPLIT, ALL_COLS - SPLIT))
+    slot_of = {}
+
+    def copy(route, stage, shift, place, target):
+        order = orders[route]
+        gathered = order[:stage]
+        index = tuple(slice(None) if d in gathered else place[d] for d in range(4))
+        slot = slot_of.setdefault((route, stage, shift), len(slot_of))
+        region = full_ref.at[index + (slice(None), lanes[route])]
+        source = packed_ref.at[:, lanes[route]] if stage == 0 else region
+        return pltpu.make_async_remote_copy(
+            src_ref=source,
+            dst_ref=region,
+            send_sem=send_sems.at[slot],
+            recv_sem=recv_sems.at[slot],
+            device_id=device(target),
+            device_id_type=pl.DeviceIdType.MESH,
+        )
+
+    def shifts(route, stage):
+        return range(1, sizes[orders[route][stage]])
+
+    sent = []
+    for stage in range(4):
+        for route in range(2):
+            dim = orders[route][stage]
+            if stage > 0:
+                before = orders[route][stage - 1]
+                for shift in shifts(route, stage - 1):
+                    came = moved(before, sizes[before] - shift)
+                    copy(route, stage - 1, shift, came, came).wait_recv()
+            if stage == 1 and route == 0:
+                own.wait()
+            for shift in shifts(route, stage):
+                one = copy(route, stage, shift, spot, moved(dim, shift))
+                one.start()
+                sent.append(one)
+    for route in range(2):
+        for shift in shifts(route, 3):
+            came = moved(orders[route][3], sizes[orders[route][3]] - shift)
+            copy(route, 3, shift, came, came).wait_recv()
+    for one in sent:
+        one.wait_send()
+
+
+def spread(packed, dp, fsdp):
+    rows, cols = packed.shape
+    minor = minor_of(fsdp)
+    sizes = (dp // 2, 2, fsdp // minor, minor)
+    copies = 2 * sum(size - 1 for size in sizes)
+    full = pl.pallas_call(
+        functools.partial(spread_kernel, sizes),
+        name="spread",
+        in_specs=[pl.BlockSpec(memory_space=pltpu.VMEM)],
+        out_specs=pl.BlockSpec(memory_space=pltpu.HBM),
+        out_shape=struct((*sizes, rows, cols), bf16),
+        scratch_shapes=[
+            pltpu.SemaphoreType.DMA(()),
+            pltpu.SemaphoreType.DMA((copies,)),
+            pltpu.SemaphoreType.DMA((copies,)),
+        ],
+        compiler_params=pltpu.CompilerParams(
+            collective_id=0, has_side_effects=True, vmem_limit_bytes=63_000_000
+        ),
+        cost_estimate=pl.CostEstimate(flops=0, bytes_accessed=100_000_000, transcendentals=0),
+    )(packed)
+    return full.reshape(dp * fsdp * rows, cols)
 
 
 def source_of(len_ref, perm_ref, place):
@@ -799,33 +902,25 @@
         )
 
     if rows_dev % 8 == 0:
-        packed_in, packed = pack(
+        packed = pack(
             odd,
             [o_bias, norm1_gain, norm1_bias, down_bias, norm2_gain, norm2_bias, q_bias, v_bias],
             up_bias, o_weight, down_weight, [q_weight, k_weight, v_weight], up_weight,
         )
     else:
         small = [o_bias, norm1_gain, norm1_bias, down_bias, norm2_gain, norm2_bias]
-        packed_in = jnp.concatenate(
-            [
-                padded(q_weight, q_bias),
-                padded(k_weight, jnp.zeros_like(q_bias)),
-                padded(v_weight, v_bias),
-            ],
-            axis=1,
-        )
         packed = jnp.concatenate(
             [
                 o_weight,
                 down_weight,
+                padded(q_weight, q_bias),
+                padded(k_weight, jnp.zeros_like(q_bias)),
+                padded(v_weight, v_bias),
                 padded(up_weight, up_bias).reshape(rows_dev, 4 * WIN),
                 jnp.pad(jnp.stack(small, axis=1), ((0, 0), (0, 122))),
             ],
             axis=1,
         )
-    full_in = lax.all_gather(packed_in, AXES, axis=0, tiled=True)
-    packed, full_in = tie(packed, full_in)
-    full = lax.all_gather(packed, AXES, axis=0, tiled=True)
 
     dealt_lengths = pick(lengths, permutation).reshape(devices, seq_dev)
     chunks = lax.axis_size("dp")
@@ -853,26 +948,42 @@
             rows = rows.transpose(1, 0, 2, 3)
         return swap_blocks(rows).reshape(seq_total, piece_len, width)
 
-    def send_pair(partial, axis):
-        count = lax.axis_size(axis)
-        parity = lax.axis_index(axis) % 2
-        blocks = partial.reshape(count // 2, 2, partial.shape[0] // count, partial.shape[1])
-        kept_part, given = (
-            lax.dynamic_slice_in_dim(blocks, which, 1, 1) for which in (parity, 1 - parity)
-        )
-        return [kept_part, lax.ppermute(given, axis, [(i, i ^ 1) for i in range(count)])]
-
-    def send_rest(partial, axis):
-        count = lax.axis_size(axis)
-        half = count // 2
-        place = lax.axis_index(axis) // 2
-        size = partial.shape[0] // half
-        block_of = lambda index: lax.dynamic_slice_in_dim(partial, index * size, size, 0)
-        parts = [block_of(place)]
-        for shift in range(1, half):
-            target = [(i, (i + 2 * shift) % count) for i in range(count)]
-            parts.append(lax.ppermute(block_of((place + shift) % half), axis, target))
+    fsdp = lax.axis_size("fsdp")
+    minor = minor_of(fsdp)
+    major = fsdp // minor
+    place = (lax.axis_index("dp") // 2, lax.axis_index("fsdp") // minor, my_index % minor)
+
+    def target_of(device, far, high, low):
+        dp_index, rest = device // fsdp, device % fsdp
+        dp_index = (dp_index + 2 * far) % chunks
+        rest = (rest // minor + high) % major * minor + (rest % minor + low) % minor
+        return dp_index * fsdp + rest
+
+    def send_blocks(partial, shifts, block_of):
+        parts = [block_of(0, 0, 0)]
+        for shift in shifts:
+            route = [(i, target_of(i, *shift)) for i in range(devices)]
+            parts.append(lax.ppermute(block_of(*shift), AXES, route))
         return parts
+
+    def send_near(partial):
+        shape = (chunks // 2, major, minor, rows_dev, partial.shape[-1])
+        blocks = partial.reshape(shape)
+
+        def block_of(far, high, low):
+            start = ((place[0] + far) % shape[0], 0, (place[2] + low) % minor, 0, 0)
+            return lax.dynamic_slice(blocks, start, (1, major, 1, *shape[3:]))
+
+        shifts = [(far, 0, low) for far in range(shape[0]) for low in range(minor)][1:]
+        return send_blocks(blocks, shifts, block_of)
+
+    def send_far(partial):
+        blocks = partial.reshape(major, rows_dev, partial.shape[-1])
+
+        def block_of(far, high, low):
+            return lax.dynamic_index_in_dim(blocks, (place[1] + high) % major, 0, False)
+
+        return send_blocks(blocks, [(0, high, 0) for high in range(1, major)], block_of)
 
     def total(parts):
         result = sum(part.astype(f32) for part in parts)
@@ -882,13 +993,18 @@
         return total(parts).astype(bf16)
 
     tok = arrive(deal(tokens, lengths, permutation))
-    dealt_cot, tok = tie(deal(cotangent, lengths, permutation), tok)
+    packed, dealt_cot = tie(packed, deal(cotangent, lengths, permutation))
+    if rows_dev % 8 == 0:
+        full = spread(packed, lax.axis_size("dp"), lax.axis_size("fsdp"))
+    else:
+        full = lax.all_gather(packed, AXES, axis=0, tiled=True)
+    dealt_cot, tok, full = tie(dealt_cot, tok, full)
     cot = arrive(dealt_cot)
 
-    x0, qa0, ka0, va0, ctx0 = attn_fwd(len_arr, tok, full_in, 0)
-    x1, qa1, ka1, va1, ctx1 = attn_fwd(len_arr, tok, full_in, 1)
-    wu = full[:, 2 * D : 2 * D + 4 * WIN].reshape(FF, WIN)
-    vecs = jnp.pad(full[:, 2 * D + 4 * WIN : 2 * D + 4 * WIN + 6].astype(f32).T, ((0, 2), (0, 0)))
+    x0, qa0, ka0, va0, ctx0 = attn_fwd(len_arr, tok, full, 0)
+    x1, qa1, ka1, va1, ctx1 = attn_fwd(len_arr, tok, full, 1)
+    wu = full[:, 3 * D : 3 * D + 4 * WIN].reshape(FF, WIN)
+    vecs = jnp.pad(full[:, 3 * D + 4 * WIN : 3 * D + 4 * WIN + 6].astype(f32).T, ((0, 2), (0, 0)))
     out, n1, n2, inv, slope, act, stat = mid_fwd(len_arr, x0, x1, ctx0, ctx1, full, wu, vecs)
     cot, out = tie(cot, out)
     back_out = leave(out)
@@ -897,16 +1013,16 @@
     )
     mine = total_low([mine, lax.ppermute(given, "dp", pairing)])
     gctx, mine = tie(gctx, mine)
-    parts = send_rest(mine, "dp")
+    parts = send_near(mine)
     ig0, dw0, given0 = attn_bwd(
-        len_arr, qa0, ka0, va0, ctx0, gctx, x0, base, full_in, 0, chunks
+        len_arr, qa0, ka0, va0, ctx0, gctx, x0, base, full, 0, chunks
     )
     ig0, dw0, given0, gctx, back_out, *parts = tie(ig0, dw0, given0, gctx, back_out, *parts)
     back0 = leave(ig0)
     given0 = lax.ppermute(given0, "dp", pairing)
-    parts = send_pair(total_low(parts), "fsdp")
+    parts = send_far(total_low(parts))
     ig1, dw1, given1 = attn_bwd(
-        len_arr, qa1, ka1, va1, ctx1, gctx, x1, base, full_in, 1, chunks
+        len_arr, qa1, ka1, va1, ctx1, gctx, x1, base, full, 1, chunks
     )
     ig1, dw0, dw1, given0, given1, back0, *parts = tie(
         ig1, dw0, dw1, given0, given1, back0, *parts
@@ -914,11 +1030,11 @@
     back1 = leave(ig1)
     given1 = lax.ppermute(given1, "dp", pairing)
     mine_in = jnp.concatenate([total_low([dw0, given0]), total_low([dw1, given1])], axis=0)
-    mine_in = total_low(send_pair(total_low(send_rest(mine_in, "dp")), "fsdp"))
-    mine = total(send_rest(jnp.concatenate([total_low(parts), mine_in], axis=1), "fsdp"))
-    mine_in = mine[:, GRAD_COLS:]
-
-    back_out, stat, dealt_lengths, mine = tie(back_out, stat, dealt_lengths, mine)
+    parts_in = send_near(mine_in)
+    back_out, stat, dealt_lengths, *parts = tie(back_out, stat, dealt_lengths, *parts)
+    mine = total(parts)
+    mine_in = total(send_far(total_low(parts_in)))
+
     swap = dealt_lengths[:, 0] < dealt_lengths[:, 1]
     my_swap = lax.dynamic_index_in_dim(swap, my_index, 0, False)
     output = restore([back_out], lengths, permutation)

time: 426 us -> 408 us (0.958)
  waiting for transfers between devices: 159 us -> 27.8 us
  Pallas kernels: 191 us -> 297 us
  starting transfers between devices: 28.2 us -> 47.2 us
  between operations: 15.2 us -> 2.03 us
    pallas_call x0 -> x1, Pallas kernels: none -> 107 us  [spread(): pl.pallas_call(functools.partial(spread_kernel, sizes), name='spread', in...]
    all_gather x2 -> x0, waiting for transfers between devices: 105 us -> none  [the longest x1 76.9 us: on_device(): full_in = lax.all_gather(packed_in, AXES, axis=0, tiled=True)]
    ppermute x7 -> x12, waiting for transfers between devices: 46.6 us -> 23.4 us  [send_blocks(): parts.append(lax.ppermute(block_of(*shift), AXES, route))]
    ppermute x7 -> x12, starting transfers between devices: 6.21 us -> 15.8 us  [send_blocks(): parts.append(lax.ppermute(block_of(*shift), AXES, route))]
    all_to_all x5, starting transfers between devices: 21.8 us -> 30.7 us  [swap_blocks(): return lax.all_to_all(rows, AXES, split_axis=0, concat_axis=0, tiled=True)]
  transfers between devices with their start and end apart: 17 -> 20, of which waited for: 9 -> 6; matrix products, arithmetic and copies ran while one was open for 6% -> 7% of each run, Pallas kernels for 43% -> 71%
where the time goes in v7:
time: 408 us; the launch traced here: 406 us
  Pallas kernels  297 us (73%)
  starting transfers between devices  47.2 us (12%)
  waiting for transfers between devices  27.8 us (7%)
  local copies, waits for them, and re-layouts  18.6 us (5%)
  other arithmetic  13.2 us (3%)
    pallas_call x1, Pallas kernels, spread(): pl.pallas_call(functools.partial(spread_kernel, sizes), name='spread', in...  107 us
    pallas_call x2, Pallas kernels, attn_bwd(): pl.pallas_call(attn_bwd_kernel, name='attn_bwd', grid_spec=pltpu.Prefetch...  68 us
    pallas_call x2, Pallas kernels, attn_fwd(): pl.pallas_call(attn_fwd_kernel, name='attn_fwd', grid_spec=pltpu.Prefetch...  50.9 us
    pallas_call x1, Pallas kernels, mid_bwd(): pl.pallas_call(mid_bwd_kernel, name='mid_bwd', grid_spec=pltpu.PrefetchSc...  32.6 us
    all_to_all x5, starting transfers between devices, swap_blocks(): return lax.all_to_all(rows, AXES, split_axis=0, concat_axis=0, tiled=True)  30.7 us
    ppermute x12, waiting for transfers between devices, send_blocks(): parts.append(lax.ppermute(block_of(*shift), AXES, route))  23.4 us
    pallas_call x1, Pallas kernels, mid_fwd(): pl.pallas_call(mid_fwd_kernel, name='mid_fwd', grid_spec=pltpu.PrefetchSc...  20 us
    pallas_call x4, Pallas kernels, moved_call(): pl.pallas_call(kernel, name=name, grid_spec=pltpu.PrefetchScalarGridSpec(...  17.2 us
  transfers between devices with their start and end apart: 20, of which 6 were waited for; matrix products, arithmetic and copies ran while one was open for 7% of the time, Pallas kernels for 71%

profile of v7, /device:TPU:0, one launch (start us, length us, event | category | flops | bytes accessed | tf_op | source)
XLA Modules:
  0.0 406.3 jit_solution(1353169900158192556)
XLA Ops:
  0.7 3.7 deal.3
  4.4 7.3 %all-to-all-start = ((bf16[32,2,32,768]{3,2,1,0:T(8,128)(2,1)}), bf16[32,2,32,768]{3,2,1,0:T(8,128)(2,1)S(1)}, u32[]{:S(2)}, u32[]{:S(2)}) async-start(bf16[32,2,32,768]{3,2,1,0:T(8,128)(2,1)} %bitcast.55), calls=%async_computation | async-start | bytes 6291456 | tf_op jit(solution)/shard_map/all_to_all | solution.py:934
  11.7 3.7 deal.2
  15.4 1.9 pack.1.packed_ref
  17.3 106.9 %spread.1 = bf16[2,2,4,2,24,3456]{5,4,3,2,1,0:T(8,128)(2,1)} custom-call(bf16[24,3456]{1,0:T(8,128)(2,1)} %pack.1.packed_ref), custom_call_target="tpu_custom_call" | custom-call | bytes 100000000 | tf_op jit(solution)/shard_map/spread/pallas_call | solution.py:758
  124.3 1.6 copy-done.4
  125.9 5.5 %all-to-all-start.1 = ((bf16[32,2,32,768]{3,2,1,0:T(8,128)(2,1)}), bf16[32,2,32,768]{3,2,1,0:T(8,128)(2,1)S(1)}, u32[]{:S(2)}, u32[]{:S(2)}) async-start(bf16[32,2,32,768]{3,2,1,0:T(8,128)(2,1)} %bitcast.14), calls=%async_computation.1 | async-start | bytes 6291456 | tf_op jit(solution)/shard_map/all_to_all | solution.py:934
  134.3 2.7 slice.101
  137.0 3.7 reshape.141.wu_ref
  142.4 25.6 %attn_fwd.2 = (bf16[1088,384]{1,0:T(8,128)(2,1)}, bf16[1088,768]{1,0:T(8,128)(2,1)}, bf16[1088,768]{1,0:T(8,128)(2,1)}, bf16[1088,768]{1,0:T(8,128)(2,1)}, bf16[1088,384]{1,0:T(8,128)(2,1)}) custom-call(s32[2]{0:T(128)} %pad_add_fusion.len_ref, bf16[32,2,32,768]{3,2,1,0:T(8,128)(2,1)} %copy-done.4, bf16[768,3456]{1,0:T(8,128)(2,1)} %bitcast.48), custom_call_target="tpu_custom_call" | custom-call | flops 20000000000 | bytes 12000000 | tf_op jit(solution)/shard_map/attn_fwd/pallas_call | solution.py:471
  168.0 25.3 %attn_fwd.3 = (bf16[1088,384]{1,0:T(8,128)(2,1)}, bf16[1088,768]{1,0:T(8,128)(2,1)}, bf16[1088,768]{1,0:T(8,128)(2,1)}, bf16[1088,768]{1,0:T(8,128)(2,1)}, bf16[1088,384]{1,0:T(8,128)(2,1)}) custom-call(s32[2]{0:T(128)} %pad_add_fusion.len_ref, bf16[32,2,32,768]{3,2,1,0:T(8,128)(2,1)} %copy-done.4, bf16[768,3456]{1,0:T(8,128)(2,1)} %bitcast.49), custom_call_target="tpu_custom_call" | custom-call | flops 20000000000 | bytes 12000000 | tf_op jit(solution)/shard_map/attn_fwd/pallas_call | solution.py:471
  193.3 20.0 %mid_fwd.1 = (bf16[32,2,32,768]{3,2,1,0:T(8,128)(2,1)}, f32[1088,768]{1,0:T(8,128)}, f32[1088,768]{1,0:T(8,128)}, f32[1088,128]{1,0:T(8,128)}, f32[1088,3072]{1,...) custom-call(s32[2]{0:T(128)} %pad_add_fusion.len_ref, bf16[1088,384]{1,0:T(8,128)(2,1)} %get-tuple-element.89.x0_ref.x_ref, ...), custom_call_target="tpu_custom_call" | custom-call | flops 15000000512 | bytes 36000000 | tf_op jit(solution)/shard_map/mid_fwd/pallas_call | solution.py:548
  213.4 1.7 copy-done.2
  215.0 6.0 %all-to-all-start.2 = ((bf16[32,2,32,768]{3,2,1,0:T(8,128)(2,1)}), bf16[32,2,32,768]{3,2,1,0:T(8,128)(2,1)S(1)}, u32[]{:S(2)}, u32[]{:S(2)}) async-start(bf16[32,2,32,768]{3,2,1,0:T(8,128)(2,1)} %get-tuple-element.107), calls=%async_computation.2 | async-start | bytes 6291456 | tf_op jit(solution)/shard_map/all_to_all | solution.py:934
  221.1 32.6 %mid_bwd.1 = (bf16[1088,768]{1,0:T(8,128)(2,1)}, f32[1088,768]{1,0:T(8,128)}, bf16[2,192,2688]{2,1,0:T(8,128)(2,1)}, bf16[2,192,2688]{2,1,0:T(8,128)(2,1)}) custom-call(s32[2]{0:T(128)} %pad_add_fusion.len_ref, bf16[32,2,32,768]{3,2,1,0:T(8,128)(2,1)} %copy-done.2, bf16[1088,384]{1,0:T(8,128)(2,1)} %get-tuple-element.87.ctx0_ref.ctx_ref, ...), custom_call_target="tpu_custom_call" | custom-call | flops 100000000 | bytes 1000000 | tf_op jit(solution)/shard_map/mid_bwd/pallas_call | solution.py:577
  253.9 4.3 %collective-permute-done = bf16[2,192,2688]{2,1,0:T(8,128)(2,1)} collective-permute-done((bf16[2,192,2688]{2,1,0:T(8,128)(2,1)}, bf16[2,192,2688]{2,1,0:T(8,128)(2,1)}, u32[]{:S(2)}, u32[]{:S(2)}) %collective-permute-start) | collective-permute-done | bytes 2064416 | tf_op jit(solution)/shard_map/ppermute | solution.py:1014
  258.2 2.7 add_convert_fusion
  262.3 1.6 collective-permute-start.1
  265.8 34.1 %attn_bwd.2 = (bf16[32,2,32,384]{3,2,1,0:T(8,128)(2,1)}, bf16[1,192,768]{2,1,0:T(8,128)(2,1)}, bf16[1,192,768]{2,1,0:T(8,128)(2,1)}) custom-call(s32[2]{0:T(128)} %pad_add_fusion.len_ref, bf16[1088,768]{1,0:T(8,128)(2,1)} %get-tuple-element.84.qa_ref, bf16[1088,768]{1,0:T(8,128)(2,1)} %get-tuple-element.85.ka_ref, ...), custom_call_target="tpu_custom_call" | custom-call | flops 100000000 | bytes 1000000 | tf_op jit(solution)/shard_map/attn_bwd/pallas_call | solution.py:505
  299.9 5.8 %all-to-all-start.3 = ((bf16[32,2,32,384]{3,2,1,0:T(8,128)(2,1)}), bf16[32,2,32,384]{3,2,1,0:T(8,128)(2,1)}, u32[]{:S(2)}, u32[]{:S(2)}) async-start(bf16[32,2,32,384]{3,2,1,0:T(8,128)(2,1)} %get-tuple-element.120), calls=%async_computation.3 | async-start | bytes 3145728 | tf_op jit(solution)/shard_map/all_to_all | solution.py:934
  306.1 1.8 add_convert_fusion.1
  308.6 1.6 collective-permute-start.5
  310.2 2.4 collective-permute-start.6
  315.4 33.9 %attn_bwd.3 = (bf16[32,2,32,384]{3,2,1,0:T(8,128)(2,1)}, bf16[1,192,768]{2,1,0:T(8,128)(2,1)}, bf16[1,192,768]{2,1,0:T(8,128)(2,1)}) custom-call(s32[2]{0:T(128)} %pad_add_fusion.len_ref, bf16[1088,768]{1,0:T(8,128)(2,1)} %get-tuple-element.111.qa_ref, bf16[1088,768]{1,0:T(8,128)(2,1)} %get-tuple-element.112.ka_ref, ...), custom_call_target="tpu_custom_call" | custom-call | flops 100000000 | bytes 1000000 | tf_op jit(solution)/shard_map/attn_bwd/pallas_call | solution.py:505
  349.3 2.6 collective-permute-done.6
  351.9 6.0 %all-to-all-start.4 = ((bf16[32,2,32,384]{3,2,1,0:T(8,128)(2,1)}), bf16[32,2,32,384]{3,2,1,0:T(8,128)(2,1)S(1)}, u32[]{:S(2)}, u32[]{:S(2)}) async-start(bf16[32,2,32,384]{3,2,1,0:T(8,128)(2,1)} %get-tuple-element.131), calls=%async_computation.4 | async-start | bytes 3145728 | tf_op jit(solution)/shard_map/all_to_all | solution.py:934
  363.0 2.6 collective-permute-start.11
  368.0 13.2 %collective-permute-done.11 = bf16[1,4,1,24,768]{4,3,2,1,0:T(8,128)(2,1)S(1)} collective-permute-done((bf16[1,4,1,24,768]{4,3,2,1,0:T(8,128)(2,1)S(1)}, bf16[1,4,1,24,768]{4,3,2,1,0:T(8,128)(2,1)S(1)}, u32[]{:S(2)}, u32[]{:S(2)}) %collective-permute-start.11) | collective-permute-done | bytes 147488 | tf_op jit(solution)/shard_map/ppermute | solution.py:966
  382.9 2.7 collective-permute-start.14
  387.0 4.9 %restore.2 = bf16[64,32,768]{2,1,0:T(8,128)(2,1)} custom-call(s32[64]{0:T(128)} %len_ref.7, s32[64]{0:T(128)} %perm_ref.7, bf16[64,32,768]{2,1,0:T(8,128)(2,1)} %bitcast.54), custom_call_target="tpu_custom_call" | custom-call | bytes 100000 | tf_op jit(solution)/shard_map/restore/pallas_call | solution.py:829
  392.5 6.0 %collective-permute-done.13 = bf16[24,768]{1,0:T(8,128)(2,1)S(1)} collective-permute-done((bf16[24,768]{1,0:T(8,128)(2,1)S(1)}, bf16[24,768]{1,0:T(8,128)(2,1)S(1)}, u32[]{:S(2)}, u32[]{:S(2)}) %collective-permute-start.13) | collective-permute-done | bytes 36896 | tf_op jit(solution)/shard_map/ppermute | solution.py:966
  401.1 4.9 %restore.3 = bf16[64,32,768]{2,1,0:T(8,128)(2,1)} custom-call(s32[64]{0:T(128)} %len_ref.7, s32[64]{0:T(128)} %perm_ref.7, bf16[64,32,384]{2,1,0:T(8,128)(2,1)} %bitcast.19.refs_0_, bf16[64,32,384]{2,1,0:T(8,128)(2,1)} %bitcast.57), custom_call_target="tpu_custom_call" | custom-call | bytes 100000 | tf_op jit(solution)/shard_map/restore/pallas_call | solution.py:829
  (78 shorter events, 24.9 us)
Async XLA Ops:
  4.4 119.9 %all-to-all-start = ((bf16[32,2,32,768]{3,2,1,0:T(8,128)(2,1)}), bf16[32,2,32,768]{3,2,1,0:T(8,128)(2,1)S(1)}, u32[]{:S(2)}, u32[]{:S(2)}) async-start(bf16[32,2,32,768]{3,2,1,0:T(8,128)(2,1)} %bitcast.55), calls=%async_computation | async-start | bytes 6291456 | tf_op jit(solution)/shard_map/all_to_all | solution.py:934
  124.2 1.7 copy-start.4
  124.2 7.2 %copy-start.7 = (s32[64]{0:T(128)S(1)}, s32[64]{0:T(128)}, u32[]{:S(2)}) copy-start(s32[64]{0:T(128)} %perm_ref.7) | copy-start | bytes 772
  124.3 7.2 %copy-start = (s32[64]{0:T(128)S(1)}, s32[64]{0:T(128)}, u32[]{:S(2)}) copy-start(s32[64]{0:T(128)} %len_ref.7) | copy-start | bytes 772
  125.9 87.5 %all-to-all-start.1 = ((bf16[32,2,32,768]{3,2,1,0:T(8,128)(2,1)}), bf16[32,2,32,768]{3,2,1,0:T(8,128)(2,1)S(1)}, u32[]{:S(2)}, u32[]{:S(2)}) async-start(bf16[32,2,32,768]{3,2,1,0:T(8,128)(2,1)} %bitcast.14), calls=%async_computation.1 | async-start | bytes 6291456 | tf_op jit(solution)/shard_map/all_to_all | solution.py:934
  213.4 1.7 copy-start.2
  215.0 84.9 %all-to-all-start.2 = ((bf16[32,2,32,768]{3,2,1,0:T(8,128)(2,1)}), bf16[32,2,32,768]{3,2,1,0:T(8,128)(2,1)S(1)}, u32[]{:S(2)}, u32[]{:S(2)}) async-start(bf16[32,2,32,768]{3,2,1,0:T(8,128)(2,1)} %get-tuple-element.107), calls=%async_computation.2 | async-start | bytes 6291456 | tf_op jit(solution)/shard_map/all_to_all | solution.py:934
  253.7 4.5 %collective-permute-start = (bf16[2,192,2688]{2,1,0:T(8,128)(2,1)}, bf16[2,192,2688]{2,1,0:T(8,128)(2,1)}, u32[]{:S(2)}, u32[]{:S(2)}) collective-permute-start(bf16[2,192,2688]{2,1,0:T(8,128)(2,1)} %get-tuple-element.101), channel_id=1, source_target_pairs={{0,8},{8,0},{16,24},{24,16},{1,9},{9,1},{17,25},{25,17},{2,10},{10... | collective-permute-start | bytes 6193160 | tf_op jit(solution)/shard_map/ppermute | solution.py:1014
  262.3 37.6 %collective-permute-start.1 = (bf16[1,4,1,24,2688]{4,3,2,1,0:T(8,128)(2,1)}, bf16[1,4,1,24,2688]{4,3,2,1,0:T(8,128)(2,1)}, u32[]{:S(2)}, u32[]{:S(2)}) collective-permute-start(bf16[1,4,1,24,2688]{4,3,2,1,0:T(8,128)(2,1)} %get-tuple-element.206), channel_id=1, source_target_pairs={{0,1},{1,0},{2,3},{3,2},{4,5},{5,4},{6,7},{7,6},{8,9},{9,8},{10,11... | collective-permute-start | bytes 1548296 | tf_op jit(solution)/shard_map/ppermute | solution.py:966
  263.9 36.0 %collective-permute-start.2 = (bf16[1,4,1,24,2688]{4,3,2,1,0:T(8,128)(2,1)}, bf16[1,4,1,24,2688]{4,3,2,1,0:T(8,128)(2,1)}, u32[]{:S(2)}, u32[]{:S(2)}) collective-permute-start(bf16[1,4,1,24,2688]{4,3,2,1,0:T(8,128)(2,1)} %get-tuple-element.205), channel_id=1, source_target_pairs={{0,16},{1,17},{2,18},{3,19},{4,20},{5,21},{6,22},{7,23},{8,24},{9,... | collective-permute-start | bytes 1548296 | tf_op jit(solution)/shard_map/ppermute | solution.py:966
  265.4 34.5 %collective-permute-start.3 = (bf16[1,4,1,24,2688]{4,3,2,1,0:T(8,128)(2,1)}, bf16[1,4,1,24,2688]{4,3,2,1,0:T(8,128)(2,1)}, u32[]{:S(2)}, u32[]{:S(2)}) collective-permute-start(bf16[1,4,1,24,2688]{4,3,2,1,0:T(8,128)(2,1)} %get-tuple-element.204), channel_id=1, source_target_pairs={{0,17},{1,16},{2,19},{3,18},{4,21},{5,20},{6,23},{7,22},{8,25},{9,... | collective-permute-start | bytes 1548296 | tf_op jit(solution)/shard_map/ppermute | solution.py:966
  299.9 7.9 %copy-start.1 = (bf16[32,2,32,768]{3,2,1,0:T(8,128)(2,1)}, bf16[32,2,32,768]{3,2,1,0:T(8,128)(2,1)S(1)}, u32[]{:S(2)}) copy-start(bf16[32,2,32,768]{3,2,1,0:T(8,128)(2,1)S(1)} %all-to-all-done.2) | copy-start | bytes 9437188
  299.9 52.0 %all-to-all-start.3 = ((bf16[32,2,32,384]{3,2,1,0:T(8,128)(2,1)}), bf16[32,2,32,384]{3,2,1,0:T(8,128)(2,1)}, u32[]{:S(2)}, u32[]{:S(2)}) async-start(bf16[32,2,32,384]{3,2,1,0:T(8,128)(2,1)} %get-tuple-element.120), calls=%async_computation.3 | async-start | bytes 3145728 | tf_op jit(solution)/shard_map/all_to_all | solution.py:934
  305.8 46.1 %collective-permute-start.4 = (bf16[1,192,768]{2,1,0:T(8,128)(2,1)}, bf16[1,192,768]{2,1,0:T(8,128)(2,1)}, u32[]{:S(2)}, u32[]{:S(2)}) collective-permute-start(bf16[1,192,768]{2,1,0:T(8,128)(2,1)} %get-tuple-element.118), channel_id=1, source_target_pairs={{0,8},{8,0},{16,24},{24,16},{1,9},{9,1},{17,25},{25,17},{2,10},{10... | collective-permute-start | bytes 884744 | tf_op jit(solution)/shard_map/ppermute | solution.py:1022
  308.6 40.7 %collective-permute-start.5 = (bf16[24,2688]{1,0:T(8,128)(2,1)}, bf16[24,2688]{1,0:T(8,128)(2,1)S(1)}, u32[]{:S(2)}, u32[]{:S(2)}) collective-permute-start(bf16[24,2688]{1,0:T(8,128)(2,1)} %get-tuple-element.213), channel_id=1, source_target_pairs={{0,2},{1,3},{2,4},{3,5},{4,6},{5,7},{6,0},{7,1},{8,10},{9,11},{10,... | collective-permute-start | bytes 387080 | tf_op jit(solution)/shard_map/ppermute | solution.py:966
  310.2 41.7 %collective-permute-start.6 = (bf16[24,2688]{1,0:T(8,128)(2,1)}, bf16[24,2688]{1,0:T(8,128)(2,1)S(1)}, u32[]{:S(2)}, u32[]{:S(2)}) collective-permute-start(bf16[24,2688]{1,0:T(8,128)(2,1)} %get-tuple-element.212), channel_id=1, source_target_pairs={{0,4},{1,5},{2,6},{3,7},{4,0},{5,1},{6,2},{7,3},{8,12},{9,13},{10,... | collective-permute-start | bytes 387080 | tf_op jit(solution)/shard_map/ppermute | solution.py:966
  312.7 39.2 %collective-permute-start.7 = (bf16[24,2688]{1,0:T(8,128)(2,1)}, bf16[24,2688]{1,0:T(8,128)(2,1)S(1)}, u32[]{:S(2)}, u32[]{:S(2)}) collective-permute-start(bf16[24,2688]{1,0:T(8,128)(2,1)} %get-tuple-element.211), channel_id=1, source_target_pairs={{0,6},{1,7},{2,0},{3,1},{4,2},{5,3},{6,4},{7,5},{8,14},{9,15},{10,... | collective-permute-start | bytes 387080 | tf_op jit(solution)/shard_map/ppermute | solution.py:966
  349.3 9.0 %copy-start.8 = (f32[8,128]{1,0:T(8,128)S(1)}, f32[8,128]{1,0:T(8,128)}, u32[]{:S(2)}) copy-start(f32[8,128]{1,0:T(8,128)} %get-tuple-element.141) | copy-start | bytes 12292
  351.9 9.8 %copy-start.5 = (bf16[1,192,768]{2,1,0:T(8,128)(2,1)S(1)}, bf16[1,192,768]{2,1,0:T(8,128)(2,1)}, u32[]{:S(2)}) copy-start(bf16[1,192,768]{2,1,0:T(8,128)(2,1)} %get-tuple-element.132) | copy-start | bytes 884740
  351.9 48.0 %all-to-all-start.4 = ((bf16[32,2,32,384]{3,2,1,0:T(8,128)(2,1)}), bf16[32,2,32,384]{3,2,1,0:T(8,128)(2,1)S(1)}, u32[]{:S(2)}, u32[]{:S(2)}) async-start(bf16[32,2,32,384]{3,2,1,0:T(8,128)(2,1)} %get-tuple-element.131), calls=%async_computation.4 | async-start | bytes 3145728 | tf_op jit(solution)/shard_map/all_to_all | solution.py:934
  357.9 4.9 %copy-start.6 = (bf16[1,192,768]{2,1,0:T(8,128)(2,1)S(1)}, bf16[1,192,768]{2,1,0:T(8,128)(2,1)}, u32[]{:S(2)}) copy-start(bf16[1,192,768]{2,1,0:T(8,128)(2,1)} %get-tuple-element.134) | copy-start | bytes 884740
  357.9 4.8 %collective-permute-start.8 = (bf16[1,192,768]{2,1,0:T(8,128)(2,1)}, bf16[1,192,768]{2,1,0:T(8,128)(2,1)S(1)}, u32[]{:S(2)}, u32[]{:S(2)}) collective-permute-start(bf16[1,192,768]{2,1,0:T(8,128)(2,1)} %get-tuple-element.135), channel_id=1, source_target_pairs={{0,8},{8,0},{16,24},{24,16},{1,9},{9,1},{17,25},{25,17},{2,10},{10... | collective-permute-start | bytes 884744 | tf_op jit(solution)/shard_map/ppermute | solution.py:1031
  363.0 18.1 %collective-permute-start.11 = (bf16[1,4,1,24,768]{4,3,2,1,0:T(8,128)(2,1)S(1)}, bf16[1,4,1,24,768]{4,3,2,1,0:T(8,128)(2,1)S(1)}, u32[]{:S(2)}, u32[]{:S(2)}) collective-permute-start(bf16[1,4,1,24,768]{4,3,2,1,0:T(8,128)(2,1)S(1)} %get-tuple-element.209), channel_id=1, source_target_pairs={{0,17},{1,16},{2,19},{3,18},{4,21},{5,20},{6,23},{7,22},{8,25},{9,... | collective-permute-start | bytes 442376 | tf_op jit(solution)/shard_map/ppermute | solution.py:966
  365.6 16.9 %collective-permute-start.10 = (bf16[1,4,1,24,768]{4,3,2,1,0:T(8,128)(2,1)S(1)}, bf16[1,4,1,24,768]{4,3,2,1,0:T(8,128)(2,1)S(1)}, u32[]{:S(2)}, u32[]{:S(2)}) collective-permute-start(bf16[1,4,1,24,768]{4,3,2,1,0:T(8,128)(2,1)S(1)} %get-tuple-element.210), channel_id=1, source_target_pairs={{0,16},{1,17},{2,18},{3,19},{4,20},{5,21},{6,22},{7,23},{8,24},{9,... | collective-permute-start | bytes 442376 | tf_op jit(solution)/shard_map/ppermute | solution.py:966
  366.1 16.6 %collective-permute-start.9 = (bf16[1,4,1,24,768]{4,3,2,1,0:T(8,128)(2,1)S(1)}, bf16[1,4,1,24,768]{4,3,2,1,0:T(8,128)(2,1)S(1)}, u32[]{:S(2)}, u32[]{:S(2)}) collective-permute-start(bf16[1,4,1,24,768]{4,3,2,1,0:T(8,128)(2,1)S(1)} %get-tuple-element.208), channel_id=1, source_target_pairs={{0,1},{1,0},{2,3},{3,2},{4,5},{5,4},{6,7},{7,6},{8,9},{9,8},{10,11... | collective-permute-start | bytes 442376 | tf_op jit(solution)/shard_map/ppermute | solution.py:966
  382.9 9.6 %collective-permute-start.14 = (bf16[24,768]{1,0:T(8,128)(2,1)S(1)}, bf16[24,768]{1,0:T(8,128)(2,1)S(1)}, u32[]{:S(2)}, u32[]{:S(2)}) collective-permute-start(bf16[24,768]{1,0:T(8,128)(2,1)S(1)} %get-tuple-element.218), channel_id=1, source_target_pairs={{0,6},{1,7},{2,0},{3,1},{4,2},{5,3},{6,4},{7,5},{8,14},{9,15},{10,... | collective-permute-start | bytes 110600 | tf_op jit(solution)/shard_map/ppermute | solution.py:966
  385.5 13.0 %collective-permute-start.13 = (bf16[24,768]{1,0:T(8,128)(2,1)S(1)}, bf16[24,768]{1,0:T(8,128)(2,1)S(1)}, u32[]{:S(2)}, u32[]{:S(2)}) collective-permute-start(bf16[24,768]{1,0:T(8,128)(2,1)S(1)} %get-tuple-element.219), channel_id=1, source_target_pairs={{0,4},{1,5},{2,6},{3,7},{4,0},{5,1},{6,2},{7,3},{8,12},{9,13},{10,... | collective-permute-start | bytes 110600 | tf_op jit(solution)/shard_map/ppermute | solution.py:966
  385.5 13.0 %collective-permute-start.12 = (bf16[24,768]{1,0:T(8,128)(2,1)S(1)}, bf16[24,768]{1,0:T(8,128)(2,1)S(1)}, u32[]{:S(2)}, u32[]{:S(2)}) collective-permute-start(bf16[24,768]{1,0:T(8,128)(2,1)S(1)} %get-tuple-element.217), channel_id=1, source_target_pairs={{0,2},{1,3},{2,4},{3,5},{4,6},{5,7},{6,0},{7,1},{8,10},{9,11},{10,... | collective-permute-start | bytes 110600 | tf_op jit(solution)/shard_map/ppermute | solution.py:966
  400.0 1.2 copy-start.3

commit v8 on v7

--- a/solution.py
+++ b/solution.py
@@ -678,10 +678,13 @@
     return max(2, count // 4)
 
 
-def spread_kernel(sizes, packed_ref, full_ref, own_sem, send_sems, recv_sems):
-    far, pair, major, minor = sizes
+def spread_kernel(sizes, orders, lanes, *refs):
+    held_ref, full_ref, own_sem, send_sems, recv_sems = refs
+    minor = sizes[3]
     dp, fsdp = lax.axis_index("dp"), lax.axis_index("fsdp")
     spot = (dp // 2, dp % 2, fsdp // minor, fsdp % minor)
+    done = (2,) if 2 not in orders[0] else ()
+    lead = 4 if done else 1
 
     def device(place):
         return (place[0] * 2 + place[1], place[2] * minor + place[3])
@@ -691,8 +694,12 @@
         place[dim] = lax.rem(place[dim] + shift, sizes[dim])
         return tuple(place)
 
+    def region(place, gathered):
+        index = tuple(slice(None) if d in gathered else place[d] for d in range(4))
+        return index if lead == 4 else (index[2],)
+
     barrier = pltpu.get_barrier_semaphore()
-    peers = [(dim, shift) for dim in range(4) for shift in range(1, sizes[dim])]
+    peers = [(dim, shift) for dim in orders[0] for shift in range(1, sizes[dim])]
     for dim, shift in peers:
         pl.semaphore_signal(
             barrier,
@@ -700,24 +707,22 @@
             device_id=device(moved(dim, shift)),
             device_id_type=pl.DeviceIdType.MESH,
         )
+    own = pltpu.make_async_copy(held_ref, full_ref.at[region(spot, done)], own_sem)
+    own.start()
     pl.semaphore_wait(barrier, len(peers))
-
-    own = pltpu.make_async_copy(packed_ref, full_ref.at[spot], own_sem)
-    own.start()
-    orders = ((2, 3, 0, 1), (2, 0, 3, 1))
-    lanes = (pl.ds(0, SPLIT), pl.ds(SPLIT, ALL_COLS - SPLIT))
     slot_of = {}
 
     def copy(route, stage, shift, place, target):
-        order = orders[route]
-        gathered = order[:stage]
-        index = tuple(slice(None) if d in gathered else place[d] for d in range(4))
+        gathered = done + orders[route][:stage]
         slot = slot_of.setdefault((route, stage, shift), len(slot_of))
-        region = full_ref.at[index + (slice(None), lanes[route])]
-        source = packed_ref.at[:, lanes[route]] if stage == 0 else region
+        window = full_ref.at[region(place, gathered)]
+        window = window.at[(slice(None),) * (len(window.shape) - 1) + (lanes[route],)]
+        source = window
+        if stage == 0:
+            source = held_ref.at[(slice(None),) * (len(held_ref.shape) - 1) + (lanes[route],)]
         return pltpu.make_async_remote_copy(
             src_ref=source,
-            dst_ref=region,
+            dst_ref=window,
             send_sem=send_sems.at[slot],
             recv_sem=recv_sems.at[slot],
             device_id=device(target),
@@ -727,51 +732,68 @@
     def shifts(route, stage):
         return range(1, sizes[orders[route][stage]])
 
+    def arrived(route, stage):
+        dim = orders[route][stage]
+        for shift in shifts(route, stage):
+            came = moved(dim, sizes[dim] - shift)
+            copy(route, stage, shift, came, came).wait_recv()
+
     sent = []
-    for stage in range(4):
-        for route in range(2):
-            dim = orders[route][stage]
+    for stage in range(len(orders[0])):
+        for route, order in enumerate(orders):
             if stage > 0:
-                before = orders[route][stage - 1]
-                for shift in shifts(route, stage - 1):
-                    came = moved(before, sizes[before] - shift)
-                    copy(route, stage - 1, shift, came, came).wait_recv()
+                arrived(route, stage - 1)
             if stage == 1 and route == 0:
                 own.wait()
             for shift in shifts(route, stage):
-                one = copy(route, stage, shift, spot, moved(dim, shift))
+                one = copy(route, stage, shift, spot, moved(order[stage], shift))
                 one.start()
                 sent.append(one)
-    for route in range(2):
-        for shift in shifts(route, 3):
-            came = moved(orders[route][3], sizes[orders[route][3]] - shift)
-            copy(route, 3, shift, came, came).wait_recv()
+    if len(orders[0]) == 1:
+        own.wait()
+    for route in range(len(orders)):
+        arrived(route, len(orders[0]) - 1)
     for one in sent:
         one.wait_send()
 
 
-def spread(packed, dp, fsdp):
-    rows, cols = packed.shape
-    minor = minor_of(fsdp)
-    sizes = (dp // 2, 2, fsdp // minor, minor)
-    copies = 2 * sum(size - 1 for size in sizes)
-    full = pl.pallas_call(
-        functools.partial(spread_kernel, sizes),
+def spread_call(held, sizes, orders, lanes, shape, space, identity):
+    copies = len(orders) * sum(sizes[dim] - 1 for dim in orders[0])
+    return pl.pallas_call(
+        functools.partial(spread_kernel, sizes, orders, lanes),
         name="spread",
         in_specs=[pl.BlockSpec(memory_space=pltpu.VMEM)],
-        out_specs=pl.BlockSpec(memory_space=pltpu.HBM),
-        out_shape=struct((*sizes, rows, cols), bf16),
+        out_specs=pl.BlockSpec(memory_space=space),
+        out_shape=struct(shape, bf16),
         scratch_shapes=[
             pltpu.SemaphoreType.DMA(()),
             pltpu.SemaphoreType.DMA((copies,)),
             pltpu.SemaphoreType.DMA((copies,)),
         ],
         compiler_params=pltpu.CompilerParams(
-            collective_id=0, has_side_effects=True, vmem_limit_bytes=63_000_000
+            collective_id=identity, has_side_effects=True, vmem_limit_bytes=63_000_000
         ),
         cost_estimate=pl.CostEstimate(flops=0, bytes_accessed=100_000_000, transcendentals=0),
-    )(packed)
-    return full.reshape(dp * fsdp * rows, cols)
+    )(held)
+
+
+def sizes_of(dp, fsdp):
+    minor = minor_of(fsdp)
+    return (dp // 2, 2, fsdp // minor, minor)
+
+
+def spread_far(packed, sizes):
+    whole_lanes = (pl.ds(0, packed.shape[1]),)
+    shape = (sizes[2], *packed.shape)
+    return spread_call(packed, sizes, ((2,),), whole_lanes, shape, pltpu.VMEM, 0)
+
+
+def spread_near(held, sizes):
+    _, rows, cols = held.shape
+    lanes = (pl.ds(0, SPLIT), pl.ds(SPLIT, cols - SPLIT))
+    orders = ((3, 0, 1), (0, 3, 1))
+    full = spread_call(held, sizes, orders, lanes, (*sizes, rows, cols), pltpu.HBM, 1)
+    return full.reshape(-1, cols)
 
 
 def source_of(len_ref, perm_ref, place):
@@ -992,19 +1014,26 @@
     def total_low(parts):
         return total(parts).astype(bf16)
 
-    tok = arrive(deal(tokens, lengths, permutation))
-    packed, dealt_cot = tie(packed, deal(cotangent, lengths, permutation))
+    dealt_tok = deal(tokens, lengths, permutation)
+    dealt_cot = deal(cotangent, lengths, permutation)
     if rows_dev % 8 == 0:
-        full = spread(packed, lax.axis_size("dp"), lax.axis_size("fsdp"))
+        sizes = sizes_of(chunks, lax.axis_size("fsdp"))
+        packed, dealt_tok = tie(packed, dealt_tok)
+        held = spread_far(packed, sizes)
+        dealt_tok, held = tie(dealt_tok, held)
+        tok = arrive(dealt_tok)
+        held, dealt_cot = tie(held, dealt_cot)
+        full = spread_near(held, sizes)
     else:
+        tok = arrive(dealt_tok)
         full = lax.all_gather(packed, AXES, axis=0, tiled=True)
-    dealt_cot, tok, full = tie(dealt_cot, tok, full)
+    wu = full[:, 3 * D : 3 * D + 4 * WIN].reshape(FF, WIN)
+    vecs = jnp.pad(full[:, 3 * D + 4 * WIN : 3 * D + 4 * WIN + 6].astype(f32).T, ((0, 2), (0, 0)))
+    dealt_cot, tok, full, wu, vecs, len_arr = tie(dealt_cot, tok, full, wu, vecs, len_arr)
     cot = arrive(dealt_cot)
 
     x0, qa0, ka0, va0, ctx0 = attn_fwd(len_arr, tok, full, 0)
     x1, qa1, ka1, va1, ctx1 = attn_fwd(len_arr, tok, full, 1)
-    wu = full[:, 3 * D : 3 * D + 4 * WIN].reshape(FF, WIN)
-    vecs = jnp.pad(full[:, 3 * D + 4 * WIN : 3 * D + 4 * WIN + 6].astype(f32).T, ((0, 2), (0, 0)))
     out, n1, n2, inv, slope, act, stat = mid_fwd(len_arr, x0, x1, ctx0, ctx1, full, wu, vecs)
     cot, out = tie(cot, out)
     back_out = leave(out)

time: 408 us -> 381 us (0.934)
  Pallas kernels: 297 us -> 269 us
  local copies, waits for them, and re-layouts: 18.6 us -> 13.6 us
    pallas_call x1 -> x2, Pallas kernels: 107 us -> 78.6 us  [spread_call(): pl.pallas_call(functools.partial(spread_kernel, sizes, orders, lanes), na...]
  transfers between devices with their start and end apart: 20 -> 20, of which waited for: 6 -> 8; matrix products, arithmetic and copies ran while one was open for 7% -> 6% of each run, Pallas kernels for 71% -> 63%
where the time goes in v8:
time: 381 us; the launch traced here: 380 us
  Pallas kernels  269 us (71%)
  starting transfers between devices  51.2 us (13%)
  waiting for transfers between devices  30.6 us (8%)
  local copies, waits for them, and re-layouts  13.6 us (4%)
  other arithmetic  13.2 us (3%)
    pallas_call x2, Pallas kernels, spread_call(): pl.pallas_call(functools.partial(spread_kernel, sizes, orders, lanes), na...  78.6 us
    pallas_call x2, Pallas kernels, attn_bwd(): pl.pallas_call(attn_bwd_kernel, name='attn_bwd', grid_spec=pltpu.Prefetch...  68 us
    pallas_call x2, Pallas kernels, attn_fwd(): pl.pallas_call(attn_fwd_kernel, name='attn_fwd', grid_spec=pltpu.Prefetch...  50.9 us
    all_to_all x5, starting transfers between devices, swap_blocks(): return lax.all_to_all(rows, AXES, split_axis=0, concat_axis=0, tiled=True)  34.7 us
    pallas_call x1, Pallas kernels, mid_bwd(): pl.pallas_call(mid_bwd_kernel, name='mid_bwd', grid_spec=pltpu.PrefetchSc...  32.6 us
    ppermute x12, waiting for transfers between devices, send_blocks(): parts.append(lax.ppermute(block_of(*shift), AXES, route))  24.1 us
    pallas_call x1, Pallas kernels, mid_fwd(): pl.pallas_call(mid_fwd_kernel, name='mid_fwd', grid_spec=pltpu.PrefetchSc...  20 us
    pallas_call x4, Pallas kernels, moved_call(): pl.pallas_call(kernel, name=name, grid_spec=pltpu.PrefetchScalarGridSpec(...  17.2 us
  transfers between devices with their start and end apart: 20, of which 8 were waited for; matrix products, arithmetic and copies ran while one was open for 6% of the time, Pallas kernels for 63%

profile of v8, /device:TPU:0, one launch (start us, length us, event | category | flops | bytes accessed | tf_op | source)
XLA Modules:
  0.0 379.7 jit_solution(17459637766734788441)
XLA Ops:
  0.7 3.7 deal.2
  4.4 1.9 pack.1.refs_0_
  6.3 18.6 %spread.2.refs_0_ = bf16[4,24,3456]{2,1,0:T(8,128)(2,1)} custom-call(bf16[24,3456]{1,0:T(8,128)(2,1)} %pack.1.refs_0_), custom_call_target="tpu_custom_call" | custom-call | bytes 100000000 | tf_op jit(solution)/shard_map/spread/pallas_call | solution.py:762
  24.8 8.2 %all-to-all-start = ((bf16[32,2,32,768]{3,2,1,0:T(8,128)(2,1)}), bf16[32,2,32,768]{3,2,1,0:T(8,128)(2,1)}, u32[]{:S(2)}, u32[]{:S(2)}) async-start(bf16[32,2,32,768]{3,2,1,0:T(8,128)(2,1)} %bitcast.55), calls=%async_computation | async-start | bytes 6291456 | tf_op jit(solution)/shard_map/all_to_all | solution.py:956
  33.1 3.7 deal.3
  36.8 60.0 %spread.3 = bf16[2,2,4,2,24,3456]{5,4,3,2,1,0:T(8,128)(2,1)} custom-call(bf16[4,24,3456]{2,1,0:T(8,128)(2,1)} %spread.2.refs_0_), custom_call_target="tpu_custom_call" | custom-call | bytes 100000000 | tf_op jit(solution)/shard_map/spread/pallas_call | solution.py:762
  96.8 1.5 slice.137
  98.4 2.3 reshape.141.wu_ref
  105.7 9.5 %all-to-all-start.1 = ((bf16[32,2,32,768]{3,2,1,0:T(8,128)(2,1)}), bf16[32,2,32,768]{3,2,1,0:T(8,128)(2,1)S(1)}, u32[]{:S(2)}, u32[]{:S(2)}) async-start(bf16[32,2,32,768]{3,2,1,0:T(8,128)(2,1)} %bitcast.15), calls=%async_computation.1 | async-start | bytes 6291456 | tf_op jit(solution)/shard_map/all_to_all | solution.py:956
  115.9 25.4 %attn_fwd.2 = (bf16[1088,384]{1,0:T(8,128)(2,1)}, bf16[1088,768]{1,0:T(8,128)(2,1)}, bf16[1088,768]{1,0:T(8,128)(2,1)}, bf16[1088,768]{1,0:T(8,128)(2,1)}, bf16[1088,384]{1,0:T(8,128)(2,1)}) custom-call(s32[2]{0:T(128)} %pad_add_fusion.len_ref, bf16[32,2,32,768]{3,2,1,0:T(8,128)(2,1)} %all-to-all-done.tok_ref, bf16[768,3456]{1,0:T(8,128)(2,1)} %bitcast.48), custom_call_target="tpu_custom_call" | custom-call | flops 20000000000 | bytes 12000000 | tf_op jit(solution)/shard_map/attn_fwd/pallas_call | solution.py:471
  141.3 25.4 %attn_fwd.3 = (bf16[1088,384]{1,0:T(8,128)(2,1)}, bf16[1088,768]{1,0:T(8,128)(2,1)}, bf16[1088,768]{1,0:T(8,128)(2,1)}, bf16[1088,768]{1,0:T(8,128)(2,1)}, bf16[1088,384]{1,0:T(8,128)(2,1)}) custom-call(s32[2]{0:T(128)} %pad_add_fusion.len_ref, bf16[32,2,32,768]{3,2,1,0:T(8,128)(2,1)} %all-to-all-done.tok_ref, bf16[768,3456]{1,0:T(8,128)(2,1)} %bitcast.49), custom_call_target="tpu_custom_call" | custom-call | flops 20000000000 | bytes 12000000 | tf_op jit(solution)/shard_map/attn_fwd/pallas_call | solution.py:471
  166.8 20.0 %mid_fwd.1 = (bf16[32,2,32,768]{3,2,1,0:T(8,128)(2,1)}, f32[1088,768]{1,0:T(8,128)}, f32[1088,768]{1,0:T(8,128)}, f32[1088,128]{1,0:T(8,128)}, f32[1088,3072]{1,...) custom-call(s32[2]{0:T(128)} %pad_add_fusion.len_ref, bf16[1088,384]{1,0:T(8,128)(2,1)} %get-tuple-element.101.x0_ref.x_ref, ...), custom_call_target="tpu_custom_call" | custom-call | flops 15000000512 | bytes 36000000 | tf_op jit(solution)/shard_map/mid_fwd/pallas_call | solution.py:548
  187.7 1.7 copy-done.2
  189.4 5.1 %all-to-all-start.2 = ((bf16[32,2,32,768]{3,2,1,0:T(8,128)(2,1)}), bf16[32,2,32,768]{3,2,1,0:T(8,128)(2,1)S(1)}, u32[]{:S(2)}, u32[]{:S(2)}) async-start(bf16[32,2,32,768]{3,2,1,0:T(8,128)(2,1)} %get-tuple-element.121), calls=%async_computation.2 | async-start | bytes 6291456 | tf_op jit(solution)/shard_map/all_to_all | solution.py:956
  194.5 32.6 %mid_bwd.1 = (bf16[1088,768]{1,0:T(8,128)(2,1)}, f32[1088,768]{1,0:T(8,128)}, bf16[2,192,2688]{2,1,0:T(8,128)(2,1)}, bf16[2,192,2688]{2,1,0:T(8,128)(2,1)}) custom-call(s32[2]{0:T(128)} %pad_add_fusion.len_ref, bf16[32,2,32,768]{3,2,1,0:T(8,128)(2,1)} %copy-done.2, bf16[1088,384]{1,0:T(8,128)(2,1)} %get-tuple-element.99.ctx0_ref.ctx_ref, ...), custom_call_target="tpu_custom_call" | custom-call | flops 100000000 | bytes 1000000 | tf_op jit(solution)/shard_map/mid_bwd/pallas_call | solution.py:577
  227.3 4.3 %collective-permute-done = bf16[2,192,2688]{2,1,0:T(8,128)(2,1)} collective-permute-done((bf16[2,192,2688]{2,1,0:T(8,128)(2,1)}, bf16[2,192,2688]{2,1,0:T(8,128)(2,1)}, u32[]{:S(2)}, u32[]{:S(2)}) %collective-permute-start) | collective-permute-done | bytes 2064416 | tf_op jit(solution)/shard_map/ppermute | solution.py:1043
  231.6 2.7 add_convert_fusion
  235.7 1.6 collective-permute-start.1
  239.2 34.1 %attn_bwd.2 = (bf16[32,2,32,384]{3,2,1,0:T(8,128)(2,1)}, bf16[1,192,768]{2,1,0:T(8,128)(2,1)}, bf16[1,192,768]{2,1,0:T(8,128)(2,1)}) custom-call(s32[2]{0:T(128)} %pad_add_fusion.len_ref, bf16[1088,768]{1,0:T(8,128)(2,1)} %get-tuple-element.96.qa_ref, bf16[1088,768]{1,0:T(8,128)(2,1)} %get-tuple-element.97.ka_ref, ...), custom_call_target="tpu_custom_call" | custom-call | flops 100000000 | bytes 1000000 | tf_op jit(solution)/shard_map/attn_bwd/pallas_call | solution.py:505
  273.4 5.8 %all-to-all-start.3 = ((bf16[32,2,32,384]{3,2,1,0:T(8,128)(2,1)}), bf16[32,2,32,384]{3,2,1,0:T(8,128)(2,1)}, u32[]{:S(2)}, u32[]{:S(2)}) async-start(bf16[32,2,32,384]{3,2,1,0:T(8,128)(2,1)} %get-tuple-element.134), calls=%async_computation.3 | async-start | bytes 3145728 | tf_op jit(solution)/shard_map/all_to_all | solution.py:956
  279.5 1.8 add_convert_fusion.1
  281.3 1.7 collective-permute-start.5
  283.0 2.4 collective-permute-start.6
  288.2 33.9 %attn_bwd.3 = (bf16[32,2,32,384]{3,2,1,0:T(8,128)(2,1)}, bf16[1,192,768]{2,1,0:T(8,128)(2,1)}, bf16[1,192,768]{2,1,0:T(8,128)(2,1)}) custom-call(s32[2]{0:T(128)} %pad_add_fusion.len_ref, bf16[1088,768]{1,0:T(8,128)(2,1)} %get-tuple-element.125.qa_ref, bf16[1088,768]{1,0:T(8,128)(2,1)} %get-tuple-element.126.ka_ref, ...), custom_call_target="tpu_custom_call" | custom-call | flops 100000000 | bytes 1000000 | tf_op jit(solution)/shard_map/attn_bwd/pallas_call | solution.py:505
  322.1 3.2 collective-permute-done.6
  325.4 6.0 %all-to-all-start.4 = ((bf16[32,2,32,384]{3,2,1,0:T(8,128)(2,1)}), bf16[32,2,32,384]{3,2,1,0:T(8,128)(2,1)S(1)}, u32[]{:S(2)}, u32[]{:S(2)}) async-start(bf16[32,2,32,384]{3,2,1,0:T(8,128)(2,1)} %get-tuple-element.145), calls=%async_computation.4 | async-start | bytes 3145728 | tf_op jit(solution)/shard_map/all_to_all | solution.py:956
  336.4 2.6 collective-permute-start.11
  341.4 13.2 %collective-permute-done.11 = bf16[1,4,1,24,768]{4,3,2,1,0:T(8,128)(2,1)S(1)} collective-permute-done((bf16[1,4,1,24,768]{4,3,2,1,0:T(8,128)(2,1)S(1)}, bf16[1,4,1,24,768]{4,3,2,1,0:T(8,128)(2,1)S(1)}, u32[]{:S(2)}, u32[]{:S(2)}) %collective-permute-start.11) | collective-permute-done | bytes 147488 | tf_op jit(solution)/shard_map/ppermute | solution.py:988
  356.3 2.7 collective-permute-start.14
  360.4 4.9 %restore.2 = bf16[64,32,768]{2,1,0:T(8,128)(2,1)} custom-call(s32[64]{0:T(128)} %len_ref.7, s32[64]{0:T(128)} %perm_ref.7, bf16[64,32,768]{2,1,0:T(8,128)(2,1)} %bitcast.54), custom_call_target="tpu_custom_call" | custom-call | bytes 100000 | tf_op jit(solution)/shard_map/restore/pallas_call | solution.py:851
  365.9 6.0 %collective-permute-done.13 = bf16[24,768]{1,0:T(8,128)(2,1)S(1)} collective-permute-done((bf16[24,768]{1,0:T(8,128)(2,1)S(1)}, bf16[24,768]{1,0:T(8,128)(2,1)S(1)}, u32[]{:S(2)}, u32[]{:S(2)}) %collective-permute-start.13) | collective-permute-done | bytes 36896 | tf_op jit(solution)/shard_map/ppermute | solution.py:988
  374.6 4.9 %restore.3 = bf16[64,32,768]{2,1,0:T(8,128)(2,1)} custom-call(s32[64]{0:T(128)} %len_ref.7, s32[64]{0:T(128)} %perm_ref.7, bf16[64,32,384]{2,1,0:T(8,128)(2,1)} %bitcast.19.refs_0_, bf16[64,32,384]{2,1,0:T(8,128)(2,1)} %bitcast.57), custom_call_target="tpu_custom_call" | custom-call | bytes 100000 | tf_op jit(solution)/shard_map/restore/pallas_call | solution.py:851
  (77 shorter events, 26.3 us)
Async XLA Ops:
  24.8 80.8 %all-to-all-start = ((bf16[32,2,32,768]{3,2,1,0:T(8,128)(2,1)}), bf16[32,2,32,768]{3,2,1,0:T(8,128)(2,1)}, u32[]{:S(2)}, u32[]{:S(2)}) async-start(bf16[32,2,32,768]{3,2,1,0:T(8,128)(2,1)} %bitcast.55), calls=%async_computation | async-start | bytes 6291456 | tf_op jit(solution)/shard_map/all_to_all | solution.py:956
  98.4 2.3 copy-start.6
  98.4 2.3 copy-start
  105.7 82.0 %all-to-all-start.1 = ((bf16[32,2,32,768]{3,2,1,0:T(8,128)(2,1)}), bf16[32,2,32,768]{3,2,1,0:T(8,128)(2,1)S(1)}, u32[]{:S(2)}, u32[]{:S(2)}) async-start(bf16[32,2,32,768]{3,2,1,0:T(8,128)(2,1)} %bitcast.15), calls=%async_computation.1 | async-start | bytes 6291456 | tf_op jit(solution)/shard_map/all_to_all | solution.py:956
  187.7 1.7 copy-start.2
  189.4 84.0 %all-to-all-start.2 = ((bf16[32,2,32,768]{3,2,1,0:T(8,128)(2,1)}), bf16[32,2,32,768]{3,2,1,0:T(8,128)(2,1)S(1)}, u32[]{:S(2)}, u32[]{:S(2)}) async-start(bf16[32,2,32,768]{3,2,1,0:T(8,128)(2,1)} %get-tuple-element.121), calls=%async_computation.2 | async-start | bytes 6291456 | tf_op jit(solution)/shard_map/all_to_all | solution.py:956
  227.1 4.5 %collective-permute-start = (bf16[2,192,2688]{2,1,0:T(8,128)(2,1)}, bf16[2,192,2688]{2,1,0:T(8,128)(2,1)}, u32[]{:S(2)}, u32[]{:S(2)}) collective-permute-start(bf16[2,192,2688]{2,1,0:T(8,128)(2,1)} %get-tuple-element.115), channel_id=1, source_target_pairs={{0,8},{8,0},{16,24},{24,16},{1,9},{9,1},{17,25},{25,17},{2,10},{10... | collective-permute-start | bytes 6193160 | tf_op jit(solution)/shard_map/ppermute | solution.py:1043
  235.7 37.6 %collective-permute-start.1 = (bf16[1,4,1,24,2688]{4,3,2,1,0:T(8,128)(2,1)}, bf16[1,4,1,24,2688]{4,3,2,1,0:T(8,128)(2,1)}, u32[]{:S(2)}, u32[]{:S(2)}) collective-permute-start(bf16[1,4,1,24,2688]{4,3,2,1,0:T(8,128)(2,1)} %get-tuple-element.202), channel_id=1, source_target_pairs={{0,1},{1,0},{2,3},{3,2},{4,5},{5,4},{6,7},{7,6},{8,9},{9,8},{10,11... | collective-permute-start | bytes 1548296 | tf_op jit(solution)/shard_map/ppermute | solution.py:988
  237.3 36.0 %collective-permute-start.2 = (bf16[1,4,1,24,2688]{4,3,2,1,0:T(8,128)(2,1)}, bf16[1,4,1,24,2688]{4,3,2,1,0:T(8,128)(2,1)}, u32[]{:S(2)}, u32[]{:S(2)}) collective-permute-start(bf16[1,4,1,24,2688]{4,3,2,1,0:T(8,128)(2,1)} %get-tuple-element.201), channel_id=1, source_target_pairs={{0,16},{1,17},{2,18},{3,19},{4,20},{5,21},{6,22},{7,23},{8,24},{9,... | collective-permute-start | bytes 1548296 | tf_op jit(solution)/shard_map/ppermute | solution.py:988
  238.8 34.5 %collective-permute-start.3 = (bf16[1,4,1,24,2688]{4,3,2,1,0:T(8,128)(2,1)}, bf16[1,4,1,24,2688]{4,3,2,1,0:T(8,128)(2,1)}, u32[]{:S(2)}, u32[]{:S(2)}) collective-permute-start(bf16[1,4,1,24,2688]{4,3,2,1,0:T(8,128)(2,1)} %get-tuple-element.200), channel_id=1, source_target_pairs={{0,17},{1,16},{2,19},{3,18},{4,21},{5,20},{6,23},{7,22},{8,25},{9,... | collective-permute-start | bytes 1548296 | tf_op jit(solution)/shard_map/ppermute | solution.py:988
  273.3 7.9 %copy-start.1 = (bf16[32,2,32,768]{3,2,1,0:T(8,128)(2,1)}, bf16[32,2,32,768]{3,2,1,0:T(8,128)(2,1)S(1)}, u32[]{:S(2)}) copy-start(bf16[32,2,32,768]{3,2,1,0:T(8,128)(2,1)S(1)} %all-to-all-done.2) | copy-start | bytes 9437188
  273.4 52.0 %all-to-all-start.3 = ((bf16[32,2,32,384]{3,2,1,0:T(8,128)(2,1)}), bf16[32,2,32,384]{3,2,1,0:T(8,128)(2,1)}, u32[]{:S(2)}, u32[]{:S(2)}) async-start(bf16[32,2,32,384]{3,2,1,0:T(8,128)(2,1)} %get-tuple-element.134), calls=%async_computation.3 | async-start | bytes 3145728 | tf_op jit(solution)/shard_map/all_to_all | solution.py:956
  279.3 46.1 %collective-permute-start.4 = (bf16[1,192,768]{2,1,0:T(8,128)(2,1)}, bf16[1,192,768]{2,1,0:T(8,128)(2,1)}, u32[]{:S(2)}, u32[]{:S(2)}) collective-permute-start(bf16[1,192,768]{2,1,0:T(8,128)(2,1)} %get-tuple-element.132), channel_id=1, source_target_pairs={{0,8},{8,0},{16,24},{24,16},{1,9},{9,1},{17,25},{25,17},{2,10},{10... | collective-permute-start | bytes 884744 | tf_op jit(solution)/shard_map/ppermute | solution.py:1051
  281.3 40.8 %collective-permute-start.5 = (bf16[24,2688]{1,0:T(8,128)(2,1)S(1)}, bf16[24,2688]{1,0:T(8,128)(2,1)S(1)}, u32[]{:S(2)}, u32[]{:S(2)}) collective-permute-start(bf16[24,2688]{1,0:T(8,128)(2,1)S(1)} %get-tuple-element.209), channel_id=1, source_target_pairs={{0,2},{1,3},{2,4},{3,5},{4,6},{5,7},{6,0},{7,1},{8,10},{9,11},{10,... | collective-permute-start | bytes 387080 | tf_op jit(solution)/shard_map/ppermute | solution.py:988
  283.0 42.3 %collective-permute-start.6 = (bf16[24,2688]{1,0:T(8,128)(2,1)S(1)}, bf16[24,2688]{1,0:T(8,128)(2,1)S(1)}, u32[]{:S(2)}, u32[]{:S(2)}) collective-permute-start(bf16[24,2688]{1,0:T(8,128)(2,1)S(1)} %get-tuple-element.208), channel_id=1, source_target_pairs={{0,4},{1,5},{2,6},{3,7},{4,0},{5,1},{6,2},{7,3},{8,12},{9,13},{10,... | collective-permute-start | bytes 387080 | tf_op jit(solution)/shard_map/ppermute | solution.py:988
  285.5 39.9 %collective-permute-start.7 = (bf16[24,2688]{1,0:T(8,128)(2,1)S(1)}, bf16[24,2688]{1,0:T(8,128)(2,1)S(1)}, u32[]{:S(2)}, u32[]{:S(2)}) collective-permute-start(bf16[24,2688]{1,0:T(8,128)(2,1)S(1)} %get-tuple-element.207), channel_id=1, source_target_pairs={{0,6},{1,7},{2,0},{3,1},{4,2},{5,3},{6,4},{7,5},{8,14},{9,15},{10,... | collective-permute-start | bytes 387080 | tf_op jit(solution)/shard_map/ppermute | solution.py:988
  322.1 9.7 %copy-start.7 = (f32[8,128]{1,0:T(8,128)S(1)}, f32[8,128]{1,0:T(8,128)}, u32[]{:S(2)}) copy-start(f32[8,128]{1,0:T(8,128)} %get-tuple-element.155) | copy-start | bytes 12292
  325.4 9.8 %copy-start.4 = (bf16[1,192,768]{2,1,0:T(8,128)(2,1)S(1)}, bf16[1,192,768]{2,1,0:T(8,128)(2,1)}, u32[]{:S(2)}) copy-start(bf16[1,192,768]{2,1,0:T(8,128)(2,1)} %get-tuple-element.146) | copy-start | bytes 884740
  325.4 48.0 %all-to-all-start.4 = ((bf16[32,2,32,384]{3,2,1,0:T(8,128)(2,1)}), bf16[32,2,32,384]{3,2,1,0:T(8,128)(2,1)S(1)}, u32[]{:S(2)}, u32[]{:S(2)}) async-start(bf16[32,2,32,384]{3,2,1,0:T(8,128)(2,1)} %get-tuple-element.145), calls=%async_computation.4 | async-start | bytes 3145728 | tf_op jit(solution)/shard_map/all_to_all | solution.py:956
  331.4 4.9 %copy-start.5 = (bf16[1,192,768]{2,1,0:T(8,128)(2,1)S(1)}, bf16[1,192,768]{2,1,0:T(8,128)(2,1)}, u32[]{:S(2)}) copy-start(bf16[1,192,768]{2,1,0:T(8,128)(2,1)} %get-tuple-element.148) | copy-start | bytes 884740
  331.4 4.8 %collective-permute-start.8 = (bf16[1,192,768]{2,1,0:T(8,128)(2,1)}, bf16[1,192,768]{2,1,0:T(8,128)(2,1)S(1)}, u32[]{:S(2)}, u32[]{:S(2)}) collective-permute-start(bf16[1,192,768]{2,1,0:T(8,128)(2,1)} %get-tuple-element.149), channel_id=1, source_target_pairs={{0,8},{8,0},{16,24},{24,16},{1,9},{9,1},{17,25},{25,17},{2,10},{10... | collective-permute-start | bytes 884744 | tf_op jit(solution)/shard_map/ppermute | solution.py:1060
  336.4 18.1 %collective-permute-start.11 = (bf16[1,4,1,24,768]{4,3,2,1,0:T(8,128)(2,1)S(1)}, bf16[1,4,1,24,768]{4,3,2,1,0:T(8,128)(2,1)S(1)}, u32[]{:S(2)}, u32[]{:S(2)}) collective-permute-start(bf16[1,4,1,24,768]{4,3,2,1,0:T(8,128)(2,1)S(1)} %get-tuple-element.205), channel_id=1, source_target_pairs={{0,17},{1,16},{2,19},{3,18},{4,21},{5,20},{6,23},{7,22},{8,25},{9,... | collective-permute-start | bytes 442376 | tf_op jit(solution)/shard_map/ppermute | solution.py:988
  339.0 16.9 %collective-permute-start.10 = (bf16[1,4,1,24,768]{4,3,2,1,0:T(8,128)(2,1)S(1)}, bf16[1,4,1,24,768]{4,3,2,1,0:T(8,128)(2,1)S(1)}, u32[]{:S(2)}, u32[]{:S(2)}) collective-permute-start(bf16[1,4,1,24,768]{4,3,2,1,0:T(8,128)(2,1)S(1)} %get-tuple-element.206), channel_id=1, source_target_pairs={{0,16},{1,17},{2,18},{3,19},{4,20},{5,21},{6,22},{7,23},{8,24},{9,... | collective-permute-start | bytes 442376 | tf_op jit(solution)/shard_map/ppermute | solution.py:988
  339.6 16.6 %collective-permute-start.9 = (bf16[1,4,1,24,768]{4,3,2,1,0:T(8,128)(2,1)S(1)}, bf16[1,4,1,24,768]{4,3,2,1,0:T(8,128)(2,1)S(1)}, u32[]{:S(2)}, u32[]{:S(2)}) collective-permute-start(bf16[1,4,1,24,768]{4,3,2,1,0:T(8,128)(2,1)S(1)} %get-tuple-element.204), channel_id=1, source_target_pairs={{0,1},{1,0},{2,3},{3,2},{4,5},{5,4},{6,7},{7,6},{8,9},{9,8},{10,11... | collective-permute-start | bytes 442376 | tf_op jit(solution)/shard_map/ppermute | solution.py:988
  356.3 9.6 %collective-permute-start.14 = (bf16[24,768]{1,0:T(8,128)(2,1)S(1)}, bf16[24,768]{1,0:T(8,128)(2,1)S(1)}, u32[]{:S(2)}, u32[]{:S(2)}) collective-permute-start(bf16[24,768]{1,0:T(8,128)(2,1)S(1)} %get-tuple-element.214), channel_id=1, source_target_pairs={{0,6},{1,7},{2,0},{3,1},{4,2},{5,3},{6,4},{7,5},{8,14},{9,15},{10,... | collective-permute-start | bytes 110600 | tf_op jit(solution)/shard_map/ppermute | solution.py:988
  359.0 13.0 %collective-permute-start.13 = (bf16[24,768]{1,0:T(8,128)(2,1)S(1)}, bf16[24,768]{1,0:T(8,128)(2,1)S(1)}, u32[]{:S(2)}, u32[]{:S(2)}) collective-permute-start(bf16[24,768]{1,0:T(8,128)(2,1)S(1)} %get-tuple-element.215), channel_id=1, source_target_pairs={{0,4},{1,5},{2,6},{3,7},{4,0},{5,1},{6,2},{7,3},{8,12},{9,13},{10,... | collective-permute-start | bytes 110600 | tf_op jit(solution)/shard_map/ppermute | solution.py:988
  359.0 13.0 %collective-permute-start.12 = (bf16[24,768]{1,0:T(8,128)(2,1)S(1)}, bf16[24,768]{1,0:T(8,128)(2,1)S(1)}, u32[]{:S(2)}, u32[]{:S(2)}) collective-permute-start(bf16[24,768]{1,0:T(8,128)(2,1)S(1)} %get-tuple-element.213), channel_id=1, source_target_pairs={{0,2},{1,3},{2,4},{3,5},{4,6},{5,7},{6,0},{7,1},{8,10},{9,11},{10,... | collective-permute-start | bytes 110600 | tf_op jit(solution)/shard_map/ppermute | solution.py:988
  373.4 1.2 copy-start.3
